TPU v7x, 256 devices: a whole 4x4x8 slice. The times are simulated.
256 devices in a mesh: depth: 8 (over y, core), lat: 32 (over x, z).
Axes of the slice: x: 4, y: 4, z: 8, core: 2. Of those that a mesh axis runs over, the one named last changes fastest.
Arguments:
- volume: float32 [256, 512, 128], P('depth', 'lat'), may hold values from -6 to 6
Outputs:
- diffused: float32 [256, 512, 128], P('depth', 'lat')
All inputs are finite; a program needn't handle non-finite values.
Results may differ from a plain program's by a relative error of at most 0.0003.
Values sent between devices are 32-bit elements; how exact they have to be, the bound alone decides.
No kernel may reach another device: no remote copies, remote signals or barrier semaphores. Data moves between devices by JAX's collectives and lax.ppermute only.
A program may use at most 64 MiB of HBM per device.

v0:
```python
import jax
import jax.numpy as jnp
from jax import lax
from jax.sharding import PartitionSpec as P

TAU = 300.0
LAMBDA = 0.5


def with_halo(block, sides, width):
    for axis, dim in sides:
        count = lax.axis_size(axis)
        forward = [(i, i + 1) for i in range(count - 1)]
        backward = [(target, source) for source, target in forward]
        low = lax.ppermute(
            lax.slice_in_dim(block, block.shape[dim] - width, None, axis=dim), axis, forward
        )
        high = lax.ppermute(lax.slice_in_dim(block, 0, width, axis=dim), axis, backward)
        block = jnp.concatenate([low, block, high], axis=dim)
    return block


def conductance(diff):
    ratio = diff / LAMBDA
    return 1.0 / (1.0 + ratio * ratio)


def shifted(field, shift_by, axis, fill):
    length = field.shape[axis]
    widths = [(0, 0)] * field.ndim
    if shift_by > 0:
        widths[axis] = (shift_by, 0)
        padded = jnp.pad(field, widths, constant_values=fill)
        return lax.slice_in_dim(padded, 0, length, axis=axis)
    widths[axis] = (0, -shift_by)
    padded = jnp.pad(field, widths, constant_values=fill)
    return lax.slice_in_dim(padded, -shift_by, length - shift_by, axis=axis)


def smooth_padded(field, axis):
    return 0.25 * (shifted(field, 1, axis, 0.0) + 2.0 * field + shifted(field, -1, axis, 0.0))


def smooth_valid(field, axis):
    length = field.shape[axis]
    before = lax.slice_in_dim(field, 0, length - 2, axis=axis)
    middle = lax.slice_in_dim(field, 1, length - 1, axis=axis)
    after = lax.slice_in_dim(field, 2, length, axis=axis)
    return 0.25 * (before + 2.0 * middle + after)


def edge_mask(count, index, total, axis):
    edges = index * count + jnp.arange(count + 1, dtype=jnp.int32) - 1
    valid = jnp.logical_and(edges >= 0, edges <= count * total - 2).astype(jnp.float32)
    shape = [1, 1, 1]
    shape[axis] = count + 1
    return valid.reshape(shape)


def cyclic_solve(lower, diag, upper, sources, axis):
    length = diag.shape[axis]
    offset = 1
    while offset < length:
        low_prev = shifted(lower, offset, axis, 0.0)
        diag_prev = shifted(diag, offset, axis, 1.0)
        up_prev = shifted(upper, offset, axis, 0.0)
        low_next = shifted(lower, -offset, axis, 0.0)
        diag_next = shifted(diag, -offset, axis, 1.0)
        up_next = shifted(upper, -offset, axis, 0.0)
        left_factor = -lower / diag_prev
        right_factor = -upper / diag_next
        sources = tuple(
            (
                source
                + left_factor * shifted(source, offset, axis, 0.0)
                + right_factor * shifted(source, -offset, axis, 0.0)
                for source in sources
            )
        )
        diag = diag + left_factor * up_prev + right_factor * low_next
        lower = left_factor * low_prev
        upper = right_factor * up_next
        offset = offset * 2
    return tuple((source / diag for source in sources))


def line_coefficients(forward, axis):
    lower = -3.0 * TAU * shifted(forward, 1, axis, 0.0)
    upper = -3.0 * TAU * forward
    return (lower, 1.0 - lower - upper, upper)


def local_spike(edges, field, axis):
    count = field.shape[axis]
    inner_lower = -3.0 * TAU * lax.slice_in_dim(edges, 0, count, axis=axis)
    inner_upper = -3.0 * TAU * lax.slice_in_dim(edges, 1, count + 1, axis=axis)
    diag = 1.0 - inner_lower - inner_upper
    shape = [1, 1, 1]
    shape[axis] = count
    position = jnp.arange(count, dtype=jnp.int32).reshape(shape)
    is_first = position == 0
    is_last = position == count - 1
    lower = jnp.where(is_first, 0.0, inner_lower)
    upper = jnp.where(is_last, 0.0, inner_upper)
    left_source = jnp.where(is_first, inner_lower, 0.0)
    right_source = jnp.where(is_last, inner_upper, 0.0)
    particular, left_spike, right_spike = cyclic_solve(
        lower, diag, upper, (field, left_source, right_source), axis
    )
    ends = []
    for solved in (particular, left_spike, right_spike):
        ends.append(lax.index_in_dim(solved, 0, axis, keepdims=False))
        ends.append(lax.index_in_dim(solved, count - 1, axis, keepdims=False))
    return (particular, left_spike, right_spike, jnp.stack(ends, axis=0)[None])


def reduced_solve(gathered):

    def sweep_down(carry, block):
        chain_prev, carry_last = carry
        first_val = block[0]
        last_val = block[1]
        left_first = block[2]
        left_last = block[3]
        right_first = block[4]
        right_last = block[5]
        pivot = 1.0 - left_first * chain_prev
        result_first = (first_val - left_first * carry_last) / pivot
        result_last = last_val - left_last * carry_last + left_last * chain_prev * result_first
        factor_first = right_first / pivot
        chain_new = right_last + left_last * chain_prev * factor_first
        return ((chain_new, result_last), (factor_first, chain_new, result_first, result_last))

    zero_lines = jnp.zeros_like(gathered[0, 0])
    _, factors = lax.scan(sweep_down, (zero_lines, zero_lines), gathered)

    def sweep_up(first_later, block):
        factor_first, chain_new, result_first, result_last = block
        first_here = result_first - factor_first * first_later
        last_here = result_last - chain_new * first_later
        return (first_here, (first_here, last_here))

    _, (firsts, lasts) = lax.scan(sweep_up, zero_lines, factors, reverse=True)
    return (firsts, lasts)


def spike_finish(particular, left_spike, right_spike, firsts, lasts, index, total, axis):
    last_prev = lax.dynamic_index_in_dim(lasts, jnp.maximum(index - 1, 0), 0, keepdims=False)
    first_next = lax.dynamic_index_in_dim(
        firsts, jnp.minimum(index + 1, total - 1), 0, keepdims=False
    )
    return (
        particular
        - left_spike * jnp.expand_dims(last_prev, axis)
        - right_spike * jnp.expand_dims(first_next, axis)
    )


def shards(volume):
    depth_total = lax.axis_size("depth")
    depth_index = lax.axis_index("depth")
    lat_total = lax.axis_size("lat")
    lat_index = lax.axis_index("lat")
    planes, rows, columns = volume.shape
    padded = with_halo(volume, (("depth", 0), ("lat", 1)), 2)
    smoothed = smooth_padded(padded, 2)
    smoothed = smooth_valid(smoothed, 1)
    smoothed = smooth_valid(smoothed, 0)
    core = smoothed[1:-1, 1:-1]
    cond_x = jnp.pad(conductance(core[:, :, 1:] - core[:, :, :-1]), ((0, 0), (0, 0), (0, 1)))
    band_y = smoothed[1:-1]
    cond_y = conductance(band_y[:, 1:] - band_y[:, :-1]) * edge_mask(rows, lat_index, lat_total, 1)
    band_z = smoothed[:, 1:-1]
    cond_z = conductance(band_z[1:] - band_z[:-1]) * edge_mask(planes, depth_index, depth_total, 0)
    lower_x, diag_x, upper_x = line_coefficients(cond_x, 2)
    (solved_x,) = cyclic_solve(lower_x, diag_x, upper_x, (volume,), 2)
    field = lax.all_to_all(volume, "lat", split_axis=2, concat_axis=1, tiled=True)
    forward = lax.all_to_all(cond_y[:, 1:], "lat", split_axis=2, concat_axis=1, tiled=True)
    count, length, width = field.shape
    flat_field = jnp.transpose(field, (1, 0, 2)).reshape(length, count * width)
    flat_forward = jnp.transpose(forward, (1, 0, 2)).reshape(length, count * width)
    lower, diag, upper = line_coefficients(flat_forward, 0)
    (solved,) = cyclic_solve(lower, diag, upper, (flat_field,), 0)
    returned = jnp.transpose(solved.reshape(length, count, width), (1, 0, 2))
    solved_y = lax.all_to_all(returned, "lat", split_axis=1, concat_axis=2, tiled=True)
    part_z, left_z, right_z, ends_z = local_spike(cond_z, volume, 0)
    gathered_z = lax.all_gather(ends_z, "depth", axis=0, tiled=True)
    firsts_z, lasts_z = reduced_solve(gathered_z)
    solved_z = spike_finish(part_z, left_z, right_z, firsts_z, lasts_z, depth_index, depth_total, 0)
    return (solved_x + solved_y + solved_z) / 3.0


def solution(mesh):
    placed = (P("depth", "lat", None),)
    return jax.shard_map(
        shards, mesh=mesh, in_specs=placed, out_specs=P("depth", "lat", None), check_vma=False
    )
```

profile of v0, /device:TPU:8, one launch (start us, length us, event | category | flops | bytes accessed | tf_op | source)
XLA Modules:
  0.0 110.5 jit_solution(14266920727948924884)
XLA Ops:
  0.0 0.7 fusion.377
  0.7 1.9 %collective-permute-start.1 = (f32[2,16,128]{2,1,0:T(8,128)S(1)}, f32[2,16,128]{2,1,0:T(8,128)S(1)}, u32[]{:S(2)}, u32[]{:S(2)}) collective-permute-start(f32[2,16,128]{2,1,0:T(8,128)S(1)} %get-tuple-element.424), channel_id=1, source_target_pairs={{32,0},{64,32},{96,64},{128,96},{160,128},{192,160},{224,192},{33,... | collective-permute-start | bytes 49160 | tf_op jit(solution)/shard_map/ppermute | solution.py:18
  2.7 2.4 %collective-permute-start = (f32[2,16,128]{2,1,0:T(8,128)S(1)}, f32[2,16,128]{2,1,0:T(8,128)S(1)}, u32[]{:S(2)}, u32[]{:S(2)}) collective-permute-start(f32[2,16,128]{2,1,0:T(8,128)S(1)} %get-tuple-element.423), channel_id=1, source_target_pairs={{0,32},{32,64},{64,96},{96,128},{128,160},{160,192},{192,224},{1,3... | collective-permute-start | bytes 49160 | tf_op jit(solution)/shard_map/ppermute | solution.py:15
  5.1 1.5 %copy.156 = f32[32,16,128]{0,1,2:T(8,128)S(1)} copy(f32[32,16,128]{2,1,0:T(8,128)} %param.5) | data formatting | bytes 524288 | tf_op args[0]
  6.5 1.2 %reshape.56 = f32[32,1,2048]{2,1,0:T(1,128)} reshape(f32[128,16,32]{2,1,0:T(8,128)S(1)} %bitcast.134) | data formatting | bytes 524288
  7.7 11.4 %all-to-all-start = ((f32[32,1,2048]{2,1,0:T(1,128)}), f32[32,1,2048]{2,1,0:T(1,128)S(1)}, u32[]{:S(2)}, u32[]{:S(2)}) async-start(f32[32,1,2048]{2,1,0:T(1,128)} %reshape.56), calls=%async_computation | async-start | bytes 524288 | tf_op jit(solution)/shard_map/all_to_all | solution.py:177
  19.3 3.7 %collective-permute-start.2 = (f32[36,2,128]{2,0,1:T(8,128)S(1)}, f32[36,2,128]{2,0,1:T(8,128)S(1)}, u32[]{:S(2)}, u32[]{:S(2)}) collective-permute-start(f32[36,2,128]{2,0,1:T(8,128)S(1)} %copy.177), channel_id=1, source_target_pairs={{0,1},{1,2},{2,3},{3,4},{4,5},{5,6},{6,7},{7,8},{8,9},{9,10},{10,1... | collective-permute-start | bytes 110600 | tf_op jit(solution)/shard_map/ppermute | solution.py:15
  23.2 1.3 %collective-permute-start.3 = (f32[36,2,128]{2,0,1:T(8,128)S(1)}, f32[36,2,128]{2,0,1:T(8,128)S(1)}, u32[]{:S(2)}, u32[]{:S(2)}) collective-permute-start(f32[36,2,128]{2,0,1:T(8,128)S(1)} %copy.178), channel_id=1, source_target_pairs={{1,0},{2,1},{3,2},{4,3},{5,4},{6,5},{7,6},{8,7},{9,8},{10,9},{11,1... | collective-permute-start | bytes 110600 | tf_op jit(solution)/shard_map/ppermute | solution.py:18
  24.5 0.9 collective-permute-done.2
  25.5 3.6 %collective-permute-done.3 = f32[36,2,128]{2,0,1:T(8,128)S(1)} collective-permute-done((f32[36,2,128]{2,0,1:T(8,128)S(1)}, f32[36,2,128]{2,0,1:T(8,128)S(1)}, u32[]{:S(2)}, u32[]{:S(2)}) %collective-permute-start.3) | collective-permute-done | bytes 36896 | tf_op jit(solution)/shard_map/ppermute | solution.py:18
  30.0 0.5 copy.159
  30.5 1.2 %reshape.58 = f32[32,1,2048]{2,1,0:T(1,128)} reshape(f32[128,16,32]{2,1,0:T(8,128)S(1)} %bitcast.132) | data formatting | bytes 524288
  32.0 0.3 fusion.167
  32.3 0.3 fusion.120
  34.6 13.2 %all-gather = f32[48,16,128]{2,1,0:T(8,128)S(1)} all-gather(f32[6,16,128]{2,1,0:T(8,128)S(1)} %constant_dynamic-update-slice_fusion.3), channel_id=2, replica_groups=mesh['depth'=8,'lat'=32] {'depth'}, dimensions={0}, use_global_device_ids=true | all-gather | bytes 442368 | tf_op jit(solution)/shard_map/all_gather | solution.py:187
  47.9 0.4 while.40
  48.4 0.3 while.41
  48.7 0.7 fusion.239
  49.5 0.7 fusion.244
  50.1 0.3 fusion.251
  50.5 0.6 fusion.256
  51.1 0.3 fusion.263
  51.5 0.6 fusion.268
  52.1 0.3 fusion.275
  52.5 0.7 copy-done.6
  53.1 10.1 %all-to-all-start.1 = ((f32[32,1,2048]{2,1,0:T(1,128)}), f32[32,1,2048]{2,1,0:T(1,128)}, u32[]{:S(2)}, u32[]{:S(2)}) async-start(f32[32,1,2048]{2,1,0:T(1,128)} %reshape.58), calls=%async_computation.1 | async-start | bytes 524288 | tf_op jit(solution)/shard_map/all_to_all | solution.py:178
  63.2 1.3 %fusion.280 = (f32[32,16,128]{2,0,1:T(8,128)}, f32[32,16,128]{2,0,1:T(8,128)S(1)}, f32[32,16,128]{2,0,1:T(8,128)S(1)}) fusion(f32[32,16,128]{2,0,1:T(8,128)S(1)} %get-tuple-element.323, f32[32,16,128]{2,0,1:T(8,128)S(1)} %fusion.275, f32[32,16,128]{2,0,1:T(8,128)S(1)} %get-tuple-element.324, f32[32,16,128]{2,0,1:T(8,128)S(1)} %fusion.263, ...), kind=kLoop, calls=%fused_computation.488 | loop fusion | flops 917504 | bytes 2097152 | tf_op jit(solution)/shard_map/add | solution.py:74
  64.6 0.3 fusion.287
  64.9 0.5 broadcast.603
  65.5 1.2 %reduce.1 = f32[32,2048]{1,0:T(8,128)S(1)} reduce(f32[32,1,2048]{2,1,0:T(1,128)S(1)} %copy-done.7, f32[]{:T(128)} %broadcast.603), dimensions={1}, to_apply=%all_to_all.39.reduce_sub_computation | reduce | bytes 524292 | tf_op jit(solution)/shard_map/all_to_all | solution.py:177
  66.7 0.3 reshape.57
  67.1 0.3 copy.158
  67.5 0.8 reshape.52
  68.2 7.4 %all-to-all-done.1 = f32[32,1,2048]{2,1,0:T(1,128)} async-done(((f32[32,1,2048]{2,1,0:T(1,128)}), f32[32,1,2048]{2,1,0:T(1,128)}, u32[]{:S(2)}, u32[]{:S(2)}) %all-to-all-start.1) | async-done | bytes 262176 | tf_op jit(solution)/shard_map/all_to_all | solution.py:178
  75.7 2.1 %reduce = f32[32,2048]{1,0:T(8,128)S(1)} reduce(f32[32,1,2048]{2,1,0:T(1,128)} %all-to-all-done.1, f32[]{:T(128)} %broadcast.603), dimensions={1}, to_apply=%all_to_all.43.reduce_sub_computation | reduce | bytes 524292 | tf_op jit(solution)/shard_map/all_to_all | solution.py:178
  77.8 0.3 reshape.59
  78.3 0.3 copy.161
  78.9 0.7 copy-done.5
  79.6 0.8 fusion.30
  80.4 0.7 fusion.35
  81.1 0.3 fusion.42
  81.5 0.6 fusion.47
  82.1 0.3 fusion.54
  82.5 0.6 fusion.59
  83.1 0.3 fusion.66
  83.4 0.6 fusion.71
  84.0 0.3 fusion.78
  84.4 0.6 fusion.83
  85.0 0.3 fusion.90
  85.4 0.6 fusion.95
  86.0 0.3 fusion.102
  86.4 0.4 fusion.107
  87.1 0.4 copy.162
  87.5 1.4 %reshape.60 = f32[32,1,2048]{2,1,0:T(1,128)} reshape(f32[512,4,32]{2,1,0:T(4,128)S(1)} %bitcast.133) | data formatting | bytes 524288
  88.9 5.1 %all-to-all-start.2 = ((f32[32,1,2048]{2,1,0:T(1,128)}), f32[32,1,2048]{2,1,0:T(1,128)S(1)}, u32[]{:S(2)}, u32[]{:S(2)}) async-start(f32[32,1,2048]{2,1,0:T(1,128)} %reshape.60), calls=%async_computation.2 | async-start | bytes 524288 | tf_op jit(solution)/shard_map/all_to_all | solution.py:185
  94.0 1.3 %fusion.292 = (f32[32,16,128]{2,0,1:T(8,128)}, f32[32,16,128]{2,0,1:T(8,128)S(1)}, f32[32,16,128]{2,0,1:T(8,128)S(1)}) fusion(f32[32,16,128]{2,0,1:T(8,128)S(1)} %copy-done.9, f32[32,16,128]{2,0,1:T(8,128)S(1)} %fusion.287, f32[32,16,128]{2,0,1:T(8,128)S(1)} %get-tuple-element.321, f32[32,16,128]{2,0,1:T(8,128)S(1)} %fusion.275, ...), kind=kLoop, calls=%fused_computation.500 | loop fusion | flops 917504 | bytes 2097152 | tf_op jit(solution)/shard_map/add | solution.py:74
  95.3 0.6 fusion.308
  95.9 10.2 %all-to-all-done.2 = f32[32,1,2048]{2,1,0:T(1,128)S(1)} async-done(((f32[32,1,2048]{2,1,0:T(1,128)}), f32[32,1,2048]{2,1,0:T(1,128)S(1)}, u32[]{:S(2)}, u32[]{:S(2)}) %all-to-all-start.2) | async-done | bytes 262176 | tf_op jit(solution)/shard_map/all_to_all | solution.py:185
  106.1 1.2 %reduce.2 = f32[32,2048]{1,0:T(8,128)S(1)} reduce(f32[32,1,2048]{2,1,0:T(1,128)S(1)} %all-to-all-done.2, f32[]{:T(128)} %broadcast.603), dimensions={1}, to_apply=%all_to_all.47.reduce_sub_computation | reduce | bytes 524292 | tf_op jit(solution)/shard_map/all_to_all | solution.py:185
  107.3 0.5 reshape.61
  108.0 0.4 copy.165
  108.5 0.5 copy-done.2
  109.1 0.5 fusion.324
  109.6 0.9 copy.175
  (95 shorter events, 5.1 us)
Async XLA Ops:
  0.7 18.5 %collective-permute-start.1 = (f32[2,16,128]{2,1,0:T(8,128)S(1)}, f32[2,16,128]{2,1,0:T(8,128)S(1)}, u32[]{:S(2)}, u32[]{:S(2)}) collective-permute-start(f32[2,16,128]{2,1,0:T(8,128)S(1)} %get-tuple-element.424), channel_id=1, source_target_pairs={{32,0},{64,32},{96,64},{128,96},{160,128},{192,160},{224,192},{33,... | collective-permute-start | bytes 49160 | tf_op jit(solution)/shard_map/ppermute | solution.py:18
  2.7 16.6 %collective-permute-start = (f32[2,16,128]{2,1,0:T(8,128)S(1)}, f32[2,16,128]{2,1,0:T(8,128)S(1)}, u32[]{:S(2)}, u32[]{:S(2)}) collective-permute-start(f32[2,16,128]{2,1,0:T(8,128)S(1)} %get-tuple-element.423), channel_id=1, source_target_pairs={{0,32},{32,64},{64,96},{96,128},{128,160},{160,192},{192,224},{1,3... | collective-permute-start | bytes 49160 | tf_op jit(solution)/shard_map/ppermute | solution.py:15
  7.7 11.5 %copy-start = (f32[32,16,128]{2,1,0:T(8,128)S(1)}, f32[32,16,128]{2,1,0:T(8,128)}, u32[]{:S(2)}) copy-start(f32[32,16,128]{2,1,0:T(8,128)} %param.5) | copy-start | bytes 786436
  7.7 44.7 %all-to-all-start = ((f32[32,1,2048]{2,1,0:T(1,128)}), f32[32,1,2048]{2,1,0:T(1,128)S(1)}, u32[]{:S(2)}, u32[]{:S(2)}) async-start(f32[32,1,2048]{2,1,0:T(1,128)} %reshape.56), calls=%async_computation | async-start | bytes 524288 | tf_op jit(solution)/shard_map/all_to_all | solution.py:177
  19.3 6.1 %collective-permute-start.2 = (f32[36,2,128]{2,0,1:T(8,128)S(1)}, f32[36,2,128]{2,0,1:T(8,128)S(1)}, u32[]{:S(2)}, u32[]{:S(2)}) collective-permute-start(f32[36,2,128]{2,0,1:T(8,128)S(1)} %copy.177), channel_id=1, source_target_pairs={{0,1},{1,2},{2,3},{3,4},{4,5},{5,6},{6,7},{7,8},{8,9},{9,10},{10,1... | collective-permute-start | bytes 110600 | tf_op jit(solution)/shard_map/ppermute | solution.py:15
  23.2 5.9 %collective-permute-start.3 = (f32[36,2,128]{2,0,1:T(8,128)S(1)}, f32[36,2,128]{2,0,1:T(8,128)S(1)}, u32[]{:S(2)}, u32[]{:S(2)}) collective-permute-start(f32[36,2,128]{2,0,1:T(8,128)S(1)} %copy.178), channel_id=1, source_target_pairs={{1,0},{2,1},{3,2},{4,3},{5,4},{6,5},{7,6},{8,7},{9,8},{10,9},{11,1... | collective-permute-start | bytes 110600 | tf_op jit(solution)/shard_map/ppermute | solution.py:18
  34.5 13.3 %copy-start.1 = (f32[32,16,128]{2,0,1:T(8,128)}, f32[32,16,128]{2,0,1:T(8,128)S(1)}, u32[]{:S(2)}) copy-start(f32[32,16,128]{2,0,1:T(8,128)S(1)} %get-tuple-element.380) | copy-start | bytes 786436
  34.5 13.3 %copy-start.3 = (f32[32,16,128]{2,0,1:T(8,128)}, f32[32,16,128]{2,0,1:T(8,128)S(1)}, u32[]{:S(2)}) copy-start(f32[32,16,128]{2,0,1:T(8,128)S(1)} %get-tuple-element.381) | copy-start | bytes 786436
  52.4 0.7 copy-start.6
  53.1 22.5 %all-to-all-start.1 = ((f32[32,1,2048]{2,1,0:T(1,128)}), f32[32,1,2048]{2,1,0:T(1,128)}, u32[]{:S(2)}, u32[]{:S(2)}) async-start(f32[32,1,2048]{2,1,0:T(1,128)} %reshape.58), calls=%async_computation.1 | async-start | bytes 524288 | tf_op jit(solution)/shard_map/all_to_all | solution.py:178
  64.5 0.9 copy-start.7
  78.7 1.0 copy-start.5
  88.9 5.1 %copy-start.9 = (f32[32,16,128]{2,0,1:T(8,128)S(1)}, f32[32,16,128]{2,0,1:T(8,128)}, u32[]{:S(2)}) copy-start(f32[32,16,128]{2,0,1:T(8,128)} %get-tuple-element.320) | copy-start | bytes 786436
  88.9 17.2 %all-to-all-start.2 = ((f32[32,1,2048]{2,1,0:T(1,128)}), f32[32,1,2048]{2,1,0:T(1,128)S(1)}, u32[]{:S(2)}, u32[]{:S(2)}) async-start(f32[32,1,2048]{2,1,0:T(1,128)} %reshape.60), calls=%async_computation.2 | async-start | bytes 524288 | tf_op jit(solution)/shard_map/all_to_all | solution.py:185
  108.0 1.0 copy-start.2
  108.0 1.0 copy-start.4
  108.0 1.1 copy-start.8
where the time goes:
time: 111 us; the launch traced here: 110 us
  starting transfers between devices  35.9 us (32%)
  other arithmetic  23.5 us (21%)
  waiting for transfers between devices  22.2 us (20%)
  local copies, waits for them, and re-layouts  14.5 us (13%)
  blocking collectives  13.2 us (12%)
    all_gather x1, blocking collectives, shards(): gathered_z = lax.all_gather(ends_z, 'depth', axis=0, tiled=True)  13.2 us
    all_to_all x1, starting transfers between devices, shards(): lax.all_to_all(volume, 'lat', split_axis=2, concat_axis=1, tiled=True)  11.4 us
    add x20, other arithmetic, cyclic_solve(): source + left_factor * shifted(source, offset, axis, 0.0)  10.9 us
    all_to_all x1, waiting for transfers between devices, shards(): lax.all_to_all(returned, 'lat', split_axis=1, concat_axis=2, tiled=True)  10.2 us
    all_to_all x1, starting transfers between devices, shards(): lax.all_to_all(cond_y[:, 1:], 'lat', split_axis=2, concat_axis=1, tiled=T...  10.1 us
    unnamed x37, local copies, waits for them, and re-layouts  8.81 us
    all_to_all x1, waiting for transfers between devices, shards(): lax.all_to_all(cond_y[:, 1:], 'lat', split_axis=2, concat_axis=1, tiled=T...  7.45 us
    ppermute x2, starting transfers between devices, with_halo(): lax.ppermute(lax.slice_in_dim(block, block.shape[dim] - width, None, axis...  6.1 us
  transfers between devices with their start and end apart: 7, of which 4 were waited for; matrix products, arithmetic and copies ran while one was open for 17% of the time, Pallas kernels for 0%

commit v1 on v0

v1 whole, which is shorter than its diff:
```python
import jax
import jax.numpy as jnp
from jax import lax
from jax.experimental import pallas as pl
from jax.experimental.pallas import tpu as pltpu
from jax.sharding import PartitionSpec as P

TAU3 = 900.0
INV_LAMBDA_SQ = 4.0
PLANES = 32
ROWS = 16
COLS = 128
BLOCKS = 32
F32 = jnp.float32


def resistance(diff):
    return (1.0 + INV_LAMBDA_SQ * (diff * diff)) * (1.0 / TAU3)


def smooth_lanes(field, first, last):
    before = jnp.where(first, 0.0, pltpu.roll(field, 1, field.ndim - 1))
    after = jnp.where(last, 0.0, pltpu.roll(field, COLS - 1, field.ndim - 1))
    return 0.25 * (before + 2.0 * field + after)


def eliminate(coupling, ground, source, near_ground, near_source, resist):
    factor = 1.0 / (1.0 + (coupling + ground) * resist)
    weight = factor * resist
    back = coupling * weight
    near_ground = near_ground + back * ground
    near_source = near_source + back * source
    saved = (factor, back, source * weight)
    return coupling * factor, ground * factor, source * factor, near_ground, near_source, saved


def eliminate_last(coupling, ground, source, near_ground, near_source, conduct):
    inverse = 1.0 / (coupling + ground + conduct)
    factor = conduct * inverse
    back = coupling * inverse
    near_ground = near_ground + back * ground
    near_source = near_source + back * source
    saved = (factor, back, source * inverse)
    return coupling * factor, ground * factor, source * factor, near_ground, near_source, saved


def join(left, right):
    lc, lg, lh, ls, lt = left
    rc, rg, rh, rs, rt = right
    ground = lh + rg
    source = lt + rs
    inverse = 1.0 / (lc + rc + ground)
    to_left = lc * inverse
    to_right = rc * inverse
    return (
        lc * to_right,
        lg + to_left * ground,
        rh + to_right * ground,
        ls + to_left * source,
        rt + to_right * source,
    ), (to_left, to_right, source * inverse)


def local_kernel(
    vol, low_plane, high_planes, low_row, high_rows,
    y_port, y_factor, y_back, y_rest, z_port, z_factor, z_back, z_rest, z_mid, x_conduct,
    mixed, deep, smooth, y_resist,
):
    depth_last = lax.axis_index("depth") == lax.axis_size("depth") - 1
    lat_last = lax.axis_index("lat") == lax.axis_size("lat") - 1
    z_open = jnp.where(depth_last, 0.0, TAU3).astype(F32)
    y_open = jnp.where(lat_last, 0.0, TAU3).astype(F32)
    lane = lax.broadcasted_iota(jnp.int32, (ROWS, COLS), 1)
    first, last = lane == 0, lane == COLS - 1
    for plane in range(PLANES):
        mixed[plane + 1, 8:24, :] = smooth_lanes(vol[plane * ROWS : (plane + 1) * ROWS, :], first, last)
    mixed[0, 8:24, :] = smooth_lanes(low_plane[...], first, last)
    mixed[PLANES + 1, 8:24, :] = smooth_lanes(high_planes[0:ROWS, :], first, last)
    mixed[PLANES + 2, 8:24, :] = smooth_lanes(high_planes[ROWS : 2 * ROWS, :], first, last)
    side_lane = lax.broadcasted_iota(jnp.int32, (PLANES + 3, COLS), 1)
    side_first, side_last = side_lane == 0, side_lane == COLS - 1
    mixed[:, 7, :] = smooth_lanes(low_row[...], side_first, side_last)
    mixed[:, 24, :] = smooth_lanes(high_rows[0], side_first, side_last)
    mixed[:, 25, :] = smooth_lanes(high_rows[1], side_first, side_last)
    for plane in range(PLANES + 1):
        deep[plane] = 0.25 * (mixed[plane] + 2.0 * mixed[plane + 1] + mixed[plane + 2])
    for plane in range(PLANES + 1):
        smooth[plane, 8:32, :] = 0.25 * (
            deep[plane, 7:31, :] + 2.0 * deep[plane, 8:32, :] + deep[plane, 9:33, :]
        )
    for plane in range(PLANES):
        here = smooth[plane, 8:24, :]
        span = slice(plane * ROWS, (plane + 1) * ROWS)
        y_resist[span, :] = resistance(smooth[plane, 9:25, :] - here)
        along = pltpu.roll(here, COLS - 1, 1) - here
        x_conduct[span, :] = jnp.where(last, 0.0, 1.0 / resistance(along))

    def y_row(ref, row):
        return ref[pl.ds(row, PLANES, stride=ROWS), :]

    half = PLANES // 2

    def z_resist(plane):
        return resistance(smooth[plane + 1, 8:24, :] - smooth[plane, 8:24, :])

    def z_cell(plane):
        return vol[plane * ROWS : (plane + 1) * ROWS, :]

    one_y = jnp.ones((PLANES, COLS), F32)
    one_z = jnp.ones((ROWS, COLS), F32)
    y_state = (1.0 / y_row(y_resist, 0), one_y, y_row(vol, 1), one_y, y_row(vol, 0))
    z_states = [
        (1.0 / z_resist(start), one_z, z_cell(start + 1), one_z, z_cell(start)) for start in (0, half)
    ]
    for step in range(1, ROWS):
        final = step == ROWS - 1
        if final:
            conduct = y_open / (TAU3 * y_row(y_resist, step))
            *y_state, saved = eliminate_last(*y_state, conduct)
        else:
            *y_state, saved = eliminate(*y_state, y_row(y_resist, step))
            y_state[1] = y_state[1] + 1.0
            y_state[2] = y_state[2] + y_row(vol, step + 1)
        y_factor[step], y_back[step], y_rest[step] = saved
        for part in range(2):
            plane = part * half + step
            span = slice(plane * ROWS, (plane + 1) * ROWS)
            resist = z_resist(plane)
            if final and part == 1:
                *state, saved = eliminate_last(*z_states[part], z_open / (TAU3 * resist))
            else:
                *state, saved = eliminate(*z_states[part], resist)
            if not final:
                state[1] = state[1] + 1.0
                state[2] = state[2] + z_cell(plane + 1)
            z_states[part] = state
            z_factor[span, :], z_back[span, :], z_rest[span, :] = saved
    coupling, far_ground, far_source, near_ground, near_source = y_state
    for place, value in enumerate((coupling, near_ground, far_ground, near_source, far_source)):
        y_port[pl.ds(place, PLANES, stride=8), :] = value
    for place in range(5, 8):
        y_port[pl.ds(place, PLANES, stride=8), :] = jnp.zeros((PLANES, COLS), F32)
    ports = [(c, ng, fg, ns, fs) for c, fg, fs, ng, ns in z_states]
    port, middle = join(*ports)
    for place, value in enumerate(port):
        z_port[place] = value
    for place, value in enumerate(middle):
        z_mid[place] = value


def lane_kernel(vol, conduct, out):
    def chunk(index, carry):
        start = pl.multiple_of(index * 64, 64)
        source = vol[pl.ds(start, 64), :]
        right = conduct[pl.ds(start, 64), :]
        ground = jnp.ones_like(source)
        step = 1
        while step < COLS:
            left = pltpu.roll(right, step, 1)
            inverse = 1.0 / (ground + left + right)
            ground_part = ground * inverse
            source_part = source * inverse
            ground = (
                ground
                + left * pltpu.roll(ground_part, step, 1)
                + right * pltpu.roll(ground_part, COLS - step, 1)
            )
            source = (
                source
                + left * pltpu.roll(source_part, step, 1)
                + right * pltpu.roll(source_part, COLS - step, 1)
            )
            right = right * pltpu.roll(right * inverse, COLS - step, 1)
            step *= 2
        out[pl.ds(start, 64), :] = source / ground
        return carry

    lax.fori_loop(0, PLANES * ROWS // 64, chunk, 0)


def row_reduced_kernel(ports, out):
    coupling, near_ground, far_ground, near_source, far_source = (
        ports[pl.ds(place, BLOCKS, stride=8), :] for place in range(5)
    )
    right = coupling
    ground = near_ground + pltpu.roll(far_ground, 1, 0)
    source = near_source + pltpu.roll(far_source, 1, 0)
    step = 1
    while step < BLOCKS:
        left = pltpu.roll(right, step, 0)
        inverse = 1.0 / (ground + left + right)
        ground_part = ground * inverse
        source_part = source * inverse
        ground = (
            ground
            + left * pltpu.roll(ground_part, step, 0)
            + right * pltpu.roll(ground_part, BLOCKS - step, 0)
        )
        source = (
            source
            + left * pltpu.roll(source_part, step, 0)
            + right * pltpu.roll(source_part, BLOCKS - step, 0)
        )
        right = right * pltpu.roll(right * inverse, BLOCKS - step, 0)
        step *= 2
    solved = source / ground
    out[:, 0, :] = solved
    out[:, 1, :] = pltpu.roll(solved, BLOCKS - 1, 0)


def pick(flag, there, here):
    return tuple(jnp.where(flag, a, b) for a, b in zip(there, here))


def join_kernel(bit, own, other, out):
    upper = (lax.axis_index("depth") & bit) != 0
    mine = tuple(own[place] for place in range(5))
    theirs = tuple(other[place] for place in range(5))
    port, _ = join(pick(upper, theirs, mine), pick(upper, mine, theirs))
    for place, value in enumerate(port):
        out[place] = value


def finish_kernel(
    ends_y, y_factor, y_back, y_rest, own, near, pair, quad, z_factor, z_back, z_rest, z_mid, solved_x,
    out, acc,
):
    index = lax.axis_index("depth")
    zero = jnp.zeros((ROWS, COLS), F32)
    left_ground, left_source, right_ground, right_source = zero, zero, zero, zero
    for bit, ref in ((4, quad), (2, pair), (1, near)):
        on_left = (index & bit) != 0
        c, ng, fg, ns, fs = (ref[place] for place in range(5))
        ground, source = ng + left_ground, ns + left_source
        share = c / (c + ground)
        left_ground = jnp.where(on_left, fg + share * ground, left_ground)
        left_source = jnp.where(on_left, fs + share * source, left_source)
        ground, source = fg + right_ground, fs + right_source
        total = c + ground
        share = jnp.where(total > 0.0, c / jnp.where(total > 0.0, total, 1.0), 0.0)
        right_ground = jnp.where(on_left, right_ground, ng + share * ground)
        right_source = jnp.where(on_left, right_source, ns + share * source)
    c, ng, fg, ns, fs = (own[place] for place in range(5))
    ground, source = fg + right_ground, fs + right_source
    total = c + ground
    inverse = jnp.where(total > 0.0, 1.0 / jnp.where(total > 0.0, total, 1.0), 0.0)
    share = c * inverse
    first = (left_source + ns + share * source) / (left_ground + ng + share * ground)
    after = share * first + source * inverse
    middle = z_mid[0] * first + z_mid[1] * after + z_mid[2]
    half = PLANES // 2
    y_first = ends_y[:, 0, :]
    y_after = ends_y[:, 1, :]
    acc[pl.ds(0, PLANES, stride=ROWS), :] = y_first
    value = y_after
    for row in range(ROWS - 1, 0, -1):
        value = y_factor[row] * value + (y_back[row] * y_first + y_rest[row])
        acc[pl.ds(row, PLANES, stride=ROWS), :] = value
    third = 1.0 / 3.0
    for start, near_value, far_value in ((0, first, middle), (half, middle, after)):
        value = far_value
        for plane in range(start + half - 1, start, -1):
            span = slice(plane * ROWS, (plane + 1) * ROWS)
            value = z_factor[span, :] * value + (z_back[span, :] * near_value + z_rest[span, :])
            out[span, :] = (solved_x[span, :] + acc[span, :] + value) * third
        span = slice(start * ROWS, (start + 1) * ROWS)
        out[span, :] = (solved_x[span, :] + acc[span, :] + near_value) * third


def call(kernel, outs, scratch=(), flops=1000000, moved=500000):
    return pl.pallas_call(
        kernel,
        out_shape=outs,
        scratch_shapes=scratch,
        compiler_params=pltpu.CompilerParams(vmem_limit_bytes=32 * 1024 * 1024),
        cost_estimate=pl.CostEstimate(flops=flops, bytes_accessed=moved, transcendentals=0),
    )


def shaped(*shape):
    return jax.ShapeDtypeStruct(shape, F32)


def line_perm(axis, step):
    count = lax.axis_size(axis)
    if step > 0:
        return [(i, i + 1) for i in range(count - 1)]
    return [(i + 1, i) for i in range(count - 1)]


def swap_perm(axis, bit):
    return [(i, i ^ bit) for i in range(lax.axis_size(axis))]


def shards(volume):
    flat = volume.reshape(PLANES * ROWS, COLS)
    low_plane = lax.ppermute(volume[PLANES - 1], "depth", line_perm("depth", 1))
    high_planes = lax.ppermute(volume[:2], "depth", line_perm("depth", -1))
    tall = jnp.concatenate([low_plane[None], volume, high_planes], axis=0)
    low_row = lax.ppermute(tall[:, ROWS - 1], "lat", line_perm("lat", 1))
    high_rows = lax.ppermute(jnp.stack([tall[:, 0], tall[:, 1]]), "lat", line_perm("lat", -1))
    lines = shaped(ROWS, PLANES, COLS)
    whole = shaped(PLANES * ROWS, COLS)
    (
        y_port, y_factor, y_back, y_rest, z_port, z_factor, z_back, z_rest, z_mid, x_conduct
    ) = call(
        local_kernel,
        (
            shaped(PLANES * 8, COLS), lines, lines, lines,
            shaped(5, ROWS, COLS), whole, whole, whole, shaped(3, ROWS, COLS), whole,
        ),
        (
            pltpu.VMEM((PLANES + 3, 40, COLS), F32),
            pltpu.VMEM((PLANES + 1, 40, COLS), F32),
            pltpu.VMEM((PLANES + 1, 32, COLS), F32),
            pltpu.VMEM((PLANES * ROWS, COLS), F32),
        ),
    )(flat, low_plane, high_planes.reshape(2 * ROWS, COLS), low_row, high_rows)
    near = lax.ppermute(z_port, "depth", swap_perm("depth", 1))
    pair_own = call(lambda *refs: join_kernel(1, *refs), shaped(5, ROWS, COLS))(z_port, near)
    y_port, pair_own = lax.optimization_barrier((y_port, pair_own))
    pair = lax.ppermute(pair_own, "depth", swap_perm("depth", 2))
    ports = lax.all_to_all(y_port, "lat", 0, 0, tiled=True)
    solved_x = call(lane_kernel, whole)(flat, x_conduct)
    ends = call(row_reduced_kernel, shaped(BLOCKS, 2, COLS))(ports)
    quad_own = call(lambda *refs: join_kernel(2, *refs), shaped(5, ROWS, COLS))(pair_own, pair)
    ends, quad_own = lax.optimization_barrier((ends, quad_own))
    quad = lax.ppermute(quad_own, "depth", swap_perm("depth", 4))
    ends_y = lax.all_to_all(ends, "lat", 0, 0, tiled=True)
    out = call(finish_kernel, whole, (pltpu.VMEM((PLANES * ROWS, COLS), F32),))(
        ends_y, y_factor, y_back, y_rest, z_port, near, pair, quad, z_factor, z_back, z_rest, z_mid, solved_x
    )
    return out.reshape(PLANES, ROWS, COLS)


def solution(mesh):
    placed = (P("depth", "lat", None),)
    return jax.shard_map(
        shards, mesh=mesh, in_specs=placed, out_specs=P("depth", "lat", None), check_vma=False
    )
```

time: 111 us -> 60.4 us (0.54)
  the two profiles are of different devices: /device:TPU:8 before, /device:TPU:6 now
where the time goes in v1:
time: 60.4 us; the launch traced here: 60.1 us
  starting transfers between devices  32.9 us (54%)
  waiting for transfers between devices  13.4 us (22%)
  Pallas kernels  12.4 us (21%)
  local copies, waits for them, and re-layouts  1.13 us (2%)
    pallas_call x1, Pallas kernels, shards(): solved_x = call(lane_kernel, whole)(flat, x_conduct)  9.08 us
    ppermute x1, starting transfers between devices, shards(): lax.ppermute(jnp.stack([tall[:, 0], tall[:, 1]]), 'lat', line_perm('lat',...  8.03 us
    all_to_all x1, starting transfers between devices, shards(): ends_y = lax.all_to_all(ends, 'lat', 0, 0, tiled=True)  6.34 us
    ppermute x1, waiting for transfers between devices, shards(): low_row = lax.ppermute(tall[:, ROWS - 1], 'lat', line_perm('lat', 1))  5.97 us
    all_to_all x1, starting transfers between devices, shards(): ports = lax.all_to_all(y_port, 'lat', 0, 0, tiled=True)  4.72 us
    ppermute x1, starting transfers between devices, shards(): quad = lax.ppermute(quad_own, 'depth', swap_perm('depth', 4))  4.3 us
    all_to_all x1, waiting for transfers between devices, shards(): ports = lax.all_to_all(y_port, 'lat', 0, 0, tiled=True)  3.46 us
    ppermute x1, starting transfers between devices, shards(): pair = lax.ppermute(pair_own, 'depth', swap_perm('depth', 2))  3.29 us
  transfers between devices with their start and end apart: 9, of which 5 were waited for; matrix products, arithmetic and copies ran while one was open for 0% of the time, Pallas kernels for 15%

profile of v1, /device:TPU:6, one launch (start us, length us, event | category | flops | bytes accessed | tf_op | source)
XLA Modules:
  0.0 60.1 jit_solution(14070749853662792241)
XLA Ops:
  0.0 0.0 copy-start
  0.0 1.1 %copy.4 = f32[32,16,128]{2,0,1:T(8,128)S(1)} copy(f32[32,16,128]{2,1,0:T(8,128)} %param.1) | data formatting | bytes 524288 | tf_op args[0]
  1.1 1.3 %collective-permute-start.1 = (f32[2,16,128]{2,0,1:T(2,128)S(1)}, f32[2,16,128]{2,0,1:T(2,128)S(1)}, u32[]{:S(2)}, u32[]{:S(2)}) collective-permute-start(f32[2,16,128]{2,0,1:T(2,128)S(1)} %slice.20), channel_id=1, source_target_pairs={{32,0},{64,32},{96,64},{128,96},{160,128},{192,160},{224,192},{33,... | collective-permute-start | bytes 49160 | tf_op jit(solution)/shard_map/ppermute | solution.py:298
  2.4 0.0 copy-done
  2.5 3.0 %collective-permute-start = (f32[16,128]{1,0:T(8,128)S(1)}, f32[16,128]{1,0:T(8,128)S(1)}, u32[]{:S(2)}, u32[]{:S(2)}) collective-permute-start(f32[16,128]{1,0:T(8,128)S(1)} %slice_bitcast_fusion), channel_id=1, source_target_pairs={{0,32},{32,64},{64,96},{96,128},{128,160},{160,192},{192,224},{1,3... | collective-permute-start | bytes 24584 | tf_op jit(solution)/shard_map/ppermute | solution.py:297
  5.5 0.8 %collective-permute-done.low_plane = f32[16,128]{1,0:T(8,128)S(1)} collective-permute-done((f32[16,128]{1,0:T(8,128)S(1)}, f32[16,128]{1,0:T(8,128)S(1)}, u32[]{:S(2)}, u32[]{:S(2)}) %collective-permute-start) | collective-permute-done | bytes 8224 | tf_op jit(solution)/shard_map/ppermute | solution.py:297
  6.3 0.0 collective-permute-done.1
  6.3 8.0 %collective-permute-start.3 = (f32[2,35,128]{2,1,0:T(8,128)S(1)}, f32[2,35,128]{2,1,0:T(8,128)S(1)}, u32[]{:S(2)}, u32[]{:S(2)}) collective-permute-start(f32[2,35,128]{2,1,0:T(8,128)S(1)} %pad_maximum_fusion), channel_id=1, source_target_pairs={{1,0},{2,1},{3,2},{4,3},{5,4},{6,5},{7,6},{8,7},{9,8},{10,9},{11,1... | collective-permute-start | bytes 107528 | tf_op jit(solution)/shard_map/ppermute | solution.py:301
  14.4 1.9 %collective-permute-start.2 = (f32[35,128]{1,0:T(8,128)S(1)}, f32[35,128]{1,0:T(8,128)S(1)}, u32[]{:S(2)}, u32[]{:S(2)}) collective-permute-start(f32[35,128]{1,0:T(8,128)S(1)} %get-tuple-element.34), channel_id=1, source_target_pairs={{0,1},{1,2},{2,3},{3,4},{4,5},{5,6},{6,7},{7,8},{8,9},{9,10},{10,1... | collective-permute-start | bytes 53768 | tf_op jit(solution)/shard_map/ppermute | solution.py:300
  16.3 6.0 %collective-permute-done.2.low_row = f32[35,128]{1,0:T(8,128)S(1)} collective-permute-done((f32[35,128]{1,0:T(8,128)S(1)}, f32[35,128]{1,0:T(8,128)S(1)}, u32[]{:S(2)}, u32[]{:S(2)}) %collective-permute-start.2) | collective-permute-done | bytes 17952 | tf_op jit(solution)/shard_map/ppermute | solution.py:300
  22.3 0.0 collective-permute-done.3.high_rows
  22.3 1.6 %shard_map.17 = (f32[256,128]{1,0:T(8,128)}, f32[16,32,128]{2,1,0:T(8,128)S(1)}, f32[16,32,128]{2,1,0:T(8,128)S(1)}, f32[16,32,128]{2,1,0:T(8,128)S(1)}, f32[5,1...) custom-call(f32[512,128]{1,0:T(8,128)S(1)} %bitcast.14, ...), custom_call_target="tpu_custom_call" | custom-call | flops 1000000 | bytes 500000 | tf_op jit(solution)/shard_map/pallas_call | solution.py:306
  23.9 0.0 collective-permute-start.4
  24.0 1.2 %collective-permute-done.4.refs_1_.near = f32[5,16,128]{2,1,0:T(8,128)S(1)} collective-permute-done((f32[5,16,128]{2,1,0:T(8,128)S(1)}, f32[5,16,128]{2,1,0:T(8,128)S(1)}, u32[]{:S(2)}, u32[]{:S(2)}) %collective-permute-start.4) | collective-permute-done | bytes 40992 | tf_op jit(solution)/shard_map/ppermute | solution.py:319
  25.2 4.7 %all-to-all-start = ((f32[32,8,128]{2,1,0:T(8,128)}), f32[32,8,128]{2,1,0:T(8,128)S(1)}, u32[]{:S(2)}, u32[]{:S(2)}) async-start(f32[32,8,128]{2,1,0:T(8,128)} %bitcast.7), calls=%async_computation | async-start | bytes 262144 | tf_op jit(solution)/shard_map/all_to_all | solution.py:323
  29.9 3.3 %collective-permute-start.5 = (f32[5,16,128]{2,1,0:T(8,128)S(1)}, f32[5,16,128]{2,1,0:T(8,128)S(1)}, u32[]{:S(2)}, u32[]{:S(2)}) collective-permute-start(f32[5,16,128]{2,1,0:T(8,128)S(1)} %shard_map.18.refs_0_), channel_id=1, source_target_pairs={{0,64},{32,96},{64,0},{96,32},{128,192},{160,224},{192,128},{224,1... | collective-permute-start | bytes 122888 | tf_op jit(solution)/shard_map/ppermute | solution.py:322
  33.2 2.0 %collective-permute-done.5.refs_1_.pair = f32[5,16,128]{2,1,0:T(8,128)S(1)} collective-permute-done((f32[5,16,128]{2,1,0:T(8,128)S(1)}, f32[5,16,128]{2,1,0:T(8,128)S(1)}, u32[]{:S(2)}, u32[]{:S(2)}) %collective-permute-start.5) | collective-permute-done | bytes 40992 | tf_op jit(solution)/shard_map/ppermute | solution.py:322
  35.2 3.5 %all-to-all-done = f32[32,8,128]{2,1,0:T(8,128)S(1)} async-done(((f32[32,8,128]{2,1,0:T(8,128)}), f32[32,8,128]{2,1,0:T(8,128)S(1)}, u32[]{:S(2)}, u32[]{:S(2)}) %all-to-all-start) | async-done | bytes 131104 | tf_op jit(solution)/shard_map/all_to_all | solution.py:323
  38.7 0.7 %shard_map.19 = f32[32,2,128]{2,1,0:T(2,128)} custom-call(f32[256,128]{1,0:T(8,128)S(1)} %bitcast.16), custom_call_target="tpu_custom_call" | custom-call | flops 1000000 | bytes 500000 | tf_op jit(solution)/shard_map/pallas_call | solution.py:325
  39.4 6.3 %all-to-all-start.1 = ((f32[32,2,128]{2,1,0:T(2,128)}), f32[32,2,128]{2,1,0:T(2,128)S(1)}, u32[]{:S(2)}, u32[]{:S(2)}) async-start(f32[32,2,128]{2,1,0:T(2,128)} %shard_map.19), calls=%async_computation.1 | async-start | bytes 65536 | tf_op jit(solution)/shard_map/all_to_all | solution.py:329
  45.7 4.3 %collective-permute-start.6 = (f32[5,16,128]{2,1,0:T(8,128)S(1)}, f32[5,16,128]{2,1,0:T(8,128)S(1)}, u32[]{:S(2)}, u32[]{:S(2)}) collective-permute-start(f32[5,16,128]{2,1,0:T(8,128)S(1)} %shard_map.20), channel_id=1, source_target_pairs={{0,128},{32,160},{64,192},{96,224},{128,0},{160,32},{192,64},{224,... | collective-permute-start | bytes 122888 | tf_op jit(solution)/shard_map/ppermute | solution.py:328
  50.0 9.1 %shard_map.21.solved_x = f32[512,128]{1,0:T(8,128)S(1)} custom-call(f32[512,128]{1,0:T(8,128)S(1)} %bitcast.15, f32[512,128]{1,0:T(8,128)S(1)} %get-tuple-element.32.conduct), custom_call_target="tpu_custom_call" | custom-call | flops 1000000 | bytes 500000 | tf_op jit(solution)/shard_map/pallas_call | solution.py:324
  59.1 0.0 collective-permute-done.6.quad
  59.1 0.0 all-to-all-done.1.ends_y
  59.2 0.9 %shard_map.22 = f32[512,128]{1,0:T(8,128)} custom-call(f32[32,2,128]{2,1,0:T(2,128)S(1)} %all-to-all-done.1.ends_y, f32[16,32,128]{2,1,0:T(8,128)S(1)} %get-tuple-element.24.y_factor, f32[16,32,128]{2,1,0:T(8,128)S(1)} %get-tuple-element.25.y_back, f32[16,32,128]{2,1,0:T(8,128)S(1)} %get-tuple-element.26.y_rest, ...), custom_call_target="tpu_custom_call" | custom-call | flops 1000000 | bytes 500000 | tf_op jit(solution)/shard_map/pallas_call | solution.py:330
  (7 shorter events, 0.1 us)
Async XLA Ops:
  0.0 2.4 %copy-start = (f32[32,16,128]{2,1,0:T(8,128)S(1)}, f32[32,16,128]{2,1,0:T(8,128)}, u32[]{:S(2)}) copy-start(f32[32,16,128]{2,1,0:T(8,128)} %param.1) | copy-start | bytes 786436
  1.1 5.2 %collective-permute-start.1 = (f32[2,16,128]{2,0,1:T(2,128)S(1)}, f32[2,16,128]{2,0,1:T(2,128)S(1)}, u32[]{:S(2)}, u32[]{:S(2)}) collective-permute-start(f32[2,16,128]{2,0,1:T(2,128)S(1)} %slice.20), channel_id=1, source_target_pairs={{32,0},{64,32},{96,64},{128,96},{160,128},{192,160},{224,192},{33,... | collective-permute-start | bytes 49160 | tf_op jit(solution)/shard_map/ppermute | solution.py:298
  2.5 3.8 %collective-permute-start = (f32[16,128]{1,0:T(8,128)S(1)}, f32[16,128]{1,0:T(8,128)S(1)}, u32[]{:S(2)}, u32[]{:S(2)}) collective-permute-start(f32[16,128]{1,0:T(8,128)S(1)} %slice_bitcast_fusion), channel_id=1, source_target_pairs={{0,32},{32,64},{64,96},{96,128},{128,160},{160,192},{192,224},{1,3... | collective-permute-start | bytes 24584 | tf_op jit(solution)/shard_map/ppermute | solution.py:297
  6.3 16.0 %collective-permute-start.3 = (f32[2,35,128]{2,1,0:T(8,128)S(1)}, f32[2,35,128]{2,1,0:T(8,128)S(1)}, u32[]{:S(2)}, u32[]{:S(2)}) collective-permute-start(f32[2,35,128]{2,1,0:T(8,128)S(1)} %pad_maximum_fusion), channel_id=1, source_target_pairs={{1,0},{2,1},{3,2},{4,3},{5,4},{6,5},{7,6},{8,7},{9,8},{10,9},{11,1... | collective-permute-start | bytes 107528 | tf_op jit(solution)/shard_map/ppermute | solution.py:301
  14.4 7.9 %collective-permute-start.2 = (f32[35,128]{1,0:T(8,128)S(1)}, f32[35,128]{1,0:T(8,128)S(1)}, u32[]{:S(2)}, u32[]{:S(2)}) collective-permute-start(f32[35,128]{1,0:T(8,128)S(1)} %get-tuple-element.34), channel_id=1, source_target_pairs={{0,1},{1,2},{2,3},{3,4},{4,5},{5,6},{6,7},{7,8},{8,9},{9,10},{10,1... | collective-permute-start | bytes 53768 | tf_op jit(solution)/shard_map/ppermute | solution.py:300
  23.9 1.2 %collective-permute-start.4 = (f32[5,16,128]{2,1,0:T(8,128)S(1)}, f32[5,16,128]{2,1,0:T(8,128)S(1)}, u32[]{:S(2)}, u32[]{:S(2)}) collective-permute-start(f32[5,16,128]{2,1,0:T(8,128)S(1)} %get-tuple-element.20.refs_0_.own), channel_id=1, source_target_pairs={{0,32},{32,0},{64,96},{96,64},{128,160},{160,128},{192,224},{224,1... | collective-permute-start | bytes 122888 | tf_op jit(solution)/shard_map/ppermute | solution.py:319
  25.2 13.5 %all-to-all-start = ((f32[32,8,128]{2,1,0:T(8,128)}), f32[32,8,128]{2,1,0:T(8,128)S(1)}, u32[]{:S(2)}, u32[]{:S(2)}) async-start(f32[32,8,128]{2,1,0:T(8,128)} %bitcast.7), calls=%async_computation | async-start | bytes 262144 | tf_op jit(solution)/shard_map/all_to_all | solution.py:323
  29.9 5.3 %collective-permute-start.5 = (f32[5,16,128]{2,1,0:T(8,128)S(1)}, f32[5,16,128]{2,1,0:T(8,128)S(1)}, u32[]{:S(2)}, u32[]{:S(2)}) collective-permute-start(f32[5,16,128]{2,1,0:T(8,128)S(1)} %shard_map.18.refs_0_), channel_id=1, source_target_pairs={{0,64},{32,96},{64,0},{96,32},{128,192},{160,224},{192,128},{224,1... | collective-permute-start | bytes 122888 | tf_op jit(solution)/shard_map/ppermute | solution.py:322
  39.4 19.8 %all-to-all-start.1 = ((f32[32,2,128]{2,1,0:T(2,128)}), f32[32,2,128]{2,1,0:T(2,128)S(1)}, u32[]{:S(2)}, u32[]{:S(2)}) async-start(f32[32,2,128]{2,1,0:T(2,128)} %shard_map.19), calls=%async_computation.1 | async-start | bytes 65536 | tf_op jit(solution)/shard_map/all_to_all | solution.py:329
  45.7 13.4 %collective-permute-start.6 = (f32[5,16,128]{2,1,0:T(8,128)S(1)}, f32[5,16,128]{2,1,0:T(8,128)S(1)}, u32[]{:S(2)}, u32[]{:S(2)}) collective-permute-start(f32[5,16,128]{2,1,0:T(8,128)S(1)} %shard_map.20), channel_id=1, source_target_pairs={{0,128},{32,160},{64,192},{96,224},{128,0},{160,32},{192,64},{224,... | collective-permute-start | bytes 122888 | tf_op jit(solution)/shard_map/ppermute | solution.py:328

commit v2 on v1

v2 whole, which is shorter than its diff:
```python
import jax
import jax.numpy as jnp
from jax import lax
from jax.experimental import pallas as pl
from jax.experimental.pallas import tpu as pltpu
from jax.sharding import PartitionSpec as P

TAU3 = 900.0
INV_LAMBDA_SQ = 4.0
PLANES = 32
ROWS = 16
COLS = 128
BLOCKS = 32
PORT = 16
F32 = jnp.float32


def resistance(diff):
    return (1.0 + INV_LAMBDA_SQ * (diff * diff)) * (1.0 / TAU3)


def smooth_lanes(field, first, last):
    before = jnp.where(first, 0.0, pltpu.roll(field, 1, field.ndim - 1))
    after = jnp.where(last, 0.0, pltpu.roll(field, COLS - 1, field.ndim - 1))
    return 0.25 * (before + 2.0 * field + after)


def eliminate(coupling, ground, source, near_ground, near_source, resist):
    factor = 1.0 / (1.0 + (coupling + ground) * resist)
    weight = factor * resist
    back = coupling * weight
    near_ground = near_ground + back * ground
    near_source = near_source + back * source
    saved = (factor, back, source * weight)
    return coupling * factor, ground * factor, source * factor, near_ground, near_source, saved


def eliminate_last(coupling, ground, source, near_ground, near_source, conduct):
    inverse = 1.0 / (coupling + ground + conduct)
    factor = conduct * inverse
    back = coupling * inverse
    near_ground = near_ground + back * ground
    near_source = near_source + back * source
    saved = (factor, back, source * inverse)
    return coupling * factor, ground * factor, source * factor, near_ground, near_source, saved


def join(left, right):
    lc, lg, lh, ls, lt = left
    rc, rg, rh, rs, rt = right
    ground = lh + rg
    source = lt + rs
    inverse = 1.0 / (lc + rc + ground)
    to_left = lc * inverse
    to_right = rc * inverse
    return (
        lc * to_right,
        lg + to_left * ground,
        rh + to_right * ground,
        ls + to_left * source,
        rt + to_right * source,
    ), (to_left, to_right, source * inverse)


def edge_kernel(vol, low_side, high_side, sems):
    copies = (
        pltpu.make_async_copy(vol.at[pl.ds((PLANES - 1) * ROWS, ROWS), :], high_side, sems.at[0]),
        pltpu.make_async_copy(vol.at[pl.ds(0, 2 * ROWS), :], low_side, sems.at[1]),
    )
    for copy in copies:
        copy.start()
    for copy in copies:
        copy.wait()


def strided(ref, row):
    return ref[pl.ds(row, 32, stride=16), :]


def row_kernel(vol, low_plane, high_planes, port, factor, back, rest, deep, low_side, high_side, mixed):
    lane = lax.broadcasted_iota(jnp.int32, (ROWS, COLS), 1)
    first, last = lane == 0, lane == COLS - 1
    mixed[0] = smooth_lanes(low_plane[...], first, last)
    for plane in range(PLANES):
        mixed[plane + 1] = smooth_lanes(vol[plane * ROWS : (plane + 1) * ROWS, :], first, last)
    mixed[PLANES + 1] = smooth_lanes(high_planes[0:ROWS, :], first, last)
    mixed[PLANES + 2] = smooth_lanes(high_planes[ROWS : 2 * ROWS, :], first, last)
    for plane in range(PLANES + 1):
        deep[plane * ROWS : (plane + 1) * ROWS, :] = 0.25 * (
            mixed[plane] + 2.0 * mixed[plane + 1] + mixed[plane + 2]
        )
    low_side[...] = deep[pl.ds(0, PLANES + 1, stride=ROWS), :]
    high_side[...] = deep[pl.ds(ROWS - 1, PLANES + 1, stride=ROWS), :]
    part = [strided(deep, row) for row in range(ROWS)]
    low_sum = 2.0 * part[0] + part[1]
    high_sum = part[ROWS - 2] + 2.0 * part[ROWS - 1]
    smooth = [None] + [0.25 * (part[r - 1] + 2.0 * part[r] + part[r + 1]) for r in range(1, ROWS - 1)]
    one = jnp.ones((PLANES, COLS), F32)
    state = (1.0 / resistance(smooth[2] - smooth[1]), one, strided(vol, 2), one, strided(vol, 1))
    for row in range(2, ROWS - 2):
        *state, saved = eliminate(*state, resistance(smooth[row + 1] - smooth[row]))
        state[1] = state[1] + 1.0
        state[2] = state[2] + strided(vol, row + 1)
        factor[row], back[row], rest[row] = saved
    coupling, far_ground, far_source, near_ground, near_source = state
    values = (
        coupling, near_ground, far_ground, near_source, far_source,
        part[0], part[ROWS - 1], low_sum, high_sum, smooth[1], smooth[ROWS - 2],
        strided(vol, 0), strided(vol, ROWS - 1),
    )
    for place, value in enumerate(values):
        port[pl.ds(place, PLANES, stride=PORT), :] = value
    for place in range(len(values), PORT):
        port[pl.ds(place, PLANES, stride=PORT), :] = jnp.zeros((PLANES, COLS), F32)


def chain_solve(coupling, near_ground, far_ground, near_source, far_source, count):
    size = coupling.shape[0]
    right = coupling
    ground = near_ground + pltpu.roll(far_ground, 1, 0)
    source = near_source + pltpu.roll(far_source, 1, 0)
    step = 1
    while step < count:
        left = pltpu.roll(right, step, 0)
        inverse = 1.0 / (ground + left + right)
        ground_part = ground * inverse
        source_part = source * inverse
        ground = (
            ground
            + left * pltpu.roll(ground_part, step, 0)
            + right * pltpu.roll(ground_part, size - step, 0)
        )
        source = (
            source
            + left * pltpu.roll(source_part, step, 0)
            + right * pltpu.roll(source_part, size - step, 0)
        )
        right = right * pltpu.roll(right * inverse, size - step, 0)
        step *= 2
    return source / ground


def plane_column_kernel(
    vol, deep, low_row, high_row,
    port, z_factor, z_back, z_rest, z_mid, solved_x,
    smooth, turned, turned_smooth, x_factor, x_back, x_rest,
):
    depth_last = lax.axis_index("depth") == lax.axis_size("depth") - 1
    z_open = jnp.where(depth_last, 0.0, TAU3).astype(F32)
    row_index = lax.broadcasted_iota(jnp.int32, (ROWS, COLS), 0)
    top, bottom = row_index == 0, row_index == ROWS - 1
    for plane in range(PLANES + 1):
        span = slice(plane * ROWS, (plane + 1) * ROWS)
        here = deep[span, :]
        above = jnp.where(top, low_row[plane : plane + 1, :], pltpu.roll(here, 1, 0))
        below = jnp.where(bottom, high_row[plane : plane + 1, :], pltpu.roll(here, ROWS - 1, 0))
        smooth[span, :] = 0.25 * (above + 2.0 * here + below)
    for group in range(4):
        span = slice(group * COLS, (group + 1) * COLS)
        turned[span, :] = vol[span, :].T
        turned_smooth[span, :] = smooth[span, :].T

    def z_cell(ref, plane):
        return ref[plane * ROWS : (plane + 1) * ROWS, :]

    def z_resist(plane):
        return resistance(z_cell(smooth, plane + 1) - z_cell(smooth, plane))

    def x_resist(step):
        if step < 15:
            return resistance(strided(turned_smooth, step + 1) - strided(turned_smooth, step))
        return resistance(pltpu.roll(strided(turned_smooth, 0), 31, 0) - strided(turned_smooth, 15))

    half = PLANES // 2
    chunk_last = (lax.broadcasted_iota(jnp.int32, (32, COLS), 0) & 7) == 7
    one_x = jnp.ones((32, COLS), F32)
    one_z = jnp.ones((ROWS, COLS), F32)
    x_state = (1.0 / x_resist(0), one_x, strided(turned, 1), one_x, strided(turned, 0))
    z_states = [
        (1.0 / z_resist(start), one_z, z_cell(vol, start + 1), one_z, z_cell(vol, start))
        for start in (0, half)
    ]
    for step in range(1, 16):
        final = step == 15
        if final:
            *x_state, saved = eliminate_last(*x_state, jnp.where(chunk_last, 0.0, 1.0 / x_resist(step)))
        else:
            *x_state, saved = eliminate(*x_state, x_resist(step))
            x_state[1] = x_state[1] + 1.0
            x_state[2] = x_state[2] + strided(turned, step + 1)
        x_factor[step], x_back[step], x_rest[step] = saved
        for part in range(2):
            plane = part * half + step
            span = slice(plane * ROWS, (plane + 1) * ROWS)
            resist = z_resist(plane)
            if final and part == 1:
                *state, saved = eliminate_last(*z_states[part], z_open / (TAU3 * resist))
            else:
                *state, saved = eliminate(*z_states[part], resist)
            if not final:
                state[1] = state[1] + 1.0
                state[2] = state[2] + z_cell(vol, plane + 1)
            z_states[part] = state
            z_factor[span, :], z_back[span, :], z_rest[span, :] = saved
    ports = [(c, ng, fg, ns, fs) for c, fg, fs, ng, ns in z_states]
    joined, middle = join(*ports)
    for place, value in enumerate(joined):
        port[place] = value
    for place, value in enumerate(middle):
        z_mid[place] = value
    coupling, far_ground, far_source, near_ground, near_source = x_state
    first = chain_solve(coupling, near_ground, far_ground, near_source, far_source, 8)
    turned[pl.ds(0, 32, stride=16), :] = first
    value = pltpu.roll(first, 31, 0)
    for step in range(15, 0, -1):
        value = x_factor[step] * value + (x_back[step] * first + x_rest[step])
        turned[pl.ds(step, 32, stride=16), :] = value
    for group in range(4):
        span = slice(group * COLS, (group + 1) * COLS)
        solved_x[span, :] = turned[span, :].T


def row_reduced_kernel(ports, out):
    (
        coupling, near_ground, far_ground, near_source, far_source,
        low, high, low_sum, high_sum, low_smooth, high_smooth, low_cell, high_cell,
    ) = (ports[pl.ds(place, BLOCKS, stride=PORT), :] for place in range(13))
    block = lax.broadcasted_iota(jnp.int32, (BLOCKS, COLS), 0)
    block_first, block_last = block == 0, block == BLOCKS - 1
    low_end = 0.25 * (jnp.where(block_first, 0.0, pltpu.roll(high, 1, 0)) + low_sum)
    high_end = 0.25 * (high_sum + jnp.where(block_last, 0.0, pltpu.roll(low, BLOCKS - 1, 0)))
    enter = 1.0 / resistance(low_smooth - low_end)
    leave = 1.0 / resistance(high_end - high_smooth)
    across = pltpu.roll(low_end, BLOCKS - 1, 0) - high_end
    across = jnp.where(block_last, 0.0, 1.0 / resistance(across))
    zero = jnp.zeros_like(coupling)
    one = jnp.ones_like(coupling)
    before, at_low = join(
        (enter, one, zero, low_cell, zero), (coupling, near_ground, far_ground, near_source, far_source)
    )
    after, at_high = join((leave, zero, one, zero, high_cell), (across, zero, zero, zero, zero))
    whole, between = join(before, after)
    first = chain_solve(*whole, BLOCKS)
    later = pltpu.roll(first, BLOCKS - 1, 0)

    def middle(weights, left, right):
        return weights[0] * left + weights[1] * right + weights[2]

    inner_high = middle(between, first, later)
    out[:, 0, :] = first
    out[:, 1, :] = middle(at_low, first, inner_high)
    out[:, 2, :] = inner_high
    out[:, 3, :] = middle(at_high, inner_high, later)


def pick(flag, there, here):
    return tuple(jnp.where(flag, a, b) for a, b in zip(there, here))


def join_kernel(bit, own, other, out):
    upper = (lax.axis_index("depth") & bit) != 0
    mine = tuple(own[place] for place in range(5))
    theirs = tuple(other[place] for place in range(5))
    port, _ = join(pick(upper, theirs, mine), pick(upper, mine, theirs))
    for place, value in enumerate(port):
        out[place] = value


def finish_kernel(
    ends_y, y_factor, y_back, y_rest, own, near, pair, across, skew, z_factor, z_back, z_rest, z_mid, solved_x,
    out, acc,
):
    index = lax.axis_index("depth")
    odd = (index & 2) != 0
    straight = tuple(across[place] for place in range(5))
    crossed = tuple(skew[place] for place in range(5))
    quad, _ = join(pick(odd, crossed, straight), pick(odd, straight, crossed))
    zero = jnp.zeros((ROWS, COLS), F32)
    left_ground, left_source, right_ground, right_source = zero, zero, zero, zero
    for bit, ref in ((4, quad), (2, pair), (1, near)):
        on_left = (index & bit) != 0
        c, ng, fg, ns, fs = (ref[place] for place in range(5))
        ground, source = ng + left_ground, ns + left_source
        share = c / (c + ground)
        left_ground = jnp.where(on_left, fg + share * ground, left_ground)
        left_source = jnp.where(on_left, fs + share * source, left_source)
        ground, source = fg + right_ground, fs + right_source
        total = c + ground
        share = jnp.where(total > 0.0, c / jnp.where(total > 0.0, total, 1.0), 0.0)
        right_ground = jnp.where(on_left, right_ground, ng + share * ground)
        right_source = jnp.where(on_left, right_source, ns + share * source)
    c, ng, fg, ns, fs = (own[place] for place in range(5))
    ground, source = fg + right_ground, fs + right_source
    total = c + ground
    inverse = jnp.where(total > 0.0, 1.0 / jnp.where(total > 0.0, total, 1.0), 0.0)
    share = c * inverse
    first = (left_source + ns + share * source) / (left_ground + ng + share * ground)
    after = share * first + source * inverse
    middle = z_mid[0] * first + z_mid[1] * after + z_mid[2]
    half = PLANES // 2
    for place, row in ((0, 0), (1, 1), (2, ROWS - 2), (3, ROWS - 1)):
        acc[pl.ds(row, PLANES, stride=ROWS), :] = ends_y[:, place, :]
    y_first = ends_y[:, 1, :]
    value = ends_y[:, 2, :]
    for row in range(ROWS - 3, 1, -1):
        value = y_factor[row] * value + (y_back[row] * y_first + y_rest[row])
        acc[pl.ds(row, PLANES, stride=ROWS), :] = value
    third = 1.0 / 3.0
    for start, near_value, far_value in ((0, first, middle), (half, middle, after)):
        value = far_value
        for plane in range(start + half - 1, start, -1):
            span = slice(plane * ROWS, (plane + 1) * ROWS)
            value = z_factor[span, :] * value + (z_back[span, :] * near_value + z_rest[span, :])
            out[span, :] = (solved_x[span, :] + acc[span, :] + value) * third
        span = slice(start * ROWS, (start + 1) * ROWS)
        out[span, :] = (solved_x[span, :] + acc[span, :] + near_value) * third


def call(kernel, outs, scratch=(), flops=1000000, moved=500000):
    return pl.pallas_call(
        kernel,
        out_shape=outs,
        scratch_shapes=scratch,
        compiler_params=pltpu.CompilerParams(vmem_limit_bytes=32 * 1024 * 1024),
        cost_estimate=pl.CostEstimate(flops=flops, bytes_accessed=moved, transcendentals=0),
    )


def shaped(*shape):
    return jax.ShapeDtypeStruct(shape, F32)


def line_perm(axis, step):
    count = lax.axis_size(axis)
    if step > 0:
        return [(i, i + 1) for i in range(count - 1)]
    return [(i + 1, i) for i in range(count - 1)]


def swap_perm(axis, bit):
    return [(i, i ^ bit) for i in range(lax.axis_size(axis))]


def shards(volume):
    flat = volume.reshape(PLANES * ROWS, COLS)
    lines = shaped(ROWS, PLANES, COLS)
    whole = shaped(PLANES * ROWS, COLS)
    port = shaped(5, ROWS, COLS)
    side = shaped(PLANES + 1, COLS)
    to_low, to_high = pl.pallas_call(
        edge_kernel,
        in_specs=[pl.BlockSpec(memory_space=pl.ANY)],
        out_shape=(shaped(2 * ROWS, COLS), shaped(ROWS, COLS)),
        scratch_shapes=[pltpu.SemaphoreType.DMA((2,))],
    )(flat)
    low_plane = lax.ppermute(to_high, "depth", line_perm("depth", 1))
    high_planes = lax.ppermute(to_low, "depth", line_perm("depth", -1))
    y_port, y_factor, y_back, y_rest, deep, row_low, row_high = call(
        row_kernel,
        (
            shaped(PLANES * PORT, COLS), lines, lines, lines,
            shaped((PLANES + 1) * ROWS, COLS), side, side,
        ),
        (pltpu.VMEM((PLANES + 3, ROWS, COLS), F32),),
    )(flat, low_plane, high_planes)
    ports = lax.all_to_all(y_port, "lat", 0, 0, tiled=True)
    low_row = lax.ppermute(row_high, "lat", line_perm("lat", 1))
    high_row = lax.ppermute(row_low, "lat", line_perm("lat", -1))
    z_port, z_factor, z_back, z_rest, z_mid, solved_x = call(
        plane_column_kernel,
        (port, whole, whole, whole, shaped(3, ROWS, COLS), whole),
        (
            pltpu.VMEM(((PLANES + 1) * ROWS, COLS), F32),
            pltpu.VMEM((512, COLS), F32),
            pltpu.VMEM((512, COLS), F32),
            pltpu.VMEM((16, 32, COLS), F32),
            pltpu.VMEM((16, 32, COLS), F32),
            pltpu.VMEM((16, 32, COLS), F32),
        ),
    )(flat, deep, low_row, high_row)
    near = lax.ppermute(z_port, "depth", swap_perm("depth", 1))
    pair_own = call(lambda *refs: join_kernel(1, *refs), port)(z_port, near)
    ends = call(row_reduced_kernel, shaped(BLOCKS, 4, COLS))(ports)
    ends, pair_own = lax.optimization_barrier((ends, pair_own))
    ends_y = lax.all_to_all(ends, "lat", 0, 0, tiled=True)
    pair, across, skew = (lax.ppermute(pair_own, "depth", swap_perm("depth", bits)) for bits in (2, 4, 6))
    out = call(finish_kernel, whole, (pltpu.VMEM((PLANES * ROWS, COLS), F32),))(
        ends_y, y_factor, y_back, y_rest, z_port, near, pair, across, skew,
        z_factor, z_back, z_rest, z_mid, solved_x,
    )
    return out.reshape(PLANES, ROWS, COLS)


def solution(mesh):
    placed = (P("depth", "lat", None),)
    return jax.shard_map(
        shards, mesh=mesh, in_specs=placed, out_specs=P("depth", "lat", None), check_vma=False
    )
```

time: 60.4 us -> 54.9 us (0.909)
  the two profiles are of different devices: /device:TPU:6 before, /device:TPU:8 now
where the time goes in v2:
time: 54.9 us; the launch traced here: 54.3 us
  starting transfers between devices  33.4 us (61%)
  waiting for transfers between devices  15.4 us (28%)
  Pallas kernels  5.39 us (10%)
    all_to_all x1, starting transfers between devices, shards(): ports = lax.all_to_all(y_port, 'lat', 0, 0, tiled=True)  10.8 us
    all_to_all x1, starting transfers between devices, shards(): ends_y = lax.all_to_all(ends, 'lat', 0, 0, tiled=True)  9.08 us
    ppermute x1, waiting for transfers between devices, shards(): high_row = lax.ppermute(row_low, 'lat', line_perm('lat', -1))  4.21 us
    ppermute x3, starting transfers between devices, shards(): lax.ppermute(pair_own, 'depth', swap_perm('depth', bits))  4.18 us
    ppermute x1, starting transfers between devices, shards(): low_row = lax.ppermute(row_high, 'lat', line_perm('lat', 1))  3.69 us
    ppermute x1, waiting for transfers between devices, shards(): low_plane = lax.ppermute(to_high, 'depth', line_perm('depth', 1))  3.32 us
    ppermute x3, waiting for transfers between devices, shards(): lax.ppermute(pair_own, 'depth', swap_perm('depth', bits))  3.23 us
    all_to_all x1, waiting for transfers between devices, shards(): ends_y = lax.all_to_all(ends, 'lat', 0, 0, tiled=True)  2.6 us
  transfers between devices with their start and end apart: 10, of which 7 were waited for; matrix products, arithmetic and copies ran while one was open for 0% of the time, Pallas kernels for 2%

profile of v2, /device:TPU:8, one launch (start us, length us, event | category | flops | bytes accessed | tf_op | source)
XLA Modules:
  0.0 54.3 jit_solution(3550803526167604095)
XLA Ops:
  0.0 0.0 copy-start
  0.0 1.4 %shard_map.17 = (f32[32,128]{1,0:T(8,128)}, f32[16,128]{1,0:T(8,128)}) custom-call(f32[512,128]{1,0:T(8,128)} %bitcast.4), custom_call_target="tpu_custom_call" | custom-call | tf_op jit(solution)/shard_map/pallas_call | solution.py:350
  1.4 1.9 %collective-permute-start.1 = (f32[32,128]{1,0:T(8,128)}, f32[32,128]{1,0:T(8,128)S(1)}, u32[]{:S(2)}, u32[]{:S(2)}) collective-permute-start(f32[32,128]{1,0:T(8,128)} %get-tuple-element.23), channel_id=1, source_target_pairs={{32,0},{64,32},{96,64},{128,96},{160,128},{192,160},{224,192},{33,... | collective-permute-start | bytes 49160 | tf_op jit(solution)/shard_map/ppermute | solution.py:357
  3.4 2.4 %collective-permute-start = (f32[16,128]{1,0:T(8,128)}, f32[16,128]{1,0:T(8,128)S(1)}, u32[]{:S(2)}, u32[]{:S(2)}) collective-permute-start(f32[16,128]{1,0:T(8,128)} %get-tuple-element.22), channel_id=1, source_target_pairs={{0,32},{32,64},{64,96},{96,128},{128,160},{160,192},{192,224},{1,3... | collective-permute-start | bytes 24584 | tf_op jit(solution)/shard_map/ppermute | solution.py:356
  5.8 3.3 %collective-permute-done.low_plane = f32[16,128]{1,0:T(8,128)S(1)} collective-permute-done((f32[16,128]{1,0:T(8,128)}, f32[16,128]{1,0:T(8,128)S(1)}, u32[]{:S(2)}, u32[]{:S(2)}) %collective-permute-start) | collective-permute-done | bytes 8224 | tf_op jit(solution)/shard_map/ppermute | solution.py:356
  9.1 0.0 collective-permute-done.1.high_planes
  9.1 0.0 copy-done
  9.1 1.3 %shard_map.18 = (f32[512,128]{1,0:T(8,128)}, f32[16,32,128]{2,1,0:T(8,128)S(1)}, f32[16,32,128]{2,1,0:T(8,128)S(1)}, f32[16,32,128]{2,1,0:T(8,128)S(1)}, f32[528...) custom-call(f32[512,128]{1,0:T(8,128)S(1)} %bitcast.5, ...), custom_call_target="tpu_custom_call" | custom-call | flops 1000000 | bytes 500000 | tf_op jit(solution)/shard_map/pallas_call | solution.py:358
  10.4 10.8 %all-to-all-start = ((f32[32,16,128]{2,1,0:T(8,128)}), f32[32,16,128]{2,1,0:T(8,128)S(1)}, u32[]{:S(2)}, u32[]{:S(2)}) async-start(f32[32,16,128]{2,1,0:T(8,128)} %bitcast.1), calls=%async_computation | async-start | bytes 524288 | tf_op jit(solution)/shard_map/all_to_all | solution.py:366
  21.1 3.7 %collective-permute-start.2 = (f32[33,128]{1,0:T(8,128)S(1)}, f32[33,128]{1,0:T(8,128)S(1)}, u32[]{:S(2)}, u32[]{:S(2)}) collective-permute-start(f32[33,128]{1,0:T(8,128)S(1)} %get-tuple-element.26), channel_id=1, source_target_pairs={{0,1},{1,2},{2,3},{3,4},{4,5},{5,6},{6,7},{7,8},{8,9},{9,10},{10,1... | collective-permute-start | bytes 50696 | tf_op jit(solution)/shard_map/ppermute | solution.py:367
  24.8 1.3 %collective-permute-start.3 = (f32[33,128]{1,0:T(8,128)S(1)}, f32[33,128]{1,0:T(8,128)S(1)}, u32[]{:S(2)}, u32[]{:S(2)}) collective-permute-start(f32[33,128]{1,0:T(8,128)S(1)} %get-tuple-element.27), channel_id=1, source_target_pairs={{1,0},{2,1},{3,2},{4,3},{5,4},{6,5},{7,6},{8,7},{9,8},{10,9},{11,1... | collective-permute-start | bytes 50696 | tf_op jit(solution)/shard_map/ppermute | solution.py:368
  26.1 0.2 collective-permute-done.2.low_row
  26.3 4.2 %collective-permute-done.3.high_row = f32[33,128]{1,0:T(8,128)S(1)} collective-permute-done((f32[33,128]{1,0:T(8,128)S(1)}, f32[33,128]{1,0:T(8,128)S(1)}, u32[]{:S(2)}, u32[]{:S(2)}) %collective-permute-start.3) | collective-permute-done | bytes 16928 | tf_op jit(solution)/shard_map/ppermute | solution.py:368
  30.5 0.9 %shard_map.20 = (f32[5,16,128]{2,1,0:T(8,128)S(1)}, f32[512,128]{1,0:T(8,128)S(1)}, f32[512,128]{1,0:T(8,128)S(1)}, f32[512,128]{1,0:T(8,128)S(1)}, f32[3,16,128]{2,1,0:T(8,128)S(1)}, /*index=5*/f32[512,128]{1,0:T(8,128)S(1)}) custom-call(f32[512,128]{1,0:T(8,128)S(1)} %bitcast.6, f32[528,128]{1,0:T(8,128)S(1)} %get-tuple-element.25.deep, ...), custom_call_target="tpu_custom_call" | custom-call | flops 1000000 | bytes 500000 | tf_op jit(solution)/shard_map/pallas_call | solution.py:369
  31.4 0.1 collective-permute-start.4
  31.5 1.2 %collective-permute-done.4.refs_1_.near = f32[5,16,128]{2,1,0:T(8,128)S(1)} collective-permute-done((f32[5,16,128]{2,1,0:T(8,128)S(1)}, f32[5,16,128]{2,1,0:T(8,128)S(1)}, u32[]{:S(2)}, u32[]{:S(2)}) %collective-permute-start.4) | collective-permute-done | bytes 40992 | tf_op jit(solution)/shard_map/ppermute | solution.py:381
  32.7 0.7 %all-to-all-done = f32[32,16,128]{2,1,0:T(8,128)S(1)} async-done(((f32[32,16,128]{2,1,0:T(8,128)}), f32[32,16,128]{2,1,0:T(8,128)S(1)}, u32[]{:S(2)}, u32[]{:S(2)}) %all-to-all-start) | async-done | bytes 262176 | tf_op jit(solution)/shard_map/all_to_all | solution.py:366
  33.4 0.8 %shard_map.19 = f32[32,4,128]{2,1,0:T(4,128)} custom-call(f32[512,128]{1,0:T(8,128)S(1)} %bitcast.7), custom_call_target="tpu_custom_call" | custom-call | flops 1000000 | bytes 500000 | tf_op jit(solution)/shard_map/pallas_call | solution.py:383
  34.3 9.1 %all-to-all-start.1 = ((f32[32,4,128]{2,1,0:T(4,128)}), f32[32,4,128]{2,1,0:T(4,128)S(1)}, u32[]{:S(2)}, u32[]{:S(2)}) async-start(f32[32,4,128]{2,1,0:T(4,128)} %shard_map.19), calls=%async_computation.1 | async-start | bytes 131072 | tf_op jit(solution)/shard_map/all_to_all | solution.py:385
  43.4 1.7 %collective-permute-start.7 = (f32[5,16,128]{2,1,0:T(8,128)S(1)}, f32[5,16,128]{2,1,0:T(8,128)S(1)}, u32[]{:S(2)}, u32[]{:S(2)}) collective-permute-start(f32[5,16,128]{2,1,0:T(8,128)S(1)} %shard_map.21), channel_id=1, source_target_pairs={{0,192},{32,224},{64,128},{96,160},{128,64},{160,96},{192,0},{224,... | collective-permute-start | bytes 122888 | tf_op jit(solution)/shard_map/ppermute | solution.py:386
  45.0 1.0 %collective-permute-start.6 = (f32[5,16,128]{2,1,0:T(8,128)S(1)}, f32[5,16,128]{2,1,0:T(8,128)S(1)}, u32[]{:S(2)}, u32[]{:S(2)}) collective-permute-start(f32[5,16,128]{2,1,0:T(8,128)S(1)} %shard_map.21), channel_id=1, source_target_pairs={{0,128},{32,160},{64,192},{96,224},{128,0},{160,32},{192,64},{224,... | collective-permute-start | bytes 122888 | tf_op jit(solution)/shard_map/ppermute | solution.py:386
  46.0 1.5 %collective-permute-start.5 = (f32[5,16,128]{2,1,0:T(8,128)S(1)}, f32[5,16,128]{2,1,0:T(8,128)S(1)}, u32[]{:S(2)}, u32[]{:S(2)}) collective-permute-start(f32[5,16,128]{2,1,0:T(8,128)S(1)} %shard_map.21), channel_id=1, source_target_pairs={{0,64},{32,96},{64,0},{96,32},{128,192},{160,224},{192,128},{224,1... | collective-permute-start | bytes 122888 | tf_op jit(solution)/shard_map/ppermute | solution.py:386
  47.6 0.0 collective-permute-done.7.skew
  47.6 3.2 %collective-permute-done.6.across = f32[5,16,128]{2,1,0:T(8,128)S(1)} collective-permute-done((f32[5,16,128]{2,1,0:T(8,128)S(1)}, f32[5,16,128]{2,1,0:T(8,128)S(1)}, u32[]{:S(2)}, u32[]{:S(2)}) %collective-permute-start.6) | collective-permute-done | bytes 40992 | tf_op jit(solution)/shard_map/ppermute | solution.py:386
  50.8 0.0 collective-permute-done.5.pair
  50.8 2.6 %all-to-all-done.1.ends_y = f32[32,4,128]{2,1,0:T(4,128)S(1)} async-done(((f32[32,4,128]{2,1,0:T(4,128)}), f32[32,4,128]{2,1,0:T(4,128)S(1)}, u32[]{:S(2)}, u32[]{:S(2)}) %all-to-all-start.1) | async-done | bytes 65568 | tf_op jit(solution)/shard_map/all_to_all | solution.py:385
  53.4 1.0 %shard_map.22 = f32[512,128]{1,0:T(8,128)} custom-call(f32[32,4,128]{2,1,0:T(4,128)S(1)} %all-to-all-done.1.ends_y, f32[16,32,128]{2,1,0:T(8,128)S(1)} %get-tuple-element.30.y_factor, f32[16,32,128]{2,1,0:T(8,128)S(1)} %get-tuple-element.31.y_back, f32[16,32,128]{2,1,0:T(8,128)S(1)} %get-tuple-element.32.y_rest, ...), custom_call_target="tpu_custom_call" | custom-call | flops 1000000 | bytes 500000 | tf_op jit(solution)/shard_map/pallas_call | solution.py:387
  (1 shorter events, 0.0 us)
Async XLA Ops:
  0.0 9.1 %copy-start = (f32[32,16,128]{2,1,0:T(8,128)S(1)}, f32[32,16,128]{2,1,0:T(8,128)}, u32[]{:S(2)}) copy-start(f32[32,16,128]{2,1,0:T(8,128)} %param.1) | copy-start | bytes 786436
  1.4 7.7 %collective-permute-start.1 = (f32[32,128]{1,0:T(8,128)}, f32[32,128]{1,0:T(8,128)S(1)}, u32[]{:S(2)}, u32[]{:S(2)}) collective-permute-start(f32[32,128]{1,0:T(8,128)} %get-tuple-element.23), channel_id=1, source_target_pairs={{32,0},{64,32},{96,64},{128,96},{160,128},{192,160},{224,192},{33,... | collective-permute-start | bytes 49160 | tf_op jit(solution)/shard_map/ppermute | solution.py:357
  3.4 5.7 %collective-permute-start = (f32[16,128]{1,0:T(8,128)}, f32[16,128]{1,0:T(8,128)S(1)}, u32[]{:S(2)}, u32[]{:S(2)}) collective-permute-start(f32[16,128]{1,0:T(8,128)} %get-tuple-element.22), channel_id=1, source_target_pairs={{0,32},{32,64},{64,96},{96,128},{128,160},{160,192},{192,224},{1,3... | collective-permute-start | bytes 24584 | tf_op jit(solution)/shard_map/ppermute | solution.py:356
  10.4 23.1 %all-to-all-start = ((f32[32,16,128]{2,1,0:T(8,128)}), f32[32,16,128]{2,1,0:T(8,128)S(1)}, u32[]{:S(2)}, u32[]{:S(2)}) async-start(f32[32,16,128]{2,1,0:T(8,128)} %bitcast.1), calls=%async_computation | async-start | bytes 524288 | tf_op jit(solution)/shard_map/all_to_all | solution.py:366
  21.1 5.2 %collective-permute-start.2 = (f32[33,128]{1,0:T(8,128)S(1)}, f32[33,128]{1,0:T(8,128)S(1)}, u32[]{:S(2)}, u32[]{:S(2)}) collective-permute-start(f32[33,128]{1,0:T(8,128)S(1)} %get-tuple-element.26), channel_id=1, source_target_pairs={{0,1},{1,2},{2,3},{3,4},{4,5},{5,6},{6,7},{7,8},{8,9},{9,10},{10,1... | collective-permute-start | bytes 50696 | tf_op jit(solution)/shard_map/ppermute | solution.py:367
  24.8 5.7 %collective-permute-start.3 = (f32[33,128]{1,0:T(8,128)S(1)}, f32[33,128]{1,0:T(8,128)S(1)}, u32[]{:S(2)}, u32[]{:S(2)}) collective-permute-start(f32[33,128]{1,0:T(8,128)S(1)} %get-tuple-element.27), channel_id=1, source_target_pairs={{1,0},{2,1},{3,2},{4,3},{5,4},{6,5},{7,6},{8,7},{9,8},{10,9},{11,1... | collective-permute-start | bytes 50696 | tf_op jit(solution)/shard_map/ppermute | solution.py:368
  31.4 1.3 %collective-permute-start.4 = (f32[5,16,128]{2,1,0:T(8,128)S(1)}, f32[5,16,128]{2,1,0:T(8,128)S(1)}, u32[]{:S(2)}, u32[]{:S(2)}) collective-permute-start(f32[5,16,128]{2,1,0:T(8,128)S(1)} %get-tuple-element.28.refs_0_.own), channel_id=1, source_target_pairs={{0,32},{32,0},{64,96},{96,64},{128,160},{160,128},{192,224},{224,1... | collective-permute-start | bytes 122888 | tf_op jit(solution)/shard_map/ppermute | solution.py:381
  34.3 19.1 %all-to-all-start.1 = ((f32[32,4,128]{2,1,0:T(4,128)}), f32[32,4,128]{2,1,0:T(4,128)S(1)}, u32[]{:S(2)}, u32[]{:S(2)}) async-start(f32[32,4,128]{2,1,0:T(4,128)} %shard_map.19), calls=%async_computation.1 | async-start | bytes 131072 | tf_op jit(solution)/shard_map/all_to_all | solution.py:385
  43.4 4.2 %collective-permute-start.7 = (f32[5,16,128]{2,1,0:T(8,128)S(1)}, f32[5,16,128]{2,1,0:T(8,128)S(1)}, u32[]{:S(2)}, u32[]{:S(2)}) collective-permute-start(f32[5,16,128]{2,1,0:T(8,128)S(1)} %shard_map.21), channel_id=1, source_target_pairs={{0,192},{32,224},{64,128},{96,160},{128,64},{160,96},{192,0},{224,... | collective-permute-start | bytes 122888 | tf_op jit(solution)/shard_map/ppermute | solution.py:386
  45.0 5.7 %collective-permute-start.6 = (f32[5,16,128]{2,1,0:T(8,128)S(1)}, f32[5,16,128]{2,1,0:T(8,128)S(1)}, u32[]{:S(2)}, u32[]{:S(2)}) collective-permute-start(f32[5,16,128]{2,1,0:T(8,128)S(1)} %shard_map.21), channel_id=1, source_target_pairs={{0,128},{32,160},{64,192},{96,224},{128,0},{160,32},{192,64},{224,... | collective-permute-start | bytes 122888 | tf_op jit(solution)/shard_map/ppermute | solution.py:386
  46.0 4.8 %collective-permute-start.5 = (f32[5,16,128]{2,1,0:T(8,128)S(1)}, f32[5,16,128]{2,1,0:T(8,128)S(1)}, u32[]{:S(2)}, u32[]{:S(2)}) collective-permute-start(f32[5,16,128]{2,1,0:T(8,128)S(1)} %shard_map.21), channel_id=1, source_target_pairs={{0,64},{32,96},{64,0},{96,32},{128,192},{160,224},{192,128},{224,1... | collective-permute-start | bytes 122888 | tf_op jit(solution)/shard_map/ppermute | solution.py:386

commit v3 on v2

v3 whole, which is shorter than its diff:
```python
import jax
import jax.numpy as jnp
from jax import lax
from jax.experimental import pallas as pl
from jax.experimental.pallas import tpu as pltpu
from jax.sharding import PartitionSpec as P

TAU3 = 900.0
INV_LAMBDA_SQ = 4.0
PLANES = 32
ROWS = 16
COLS = 128
BLOCKS = 32
PORT = 8
F32 = jnp.float32


def resistance(diff):
    return (1.0 + INV_LAMBDA_SQ * (diff * diff)) * (1.0 / TAU3)


def smooth_lanes(field, first, last):
    before = jnp.where(first, 0.0, pltpu.roll(field, 1, field.ndim - 1))
    after = jnp.where(last, 0.0, pltpu.roll(field, COLS - 1, field.ndim - 1))
    return 0.25 * (before + 2.0 * field + after)


def eliminate(coupling, ground, source, near_ground, near_source, resist):
    factor = 1.0 / (1.0 + (coupling + ground) * resist)
    weight = factor * resist
    back = coupling * weight
    near_ground = near_ground + back * ground
    near_source = near_source + back * source
    saved = (factor, back, source * weight)
    return coupling * factor, ground * factor, source * factor, near_ground, near_source, saved


def eliminate_last(coupling, ground, source, near_ground, near_source, conduct):
    inverse = 1.0 / (coupling + ground + conduct)
    factor = conduct * inverse
    back = coupling * inverse
    near_ground = near_ground + back * ground
    near_source = near_source + back * source
    saved = (factor, back, source * inverse)
    return coupling * factor, ground * factor, source * factor, near_ground, near_source, saved


def join(left, right):
    lc, lg, lh, ls, lt = left
    rc, rg, rh, rs, rt = right
    ground = lh + rg
    source = lt + rs
    inverse = 1.0 / (lc + rc + ground)
    to_left = lc * inverse
    to_right = rc * inverse
    return (
        lc * to_right,
        lg + to_left * ground,
        rh + to_right * ground,
        ls + to_left * source,
        rt + to_right * source,
    ), (to_left, to_right, source * inverse)


def edge_kernel(vol, near_side, far_side, sems):
    odd = lax.axis_index("depth") & 1
    high = (PLANES - 2) * ROWS
    near_start = pl.multiple_of((1 - odd) * high, ROWS)
    far_start = pl.multiple_of(odd * high, ROWS)
    copies = (
        pltpu.make_async_copy(vol.at[pl.ds(near_start, 2 * ROWS), :], near_side, sems.at[0]),
        pltpu.make_async_copy(vol.at[pl.ds(far_start, 2 * ROWS), :], far_side, sems.at[1]),
    )
    for copy in copies:
        copy.start()
    for copy in copies:
        copy.wait()


def strided(ref, row):
    return ref[pl.ds(row, 32, stride=16), :]


def cells(ref, plane):
    return ref[plane * ROWS : (plane + 1) * ROWS, :]


def deep_kernel(vol, near_side, far_side, deep, low_side, high_side, mixed):
    odd = (lax.axis_index("depth") & 1) == 1
    lane = lax.broadcasted_iota(jnp.int32, (ROWS, COLS), 1)
    first, last = lane == 0, lane == COLS - 1
    mixed[0] = smooth_lanes(jnp.where(odd, cells(near_side, 1), cells(far_side, 1)), first, last)
    for plane in range(PLANES):
        mixed[plane + 1] = smooth_lanes(cells(vol, plane), first, last)
    for plane in range(2):
        mixed[PLANES + 1 + plane] = smooth_lanes(
            jnp.where(odd, cells(far_side, plane), cells(near_side, plane)), first, last
        )
    for plane in range(PLANES + 1):
        deep[plane * ROWS : (plane + 1) * ROWS, :] = 0.25 * (
            mixed[plane] + 2.0 * mixed[plane + 1] + mixed[plane + 2]
        )
    low_side[...] = deep[pl.ds(0, PLANES + 1, stride=ROWS), :]
    high_side[...] = deep[pl.ds(ROWS - 1, PLANES + 1, stride=ROWS), :]


def plane_kernel(vol, deep, low_row, high_row, port, factor, back, rest, mid, smooth):
    depth_last = lax.axis_index("depth") == lax.axis_size("depth") - 1
    z_open = jnp.where(depth_last, 0.0, TAU3).astype(F32)
    row_index = lax.broadcasted_iota(jnp.int32, (ROWS, COLS), 0)
    top, bottom = row_index == 0, row_index == ROWS - 1
    for plane in range(PLANES + 1):
        span = slice(plane * ROWS, (plane + 1) * ROWS)
        here = deep[span, :]
        above = jnp.where(top, low_row[plane : plane + 1, :], pltpu.roll(here, 1, 0))
        below = jnp.where(bottom, high_row[plane : plane + 1, :], pltpu.roll(here, ROWS - 1, 0))
        smooth[span, :] = 0.25 * (above + 2.0 * here + below)

    def resist(plane):
        return resistance(cells(smooth, plane + 1) - cells(smooth, plane))

    half = PLANES // 2
    one = jnp.ones((ROWS, COLS), F32)
    states = [
        (1.0 / resist(start), one, cells(vol, start + 1), one, cells(vol, start)) for start in (0, half)
    ]
    for step in range(1, half):
        final = step == half - 1
        for part in range(2):
            plane = part * half + step
            span = slice(plane * ROWS, (plane + 1) * ROWS)
            if final and part == 1:
                *state, saved = eliminate_last(*states[part], z_open / (TAU3 * resist(plane)))
            else:
                *state, saved = eliminate(*states[part], resist(plane))
            if not final:
                state[1] = state[1] + 1.0
                state[2] = state[2] + cells(vol, plane + 1)
            states[part] = state
            factor[span, :], back[span, :], rest[span, :] = saved
    joined, middle = join(*[(c, ng, fg, ns, fs) for c, fg, fs, ng, ns in states])
    for place, value in enumerate(joined):
        port[place] = value
    for place, value in enumerate(middle):
        mid[place] = value


def row_kernel(vol, smooth, port, factor, back, rest):
    def resist(row):
        return resistance(strided(smooth, row + 1) - strided(smooth, row))

    one = jnp.ones((PLANES, COLS), F32)
    state = (1.0 / resist(0), one, strided(vol, 1), one, strided(vol, 0))
    for row in range(1, ROWS - 1):
        *state, saved = eliminate(*state, resist(row))
        state[1] = state[1] + 1.0
        state[2] = state[2] + strided(vol, row + 1)
        factor[row], back[row], rest[row] = saved
    coupling, far_ground, far_source, near_ground, near_source = state
    values = (
        coupling, near_ground, far_ground, near_source, far_source,
        strided(smooth, 0), strided(smooth, ROWS - 1), jnp.zeros((PLANES, COLS), F32),
    )
    for place, value in enumerate(values):
        port[pl.ds(place, PLANES, stride=PORT), :] = value


def chain_solve(coupling, near_ground, far_ground, near_source, far_source, count):
    size = coupling.shape[0]
    right = coupling
    ground = near_ground + pltpu.roll(far_ground, 1, 0)
    source = near_source + pltpu.roll(far_source, 1, 0)
    step = 1
    while step < count:
        left = pltpu.roll(right, step, 0)
        inverse = 1.0 / (ground + left + right)
        ground_part = ground * inverse
        source_part = source * inverse
        ground = (
            ground
            + left * pltpu.roll(ground_part, step, 0)
            + right * pltpu.roll(ground_part, size - step, 0)
        )
        source = (
            source
            + left * pltpu.roll(source_part, step, 0)
            + right * pltpu.roll(source_part, size - step, 0)
        )
        right = right * pltpu.roll(right * inverse, size - step, 0)
        step *= 2
    return source / ground


def column_kernel(vol, smooth, solved_x, turned, turned_smooth, factor, back, rest):
    for group in range(4):
        span = slice(group * COLS, (group + 1) * COLS)
        turned[span, :] = vol[span, :].T
        turned_smooth[span, :] = smooth[span, :].T

    def resist(step):
        if step < 15:
            return resistance(strided(turned_smooth, step + 1) - strided(turned_smooth, step))
        return resistance(pltpu.roll(strided(turned_smooth, 0), 31, 0) - strided(turned_smooth, 15))

    chunk_last = (lax.broadcasted_iota(jnp.int32, (32, COLS), 0) & 7) == 7
    one = jnp.ones((32, COLS), F32)
    state = (1.0 / resist(0), one, strided(turned, 1), one, strided(turned, 0))
    for step in range(1, 16):
        if step == 15:
            *state, saved = eliminate_last(*state, jnp.where(chunk_last, 0.0, 1.0 / resist(step)))
        else:
            *state, saved = eliminate(*state, resist(step))
            state[1] = state[1] + 1.0
            state[2] = state[2] + strided(turned, step + 1)
        factor[step], back[step], rest[step] = saved
    coupling, far_ground, far_source, near_ground, near_source = state
    first = chain_solve(coupling, near_ground, far_ground, near_source, far_source, 8)
    turned[pl.ds(0, 32, stride=16), :] = first
    value = pltpu.roll(first, 31, 0)
    for step in range(15, 0, -1):
        value = factor[step] * value + (back[step] * first + rest[step])
        turned[pl.ds(step, 32, stride=16), :] = value
    for group in range(4):
        span = slice(group * COLS, (group + 1) * COLS)
        solved_x[span, :] = turned[span, :].T


def row_reduced_kernel(ports, out):
    coupling, near_ground, far_ground, near_source, far_source, low, high = (
        ports[pl.ds(place, BLOCKS, stride=PORT), :] for place in range(7)
    )
    block_last = lax.broadcasted_iota(jnp.int32, (BLOCKS, COLS), 0) == BLOCKS - 1
    across = pltpu.roll(low, BLOCKS - 1, 0) - high
    across = jnp.where(block_last, 0.0, 1.0 / resistance(across))
    zero = jnp.zeros_like(coupling)
    whole, at_high = join(
        (coupling, near_ground, far_ground, near_source, far_source), (across, zero, zero, zero, zero)
    )
    first = chain_solve(*whole, BLOCKS)
    out[:, 0, :] = first
    out[:, 1, :] = at_high[0] * first + at_high[1] * pltpu.roll(first, BLOCKS - 1, 0) + at_high[2]


def pick(flag, there, here):
    return tuple(jnp.where(flag, a, b) for a, b in zip(there, here))


def join_kernel(bit, own, other, out):
    upper = (lax.axis_index("depth") & bit) != 0
    mine = tuple(own[place] for place in range(5))
    theirs = tuple(other[place] for place in range(5))
    port, _ = join(pick(upper, theirs, mine), pick(upper, mine, theirs))
    for place, value in enumerate(port):
        out[place] = value


def finish_kernel(
    ends_y, y_factor, y_back, y_rest, own, near, pair, quad, z_factor, z_back, z_rest, z_mid, solved_x,
    out, acc,
):
    index = lax.axis_index("depth")
    zero = jnp.zeros((ROWS, COLS), F32)
    left_ground, left_source, right_ground, right_source = zero, zero, zero, zero
    for bit, ref in ((4, quad), (2, pair), (1, near)):
        on_left = (index & bit) != 0
        c, ng, fg, ns, fs = (ref[place] for place in range(5))
        ground, source = ng + left_ground, ns + left_source
        share = c / (c + ground)
        left_ground = jnp.where(on_left, fg + share * ground, left_ground)
        left_source = jnp.where(on_left, fs + share * source, left_source)
        ground, source = fg + right_ground, fs + right_source
        total = c + ground
        share = jnp.where(total > 0.0, c / jnp.where(total > 0.0, total, 1.0), 0.0)
        right_ground = jnp.where(on_left, right_ground, ng + share * ground)
        right_source = jnp.where(on_left, right_source, ns + share * source)
    c, ng, fg, ns, fs = (own[place] for place in range(5))
    ground, source = fg + right_ground, fs + right_source
    total = c + ground
    inverse = jnp.where(total > 0.0, 1.0 / jnp.where(total > 0.0, total, 1.0), 0.0)
    share = c * inverse
    first = (left_source + ns + share * source) / (left_ground + ng + share * ground)
    after = share * first + source * inverse
    middle = z_mid[0] * first + z_mid[1] * after + z_mid[2]
    half = PLANES // 2
    y_first = ends_y[:, 0, :]
    value = ends_y[:, 1, :]
    acc[pl.ds(0, PLANES, stride=ROWS), :] = y_first
    acc[pl.ds(ROWS - 1, PLANES, stride=ROWS), :] = value
    for row in range(ROWS - 2, 0, -1):
        value = y_factor[row] * value + (y_back[row] * y_first + y_rest[row])
        acc[pl.ds(row, PLANES, stride=ROWS), :] = value
    third = 1.0 / 3.0
    for start, near_value, far_value in ((0, first, middle), (half, middle, after)):
        value = far_value
        for plane in range(start + half - 1, start, -1):
            span = slice(plane * ROWS, (plane + 1) * ROWS)
            value = z_factor[span, :] * value + (z_back[span, :] * near_value + z_rest[span, :])
            out[span, :] = (solved_x[span, :] + acc[span, :] + value) * third
        span = slice(start * ROWS, (start + 1) * ROWS)
        out[span, :] = (solved_x[span, :] + acc[span, :] + near_value) * third


def call(kernel, outs, scratch=(), flops=1000000, moved=500000, **options):
    return pl.pallas_call(
        kernel,
        out_shape=outs,
        scratch_shapes=scratch,
        compiler_params=pltpu.CompilerParams(vmem_limit_bytes=16 * 1024 * 1024),
        cost_estimate=pl.CostEstimate(flops=flops, bytes_accessed=moved, transcendentals=0),
        **options,
    )


def shaped(*shape):
    return jax.ShapeDtypeStruct(shape, F32)


def line_perm(axis, step):
    count = lax.axis_size(axis)
    if step > 0:
        return [(i, i + 1) for i in range(count - 1)]
    return [(i + 1, i) for i in range(count - 1)]


def swap_perm(axis, bit):
    return [(i, i ^ bit) for i in range(lax.axis_size(axis))]


def next_perm(axis):
    pairs = []
    for i in range(1, lax.axis_size(axis) - 1, 2):
        pairs += [(i, i + 1), (i + 1, i)]
    return pairs


def shards(volume):
    flat = volume.reshape(PLANES * ROWS, COLS)
    lines = shaped(ROWS, PLANES, COLS)
    whole = shaped(PLANES * ROWS, COLS)
    tall = shaped((PLANES + 1) * ROWS, COLS)
    port = shaped(5, ROWS, COLS)
    side = shaped(PLANES + 1, COLS)
    to_near, to_far = call(
        edge_kernel,
        (shaped(2 * ROWS, COLS), shaped(2 * ROWS, COLS)),
        (pltpu.SemaphoreType.DMA((2,)),),
        in_specs=[pl.BlockSpec(memory_space=pl.ANY)],
    )(flat)
    far_side = lax.ppermute(to_far, "depth", next_perm("depth"))
    near_side = lax.ppermute(to_near, "depth", swap_perm("depth", 1))
    deep, row_low, row_high = call(
        deep_kernel, (tall, side, side), (pltpu.VMEM((PLANES + 3, ROWS, COLS), F32),)
    )(flat, near_side, far_side)
    low_row = lax.ppermute(row_high, "lat", line_perm("lat", 1))
    high_row = lax.ppermute(row_low, "lat", line_perm("lat", -1))
    z_port, z_factor, z_back, z_rest, z_mid, smooth = call(
        plane_kernel, (port, whole, whole, whole, shaped(3, ROWS, COLS), tall)
    )(flat, deep, low_row, high_row)
    near = lax.ppermute(z_port, "depth", swap_perm("depth", 1))
    y_port, y_factor, y_back, y_rest = call(row_kernel, (shaped(PLANES * PORT, COLS), lines, lines, lines))(
        flat, smooth
    )
    pair_own = call(lambda *refs: join_kernel(1, *refs), port)(z_port, near)
    flat_later, smooth_later, pair_own = lax.optimization_barrier((flat, smooth, pair_own))
    pair = lax.ppermute(pair_own, "depth", swap_perm("depth", 2))
    solved_x = call(
        column_kernel,
        whole,
        (
            pltpu.VMEM((512, COLS), F32),
            pltpu.VMEM((512, COLS), F32),
            pltpu.VMEM((16, 32, COLS), F32),
            pltpu.VMEM((16, 32, COLS), F32),
            pltpu.VMEM((16, 32, COLS), F32),
        ),
    )(flat_later, smooth_later)
    y_port, solved_x = lax.optimization_barrier((y_port, solved_x))
    ports = lax.all_to_all(y_port, "lat", 0, 0, tiled=True)
    ports, pair = lax.optimization_barrier((ports, pair))
    quad_own = call(lambda *refs: join_kernel(2, *refs), port)(pair_own, pair)
    ports, quad_own = lax.optimization_barrier((ports, quad_own))
    quad = lax.ppermute(quad_own, "depth", swap_perm("depth", 4))
    ends = call(row_reduced_kernel, shaped(BLOCKS, 2, COLS))(ports)
    ends_y = lax.all_to_all(ends, "lat", 0, 0, tiled=True)
    ends_y, quad = lax.optimization_barrier((ends_y, quad))
    out = call(finish_kernel, whole, (pltpu.VMEM((PLANES * ROWS, COLS), F32),))(
        ends_y, y_factor, y_back, y_rest, z_port, near, pair, quad, z_factor, z_back, z_rest, z_mid, solved_x
    )
    return out.reshape(PLANES, ROWS, COLS)


def solution(mesh):
    placed = (P("depth", "lat", None),)
    return jax.shard_map(
        shards, mesh=mesh, in_specs=placed, out_specs=P("depth", "lat", None), check_vma=False
    )
```

time: 54.9 us -> 55.9 us (1.018)
  waiting for transfers between devices: 15.4 us -> 24.1 us
  starting transfers between devices: 33.4 us -> 26.4 us
  Pallas kernels: 5.39 us -> 3.98 us
  local copies, waits for them, and re-layouts: 0.01 us -> 0.96 us
    all_to_all x1, waiting for transfers between devices: 0.71 us -> 6.67 us  [shards(): ports = lax.all_to_all(y_port, 'lat', 0, 0, tiled=True)]
    all_to_all x1, starting transfers between devices: 9.08 us -> 3.85 us  [shards(): ends_y = lax.all_to_all(ends, 'lat', 0, 0, tiled=True)]
    ppermute x5 -> x4, waiting for transfers between devices: 6.56 us -> 8.61 us  [the longest x1 3.99 us: shards(): pair = lax.ppermute(pair_own, 'depth', swap_perm('depth', 2))]
    ppermute x5 -> x4, starting transfers between devices: 8.51 us -> 6.75 us  [the longest x1 4.18 us: shards(): far_side = lax.ppermute(to_far, 'depth', next_perm('depth'))]
    all_to_all x1, waiting for transfers between devices: 2.6 us -> 4.25 us  [shards(): ends_y = lax.all_to_all(ends, 'lat', 0, 0, tiled=True)]
    pallas_call x4 -> x7, Pallas kernels: 4.42 us -> 3.04 us  [the longest x1 1 us: shards(): call(row_kernel, (shaped(PLANES * PORT, COLS), lines, lines, lines))]
    ppermute x1, waiting for transfers between devices: 1.21 us -> 0.19 us  [shards(): near = lax.ppermute(z_port, 'depth', swap_perm('depth', 1))]
    unnamed x2 -> x4, local copies, waits for them, and re-layouts: 0.01 us -> 0.96 us
  transfers between devices with their start and end apart: 10 -> 9, of which waited for: 7 -> 8; matrix products, arithmetic and copies ran while one was open for 0% -> 0% of each run, Pallas kernels for 2% -> 2%
where the time goes in v3:
time: 55.9 us; the launch traced here: 55.6 us
  starting transfers between devices  26.4 us (47%)
  waiting for transfers between devices  24.1 us (43%)
  Pallas kernels  3.98 us (7%)
  local copies, waits for them, and re-layouts  0.96 us (2%)
    all_to_all x1, starting transfers between devices, shards(): ports = lax.all_to_all(y_port, 'lat', 0, 0, tiled=True)  11.2 us
    all_to_all x1, waiting for transfers between devices, shards(): ports = lax.all_to_all(y_port, 'lat', 0, 0, tiled=True)  6.67 us
    all_to_all x1, waiting for transfers between devices, shards(): ends_y = lax.all_to_all(ends, 'lat', 0, 0, tiled=True)  4.25 us
    ppermute x1, waiting for transfers between devices, shards(): high_row = lax.ppermute(row_low, 'lat', line_perm('lat', -1))  4.21 us
    ppermute x1, starting transfers between devices, shards(): far_side = lax.ppermute(to_far, 'depth', next_perm('depth'))  4.18 us
    ppermute x1, waiting for transfers between devices, shards(): pair = lax.ppermute(pair_own, 'depth', swap_perm('depth', 2))  3.99 us
    all_to_all x1, starting transfers between devices, shards(): ends_y = lax.all_to_all(ends, 'lat', 0, 0, tiled=True)  3.85 us
    ppermute x1, starting transfers between devices, shards(): low_row = lax.ppermute(row_high, 'lat', line_perm('lat', 1))  3.27 us
  transfers between devices with their start and end apart: 9, of which 8 were waited for; matrix products, arithmetic and copies ran while one was open for 0% of the time, Pallas kernels for 2%

profile of v3, /device:TPU:8, one launch (start us, length us, event | category | flops | bytes accessed | tf_op | source)
XLA Modules:
  0.0 55.6 jit_solution(6081967953717769442)
XLA Ops:
  0.0 0.0 copy-start
  0.0 0.9 %copy-done = f32[32,16,128]{2,1,0:T(8,128)S(1)} copy-done((f32[32,16,128]{2,1,0:T(8,128)S(1)}, f32[32,16,128]{2,1,0:T(8,128)}, u32[]{:S(2)}) %copy-start) | copy-done | bytes 262168
  1.0 0.1 collective-permute-start
  1.1 4.2 %collective-permute-start.1 = (f32[32,128]{1,0:T(8,128)S(1)}, f32[32,128]{1,0:T(8,128)S(1)}, u32[]{:S(2)}, u32[]{:S(2)}) collective-permute-start(f32[32,128]{1,0:T(8,128)S(1)} %get-tuple-element.32), channel_id=1, source_target_pairs={{32,64},{64,32},{96,128},{128,96},{160,192},{192,160},{33,65},{65,... | collective-permute-start | bytes 49160 | tf_op jit(solution)/shard_map/ppermute | solution.py:349
  5.3 0.0 collective-permute-done.near_side
  5.3 1.4 %collective-permute-done.1.far_side = f32[32,128]{1,0:T(8,128)S(1)} collective-permute-done((f32[32,128]{1,0:T(8,128)S(1)}, f32[32,128]{1,0:T(8,128)S(1)}, u32[]{:S(2)}, u32[]{:S(2)}) %collective-permute-start.1) | collective-permute-done | bytes 16416 | tf_op jit(solution)/shard_map/ppermute | solution.py:349
  6.7 0.2 shard_map.18
  6.9 3.3 %collective-permute-start.2 = (f32[33,128]{1,0:T(8,128)S(1)}, f32[33,128]{1,0:T(8,128)S(1)}, u32[]{:S(2)}, u32[]{:S(2)}) collective-permute-start(f32[33,128]{1,0:T(8,128)S(1)} %get-tuple-element.34), channel_id=1, source_target_pairs={{0,1},{1,2},{2,3},{3,4},{4,5},{5,6},{6,7},{7,8},{8,9},{9,10},{10,1... | collective-permute-start | bytes 50696 | tf_op jit(solution)/shard_map/ppermute | solution.py:354
  10.2 1.3 %collective-permute-start.3 = (f32[33,128]{1,0:T(8,128)S(1)}, f32[33,128]{1,0:T(8,128)S(1)}, u32[]{:S(2)}, u32[]{:S(2)}) collective-permute-start(f32[33,128]{1,0:T(8,128)S(1)} %get-tuple-element.35), channel_id=1, source_target_pairs={{1,0},{2,1},{3,2},{4,3},{5,4},{6,5},{7,6},{8,7},{9,8},{10,9},{11,1... | collective-permute-start | bytes 50696 | tf_op jit(solution)/shard_map/ppermute | solution.py:355
  11.5 0.2 collective-permute-done.2.low_row
  11.7 4.2 %collective-permute-done.3.high_row = f32[33,128]{1,0:T(8,128)S(1)} collective-permute-done((f32[33,128]{1,0:T(8,128)S(1)}, f32[33,128]{1,0:T(8,128)S(1)}, u32[]{:S(2)}, u32[]{:S(2)}) %collective-permute-start.3) | collective-permute-done | bytes 16928 | tf_op jit(solution)/shard_map/ppermute | solution.py:355
  15.9 0.3 shard_map.19
  16.2 0.1 collective-permute-start.4
  16.3 0.0 copy-start.1
  16.3 1.0 %shard_map.20 = (f32[256,128]{1,0:T(8,128)}, f32[16,32,128]{2,1,0:T(8,128)S(1)}, f32[16,32,128]{2,1,0:T(8,128)S(1)}, f32[16,32,128]{2,1,0:T(8,128)S(1)}) custom-call(f32[512,128]{1,0:T(8,128)S(1)} %bitcast.7, f32[528,128]{1,0:T(8,128)S(1)} %get-tuple-element.40.smooth), custom_call_target="tpu_custom_call" | custom-call | flops 1000000 | bytes 500000 | tf_op jit(solution)/shard_map/pallas_call | solution.py:360
  17.3 0.2 collective-permute-done.4.refs_1_.near
  17.5 0.0 copy-done.1
  17.6 0.7 %shard_map.22.solved_x = f32[512,128]{1,0:T(8,128)S(1)} custom-call(f32[512,128]{1,0:T(8,128)S(1)} %bitcast.8, f32[528,128]{1,0:T(8,128)S(1)} %get-tuple-element.40.smooth), custom_call_target="tpu_custom_call" | custom-call | flops 1000000 | bytes 500000 | tf_op jit(solution)/shard_map/pallas_call | solution.py:366
  18.2 11.2 %all-to-all-start = ((f32[32,8,128]{2,1,0:T(8,128)}), f32[32,8,128]{2,1,0:T(8,128)S(1)}, u32[]{:S(2)}, u32[]{:S(2)}) async-start(f32[32,8,128]{2,1,0:T(8,128)} %bitcast.1), calls=%async_computation | async-start | bytes 262144 | tf_op jit(solution)/shard_map/all_to_all | solution.py:378
  29.4 0.1 collective-permute-start.5
  29.5 4.0 %collective-permute-done.5.refs_1_.pair = f32[5,16,128]{2,1,0:T(8,128)S(1)} collective-permute-done((f32[5,16,128]{2,1,0:T(8,128)S(1)}, f32[5,16,128]{2,1,0:T(8,128)S(1)}, u32[]{:S(2)}, u32[]{:S(2)}) %collective-permute-start.5) | collective-permute-done | bytes 40992 | tf_op jit(solution)/shard_map/ppermute | solution.py:365
  33.5 6.7 %all-to-all-done = f32[32,8,128]{2,1,0:T(8,128)S(1)} async-done(((f32[32,8,128]{2,1,0:T(8,128)}), f32[32,8,128]{2,1,0:T(8,128)S(1)}, u32[]{:S(2)}, u32[]{:S(2)}) %all-to-all-start) | async-done | bytes 131104 | tf_op jit(solution)/shard_map/all_to_all | solution.py:378
  40.2 0.8 %shard_map.24 = f32[32,2,128]{2,1,0:T(2,128)} custom-call(f32[256,128]{1,0:T(8,128)S(1)} %bitcast.9), custom_call_target="tpu_custom_call" | custom-call | flops 1000000 | bytes 500000 | tf_op jit(solution)/shard_map/pallas_call | solution.py:383
  41.0 3.9 %all-to-all-start.1 = ((f32[32,2,128]{2,1,0:T(2,128)}), f32[32,2,128]{2,1,0:T(2,128)S(1)}, u32[]{:S(2)}, u32[]{:S(2)}) async-start(f32[32,2,128]{2,1,0:T(2,128)} %shard_map.24), calls=%async_computation.1 | async-start | bytes 65536 | tf_op jit(solution)/shard_map/all_to_all | solution.py:384
  44.8 2.4 %collective-permute-start.6 = (f32[5,16,128]{2,1,0:T(8,128)S(1)}, f32[5,16,128]{2,1,0:T(8,128)S(1)}, u32[]{:S(2)}, u32[]{:S(2)}) collective-permute-start(f32[5,16,128]{2,1,0:T(8,128)S(1)} %shard_map.23), channel_id=1, source_target_pairs={{0,128},{32,160},{64,192},{96,224},{128,0},{160,32},{192,64},{224,... | collective-permute-start | bytes 122888 | tf_op jit(solution)/shard_map/ppermute | solution.py:382
  47.2 3.2 %collective-permute-done.6.quad = f32[5,16,128]{2,1,0:T(8,128)S(1)} collective-permute-done((f32[5,16,128]{2,1,0:T(8,128)S(1)}, f32[5,16,128]{2,1,0:T(8,128)S(1)}, u32[]{:S(2)}, u32[]{:S(2)}) %collective-permute-start.6) | collective-permute-done | bytes 40992 | tf_op jit(solution)/shard_map/ppermute | solution.py:382
  50.4 4.3 %all-to-all-done.1.ends_y = f32[32,2,128]{2,1,0:T(2,128)S(1)} async-done(((f32[32,2,128]{2,1,0:T(2,128)}), f32[32,2,128]{2,1,0:T(2,128)S(1)}, u32[]{:S(2)}, u32[]{:S(2)}) %all-to-all-start.1) | async-done | bytes 32800 | tf_op jit(solution)/shard_map/all_to_all | solution.py:384
  54.7 0.9 %shard_map.25 = f32[512,128]{1,0:T(8,128)} custom-call(f32[32,2,128]{2,1,0:T(2,128)S(1)} %all-to-all-done.1.ends_y, f32[16,32,128]{2,1,0:T(8,128)S(1)} %get-tuple-element.48.y_factor, f32[16,32,128]{2,1,0:T(8,128)S(1)} %get-tuple-element.49.y_back, f32[16,32,128]{2,1,0:T(8,128)S(1)} %get-tuple-element.50.y_rest, ...), custom_call_target="tpu_custom_call" | custom-call | flops 1000000 | bytes 500000 | tf_op jit(solution)/shard_map/pallas_call | solution.py:386
  (3 shorter events, 0.1 us)
Async XLA Ops:
  0.0 0.9 %copy-start = (f32[32,16,128]{2,1,0:T(8,128)S(1)}, f32[32,16,128]{2,1,0:T(8,128)}, u32[]{:S(2)}) copy-start(f32[32,16,128]{2,1,0:T(8,128)} %param.1) | copy-start | bytes 786436
  1.0 4.3 %collective-permute-start = (f32[32,128]{1,0:T(8,128)S(1)}, f32[32,128]{1,0:T(8,128)S(1)}, u32[]{:S(2)}, u32[]{:S(2)}) collective-permute-start(f32[32,128]{1,0:T(8,128)S(1)} %get-tuple-element.31), channel_id=1, source_target_pairs={{0,32},{32,0},{64,96},{96,64},{128,160},{160,128},{192,224},{224,1... | collective-permute-start | bytes 49160 | tf_op jit(solution)/shard_map/ppermute | solution.py:350
  1.1 5.6 %collective-permute-start.1 = (f32[32,128]{1,0:T(8,128)S(1)}, f32[32,128]{1,0:T(8,128)S(1)}, u32[]{:S(2)}, u32[]{:S(2)}) collective-permute-start(f32[32,128]{1,0:T(8,128)S(1)} %get-tuple-element.32), channel_id=1, source_target_pairs={{32,64},{64,32},{96,128},{128,96},{160,192},{192,160},{33,65},{65,... | collective-permute-start | bytes 49160 | tf_op jit(solution)/shard_map/ppermute | solution.py:349
  6.9 4.7 %collective-permute-start.2 = (f32[33,128]{1,0:T(8,128)S(1)}, f32[33,128]{1,0:T(8,128)S(1)}, u32[]{:S(2)}, u32[]{:S(2)}) collective-permute-start(f32[33,128]{1,0:T(8,128)S(1)} %get-tuple-element.34), channel_id=1, source_target_pairs={{0,1},{1,2},{2,3},{3,4},{4,5},{5,6},{6,7},{7,8},{8,9},{9,10},{10,1... | collective-permute-start | bytes 50696 | tf_op jit(solution)/shard_map/ppermute | solution.py:354
  10.2 5.7 %collective-permute-start.3 = (f32[33,128]{1,0:T(8,128)S(1)}, f32[33,128]{1,0:T(8,128)S(1)}, u32[]{:S(2)}, u32[]{:S(2)}) collective-permute-start(f32[33,128]{1,0:T(8,128)S(1)} %get-tuple-element.35), channel_id=1, source_target_pairs={{1,0},{2,1},{3,2},{4,3},{5,4},{6,5},{7,6},{8,7},{9,8},{10,9},{11,1... | collective-permute-start | bytes 50696 | tf_op jit(solution)/shard_map/ppermute | solution.py:355
  16.2 1.3 %collective-permute-start.4 = (f32[5,16,128]{2,1,0:T(8,128)S(1)}, f32[5,16,128]{2,1,0:T(8,128)S(1)}, u32[]{:S(2)}, u32[]{:S(2)}) collective-permute-start(f32[5,16,128]{2,1,0:T(8,128)S(1)} %get-tuple-element.38.refs_0_.own), channel_id=1, source_target_pairs={{0,32},{32,0},{64,96},{96,64},{128,160},{160,128},{192,224},{224,1... | collective-permute-start | bytes 122888 | tf_op jit(solution)/shard_map/ppermute | solution.py:359
  16.3 1.2 %copy-start.1 = (f32[32,16,128]{2,1,0:T(8,128)S(1)}, f32[32,16,128]{2,1,0:T(8,128)}, u32[]{:S(2)}) copy-start(f32[32,16,128]{2,1,0:T(8,128)} %param.1) | copy-start | bytes 786436
  18.2 22.0 %all-to-all-start = ((f32[32,8,128]{2,1,0:T(8,128)}), f32[32,8,128]{2,1,0:T(8,128)S(1)}, u32[]{:S(2)}, u32[]{:S(2)}) async-start(f32[32,8,128]{2,1,0:T(8,128)} %bitcast.1), calls=%async_computation | async-start | bytes 262144 | tf_op jit(solution)/shard_map/all_to_all | solution.py:378
  29.4 4.1 %collective-permute-start.5 = (f32[5,16,128]{2,1,0:T(8,128)S(1)}, f32[5,16,128]{2,1,0:T(8,128)S(1)}, u32[]{:S(2)}, u32[]{:S(2)}) collective-permute-start(f32[5,16,128]{2,1,0:T(8,128)S(1)} %shard_map.21.refs_0_), channel_id=1, source_target_pairs={{0,64},{32,96},{64,0},{96,32},{128,192},{160,224},{192,128},{224,1... | collective-permute-start | bytes 122888 | tf_op jit(solution)/shard_map/ppermute | solution.py:365
  41.0 13.7 %all-to-all-start.1 = ((f32[32,2,128]{2,1,0:T(2,128)}), f32[32,2,128]{2,1,0:T(2,128)S(1)}, u32[]{:S(2)}, u32[]{:S(2)}) async-start(f32[32,2,128]{2,1,0:T(2,128)} %shard_map.24), calls=%async_computation.1 | async-start | bytes 65536 | tf_op jit(solution)/shard_map/all_to_all | solution.py:384
  44.8 5.6 %collective-permute-start.6 = (f32[5,16,128]{2,1,0:T(8,128)S(1)}, f32[5,16,128]{2,1,0:T(8,128)S(1)}, u32[]{:S(2)}, u32[]{:S(2)}) collective-permute-start(f32[5,16,128]{2,1,0:T(8,128)S(1)} %shard_map.23), channel_id=1, source_target_pairs={{0,128},{32,160},{64,192},{96,224},{128,0},{160,32},{192,64},{224,... | collective-permute-start | bytes 122888 | tf_op jit(solution)/shard_map/ppermute | solution.py:382

commit v4 on v3

--- a/solution.py
+++ b/solution.py
@@ -11,7 +11,8 @@
 ROWS = 16
 COLS = 128
 BLOCKS = 32
-PORT = 8
+PORT = 16
+LONG = 100_000_000_000
 F32 = jnp.float32
 
 
@@ -85,7 +86,7 @@
     return ref[plane * ROWS : (plane + 1) * ROWS, :]
 
 
-def deep_kernel(vol, near_side, far_side, deep, low_side, high_side, mixed):
+def deep_kernel(vol, near_side, far_side, deep, pair_row, next_row, mixed):
     odd = (lax.axis_index("depth") & 1) == 1
     lane = lax.broadcasted_iota(jnp.int32, (ROWS, COLS), 1)
     first, last = lane == 0, lane == COLS - 1
@@ -100,11 +101,17 @@
         deep[plane * ROWS : (plane + 1) * ROWS, :] = 0.25 * (
             mixed[plane] + 2.0 * mixed[plane + 1] + mixed[plane + 2]
         )
-    low_side[...] = deep[pl.ds(0, PLANES + 1, stride=ROWS), :]
-    high_side[...] = deep[pl.ds(ROWS - 1, PLANES + 1, stride=ROWS), :]
-
-
-def plane_kernel(vol, deep, low_row, high_row, port, factor, back, rest, mid, smooth):
+    odd_row = (lax.axis_index("lat") & 1) == 1
+    low = deep[pl.ds(0, PLANES + 1, stride=ROWS), :]
+    high = deep[pl.ds(ROWS - 1, PLANES + 1, stride=ROWS), :]
+    pair_row[...] = jnp.where(odd_row, low, high)
+    next_row[...] = jnp.where(odd_row, high, low)
+
+
+def plane_kernel(vol, deep, pair_row, next_row, port, factor, back, rest, mid, smooth):
+    odd_row = (lax.axis_index("lat") & 1) == 1
+    low_row = jnp.where(odd_row, pair_row[...], next_row[...])
+    high_row = jnp.where(odd_row, next_row[...], pair_row[...])
     depth_last = lax.axis_index("depth") == lax.axis_size("depth") - 1
     z_open = jnp.where(depth_last, 0.0, TAU3).astype(F32)
     row_index = lax.broadcasted_iota(jnp.int32, (ROWS, COLS), 0)
@@ -145,24 +152,28 @@
         mid[place] = value
 
 
-def row_kernel(vol, smooth, port, factor, back, rest):
-    def resist(row):
-        return resistance(strided(smooth, row + 1) - strided(smooth, row))
-
+def row_kernel(vol, deep, port, factor, back, rest):
+    part = [strided(deep, row) for row in range(ROWS)]
+    low_sum = 2.0 * part[0] + part[1]
+    high_sum = part[ROWS - 2] + 2.0 * part[ROWS - 1]
+    smooth = [None] + [0.25 * (part[r - 1] + 2.0 * part[r] + part[r + 1]) for r in range(1, ROWS - 1)]
     one = jnp.ones((PLANES, COLS), F32)
-    state = (1.0 / resist(0), one, strided(vol, 1), one, strided(vol, 0))
-    for row in range(1, ROWS - 1):
-        *state, saved = eliminate(*state, resist(row))
+    state = (1.0 / resistance(smooth[2] - smooth[1]), one, strided(vol, 2), one, strided(vol, 1))
+    for row in range(2, ROWS - 2):
+        *state, saved = eliminate(*state, resistance(smooth[row + 1] - smooth[row]))
         state[1] = state[1] + 1.0
         state[2] = state[2] + strided(vol, row + 1)
         factor[row], back[row], rest[row] = saved
     coupling, far_ground, far_source, near_ground, near_source = state
     values = (
         coupling, near_ground, far_ground, near_source, far_source,
-        strided(smooth, 0), strided(smooth, ROWS - 1), jnp.zeros((PLANES, COLS), F32),
+        part[0], part[ROWS - 1], low_sum, high_sum, smooth[1], smooth[ROWS - 2],
+        strided(vol, 0), strided(vol, ROWS - 1),
     )
     for place, value in enumerate(values):
         port[pl.ds(place, PLANES, stride=PORT), :] = value
+    for place in range(len(values), PORT):
+        port[pl.ds(place, PLANES, stride=PORT), :] = jnp.zeros((PLANES, COLS), F32)
 
 
 def chain_solve(coupling, near_ground, far_ground, near_source, far_source, count):
@@ -226,19 +237,36 @@
 
 
 def row_reduced_kernel(ports, out):
-    coupling, near_ground, far_ground, near_source, far_source, low, high = (
-        ports[pl.ds(place, BLOCKS, stride=PORT), :] for place in range(7)
-    )
-    block_last = lax.broadcasted_iota(jnp.int32, (BLOCKS, COLS), 0) == BLOCKS - 1
-    across = pltpu.roll(low, BLOCKS - 1, 0) - high
+    (
+        coupling, near_ground, far_ground, near_source, far_source,
+        low, high, low_sum, high_sum, low_smooth, high_smooth, low_cell, high_cell,
+    ) = (ports[pl.ds(place, BLOCKS, stride=PORT), :] for place in range(13))
+    block = lax.broadcasted_iota(jnp.int32, (BLOCKS, COLS), 0)
+    block_first, block_last = block == 0, block == BLOCKS - 1
+    low_end = 0.25 * (jnp.where(block_first, 0.0, pltpu.roll(high, 1, 0)) + low_sum)
+    high_end = 0.25 * (high_sum + jnp.where(block_last, 0.0, pltpu.roll(low, BLOCKS - 1, 0)))
+    enter = 1.0 / resistance(low_smooth - low_end)
+    leave = 1.0 / resistance(high_end - high_smooth)
+    across = pltpu.roll(low_end, BLOCKS - 1, 0) - high_end
     across = jnp.where(block_last, 0.0, 1.0 / resistance(across))
     zero = jnp.zeros_like(coupling)
-    whole, at_high = join(
-        (coupling, near_ground, far_ground, near_source, far_source), (across, zero, zero, zero, zero)
-    )
+    one = jnp.ones_like(coupling)
+    before, at_low = join(
+        (enter, one, zero, low_cell, zero), (coupling, near_ground, far_ground, near_source, far_source)
+    )
+    after, at_high = join((leave, zero, one, zero, high_cell), (across, zero, zero, zero, zero))
+    whole, between = join(before, after)
     first = chain_solve(*whole, BLOCKS)
+    later = pltpu.roll(first, BLOCKS - 1, 0)
+
+    def middle(weights, left, right):
+        return weights[0] * left + weights[1] * right + weights[2]
+
+    inner_high = middle(between, first, later)
     out[:, 0, :] = first
-    out[:, 1, :] = at_high[0] * first + at_high[1] * pltpu.roll(first, BLOCKS - 1, 0) + at_high[2]
+    out[:, 1, :] = middle(at_low, first, inner_high)
+    out[:, 2, :] = inner_high
+    out[:, 3, :] = middle(at_high, inner_high, later)
 
 
 def pick(flag, there, here):
@@ -254,11 +282,14 @@
         out[place] = value
 
 
-def finish_kernel(
-    ends_y, y_factor, y_back, y_rest, own, near, pair, quad, z_factor, z_back, z_rest, z_mid, solved_x,
-    out, acc,
+def finish_plane_kernel(
+    own, near, pair, across, skew, factor, back, rest, mid, solved_x, out,
 ):
     index = lax.axis_index("depth")
+    odd = (index & 2) != 0
+    straight = tuple(across[place] for place in range(5))
+    crossed = tuple(skew[place] for place in range(5))
+    quad, _ = join(pick(odd, crossed, straight), pick(odd, straight, crossed))
     zero = jnp.zeros((ROWS, COLS), F32)
     left_ground, left_source, right_ground, right_source = zero, zero, zero, zero
     for bit, ref in ((4, quad), (2, pair), (1, near)):
@@ -280,24 +311,32 @@
     share = c * inverse
     first = (left_source + ns + share * source) / (left_ground + ng + share * ground)
     after = share * first + source * inverse
-    middle = z_mid[0] * first + z_mid[1] * after + z_mid[2]
+    middle = mid[0] * first + mid[1] * after + mid[2]
     half = PLANES // 2
-    y_first = ends_y[:, 0, :]
-    value = ends_y[:, 1, :]
-    acc[pl.ds(0, PLANES, stride=ROWS), :] = y_first
-    acc[pl.ds(ROWS - 1, PLANES, stride=ROWS), :] = value
-    for row in range(ROWS - 2, 0, -1):
-        value = y_factor[row] * value + (y_back[row] * y_first + y_rest[row])
-        acc[pl.ds(row, PLANES, stride=ROWS), :] = value
-    third = 1.0 / 3.0
     for start, near_value, far_value in ((0, first, middle), (half, middle, after)):
         value = far_value
         for plane in range(start + half - 1, start, -1):
             span = slice(plane * ROWS, (plane + 1) * ROWS)
-            value = z_factor[span, :] * value + (z_back[span, :] * near_value + z_rest[span, :])
-            out[span, :] = (solved_x[span, :] + acc[span, :] + value) * third
+            value = factor[span, :] * value + (back[span, :] * near_value + rest[span, :])
+            out[span, :] = solved_x[span, :] + value
         span = slice(start * ROWS, (start + 1) * ROWS)
-        out[span, :] = (solved_x[span, :] + acc[span, :] + near_value) * third
+        out[span, :] = solved_x[span, :] + near_value
+
+
+def finish_row_kernel(ends, factor, back, rest, others, out):
+    third = 1.0 / 3.0
+
+    def put(row, value):
+        place = pl.ds(row, PLANES, stride=ROWS)
+        out[place, :] = (others[place, :] + value) * third
+
+    for place, row in ((0, 0), (1, 1), (2, ROWS - 2), (3, ROWS - 1)):
+        put(row, ends[:, place, :])
+    first = ends[:, 1, :]
+    value = ends[:, 2, :]
+    for row in range(ROWS - 3, 1, -1):
+        value = factor[row] * value + (back[row] * first + rest[row])
+        put(row, value)
 
 
 def call(kernel, outs, scratch=(), flops=1000000, moved=500000, **options):
@@ -348,21 +387,19 @@
     )(flat)
     far_side = lax.ppermute(to_far, "depth", next_perm("depth"))
     near_side = lax.ppermute(to_near, "depth", swap_perm("depth", 1))
-    deep, row_low, row_high = call(
+    deep, to_pair, to_next = call(
         deep_kernel, (tall, side, side), (pltpu.VMEM((PLANES + 3, ROWS, COLS), F32),)
     )(flat, near_side, far_side)
-    low_row = lax.ppermute(row_high, "lat", line_perm("lat", 1))
-    high_row = lax.ppermute(row_low, "lat", line_perm("lat", -1))
+    next_row = lax.ppermute(to_next, "lat", next_perm("lat"))
+    pair_row = lax.ppermute(to_pair, "lat", swap_perm("lat", 1))
+    y_port, y_factor, y_back, y_rest = call(row_kernel, (shaped(PLANES * PORT, COLS), lines, lines, lines))(
+        flat, deep
+    )
+    ports = lax.all_to_all(y_port, "lat", 0, 0, tiled=True)
     z_port, z_factor, z_back, z_rest, z_mid, smooth = call(
-        plane_kernel, (port, whole, whole, whole, shaped(3, ROWS, COLS), tall)
-    )(flat, deep, low_row, high_row)
+        plane_kernel, (port, whole, whole, whole, shaped(3, ROWS, COLS), tall), moved=500000,flops=LONG
+    )(flat, deep, pair_row, next_row)
     near = lax.ppermute(z_port, "depth", swap_perm("depth", 1))
-    y_port, y_factor, y_back, y_rest = call(row_kernel, (shaped(PLANES * PORT, COLS), lines, lines, lines))(
-        flat, smooth
-    )
-    pair_own = call(lambda *refs: join_kernel(1, *refs), port)(z_port, near)
-    flat_later, smooth_later, pair_own = lax.optimization_barrier((flat, smooth, pair_own))
-    pair = lax.ppermute(pair_own, "depth", swap_perm("depth", 2))
     solved_x = call(
         column_kernel,
         whole,
@@ -373,19 +410,16 @@
             pltpu.VMEM((16, 32, COLS), F32),
             pltpu.VMEM((16, 32, COLS), F32),
         ),
-    )(flat_later, smooth_later)
-    y_port, solved_x = lax.optimization_barrier((y_port, solved_x))
-    ports = lax.all_to_all(y_port, "lat", 0, 0, tiled=True)
-    ports, pair = lax.optimization_barrier((ports, pair))
-    quad_own = call(lambda *refs: join_kernel(2, *refs), port)(pair_own, pair)
-    ports, quad_own = lax.optimization_barrier((ports, quad_own))
-    quad = lax.ppermute(quad_own, "depth", swap_perm("depth", 4))
-    ends = call(row_reduced_kernel, shaped(BLOCKS, 2, COLS))(ports)
+    )(flat, smooth)
+    pair_own = call(lambda *refs: join_kernel(1, *refs), port)(z_port, near)
+    ports, pair_own, solved_x = lax.optimization_barrier((ports, pair_own, solved_x))
+    ends = call(row_reduced_kernel, shaped(BLOCKS, 4, COLS))(ports)
+    across, skew, pair = (lax.ppermute(pair_own, "depth", swap_perm("depth", bits)) for bits in (4, 6, 2))
+    others = call(finish_plane_kernel, whole, flops=LONG)(
+        z_port, near, pair, across, skew, z_factor, z_back, z_rest, z_mid, solved_x
+    )
     ends_y = lax.all_to_all(ends, "lat", 0, 0, tiled=True)
-    ends_y, quad = lax.optimization_barrier((ends_y, quad))
-    out = call(finish_kernel, whole, (pltpu.VMEM((PLANES * ROWS, COLS), F32),))(
-        ends_y, y_factor, y_back, y_rest, z_port, near, pair, quad, z_factor, z_back, z_rest, z_mid, solved_x
-    )
+    out = call(finish_row_kernel, whole)(ends_y, y_factor, y_back, y_rest, others)
     return out.reshape(PLANES, ROWS, COLS)
 
 

time: 55.9 us -> 55.7 us (level)
  waiting for transfers between devices: 24.1 us -> 22.7 us
  starting transfers between devices: 26.4 us -> 27.4 us
    ppermute x4 -> x5, waiting for transfers between devices: 11.6 us -> 0.01 us  [the longest x3 0.01 us: shards(): lax.ppermute(pair_own, 'depth', swap_perm('depth', bits))]
    all_to_all x1, waiting for transfers between devices: 4.25 us -> 9.91 us  [shards(): ends_y = lax.all_to_all(ends, 'lat', 0, 0, tiled=True)]
    all_to_all x1, waiting for transfers between devices: 6.67 us -> 10.8 us  [shards(): ports = lax.all_to_all(y_port, 'lat', 0, 0, tiled=True)]
    all_to_all x1, starting transfers between devices: 11.2 us -> 12.4 us  [shards(): ports = lax.all_to_all(y_port, 'lat', 0, 0, tiled=True)]
    ppermute x4 -> x5, starting transfers between devices: 7.04 us -> 6.19 us  [the longest x3 4.09 us: shards(): lax.ppermute(pair_own, 'depth', swap_perm('depth', bits))]
    all_to_all x1, starting transfers between devices: 3.85 us -> 4.44 us  [shards(): ends_y = lax.all_to_all(ends, 'lat', 0, 0, tiled=True)]
  transfers between devices with their start and end apart: 9 -> 10, of which waited for: 8 -> 4; matrix products, arithmetic and copies ran while one was open for 0% -> 0% of each run, Pallas kernels for 2% -> 6%
where the time goes in v4:
time: 55.7 us; the launch traced here: 55.4 us
  starting transfers between devices  27.4 us (49%)
  waiting for transfers between devices  22.7 us (41%)
  Pallas kernels  4.24 us (8%)
  local copies, waits for them, and re-layouts  0.95 us (2%)
    all_to_all x1, starting transfers between devices, shards(): ports = lax.all_to_all(y_port, 'lat', 0, 0, tiled=True)  12.4 us
    all_to_all x1, waiting for transfers between devices, shards(): ports = lax.all_to_all(y_port, 'lat', 0, 0, tiled=True)  10.8 us
    all_to_all x1, waiting for transfers between devices, shards(): ends_y = lax.all_to_all(ends, 'lat', 0, 0, tiled=True)  9.91 us
    all_to_all x1, starting transfers between devices, shards(): ends_y = lax.all_to_all(ends, 'lat', 0, 0, tiled=True)  4.44 us
    ppermute x1, starting transfers between devices, shards(): far_side = lax.ppermute(to_far, 'depth', next_perm('depth'))  4.18 us
    ppermute x3, starting transfers between devices, shards(): lax.ppermute(pair_own, 'depth', swap_perm('depth', bits))  4.09 us
    ppermute x1, starting transfers between devices, shards(): pair_row = lax.ppermute(to_pair, 'lat', swap_perm('lat', 1))  1.45 us
    ppermute x1, waiting for transfers between devices, shards(): far_side = lax.ppermute(to_far, 'depth', next_perm('depth'))  1.41 us
  transfers between devices with their start and end apart: 10, of which 4 were waited for; matrix products, arithmetic and copies ran while one was open for 0% of the time, Pallas kernels for 6%

profile of v4, /device:TPU:8, one launch (start us, length us, event | category | flops | bytes accessed | tf_op | source)
XLA Modules:
  0.0 55.4 jit_solution(9683615964910935275)
XLA Ops:
  0.0 0.0 copy-start
  0.0 0.9 %copy-done = f32[32,16,128]{2,1,0:T(8,128)S(1)} copy-done((f32[32,16,128]{2,1,0:T(8,128)S(1)}, f32[32,16,128]{2,1,0:T(8,128)}, u32[]{:S(2)}) %copy-start) | copy-done | bytes 262168
  1.0 0.1 collective-permute-start
  1.1 4.2 %collective-permute-start.1 = (f32[32,128]{1,0:T(8,128)S(1)}, f32[32,128]{1,0:T(8,128)S(1)}, u32[]{:S(2)}, u32[]{:S(2)}) collective-permute-start(f32[32,128]{1,0:T(8,128)S(1)} %get-tuple-element.24), channel_id=1, source_target_pairs={{32,64},{64,32},{96,128},{128,96},{160,192},{192,160},{33,65},{65,... | collective-permute-start | bytes 49160 | tf_op jit(solution)/shard_map/ppermute | solution.py:388
  5.3 0.0 collective-permute-done.near_side
  5.3 1.4 %collective-permute-done.1.far_side = f32[32,128]{1,0:T(8,128)S(1)} collective-permute-done((f32[32,128]{1,0:T(8,128)S(1)}, f32[32,128]{1,0:T(8,128)S(1)}, u32[]{:S(2)}, u32[]{:S(2)}) %collective-permute-start.1) | collective-permute-done | bytes 16416 | tf_op jit(solution)/shard_map/ppermute | solution.py:388
  6.7 0.2 shard_map.18
  6.9 1.4 %collective-permute-start.2 = (f32[33,128]{1,0:T(8,128)S(1)}, f32[33,128]{1,0:T(8,128)S(1)}, u32[]{:S(2)}, u32[]{:S(2)}) collective-permute-start(f32[33,128]{1,0:T(8,128)S(1)} %get-tuple-element.27), channel_id=1, source_target_pairs={{0,1},{1,0},{2,3},{3,2},{4,5},{5,4},{6,7},{7,6},{8,9},{9,8},{10,11... | collective-permute-start | bytes 50696 | tf_op jit(solution)/shard_map/ppermute | solution.py:394
  8.4 0.7 %collective-permute-start.3 = (f32[33,128]{1,0:T(8,128)S(1)}, f32[33,128]{1,0:T(8,128)S(1)}, u32[]{:S(2)}, u32[]{:S(2)}) collective-permute-start(f32[33,128]{1,0:T(8,128)S(1)} %get-tuple-element.28), channel_id=1, source_target_pairs={{1,2},{2,1},{3,4},{4,3},{5,6},{6,5},{7,8},{8,7},{9,10},{10,9},{11,... | collective-permute-start | bytes 50696 | tf_op jit(solution)/shard_map/ppermute | solution.py:393
  9.1 1.1 %shard_map.19 = (f32[512,128]{1,0:T(8,128)}, f32[16,32,128]{2,1,0:T(8,128)S(1)}, f32[16,32,128]{2,1,0:T(8,128)S(1)}, f32[16,32,128]{2,1,0:T(8,128)S(1)}) custom-call(f32[512,128]{1,0:T(8,128)S(1)} %bitcast.6, f32[528,128]{1,0:T(8,128)S(1)} %get-tuple-element.25.deep), custom_call_target="tpu_custom_call" | custom-call | flops 1000000 | bytes 500000 | tf_op jit(solution)/shard_map/pallas_call | solution.py:395
  10.1 0.0 copy-start.1
  10.1 12.4 %all-to-all-start = ((f32[32,16,128]{2,1,0:T(8,128)}), f32[32,16,128]{2,1,0:T(8,128)S(1)}, u32[]{:S(2)}, u32[]{:S(2)}) async-start(f32[32,16,128]{2,1,0:T(8,128)} %bitcast.1), calls=%async_computation | async-start | bytes 524288 | tf_op jit(solution)/shard_map/all_to_all | solution.py:398
  22.5 0.0 collective-permute-done.2.pair_row
  22.5 0.0 collective-permute-done.3.next_row
  22.5 0.0 copy-done.1
  22.5 0.3 shard_map.20
  22.9 0.1 collective-permute-start.4
  23.0 0.7 %shard_map.22.solved_x = f32[512,128]{1,0:T(8,128)S(1)} custom-call(f32[512,128]{1,0:T(8,128)S(1)} %bitcast.8, f32[528,128]{1,0:T(8,128)S(1)} %get-tuple-element.30.smooth), custom_call_target="tpu_custom_call" | custom-call | flops 1000000 | bytes 500000 | tf_op jit(solution)/shard_map/pallas_call | solution.py:403
  23.7 0.5 collective-permute-done.4.refs_1_.near
  24.2 10.8 %all-to-all-done = f32[32,16,128]{2,1,0:T(8,128)S(1)} async-done(((f32[32,16,128]{2,1,0:T(8,128)}), f32[32,16,128]{2,1,0:T(8,128)S(1)}, u32[]{:S(2)}, u32[]{:S(2)}) %all-to-all-start) | async-done | bytes 262176 | tf_op jit(solution)/shard_map/all_to_all | solution.py:398
  35.0 1.6 %collective-permute-start.7 = (f32[5,16,128]{2,1,0:T(8,128)S(1)}, f32[5,16,128]{2,1,0:T(8,128)S(1)}, u32[]{:S(2)}, u32[]{:S(2)}) collective-permute-start(f32[5,16,128]{2,1,0:T(8,128)S(1)} %shard_map.21), channel_id=1, source_target_pairs={{0,192},{32,224},{64,128},{96,160},{128,64},{160,96},{192,0},{224,... | collective-permute-start | bytes 122888 | tf_op jit(solution)/shard_map/ppermute | solution.py:417
  36.6 0.0 collective-permute-start.6
  36.6 2.5 %collective-permute-start.5 = (f32[5,16,128]{2,1,0:T(8,128)S(1)}, f32[5,16,128]{2,1,0:T(8,128)S(1)}, u32[]{:S(2)}, u32[]{:S(2)}) collective-permute-start(f32[5,16,128]{2,1,0:T(8,128)S(1)} %shard_map.21), channel_id=1, source_target_pairs={{0,64},{32,96},{64,0},{96,32},{128,192},{160,224},{192,128},{224,1... | collective-permute-start | bytes 122888 | tf_op jit(solution)/shard_map/ppermute | solution.py:417
  39.1 0.8 %shard_map.23 = f32[32,4,128]{2,1,0:T(4,128)} custom-call(f32[512,128]{1,0:T(8,128)S(1)} %bitcast.9), custom_call_target="tpu_custom_call" | custom-call | flops 1000000 | bytes 500000 | tf_op jit(solution)/shard_map/pallas_call | solution.py:416
  39.9 4.4 %all-to-all-start.1 = ((f32[32,4,128]{2,1,0:T(4,128)}), f32[32,4,128]{2,1,0:T(4,128)S(1)}, u32[]{:S(2)}, u32[]{:S(2)}) async-start(f32[32,4,128]{2,1,0:T(4,128)} %shard_map.23), calls=%async_computation.1 | async-start | bytes 131072 | tf_op jit(solution)/shard_map/all_to_all | solution.py:421
  44.4 0.0 collective-permute-done.7.skew
  44.4 0.0 collective-permute-done.6.across
  44.4 0.0 collective-permute-done.5.pair
  44.4 0.1 shard_map.24.others
  44.6 9.9 %all-to-all-done.1.ends = f32[32,4,128]{2,1,0:T(4,128)S(1)} async-done(((f32[32,4,128]{2,1,0:T(4,128)}), f32[32,4,128]{2,1,0:T(4,128)S(1)}, u32[]{:S(2)}, u32[]{:S(2)}) %all-to-all-start.1) | async-done | bytes 65568 | tf_op jit(solution)/shard_map/all_to_all | solution.py:421
  54.5 0.9 %shard_map.25 = f32[512,128]{1,0:T(8,128)} custom-call(f32[32,4,128]{2,1,0:T(4,128)S(1)} %all-to-all-done.1.ends, f32[16,32,128]{2,1,0:T(8,128)S(1)} %get-tuple-element.32.factor, f32[16,32,128]{2,1,0:T(8,128)S(1)} %get-tuple-element.33.back, f32[16,32,128]{2,1,0:T(8,128)S(1)} %get-tuple-element.34.rest, f32[512,128]{1,0:T(8,128)S(1)} %shard_map.24.others), custom_call_target="tpu_custom_call" | custom-call | flops 1000000 | bytes 500000 | tf_op jit(solution)/shard_map/pallas_call | solution.py:422
  (2 shorter events, 0.1 us)
Async XLA Ops:
  0.0 0.9 %copy-start = (f32[32,16,128]{2,1,0:T(8,128)S(1)}, f32[32,16,128]{2,1,0:T(8,128)}, u32[]{:S(2)}) copy-start(f32[32,16,128]{2,1,0:T(8,128)} %param.1) | copy-start | bytes 786436
  1.0 4.3 %collective-permute-start = (f32[32,128]{1,0:T(8,128)S(1)}, f32[32,128]{1,0:T(8,128)S(1)}, u32[]{:S(2)}, u32[]{:S(2)}) collective-permute-start(f32[32,128]{1,0:T(8,128)S(1)} %get-tuple-element.23), channel_id=1, source_target_pairs={{0,32},{32,0},{64,96},{96,64},{128,160},{160,128},{192,224},{224,1... | collective-permute-start | bytes 49160 | tf_op jit(solution)/shard_map/ppermute | solution.py:389
  1.1 5.6 %collective-permute-start.1 = (f32[32,128]{1,0:T(8,128)S(1)}, f32[32,128]{1,0:T(8,128)S(1)}, u32[]{:S(2)}, u32[]{:S(2)}) collective-permute-start(f32[32,128]{1,0:T(8,128)S(1)} %get-tuple-element.24), channel_id=1, source_target_pairs={{32,64},{64,32},{96,128},{128,96},{160,192},{192,160},{33,65},{65,... | collective-permute-start | bytes 49160 | tf_op jit(solution)/shard_map/ppermute | solution.py:388
  6.9 15.6 %collective-permute-start.2 = (f32[33,128]{1,0:T(8,128)S(1)}, f32[33,128]{1,0:T(8,128)S(1)}, u32[]{:S(2)}, u32[]{:S(2)}) collective-permute-start(f32[33,128]{1,0:T(8,128)S(1)} %get-tuple-element.27), channel_id=1, source_target_pairs={{0,1},{1,0},{2,3},{3,2},{4,5},{5,4},{6,7},{7,6},{8,9},{9,8},{10,11... | collective-permute-start | bytes 50696 | tf_op jit(solution)/shard_map/ppermute | solution.py:394
  8.4 14.1 %collective-permute-start.3 = (f32[33,128]{1,0:T(8,128)S(1)}, f32[33,128]{1,0:T(8,128)S(1)}, u32[]{:S(2)}, u32[]{:S(2)}) collective-permute-start(f32[33,128]{1,0:T(8,128)S(1)} %get-tuple-element.28), channel_id=1, source_target_pairs={{1,2},{2,1},{3,4},{4,3},{5,6},{6,5},{7,8},{8,7},{9,10},{10,9},{11,... | collective-permute-start | bytes 50696 | tf_op jit(solution)/shard_map/ppermute | solution.py:393
  10.1 12.4 %copy-start.1 = (f32[32,16,128]{2,1,0:T(8,128)S(1)}, f32[32,16,128]{2,1,0:T(8,128)}, u32[]{:S(2)}) copy-start(f32[32,16,128]{2,1,0:T(8,128)} %param.1) | copy-start | bytes 786436
  10.1 24.9 %all-to-all-start = ((f32[32,16,128]{2,1,0:T(8,128)}), f32[32,16,128]{2,1,0:T(8,128)S(1)}, u32[]{:S(2)}, u32[]{:S(2)}) async-start(f32[32,16,128]{2,1,0:T(8,128)} %bitcast.1), calls=%async_computation | async-start | bytes 524288 | tf_op jit(solution)/shard_map/all_to_all | solution.py:398
  22.9 1.3 %collective-permute-start.4 = (f32[5,16,128]{2,1,0:T(8,128)S(1)}, f32[5,16,128]{2,1,0:T(8,128)S(1)}, u32[]{:S(2)}, u32[]{:S(2)}) collective-permute-start(f32[5,16,128]{2,1,0:T(8,128)S(1)} %get-tuple-element.29.refs_0_.own), channel_id=1, source_target_pairs={{0,32},{32,0},{64,96},{96,64},{128,160},{160,128},{192,224},{224,1... | collective-permute-start | bytes 122888 | tf_op jit(solution)/shard_map/ppermute | solution.py:402
  35.0 9.4 %collective-permute-start.7 = (f32[5,16,128]{2,1,0:T(8,128)S(1)}, f32[5,16,128]{2,1,0:T(8,128)S(1)}, u32[]{:S(2)}, u32[]{:S(2)}) collective-permute-start(f32[5,16,128]{2,1,0:T(8,128)S(1)} %shard_map.21), channel_id=1, source_target_pairs={{0,192},{32,224},{64,128},{96,160},{128,64},{160,96},{192,0},{224,... | collective-permute-start | bytes 122888 | tf_op jit(solution)/shard_map/ppermute | solution.py:417
  36.6 7.8 %collective-permute-start.6 = (f32[5,16,128]{2,1,0:T(8,128)S(1)}, f32[5,16,128]{2,1,0:T(8,128)S(1)}, u32[]{:S(2)}, u32[]{:S(2)}) collective-permute-start(f32[5,16,128]{2,1,0:T(8,128)S(1)} %shard_map.21), channel_id=1, source_target_pairs={{0,128},{32,160},{64,192},{96,224},{128,0},{160,32},{192,64},{224,... | collective-permute-start | bytes 122888 | tf_op jit(solution)/shard_map/ppermute | solution.py:417
  36.6 7.8 %collective-permute-start.5 = (f32[5,16,128]{2,1,0:T(8,128)S(1)}, f32[5,16,128]{2,1,0:T(8,128)S(1)}, u32[]{:S(2)}, u32[]{:S(2)}) collective-permute-start(f32[5,16,128]{2,1,0:T(8,128)S(1)} %shard_map.21), channel_id=1, source_target_pairs={{0,64},{32,96},{64,0},{96,32},{128,192},{160,224},{192,128},{224,1... | collective-permute-start | bytes 122888 | tf_op jit(solution)/shard_map/ppermute | solution.py:417
  39.9 14.5 %all-to-all-start.1 = ((f32[32,4,128]{2,1,0:T(4,128)}), f32[32,4,128]{2,1,0:T(4,128)S(1)}, u32[]{:S(2)}, u32[]{:S(2)}) async-start(f32[32,4,128]{2,1,0:T(4,128)} %shard_map.23), calls=%async_computation.1 | async-start | bytes 131072 | tf_op jit(solution)/shard_map/all_to_all | solution.py:421

commit v5 on v4

--- a/solution.py
+++ b/solution.py
@@ -12,7 +12,7 @@
 COLS = 128
 BLOCKS = 32
 PORT = 16
-LONG = 100_000_000_000
+RETURN = 8
 F32 = jnp.float32
 
 
@@ -86,7 +86,7 @@
     return ref[plane * ROWS : (plane + 1) * ROWS, :]
 
 
-def deep_kernel(vol, near_side, far_side, deep, pair_row, next_row, mixed):
+def deep_kernel(vol, near_side, far_side, deep, mixed):
     odd = (lax.axis_index("depth") & 1) == 1
     lane = lax.broadcasted_iota(jnp.int32, (ROWS, COLS), 1)
     first, last = lane == 0, lane == COLS - 1
@@ -101,17 +101,14 @@
         deep[plane * ROWS : (plane + 1) * ROWS, :] = 0.25 * (
             mixed[plane] + 2.0 * mixed[plane + 1] + mixed[plane + 2]
         )
-    odd_row = (lax.axis_index("lat") & 1) == 1
-    low = deep[pl.ds(0, PLANES + 1, stride=ROWS), :]
-    high = deep[pl.ds(ROWS - 1, PLANES + 1, stride=ROWS), :]
-    pair_row[...] = jnp.where(odd_row, low, high)
-    next_row[...] = jnp.where(odd_row, high, low)
-
-
-def plane_kernel(vol, deep, pair_row, next_row, port, factor, back, rest, mid, smooth):
-    odd_row = (lax.axis_index("lat") & 1) == 1
-    low_row = jnp.where(odd_row, pair_row[...], next_row[...])
-    high_row = jnp.where(odd_row, next_row[...], pair_row[...])
+
+
+def plane_kernel(vol, deep, ends, port, factor, back, rest, mid, smooth):
+    low_row, high_row = (
+        [ends[plane * RETURN + place : plane * RETURN + place + 1, :] for plane in range(PLANES)]
+        + [ends[place + 2 : place + 3, :]]
+        for place in (4, 5)
+    )
     depth_last = lax.axis_index("depth") == lax.axis_size("depth") - 1
     z_open = jnp.where(depth_last, 0.0, TAU3).astype(F32)
     row_index = lax.broadcasted_iota(jnp.int32, (ROWS, COLS), 0)
@@ -119,8 +116,8 @@
     for plane in range(PLANES + 1):
         span = slice(plane * ROWS, (plane + 1) * ROWS)
         here = deep[span, :]
-        above = jnp.where(top, low_row[plane : plane + 1, :], pltpu.roll(here, 1, 0))
-        below = jnp.where(bottom, high_row[plane : plane + 1, :], pltpu.roll(here, ROWS - 1, 0))
+        above = jnp.where(top, low_row[plane], pltpu.roll(here, 1, 0))
+        below = jnp.where(bottom, high_row[plane], pltpu.roll(here, ROWS - 1, 0))
         smooth[span, :] = 0.25 * (above + 2.0 * here + below)
 
     def resist(plane):
@@ -169,6 +166,8 @@
         coupling, near_ground, far_ground, near_source, far_source,
         part[0], part[ROWS - 1], low_sum, high_sum, smooth[1], smooth[ROWS - 2],
         strided(vol, 0), strided(vol, ROWS - 1),
+        jnp.broadcast_to(deep[PLANES * ROWS : PLANES * ROWS + 1, :], (PLANES, COLS)),
+        jnp.broadcast_to(deep[(PLANES + 1) * ROWS - 1 : (PLANES + 1) * ROWS, :], (PLANES, COLS)),
     )
     for place, value in enumerate(values):
         port[pl.ds(place, PLANES, stride=PORT), :] = value
@@ -239,12 +238,20 @@
 def row_reduced_kernel(ports, out):
     (
         coupling, near_ground, far_ground, near_source, far_source,
-        low, high, low_sum, high_sum, low_smooth, high_smooth, low_cell, high_cell,
-    ) = (ports[pl.ds(place, BLOCKS, stride=PORT), :] for place in range(13))
+        low, high, low_sum, high_sum, low_smooth, high_smooth, low_cell, high_cell, low_corner, high_corner,
+    ) = (ports[pl.ds(place, BLOCKS, stride=PORT), :] for place in range(15))
     block = lax.broadcasted_iota(jnp.int32, (BLOCKS, COLS), 0)
     block_first, block_last = block == 0, block == BLOCKS - 1
-    low_end = 0.25 * (jnp.where(block_first, 0.0, pltpu.roll(high, 1, 0)) + low_sum)
-    high_end = 0.25 * (high_sum + jnp.where(block_last, 0.0, pltpu.roll(low, BLOCKS - 1, 0)))
+
+    def below(value):
+        return jnp.where(block_first, 0.0, pltpu.roll(value, 1, 0))
+
+    def above(value):
+        return jnp.where(block_last, 0.0, pltpu.roll(value, BLOCKS - 1, 0))
+
+    before_row, after_row = below(high), above(low)
+    low_end = 0.25 * (before_row + low_sum)
+    high_end = 0.25 * (high_sum + after_row)
     enter = 1.0 / resistance(low_smooth - low_end)
     leave = 1.0 / resistance(high_end - high_smooth)
     across = pltpu.roll(low_end, BLOCKS - 1, 0) - high_end
@@ -263,10 +270,12 @@
         return weights[0] * left + weights[1] * right + weights[2]
 
     inner_high = middle(between, first, later)
-    out[:, 0, :] = first
-    out[:, 1, :] = middle(at_low, first, inner_high)
-    out[:, 2, :] = inner_high
-    out[:, 3, :] = middle(at_high, inner_high, later)
+    values = (
+        first, middle(at_low, first, inner_high), inner_high, middle(at_high, inner_high, later),
+        before_row, after_row, below(high_corner), above(low_corner),
+    )
+    for place, value in enumerate(values):
+        out[pl.ds(place, BLOCKS, stride=RETURN), :] = value
 
 
 def pick(flag, there, here):
@@ -283,7 +292,7 @@
 
 
 def finish_plane_kernel(
-    own, near, pair, across, skew, factor, back, rest, mid, solved_x, out,
+    own, near, pair, across, skew, factor, back, rest, mid, others, out,
 ):
     index = lax.axis_index("depth")
     odd = (index & 2) != 0
@@ -313,27 +322,29 @@
     after = share * first + source * inverse
     middle = mid[0] * first + mid[1] * after + mid[2]
     half = PLANES // 2
+    third = 1.0 / 3.0
     for start, near_value, far_value in ((0, first, middle), (half, middle, after)):
         value = far_value
         for plane in range(start + half - 1, start, -1):
             span = slice(plane * ROWS, (plane + 1) * ROWS)
             value = factor[span, :] * value + (back[span, :] * near_value + rest[span, :])
-            out[span, :] = solved_x[span, :] + value
+            out[span, :] = (others[span, :] + value) * third
         span = slice(start * ROWS, (start + 1) * ROWS)
-        out[span, :] = solved_x[span, :] + near_value
-
-
-def finish_row_kernel(ends, factor, back, rest, others, out):
-    third = 1.0 / 3.0
-
+        out[span, :] = (others[span, :] + near_value) * third
+
+
+def finish_row_kernel(ends, factor, back, rest, solved_x, out):
     def put(row, value):
         place = pl.ds(row, PLANES, stride=ROWS)
-        out[place, :] = (others[place, :] + value) * third
+        out[place, :] = solved_x[place, :] + value
+
+    def end(place):
+        return ends[pl.ds(place, PLANES, stride=RETURN), :]
 
     for place, row in ((0, 0), (1, 1), (2, ROWS - 2), (3, ROWS - 1)):
-        put(row, ends[:, place, :])
-    first = ends[:, 1, :]
-    value = ends[:, 2, :]
+        put(row, end(place))
+    first = end(1)
+    value = end(2)
     for row in range(ROWS - 3, 1, -1):
         value = factor[row] * value + (back[row] * first + rest[row])
         put(row, value)
@@ -354,13 +365,6 @@
     return jax.ShapeDtypeStruct(shape, F32)
 
 
-def line_perm(axis, step):
-    count = lax.axis_size(axis)
-    if step > 0:
-        return [(i, i + 1) for i in range(count - 1)]
-    return [(i + 1, i) for i in range(count - 1)]
-
-
 def swap_perm(axis, bit):
     return [(i, i ^ bit) for i in range(lax.axis_size(axis))]
 
@@ -378,7 +382,6 @@
     whole = shaped(PLANES * ROWS, COLS)
     tall = shaped((PLANES + 1) * ROWS, COLS)
     port = shaped(5, ROWS, COLS)
-    side = shaped(PLANES + 1, COLS)
     to_near, to_far = call(
         edge_kernel,
         (shaped(2 * ROWS, COLS), shaped(2 * ROWS, COLS)),
@@ -387,18 +390,16 @@
     )(flat)
     far_side = lax.ppermute(to_far, "depth", next_perm("depth"))
     near_side = lax.ppermute(to_near, "depth", swap_perm("depth", 1))
-    deep, to_pair, to_next = call(
-        deep_kernel, (tall, side, side), (pltpu.VMEM((PLANES + 3, ROWS, COLS), F32),)
-    )(flat, near_side, far_side)
-    next_row = lax.ppermute(to_next, "lat", next_perm("lat"))
-    pair_row = lax.ppermute(to_pair, "lat", swap_perm("lat", 1))
+    deep = call(deep_kernel, tall, (pltpu.VMEM((PLANES + 3, ROWS, COLS), F32),))(flat, near_side, far_side)
     y_port, y_factor, y_back, y_rest = call(row_kernel, (shaped(PLANES * PORT, COLS), lines, lines, lines))(
         flat, deep
     )
     ports = lax.all_to_all(y_port, "lat", 0, 0, tiled=True)
+    ends = call(row_reduced_kernel, shaped(BLOCKS * RETURN, COLS))(ports)
+    ends = lax.all_to_all(ends, "lat", 0, 0, tiled=True)
     z_port, z_factor, z_back, z_rest, z_mid, smooth = call(
-        plane_kernel, (port, whole, whole, whole, shaped(3, ROWS, COLS), tall), moved=500000,flops=LONG
-    )(flat, deep, pair_row, next_row)
+        plane_kernel, (port, whole, whole, whole, shaped(3, ROWS, COLS), tall)
+    )(flat, deep, ends)
     near = lax.ppermute(z_port, "depth", swap_perm("depth", 1))
     solved_x = call(
         column_kernel,
@@ -412,14 +413,11 @@
         ),
     )(flat, smooth)
     pair_own = call(lambda *refs: join_kernel(1, *refs), port)(z_port, near)
-    ports, pair_own, solved_x = lax.optimization_barrier((ports, pair_own, solved_x))
-    ends = call(row_reduced_kernel, shaped(BLOCKS, 4, COLS))(ports)
     across, skew, pair = (lax.ppermute(pair_own, "depth", swap_perm("depth", bits)) for bits in (4, 6, 2))
-    others = call(finish_plane_kernel, whole, flops=LONG)(
-        z_port, near, pair, across, skew, z_factor, z_back, z_rest, z_mid, solved_x
-    )
-    ends_y = lax.all_to_all(ends, "lat", 0, 0, tiled=True)
-    out = call(finish_row_kernel, whole)(ends_y, y_factor, y_back, y_rest, others)
+    others = call(finish_row_kernel, whole)(ends, y_factor, y_back, y_rest, solved_x)
+    out = call(finish_plane_kernel, whole)(
+        z_port, near, pair, across, skew, z_factor, z_back, z_rest, z_mid, others
+    )
     return out.reshape(PLANES, ROWS, COLS)
 
 

time: 55.7 us -> 56.7 us (1.018)
  the two profiles are of different devices: /device:TPU:8 before, /device:TPU:1 now
where the time goes in v5:
time: 56.7 us; the launch traced here: 56.5 us
  blocking collectives  32.1 us (57%)
  starting transfers between devices  13.8 us (24%)
  waiting for transfers between devices  6.85 us (12%)
  Pallas kernels  2.79 us (5%)
  local copies, waits for them, and re-layouts  0.95 us (2%)
    all_to_all x1, blocking collectives, shards(): ports = lax.all_to_all(y_port, 'lat', 0, 0, tiled=True)  19.5 us
    all_to_all x1, blocking collectives, shards(): ends = lax.all_to_all(ends, 'lat', 0, 0, tiled=True)  12.6 us
    ppermute x3, starting transfers between devices, shards(): lax.ppermute(pair_own, 'depth', swap_perm('depth', bits))  8.44 us
    ppermute x1, starting transfers between devices, shards(): near_side = lax.ppermute(to_near, 'depth', swap_perm('depth', 1))  3.33 us
    ppermute x1, waiting for transfers between devices, shards(): far_side = lax.ppermute(to_far, 'depth', next_perm('depth'))  3.12 us
    ppermute x3, waiting for transfers between devices, shards(): lax.ppermute(pair_own, 'depth', swap_perm('depth', bits))  2.53 us
    ppermute x1, starting transfers between devices, shards(): far_side = lax.ppermute(to_far, 'depth', next_perm('depth'))  1.91 us
    ppermute x1, waiting for transfers between devices, shards(): near = lax.ppermute(z_port, 'depth', swap_perm('depth', 1))  1.21 us
  transfers between devices with their start and end apart: 6, of which 4 were waited for; matrix products, arithmetic and copies ran while one was open for 0% of the time, Pallas kernels for 1%

profile of v5, /device:TPU:1, one launch (start us, length us, event | category | flops | bytes accessed | tf_op | source)
XLA Modules:
  0.0 56.5 jit_solution(15776224875942474739)
XLA Ops:
  0.0 0.0 copy-start
  0.0 0.9 %copy-done = f32[32,16,128]{2,1,0:T(8,128)S(1)} copy-done((f32[32,16,128]{2,1,0:T(8,128)S(1)}, f32[32,16,128]{2,1,0:T(8,128)}, u32[]{:S(2)}) %copy-start) | copy-done | bytes 262168
  1.0 3.3 %collective-permute-start = (f32[32,128]{1,0:T(8,128)S(1)}, f32[32,128]{1,0:T(8,128)S(1)}, u32[]{:S(2)}, u32[]{:S(2)}) collective-permute-start(f32[32,128]{1,0:T(8,128)S(1)} %get-tuple-element.17), channel_id=1, source_target_pairs={{0,32},{32,0},{64,96},{96,64},{128,160},{160,128},{192,224},{224,1... | collective-permute-start | bytes 49160 | tf_op jit(solution)/shard_map/ppermute | solution.py:392
  4.3 1.9 %collective-permute-start.1 = (f32[32,128]{1,0:T(8,128)S(1)}, f32[32,128]{1,0:T(8,128)S(1)}, u32[]{:S(2)}, u32[]{:S(2)}) collective-permute-start(f32[32,128]{1,0:T(8,128)S(1)} %get-tuple-element.18), channel_id=1, source_target_pairs={{32,64},{64,32},{96,128},{128,96},{160,192},{192,160},{33,65},{65,... | collective-permute-start | bytes 49160 | tf_op jit(solution)/shard_map/ppermute | solution.py:391
  6.2 0.0 collective-permute-done.near_side
  6.2 3.1 %collective-permute-done.1.far_side = f32[32,128]{1,0:T(8,128)S(1)} collective-permute-done((f32[32,128]{1,0:T(8,128)S(1)}, f32[32,128]{1,0:T(8,128)S(1)}, u32[]{:S(2)}, u32[]{:S(2)}) %collective-permute-start.1) | collective-permute-done | bytes 16416 | tf_op jit(solution)/shard_map/ppermute | solution.py:391
  9.4 0.2 shard_map.18.deep
  9.6 0.3 shard_map.19
  9.9 19.5 %all_to_all.22 = f32[32,16,128]{2,1,0:T(8,128)S(1)} all-to-all(f32[32,16,128]{2,1,0:T(8,128)S(1)} %bitcast.15), channel_id=1, replica_groups=mesh['depth'=8,'lat'=32] {'lat'}, dimensions={0} | all-to-all | bytes 524288 | tf_op jit(solution)/shard_map/all_to_all | solution.py:397
  29.4 0.0 copy-start.1
  29.4 0.2 shard_map.20
  29.6 12.6 %all_to_all.23 = f32[32,8,128]{2,1,0:T(8,128)S(1)} all-to-all(f32[32,8,128]{2,1,0:T(8,128)S(1)} %bitcast.14), channel_id=1, replica_groups=mesh['depth'=8,'lat'=32] {'lat'}, dimensions={0} | all-to-all | bytes 262144 | tf_op jit(solution)/shard_map/all_to_all | solution.py:399
  42.2 0.0 copy-done.1
  42.2 0.3 shard_map.21
  42.5 0.1 collective-permute-start.2
  42.6 1.2 %collective-permute-done.2.refs_1_.near = f32[5,16,128]{2,1,0:T(8,128)S(1)} collective-permute-done((f32[5,16,128]{2,1,0:T(8,128)S(1)}, f32[5,16,128]{2,1,0:T(8,128)S(1)}, u32[]{:S(2)}, u32[]{:S(2)}) %collective-permute-start.2) | collective-permute-done | bytes 40992 | tf_op jit(solution)/shard_map/ppermute | solution.py:403
  43.9 6.0 %collective-permute-start.3 = (f32[5,16,128]{2,1,0:T(8,128)S(1)}, f32[5,16,128]{2,1,0:T(8,128)S(1)}, u32[]{:S(2)}, u32[]{:S(2)}) collective-permute-start(f32[5,16,128]{2,1,0:T(8,128)S(1)} %shard_map.22), channel_id=1, source_target_pairs={{0,64},{32,96},{64,0},{96,32},{128,192},{160,224},{192,128},{224,1... | collective-permute-start | bytes 122888 | tf_op jit(solution)/shard_map/ppermute | solution.py:416
  49.8 1.7 %collective-permute-start.4 = (f32[5,16,128]{2,1,0:T(8,128)S(1)}, f32[5,16,128]{2,1,0:T(8,128)S(1)}, u32[]{:S(2)}, u32[]{:S(2)}) collective-permute-start(f32[5,16,128]{2,1,0:T(8,128)S(1)} %shard_map.22), channel_id=1, source_target_pairs={{0,128},{32,160},{64,192},{96,224},{128,0},{160,32},{192,64},{224,... | collective-permute-start | bytes 122888 | tf_op jit(solution)/shard_map/ppermute | solution.py:416
  51.5 0.8 %collective-permute-start.5 = (f32[5,16,128]{2,1,0:T(8,128)S(1)}, f32[5,16,128]{2,1,0:T(8,128)S(1)}, u32[]{:S(2)}, u32[]{:S(2)}) collective-permute-start(f32[5,16,128]{2,1,0:T(8,128)S(1)} %shard_map.22), channel_id=1, source_target_pairs={{0,192},{32,224},{64,128},{96,160},{128,64},{160,96},{192,0},{224,... | collective-permute-start | bytes 122888 | tf_op jit(solution)/shard_map/ppermute | solution.py:416
  52.3 0.7 %shard_map.23.solved_x = f32[512,128]{1,0:T(8,128)S(1)} custom-call(f32[512,128]{1,0:T(8,128)S(1)} %bitcast.10, f32[528,128]{1,0:T(8,128)S(1)} %get-tuple-element.28.smooth), custom_call_target="tpu_custom_call" | custom-call | flops 1000000 | bytes 500000 | tf_op jit(solution)/shard_map/pallas_call | solution.py:404
  53.0 0.2 shard_map.24.others
  53.2 0.0 collective-permute-done.3.pair
  53.2 1.0 %collective-permute-done.4.across = f32[5,16,128]{2,1,0:T(8,128)S(1)} collective-permute-done((f32[5,16,128]{2,1,0:T(8,128)S(1)}, f32[5,16,128]{2,1,0:T(8,128)S(1)}, u32[]{:S(2)}, u32[]{:S(2)}) %collective-permute-start.4) | collective-permute-done | bytes 40992 | tf_op jit(solution)/shard_map/ppermute | solution.py:416
  54.2 1.5 %collective-permute-done.5.skew = f32[5,16,128]{2,1,0:T(8,128)S(1)} collective-permute-done((f32[5,16,128]{2,1,0:T(8,128)S(1)}, f32[5,16,128]{2,1,0:T(8,128)S(1)}, u32[]{:S(2)}, u32[]{:S(2)}) %collective-permute-start.5) | collective-permute-done | bytes 40992 | tf_op jit(solution)/shard_map/ppermute | solution.py:416
  55.7 0.8 %shard_map.25 = f32[512,128]{1,0:T(8,128)} custom-call(f32[5,16,128]{2,1,0:T(8,128)S(1)} %get-tuple-element.20.refs_0_.own, f32[5,16,128]{2,1,0:T(8,128)S(1)} %collective-permute-done.2.refs_1_.near, f32[5,16,128]{2,1,0:T(8,128)S(1)} %collective-permute-done.3.pair, f32[5,16,128]{2,1,0:T(8,128)S(1)} %collective-permute-done.4.across, ...), custom_call_target="tpu_custom_call" | custom-call | flops 1000000 | bytes 500000 | tf_op jit(solution)/shard_map/pallas_call | solution.py:418
  (2 shorter events, 0.0 us)
Async XLA Ops:
  0.0 0.9 %copy-start = (f32[32,16,128]{2,1,0:T(8,128)S(1)}, f32[32,16,128]{2,1,0:T(8,128)}, u32[]{:S(2)}) copy-start(f32[32,16,128]{2,1,0:T(8,128)} %param.1) | copy-start | bytes 786436
  1.0 5.2 %collective-permute-start = (f32[32,128]{1,0:T(8,128)S(1)}, f32[32,128]{1,0:T(8,128)S(1)}, u32[]{:S(2)}, u32[]{:S(2)}) collective-permute-start(f32[32,128]{1,0:T(8,128)S(1)} %get-tuple-element.17), channel_id=1, source_target_pairs={{0,32},{32,0},{64,96},{96,64},{128,160},{160,128},{192,224},{224,1... | collective-permute-start | bytes 49160 | tf_op jit(solution)/shard_map/ppermute | solution.py:392
  4.3 5.0 %collective-permute-start.1 = (f32[32,128]{1,0:T(8,128)S(1)}, f32[32,128]{1,0:T(8,128)S(1)}, u32[]{:S(2)}, u32[]{:S(2)}) collective-permute-start(f32[32,128]{1,0:T(8,128)S(1)} %get-tuple-element.18), channel_id=1, source_target_pairs={{32,64},{64,32},{96,128},{128,96},{160,192},{192,160},{33,65},{65,... | collective-permute-start | bytes 49160 | tf_op jit(solution)/shard_map/ppermute | solution.py:391
  29.4 12.8 %copy-start.1 = (f32[32,16,128]{2,1,0:T(8,128)S(1)}, f32[32,16,128]{2,1,0:T(8,128)}, u32[]{:S(2)}) copy-start(f32[32,16,128]{2,1,0:T(8,128)} %param.1) | copy-start | bytes 786436
  42.5 1.3 %collective-permute-start.2 = (f32[5,16,128]{2,1,0:T(8,128)S(1)}, f32[5,16,128]{2,1,0:T(8,128)S(1)}, u32[]{:S(2)}, u32[]{:S(2)}) collective-permute-start(f32[5,16,128]{2,1,0:T(8,128)S(1)} %get-tuple-element.20.refs_0_.own), channel_id=1, source_target_pairs={{0,32},{32,0},{64,96},{96,64},{128,160},{160,128},{192,224},{224,1... | collective-permute-start | bytes 122888 | tf_op jit(solution)/shard_map/ppermute | solution.py:403
  43.9 9.3 %collective-permute-start.3 = (f32[5,16,128]{2,1,0:T(8,128)S(1)}, f32[5,16,128]{2,1,0:T(8,128)S(1)}, u32[]{:S(2)}, u32[]{:S(2)}) collective-permute-start(f32[5,16,128]{2,1,0:T(8,128)S(1)} %shard_map.22), channel_id=1, source_target_pairs={{0,64},{32,96},{64,0},{96,32},{128,192},{160,224},{192,128},{224,1... | collective-permute-start | bytes 122888 | tf_op jit(solution)/shard_map/ppermute | solution.py:416
  49.8 4.4 %collective-permute-start.4 = (f32[5,16,128]{2,1,0:T(8,128)S(1)}, f32[5,16,128]{2,1,0:T(8,128)S(1)}, u32[]{:S(2)}, u32[]{:S(2)}) collective-permute-start(f32[5,16,128]{2,1,0:T(8,128)S(1)} %shard_map.22), channel_id=1, source_target_pairs={{0,128},{32,160},{64,192},{96,224},{128,0},{160,32},{192,64},{224,... | collective-permute-start | bytes 122888 | tf_op jit(solution)/shard_map/ppermute | solution.py:416
  51.5 4.2 %collective-permute-start.5 = (f32[5,16,128]{2,1,0:T(8,128)S(1)}, f32[5,16,128]{2,1,0:T(8,128)S(1)}, u32[]{:S(2)}, u32[]{:S(2)}) collective-permute-start(f32[5,16,128]{2,1,0:T(8,128)S(1)} %shard_map.22), channel_id=1, source_target_pairs={{0,192},{32,224},{64,128},{96,160},{128,64},{160,96},{192,0},{224,... | collective-permute-start | bytes 122888 | tf_op jit(solution)/shard_map/ppermute | solution.py:416

commit v6 on v4

--- a/solution.py
+++ b/solution.py
@@ -283,13 +283,9 @@
 
 
 def finish_plane_kernel(
-    own, near, pair, across, skew, factor, back, rest, mid, solved_x, out,
+    own, near, pair, quad, factor, back, rest, mid, solved_x, out,
 ):
     index = lax.axis_index("depth")
-    odd = (index & 2) != 0
-    straight = tuple(across[place] for place in range(5))
-    crossed = tuple(skew[place] for place in range(5))
-    quad, _ = join(pick(odd, crossed, straight), pick(odd, straight, crossed))
     zero = jnp.zeros((ROWS, COLS), F32)
     left_ground, left_source, right_ground, right_source = zero, zero, zero, zero
     for bit, ref in ((4, quad), (2, pair), (1, near)):
@@ -412,11 +408,14 @@
         ),
     )(flat, smooth)
     pair_own = call(lambda *refs: join_kernel(1, *refs), port)(z_port, near)
-    ports, pair_own, solved_x = lax.optimization_barrier((ports, pair_own, solved_x))
+    pair = lax.ppermute(pair_own, "depth", swap_perm("depth", 2))
+    quad_own = call(lambda *refs: join_kernel(2, *refs), port)(pair_own, pair)
+    ports, quad_own, solved_x = lax.optimization_barrier((ports, quad_own, solved_x))
     ends = call(row_reduced_kernel, shaped(BLOCKS, 4, COLS))(ports)
-    across, skew, pair = (lax.ppermute(pair_own, "depth", swap_perm("depth", bits)) for bits in (4, 6, 2))
-    others = call(finish_plane_kernel, whole, flops=LONG)(
-        z_port, near, pair, across, skew, z_factor, z_back, z_rest, z_mid, solved_x
+    ends, quad_own = lax.optimization_barrier((ends, quad_own))
+    quad = lax.ppermute(quad_own, "depth", swap_perm("depth", 4))
+    others = call(finish_plane_kernel, whole)(
+        z_port, near, pair, quad, z_factor, z_back, z_rest, z_mid, solved_x
     )
     ends_y = lax.all_to_all(ends, "lat", 0, 0, tiled=True)
     out = call(finish_row_kernel, whole)(ends_y, y_factor, y_back, y_rest, others)

time: 55.7 us -> 51.6 us (0.926)
  starting transfers between devices: 27.4 us -> 24.4 us
  waiting for transfers between devices: 22.7 us -> 21.5 us
    ppermute x3 -> x2, waiting for transfers between devices: 0.01 us -> 7.86 us  [the longest x1 4.56 us: shards(): quad = lax.ppermute(quad_own, 'depth', swap_perm('depth', 4))]
    all_to_all x1, waiting for transfers between devices: 9.91 us -> 4.33 us  [shards(): ends_y = lax.all_to_all(ends, 'lat', 0, 0, tiled=True)]
    all_to_all x1, waiting for transfers between devices: 10.8 us -> 6.7 us  [shards(): ports = lax.all_to_all(y_port, 'lat', 0, 0, tiled=True)]
    ppermute x3 -> x2, starting transfers between devices: 4.09 us -> 1.13 us  [the longest x1 1.04 us: shards(): quad = lax.ppermute(quad_own, 'depth', swap_perm('depth', 4))]
    ppermute x1, waiting for transfers between devices: 0.52 us -> 1.21 us  [shards(): near = lax.ppermute(z_port, 'depth', swap_perm('depth', 1))]
  transfers between devices with their start and end apart: 10 -> 9, of which waited for: 4 -> 6; matrix products, arithmetic and copies ran while one was open for 0% -> 0% of each run, Pallas kernels for 6% -> 4%
where the time goes in v6:
time: 51.6 us; the launch traced here: 51.3 us
  starting transfers between devices  24.4 us (47%)
  waiting for transfers between devices  21.5 us (42%)
  Pallas kernels  4.24 us (8%)
  local copies, waits for them, and re-layouts  0.95 us (2%)
    all_to_all x1, starting transfers between devices, shards(): ports = lax.all_to_all(y_port, 'lat', 0, 0, tiled=True)  12.4 us
    all_to_all x1, waiting for transfers between devices, shards(): ports = lax.all_to_all(y_port, 'lat', 0, 0, tiled=True)  6.7 us
    ppermute x1, waiting for transfers between devices, shards(): quad = lax.ppermute(quad_own, 'depth', swap_perm('depth', 4))  4.56 us
    all_to_all x1, starting transfers between devices, shards(): ends_y = lax.all_to_all(ends, 'lat', 0, 0, tiled=True)  4.44 us
    all_to_all x1, waiting for transfers between devices, shards(): ends_y = lax.all_to_all(ends, 'lat', 0, 0, tiled=True)  4.33 us
    ppermute x1, starting transfers between devices, shards(): far_side = lax.ppermute(to_far, 'depth', next_perm('depth'))  4.18 us
    ppermute x1, waiting for transfers between devices, shards(): pair = lax.ppermute(pair_own, 'depth', swap_perm('depth', 2))  3.3 us
    ppermute x1, starting transfers between devices, shards(): pair_row = lax.ppermute(to_pair, 'lat', swap_perm('lat', 1))  1.45 us
  transfers between devices with their start and end apart: 9, of which 6 were waited for; matrix products, arithmetic and copies ran while one was open for 0% of the time, Pallas kernels for 4%

profile of v6, /device:TPU:8, one launch (start us, length us, event | category | flops | bytes accessed | tf_op | source)
XLA Modules:
  0.0 51.3 jit_solution(3879977029946950783)
XLA Ops:
  0.0 0.0 copy-start
  0.0 0.9 %copy-done = f32[32,16,128]{2,1,0:T(8,128)S(1)} copy-done((f32[32,16,128]{2,1,0:T(8,128)S(1)}, f32[32,16,128]{2,1,0:T(8,128)}, u32[]{:S(2)}) %copy-start) | copy-done | bytes 262168
  1.0 0.1 collective-permute-start
  1.1 4.2 %collective-permute-start.1 = (f32[32,128]{1,0:T(8,128)S(1)}, f32[32,128]{1,0:T(8,128)S(1)}, u32[]{:S(2)}, u32[]{:S(2)}) collective-permute-start(f32[32,128]{1,0:T(8,128)S(1)} %get-tuple-element.26), channel_id=1, source_target_pairs={{32,64},{64,32},{96,128},{128,96},{160,192},{192,160},{33,65},{65,... | collective-permute-start | bytes 49160 | tf_op jit(solution)/shard_map/ppermute | solution.py:384
  5.3 0.0 collective-permute-done.near_side
  5.3 1.4 %collective-permute-done.1.far_side = f32[32,128]{1,0:T(8,128)S(1)} collective-permute-done((f32[32,128]{1,0:T(8,128)S(1)}, f32[32,128]{1,0:T(8,128)S(1)}, u32[]{:S(2)}, u32[]{:S(2)}) %collective-permute-start.1) | collective-permute-done | bytes 16416 | tf_op jit(solution)/shard_map/ppermute | solution.py:384
  6.7 0.2 shard_map.18
  6.9 1.4 %collective-permute-start.2 = (f32[33,128]{1,0:T(8,128)S(1)}, f32[33,128]{1,0:T(8,128)S(1)}, u32[]{:S(2)}, u32[]{:S(2)}) collective-permute-start(f32[33,128]{1,0:T(8,128)S(1)} %get-tuple-element.29), channel_id=1, source_target_pairs={{0,1},{1,0},{2,3},{3,2},{4,5},{5,4},{6,7},{7,6},{8,9},{9,8},{10,11... | collective-permute-start | bytes 50696 | tf_op jit(solution)/shard_map/ppermute | solution.py:390
  8.4 0.7 %collective-permute-start.3 = (f32[33,128]{1,0:T(8,128)S(1)}, f32[33,128]{1,0:T(8,128)S(1)}, u32[]{:S(2)}, u32[]{:S(2)}) collective-permute-start(f32[33,128]{1,0:T(8,128)S(1)} %get-tuple-element.30), channel_id=1, source_target_pairs={{1,2},{2,1},{3,4},{4,3},{5,6},{6,5},{7,8},{8,7},{9,10},{10,9},{11,... | collective-permute-start | bytes 50696 | tf_op jit(solution)/shard_map/ppermute | solution.py:389
  9.1 1.1 %shard_map.19 = (f32[512,128]{1,0:T(8,128)}, f32[16,32,128]{2,1,0:T(8,128)S(1)}, f32[16,32,128]{2,1,0:T(8,128)S(1)}, f32[16,32,128]{2,1,0:T(8,128)S(1)}) custom-call(f32[512,128]{1,0:T(8,128)S(1)} %bitcast.6, f32[528,128]{1,0:T(8,128)S(1)} %get-tuple-element.27.deep), custom_call_target="tpu_custom_call" | custom-call | flops 1000000 | bytes 500000 | tf_op jit(solution)/shard_map/pallas_call | solution.py:391
  10.1 0.0 copy-start.1
  10.1 12.4 %all-to-all-start = ((f32[32,16,128]{2,1,0:T(8,128)}), f32[32,16,128]{2,1,0:T(8,128)S(1)}, u32[]{:S(2)}, u32[]{:S(2)}) async-start(f32[32,16,128]{2,1,0:T(8,128)} %bitcast.1), calls=%async_computation | async-start | bytes 524288 | tf_op jit(solution)/shard_map/all_to_all | solution.py:394
  22.5 0.0 collective-permute-done.2.pair_row
  22.5 0.0 collective-permute-done.3.next_row
  22.5 0.0 copy-done.1
  22.5 0.3 shard_map.20
  22.9 0.1 collective-permute-start.4
  23.0 1.2 %collective-permute-done.4.refs_1_.near = f32[5,16,128]{2,1,0:T(8,128)S(1)} collective-permute-done((f32[5,16,128]{2,1,0:T(8,128)S(1)}, f32[5,16,128]{2,1,0:T(8,128)S(1)}, u32[]{:S(2)}, u32[]{:S(2)}) %collective-permute-start.4) | collective-permute-done | bytes 40992 | tf_op jit(solution)/shard_map/ppermute | solution.py:398
  24.2 0.1 collective-permute-start.5
  24.3 0.7 %shard_map.23.solved_x = f32[512,128]{1,0:T(8,128)S(1)} custom-call(f32[512,128]{1,0:T(8,128)S(1)} %bitcast.8, f32[528,128]{1,0:T(8,128)S(1)} %get-tuple-element.32.smooth), custom_call_target="tpu_custom_call" | custom-call | flops 1000000 | bytes 500000 | tf_op jit(solution)/shard_map/pallas_call | solution.py:399
  25.0 3.3 %collective-permute-done.5.refs_1_.pair = f32[5,16,128]{2,1,0:T(8,128)S(1)} collective-permute-done((f32[5,16,128]{2,1,0:T(8,128)S(1)}, f32[5,16,128]{2,1,0:T(8,128)S(1)}, u32[]{:S(2)}, u32[]{:S(2)}) %collective-permute-start.5) | collective-permute-done | bytes 40992 | tf_op jit(solution)/shard_map/ppermute | solution.py:411
  28.3 6.7 %all-to-all-done = f32[32,16,128]{2,1,0:T(8,128)S(1)} async-done(((f32[32,16,128]{2,1,0:T(8,128)}), f32[32,16,128]{2,1,0:T(8,128)S(1)}, u32[]{:S(2)}, u32[]{:S(2)}) %all-to-all-start) | async-done | bytes 262176 | tf_op jit(solution)/shard_map/all_to_all | solution.py:394
  35.0 0.8 %shard_map.24 = f32[32,4,128]{2,1,0:T(4,128)} custom-call(f32[512,128]{1,0:T(8,128)S(1)} %bitcast.9), custom_call_target="tpu_custom_call" | custom-call | flops 1000000 | bytes 500000 | tf_op jit(solution)/shard_map/pallas_call | solution.py:414
  35.9 4.4 %all-to-all-start.1 = ((f32[32,4,128]{2,1,0:T(4,128)}), f32[32,4,128]{2,1,0:T(4,128)S(1)}, u32[]{:S(2)}, u32[]{:S(2)}) async-start(f32[32,4,128]{2,1,0:T(4,128)} %shard_map.24), calls=%async_computation.1 | async-start | bytes 131072 | tf_op jit(solution)/shard_map/all_to_all | solution.py:420
  40.3 1.0 %collective-permute-start.6 = (f32[5,16,128]{2,1,0:T(8,128)S(1)}, f32[5,16,128]{2,1,0:T(8,128)S(1)}, u32[]{:S(2)}, u32[]{:S(2)}) collective-permute-start(f32[5,16,128]{2,1,0:T(8,128)S(1)} %shard_map.22), channel_id=1, source_target_pairs={{0,128},{32,160},{64,192},{96,224},{128,0},{160,32},{192,64},{224,... | collective-permute-start | bytes 122888 | tf_op jit(solution)/shard_map/ppermute | solution.py:416
  41.3 4.6 %collective-permute-done.6.quad = f32[5,16,128]{2,1,0:T(8,128)S(1)} collective-permute-done((f32[5,16,128]{2,1,0:T(8,128)S(1)}, f32[5,16,128]{2,1,0:T(8,128)S(1)}, u32[]{:S(2)}, u32[]{:S(2)}) %collective-permute-start.6) | collective-permute-done | bytes 40992 | tf_op jit(solution)/shard_map/ppermute | solution.py:416
  45.9 0.1 shard_map.25.others
  46.0 4.3 %all-to-all-done.1.ends = f32[32,4,128]{2,1,0:T(4,128)S(1)} async-done(((f32[32,4,128]{2,1,0:T(4,128)}), f32[32,4,128]{2,1,0:T(4,128)S(1)}, u32[]{:S(2)}, u32[]{:S(2)}) %all-to-all-start.1) | async-done | bytes 65568 | tf_op jit(solution)/shard_map/all_to_all | solution.py:420
  50.4 0.9 %shard_map.26 = f32[512,128]{1,0:T(8,128)} custom-call(f32[32,4,128]{2,1,0:T(4,128)S(1)} %all-to-all-done.1.ends, f32[16,32,128]{2,1,0:T(8,128)S(1)} %get-tuple-element.36.factor, f32[16,32,128]{2,1,0:T(8,128)S(1)} %get-tuple-element.37.back, f32[16,32,128]{2,1,0:T(8,128)S(1)} %get-tuple-element.38.rest, f32[512,128]{1,0:T(8,128)S(1)} %shard_map.25.others), custom_call_target="tpu_custom_call" | custom-call | flops 1000000 | bytes 500000 | tf_op jit(solution)/shard_map/pallas_call | solution.py:421
  (3 shorter events, 0.1 us)
Async XLA Ops:
  0.0 0.9 %copy-start = (f32[32,16,128]{2,1,0:T(8,128)S(1)}, f32[32,16,128]{2,1,0:T(8,128)}, u32[]{:S(2)}) copy-start(f32[32,16,128]{2,1,0:T(8,128)} %param.1) | copy-start | bytes 786436
  1.0 4.3 %collective-permute-start = (f32[32,128]{1,0:T(8,128)S(1)}, f32[32,128]{1,0:T(8,128)S(1)}, u32[]{:S(2)}, u32[]{:S(2)}) collective-permute-start(f32[32,128]{1,0:T(8,128)S(1)} %get-tuple-element.25), channel_id=1, source_target_pairs={{0,32},{32,0},{64,96},{96,64},{128,160},{160,128},{192,224},{224,1... | collective-permute-start | bytes 49160 | tf_op jit(solution)/shard_map/ppermute | solution.py:385
  1.1 5.6 %collective-permute-start.1 = (f32[32,128]{1,0:T(8,128)S(1)}, f32[32,128]{1,0:T(8,128)S(1)}, u32[]{:S(2)}, u32[]{:S(2)}) collective-permute-start(f32[32,128]{1,0:T(8,128)S(1)} %get-tuple-element.26), channel_id=1, source_target_pairs={{32,64},{64,32},{96,128},{128,96},{160,192},{192,160},{33,65},{65,... | collective-permute-start | bytes 49160 | tf_op jit(solution)/shard_map/ppermute | solution.py:384
  6.9 15.6 %collective-permute-start.2 = (f32[33,128]{1,0:T(8,128)S(1)}, f32[33,128]{1,0:T(8,128)S(1)}, u32[]{:S(2)}, u32[]{:S(2)}) collective-permute-start(f32[33,128]{1,0:T(8,128)S(1)} %get-tuple-element.29), channel_id=1, source_target_pairs={{0,1},{1,0},{2,3},{3,2},{4,5},{5,4},{6,7},{7,6},{8,9},{9,8},{10,11... | collective-permute-start | bytes 50696 | tf_op jit(solution)/shard_map/ppermute | solution.py:390
  8.4 14.1 %collective-permute-start.3 = (f32[33,128]{1,0:T(8,128)S(1)}, f32[33,128]{1,0:T(8,128)S(1)}, u32[]{:S(2)}, u32[]{:S(2)}) collective-permute-start(f32[33,128]{1,0:T(8,128)S(1)} %get-tuple-element.30), channel_id=1, source_target_pairs={{1,2},{2,1},{3,4},{4,3},{5,6},{6,5},{7,8},{8,7},{9,10},{10,9},{11,... | collective-permute-start | bytes 50696 | tf_op jit(solution)/shard_map/ppermute | solution.py:389
  10.1 12.4 %copy-start.1 = (f32[32,16,128]{2,1,0:T(8,128)S(1)}, f32[32,16,128]{2,1,0:T(8,128)}, u32[]{:S(2)}) copy-start(f32[32,16,128]{2,1,0:T(8,128)} %param.1) | copy-start | bytes 786436
  10.1 24.9 %all-to-all-start = ((f32[32,16,128]{2,1,0:T(8,128)}), f32[32,16,128]{2,1,0:T(8,128)S(1)}, u32[]{:S(2)}, u32[]{:S(2)}) async-start(f32[32,16,128]{2,1,0:T(8,128)} %bitcast.1), calls=%async_computation | async-start | bytes 524288 | tf_op jit(solution)/shard_map/all_to_all | solution.py:394
  22.9 1.3 %collective-permute-start.4 = (f32[5,16,128]{2,1,0:T(8,128)S(1)}, f32[5,16,128]{2,1,0:T(8,128)S(1)}, u32[]{:S(2)}, u32[]{:S(2)}) collective-permute-start(f32[5,16,128]{2,1,0:T(8,128)S(1)} %get-tuple-element.31.refs_0_.own), channel_id=1, source_target_pairs={{0,32},{32,0},{64,96},{96,64},{128,160},{160,128},{192,224},{224,1... | collective-permute-start | bytes 122888 | tf_op jit(solution)/shard_map/ppermute | solution.py:398
  24.2 4.1 %collective-permute-start.5 = (f32[5,16,128]{2,1,0:T(8,128)S(1)}, f32[5,16,128]{2,1,0:T(8,128)S(1)}, u32[]{:S(2)}, u32[]{:S(2)}) collective-permute-start(f32[5,16,128]{2,1,0:T(8,128)S(1)} %shard_map.21.refs_0_), channel_id=1, source_target_pairs={{0,64},{32,96},{64,0},{96,32},{128,192},{160,224},{192,128},{224,1... | collective-permute-start | bytes 122888 | tf_op jit(solution)/shard_map/ppermute | solution.py:411
  35.9 14.5 %all-to-all-start.1 = ((f32[32,4,128]{2,1,0:T(4,128)}), f32[32,4,128]{2,1,0:T(4,128)S(1)}, u32[]{:S(2)}, u32[]{:S(2)}) async-start(f32[32,4,128]{2,1,0:T(4,128)} %shard_map.24), calls=%async_computation.1 | async-start | bytes 131072 | tf_op jit(solution)/shard_map/all_to_all | solution.py:420
  40.3 5.6 %collective-permute-start.6 = (f32[5,16,128]{2,1,0:T(8,128)S(1)}, f32[5,16,128]{2,1,0:T(8,128)S(1)}, u32[]{:S(2)}, u32[]{:S(2)}) collective-permute-start(f32[5,16,128]{2,1,0:T(8,128)S(1)} %shard_map.22), channel_id=1, source_target_pairs={{0,128},{32,160},{64,192},{96,224},{128,0},{160,32},{192,64},{224,... | collective-permute-start | bytes 122888 | tf_op jit(solution)/shard_map/ppermute | solution.py:416

commit v7 on v6

--- a/solution.py
+++ b/solution.py
@@ -108,12 +108,11 @@
     next_row[...] = jnp.where(odd_row, high, low)
 
 
-def plane_kernel(vol, deep, pair_row, next_row, port, factor, back, rest, mid, smooth):
+def first_smooth_kernel(deep, next_row, smooth):
     odd_row = (lax.axis_index("lat") & 1) == 1
-    low_row = jnp.where(odd_row, pair_row[...], next_row[...])
-    high_row = jnp.where(odd_row, next_row[...], pair_row[...])
-    depth_last = lax.axis_index("depth") == lax.axis_size("depth") - 1
-    z_open = jnp.where(depth_last, 0.0, TAU3).astype(F32)
+    side = next_row[...]
+    low_row = jnp.where(odd_row, 0.0, side)
+    high_row = jnp.where(odd_row, side, 0.0)
     row_index = lax.broadcasted_iota(jnp.int32, (ROWS, COLS), 0)
     top, bottom = row_index == 0, row_index == ROWS - 1
     for plane in range(PLANES + 1):
@@ -122,6 +121,20 @@
         above = jnp.where(top, low_row[plane : plane + 1, :], pltpu.roll(here, 1, 0))
         below = jnp.where(bottom, high_row[plane : plane + 1, :], pltpu.roll(here, ROWS - 1, 0))
         smooth[span, :] = 0.25 * (above + 2.0 * here + below)
+
+
+def plane_kernel(vol, first_smooth, pair_row, port, factor, back, rest, mid, smooth):
+    odd_row = (lax.axis_index("lat") & 1) == 1
+    depth_last = lax.axis_index("depth") == lax.axis_size("depth") - 1
+    z_open = jnp.where(depth_last, 0.0, TAU3).astype(F32)
+    side = 0.25 * pair_row[...]
+    low_row = jnp.where(odd_row, side, 0.0)
+    high_row = jnp.where(odd_row, 0.0, side)
+    smooth[...] = first_smooth[...]
+    low_place = pl.ds(0, PLANES + 1, stride=ROWS)
+    high_place = pl.ds(ROWS - 1, PLANES + 1, stride=ROWS)
+    smooth[low_place, :] = smooth[low_place, :] + low_row
+    smooth[high_place, :] = smooth[high_place, :] + high_row
 
     def resist(plane):
         return resistance(cells(smooth, plane + 1) - cells(smooth, plane))
@@ -387,14 +400,16 @@
         deep_kernel, (tall, side, side), (pltpu.VMEM((PLANES + 3, ROWS, COLS), F32),)
     )(flat, near_side, far_side)
     next_row = lax.ppermute(to_next, "lat", next_perm("lat"))
+    first_smooth = call(first_smooth_kernel, tall, flops=LONG)(deep, next_row)
+    first_smooth, to_pair = lax.optimization_barrier((first_smooth, to_pair))
     pair_row = lax.ppermute(to_pair, "lat", swap_perm("lat", 1))
     y_port, y_factor, y_back, y_rest = call(row_kernel, (shaped(PLANES * PORT, COLS), lines, lines, lines))(
         flat, deep
     )
     ports = lax.all_to_all(y_port, "lat", 0, 0, tiled=True)
     z_port, z_factor, z_back, z_rest, z_mid, smooth = call(
-        plane_kernel, (port, whole, whole, whole, shaped(3, ROWS, COLS), tall), moved=500000,flops=LONG
-    )(flat, deep, pair_row, next_row)
+        plane_kernel, (port, whole, whole, whole, shaped(3, ROWS, COLS), tall), moved=500000,
+    )(flat, first_smooth, pair_row)
     near = lax.ppermute(z_port, "depth", swap_perm("depth", 1))
     solved_x = call(
         column_kernel,

time: 51.6 us -> 56.1 us (1.087)
  starting transfers between devices: 24.4 us -> 29.3 us
    all_to_all x1, waiting for transfers between devices: 6.7 us -> 0.01 us  [shards(): ports = lax.all_to_all(y_port, 'lat', 0, 0, tiled=True)]
    ppermute x1, waiting for transfers between devices: 0.01 us -> 6.43 us  [shards(): pair_row = lax.ppermute(to_pair, 'lat', swap_perm('lat', 1))]
    all_to_all x1, starting transfers between devices: 4.44 us -> 8.57 us  [shards(): ends_y = lax.all_to_all(ends, 'lat', 0, 0, tiled=True)]
where the time goes in v7:
time: 56.1 us; the launch traced here: 55.8 us
  starting transfers between devices  29.3 us (52%)
  waiting for transfers between devices  21.2 us (38%)
  Pallas kernels  4.29 us (8%)
  local copies, waits for them, and re-layouts  0.96 us (2%)
    all_to_all x1, starting transfers between devices, shards(): ports = lax.all_to_all(y_port, 'lat', 0, 0, tiled=True)  12.6 us
    all_to_all x1, starting transfers between devices, shards(): ends_y = lax.all_to_all(ends, 'lat', 0, 0, tiled=True)  8.57 us
    ppermute x1, waiting for transfers between devices, shards(): pair_row = lax.ppermute(to_pair, 'lat', swap_perm('lat', 1))  6.43 us
    ppermute x1, waiting for transfers between devices, shards(): quad = lax.ppermute(quad_own, 'depth', swap_perm('depth', 4))  4.49 us
    all_to_all x1, waiting for transfers between devices, shards(): ends_y = lax.all_to_all(ends, 'lat', 0, 0, tiled=True)  4.33 us
    ppermute x1, starting transfers between devices, shards(): far_side = lax.ppermute(to_far, 'depth', next_perm('depth'))  4.18 us
    ppermute x1, waiting for transfers between devices, shards(): pair = lax.ppermute(pair_own, 'depth', swap_perm('depth', 2))  3.3 us
    ppermute x1, starting transfers between devices, shards(): pair_row = lax.ppermute(to_pair, 'lat', swap_perm('lat', 1))  1.88 us
  transfers between devices with their start and end apart: 9, of which 6 were waited for; matrix products, arithmetic and copies ran while one was open for 0% of the time, Pallas kernels for 4%

profile of v7, /device:TPU:8, one launch (start us, length us, event | category | flops | bytes accessed | tf_op | source)
XLA Modules:
  0.0 55.8 jit_solution(10121613745426717500)
XLA Ops:
  0.0 0.0 copy-start
  0.0 0.9 %copy-done = f32[32,16,128]{2,1,0:T(8,128)S(1)} copy-done((f32[32,16,128]{2,1,0:T(8,128)S(1)}, f32[32,16,128]{2,1,0:T(8,128)}, u32[]{:S(2)}) %copy-start) | copy-done | bytes 262168
  1.0 0.1 collective-permute-start
  1.1 4.2 %collective-permute-start.1 = (f32[32,128]{1,0:T(8,128)S(1)}, f32[32,128]{1,0:T(8,128)S(1)}, u32[]{:S(2)}, u32[]{:S(2)}) collective-permute-start(f32[32,128]{1,0:T(8,128)S(1)} %get-tuple-element.28), channel_id=1, source_target_pairs={{32,64},{64,32},{96,128},{128,96},{160,192},{192,160},{33,65},{65,... | collective-permute-start | bytes 49160 | tf_op jit(solution)/shard_map/ppermute | solution.py:397
  5.3 0.0 collective-permute-done.near_side
  5.3 1.4 %collective-permute-done.1.far_side = f32[32,128]{1,0:T(8,128)S(1)} collective-permute-done((f32[32,128]{1,0:T(8,128)S(1)}, f32[32,128]{1,0:T(8,128)S(1)}, u32[]{:S(2)}, u32[]{:S(2)}) %collective-permute-start.1) | collective-permute-done | bytes 16416 | tf_op jit(solution)/shard_map/ppermute | solution.py:397
  6.7 0.2 shard_map.18
  6.9 0.7 %collective-permute-start.2 = (f32[33,128]{1,0:T(8,128)S(1)}, f32[33,128]{1,0:T(8,128)S(1)}, u32[]{:S(2)}, u32[]{:S(2)}) collective-permute-start(f32[33,128]{1,0:T(8,128)S(1)} %get-tuple-element.31), channel_id=1, source_target_pairs={{1,2},{2,1},{3,4},{4,3},{5,6},{6,5},{7,8},{8,7},{9,10},{10,9},{11,... | collective-permute-start | bytes 50696 | tf_op jit(solution)/shard_map/ppermute | solution.py:402
  7.6 1.1 %shard_map.19 = (f32[512,128]{1,0:T(8,128)}, f32[16,32,128]{2,1,0:T(8,128)S(1)}, f32[16,32,128]{2,1,0:T(8,128)S(1)}, f32[16,32,128]{2,1,0:T(8,128)S(1)}) custom-call(f32[512,128]{1,0:T(8,128)S(1)} %bitcast.6, f32[528,128]{1,0:T(8,128)S(1)} %get-tuple-element.29.deep), custom_call_target="tpu_custom_call" | custom-call | flops 1000000 | bytes 500000 | tf_op jit(solution)/shard_map/pallas_call | solution.py:406
  8.7 12.6 %all-to-all-start = ((f32[32,16,128]{2,1,0:T(8,128)}), f32[32,16,128]{2,1,0:T(8,128)S(1)}, u32[]{:S(2)}, u32[]{:S(2)}) async-start(f32[32,16,128]{2,1,0:T(8,128)} %bitcast.1), calls=%async_computation | async-start | bytes 524288 | tf_op jit(solution)/shard_map/all_to_all | solution.py:409
  21.3 0.0 copy-start.1
  21.3 0.0 collective-permute-done.2.next_row
  21.3 0.1 shard_map.20.first_smooth
  21.4 1.9 %collective-permute-start.3 = (f32[33,128]{1,0:T(8,128)S(1)}, f32[33,128]{1,0:T(8,128)S(1)}, u32[]{:S(2)}, u32[]{:S(2)}) collective-permute-start(f32[33,128]{1,0:T(8,128)S(1)} %get-tuple-element.34), channel_id=1, source_target_pairs={{0,1},{1,0},{2,3},{3,2},{4,5},{5,4},{6,7},{7,6},{8,9},{9,8},{10,11... | collective-permute-start | bytes 50696 | tf_op jit(solution)/shard_map/ppermute | solution.py:405
  23.3 6.4 %collective-permute-done.3.pair_row = f32[33,128]{1,0:T(8,128)S(1)} collective-permute-done((f32[33,128]{1,0:T(8,128)S(1)}, f32[33,128]{1,0:T(8,128)S(1)}, u32[]{:S(2)}, u32[]{:S(2)}) %collective-permute-start.3) | collective-permute-done | bytes 16928 | tf_op jit(solution)/shard_map/ppermute | solution.py:405
  29.7 0.0 copy-done.1
  29.7 0.3 shard_map.21
  30.0 0.1 collective-permute-start.4
  30.1 1.2 %collective-permute-done.4.refs_1_.near = f32[5,16,128]{2,1,0:T(8,128)S(1)} collective-permute-done((f32[5,16,128]{2,1,0:T(8,128)S(1)}, f32[5,16,128]{2,1,0:T(8,128)S(1)}, u32[]{:S(2)}, u32[]{:S(2)}) %collective-permute-start.4) | collective-permute-done | bytes 40992 | tf_op jit(solution)/shard_map/ppermute | solution.py:413
  31.3 0.1 collective-permute-start.5
  31.4 0.7 %shard_map.24.solved_x = f32[512,128]{1,0:T(8,128)S(1)} custom-call(f32[512,128]{1,0:T(8,128)S(1)} %bitcast.8, f32[528,128]{1,0:T(8,128)S(1)} %get-tuple-element.36.smooth), custom_call_target="tpu_custom_call" | custom-call | flops 1000000 | bytes 500000 | tf_op jit(solution)/shard_map/pallas_call | solution.py:414
  32.1 3.3 %collective-permute-done.5.refs_1_.pair = f32[5,16,128]{2,1,0:T(8,128)S(1)} collective-permute-done((f32[5,16,128]{2,1,0:T(8,128)S(1)}, f32[5,16,128]{2,1,0:T(8,128)S(1)}, u32[]{:S(2)}, u32[]{:S(2)}) %collective-permute-start.5) | collective-permute-done | bytes 40992 | tf_op jit(solution)/shard_map/ppermute | solution.py:426
  35.4 0.0 all-to-all-done
  35.4 0.8 %shard_map.25 = f32[32,4,128]{2,1,0:T(4,128)} custom-call(f32[512,128]{1,0:T(8,128)S(1)} %bitcast.9), custom_call_target="tpu_custom_call" | custom-call | flops 1000000 | bytes 500000 | tf_op jit(solution)/shard_map/pallas_call | solution.py:429
  36.3 8.6 %all-to-all-start.1 = ((f32[32,4,128]{2,1,0:T(4,128)}), f32[32,4,128]{2,1,0:T(4,128)S(1)}, u32[]{:S(2)}, u32[]{:S(2)}) async-start(f32[32,4,128]{2,1,0:T(4,128)} %shard_map.25), calls=%async_computation.1 | async-start | bytes 131072 | tf_op jit(solution)/shard_map/all_to_all | solution.py:435
  44.9 1.1 %collective-permute-start.6 = (f32[5,16,128]{2,1,0:T(8,128)S(1)}, f32[5,16,128]{2,1,0:T(8,128)S(1)}, u32[]{:S(2)}, u32[]{:S(2)}) collective-permute-start(f32[5,16,128]{2,1,0:T(8,128)S(1)} %shard_map.23), channel_id=1, source_target_pairs={{0,128},{32,160},{64,192},{96,224},{128,0},{160,32},{192,64},{224,... | collective-permute-start | bytes 122888 | tf_op jit(solution)/shard_map/ppermute | solution.py:431
  46.0 4.5 %collective-permute-done.6.quad = f32[5,16,128]{2,1,0:T(8,128)S(1)} collective-permute-done((f32[5,16,128]{2,1,0:T(8,128)S(1)}, f32[5,16,128]{2,1,0:T(8,128)S(1)}, u32[]{:S(2)}, u32[]{:S(2)}) %collective-permute-start.6) | collective-permute-done | bytes 40992 | tf_op jit(solution)/shard_map/ppermute | solution.py:431
  50.5 0.1 shard_map.26.others
  50.6 4.3 %all-to-all-done.1.ends = f32[32,4,128]{2,1,0:T(4,128)S(1)} async-done(((f32[32,4,128]{2,1,0:T(4,128)}), f32[32,4,128]{2,1,0:T(4,128)S(1)}, u32[]{:S(2)}, u32[]{:S(2)}) %all-to-all-start.1) | async-done | bytes 65568 | tf_op jit(solution)/shard_map/all_to_all | solution.py:435
  54.9 0.9 %shard_map.27 = f32[512,128]{1,0:T(8,128)} custom-call(f32[32,4,128]{2,1,0:T(4,128)S(1)} %all-to-all-done.1.ends, f32[16,32,128]{2,1,0:T(8,128)S(1)} %get-tuple-element.40.factor, f32[16,32,128]{2,1,0:T(8,128)S(1)} %get-tuple-element.41.back, f32[16,32,128]{2,1,0:T(8,128)S(1)} %get-tuple-element.42.rest, f32[512,128]{1,0:T(8,128)S(1)} %shard_map.26.others), custom_call_target="tpu_custom_call" | custom-call | flops 1000000 | bytes 500000 | tf_op jit(solution)/shard_map/pallas_call | solution.py:436
  (3 shorter events, 0.1 us)
Async XLA Ops:
  0.0 0.9 %copy-start = (f32[32,16,128]{2,1,0:T(8,128)S(1)}, f32[32,16,128]{2,1,0:T(8,128)}, u32[]{:S(2)}) copy-start(f32[32,16,128]{2,1,0:T(8,128)} %param.1) | copy-start | bytes 786436
  1.0 4.3 %collective-permute-start = (f32[32,128]{1,0:T(8,128)S(1)}, f32[32,128]{1,0:T(8,128)S(1)}, u32[]{:S(2)}, u32[]{:S(2)}) collective-permute-start(f32[32,128]{1,0:T(8,128)S(1)} %get-tuple-element.27), channel_id=1, source_target_pairs={{0,32},{32,0},{64,96},{96,64},{128,160},{160,128},{192,224},{224,1... | collective-permute-start | bytes 49160 | tf_op jit(solution)/shard_map/ppermute | solution.py:398
  1.1 5.6 %collective-permute-start.1 = (f32[32,128]{1,0:T(8,128)S(1)}, f32[32,128]{1,0:T(8,128)S(1)}, u32[]{:S(2)}, u32[]{:S(2)}) collective-permute-start(f32[32,128]{1,0:T(8,128)S(1)} %get-tuple-element.28), channel_id=1, source_target_pairs={{32,64},{64,32},{96,128},{128,96},{160,192},{192,160},{33,65},{65,... | collective-permute-start | bytes 49160 | tf_op jit(solution)/shard_map/ppermute | solution.py:397
  6.9 14.4 %collective-permute-start.2 = (f32[33,128]{1,0:T(8,128)S(1)}, f32[33,128]{1,0:T(8,128)S(1)}, u32[]{:S(2)}, u32[]{:S(2)}) collective-permute-start(f32[33,128]{1,0:T(8,128)S(1)} %get-tuple-element.31), channel_id=1, source_target_pairs={{1,2},{2,1},{3,4},{4,3},{5,6},{6,5},{7,8},{8,7},{9,10},{10,9},{11,... | collective-permute-start | bytes 50696 | tf_op jit(solution)/shard_map/ppermute | solution.py:402
  8.7 26.7 %all-to-all-start = ((f32[32,16,128]{2,1,0:T(8,128)}), f32[32,16,128]{2,1,0:T(8,128)S(1)}, u32[]{:S(2)}, u32[]{:S(2)}) async-start(f32[32,16,128]{2,1,0:T(8,128)} %bitcast.1), calls=%async_computation | async-start | bytes 524288 | tf_op jit(solution)/shard_map/all_to_all | solution.py:409
  21.3 8.4 %copy-start.1 = (f32[32,16,128]{2,1,0:T(8,128)S(1)}, f32[32,16,128]{2,1,0:T(8,128)}, u32[]{:S(2)}) copy-start(f32[32,16,128]{2,1,0:T(8,128)} %param.1) | copy-start | bytes 786436
  21.4 8.3 %collective-permute-start.3 = (f32[33,128]{1,0:T(8,128)S(1)}, f32[33,128]{1,0:T(8,128)S(1)}, u32[]{:S(2)}, u32[]{:S(2)}) collective-permute-start(f32[33,128]{1,0:T(8,128)S(1)} %get-tuple-element.34), channel_id=1, source_target_pairs={{0,1},{1,0},{2,3},{3,2},{4,5},{5,4},{6,7},{7,6},{8,9},{9,8},{10,11... | collective-permute-start | bytes 50696 | tf_op jit(solution)/shard_map/ppermute | solution.py:405
  30.0 1.3 %collective-permute-start.4 = (f32[5,16,128]{2,1,0:T(8,128)S(1)}, f32[5,16,128]{2,1,0:T(8,128)S(1)}, u32[]{:S(2)}, u32[]{:S(2)}) collective-permute-start(f32[5,16,128]{2,1,0:T(8,128)S(1)} %get-tuple-element.35.refs_0_.own), channel_id=1, source_target_pairs={{0,32},{32,0},{64,96},{96,64},{128,160},{160,128},{192,224},{224,1... | collective-permute-start | bytes 122888 | tf_op jit(solution)/shard_map/ppermute | solution.py:413
  31.3 4.1 %collective-permute-start.5 = (f32[5,16,128]{2,1,0:T(8,128)S(1)}, f32[5,16,128]{2,1,0:T(8,128)S(1)}, u32[]{:S(2)}, u32[]{:S(2)}) collective-permute-start(f32[5,16,128]{2,1,0:T(8,128)S(1)} %shard_map.22.refs_0_), channel_id=1, source_target_pairs={{0,64},{32,96},{64,0},{96,32},{128,192},{160,224},{192,128},{224,1... | collective-permute-start | bytes 122888 | tf_op jit(solution)/shard_map/ppermute | solution.py:426
  36.3 18.6 %all-to-all-start.1 = ((f32[32,4,128]{2,1,0:T(4,128)}), f32[32,4,128]{2,1,0:T(4,128)S(1)}, u32[]{:S(2)}, u32[]{:S(2)}) async-start(f32[32,4,128]{2,1,0:T(4,128)} %shard_map.25), calls=%async_computation.1 | async-start | bytes 131072 | tf_op jit(solution)/shard_map/all_to_all | solution.py:435
  44.9 5.6 %collective-permute-start.6 = (f32[5,16,128]{2,1,0:T(8,128)S(1)}, f32[5,16,128]{2,1,0:T(8,128)S(1)}, u32[]{:S(2)}, u32[]{:S(2)}) collective-permute-start(f32[5,16,128]{2,1,0:T(8,128)S(1)} %shard_map.23), channel_id=1, source_target_pairs={{0,128},{32,160},{64,192},{96,224},{128,0},{160,32},{192,64},{224,... | collective-permute-start | bytes 122888 | tf_op jit(solution)/shard_map/ppermute | solution.py:431

commit v8 on v3

--- a/solution.py
+++ b/solution.py
@@ -12,6 +12,7 @@
 COLS = 128
 BLOCKS = 32
 PORT = 8
+FACE = 40
 F32 = jnp.float32
 
 
@@ -62,19 +63,31 @@
     ), (to_left, to_right, source * inverse)
 
 
-def edge_kernel(vol, near_side, far_side, sems):
-    odd = lax.axis_index("depth") & 1
-    high = (PLANES - 2) * ROWS
-    near_start = pl.multiple_of((1 - odd) * high, ROWS)
-    far_start = pl.multiple_of(odd * high, ROWS)
-    copies = (
-        pltpu.make_async_copy(vol.at[pl.ds(near_start, 2 * ROWS), :], near_side, sems.at[0]),
-        pltpu.make_async_copy(vol.at[pl.ds(far_start, 2 * ROWS), :], far_side, sems.at[1]),
-    )
-    for copy in copies:
-        copy.start()
-    for copy in copies:
-        copy.wait()
+def side_kernel(vol, pair_row, next_row):
+    odd = (lax.axis_index("lat") & 1) == 1
+    low = vol[pl.ds(0, PLANES, stride=ROWS), :]
+    high = vol[pl.ds(ROWS - 1, PLANES, stride=ROWS), :]
+    pair_row[...] = jnp.where(odd, low, high)
+    next_row[...] = jnp.where(odd, high, low)
+
+
+def side_rows(pair_row, next_row):
+    odd = (lax.axis_index("lat") & 1) == 1
+    return jnp.where(odd, pair_row, next_row), jnp.where(odd, next_row, pair_row)
+
+
+def face_kernel(vol, pair_row, next_row, near_face, far_face):
+    odd = (lax.axis_index("depth") & 1) == 1
+    low_row, high_row = side_rows(pair_row[...], next_row[...])
+    size = 2 * ROWS
+    low_planes, high_planes = vol[0:size, :], vol[(PLANES - 2) * ROWS :, :]
+    near_face[0:size, :] = jnp.where(odd, low_planes, high_planes)
+    far_face[0:size, :] = jnp.where(odd, high_planes, low_planes)
+    for place, side in ((size, low_row), (size + 2, high_row)):
+        near_face[place : place + 2, :] = jnp.where(odd, side[0:2, :], side[PLANES - 2 :, :])
+        far_face[place : place + 2, :] = jnp.where(odd, side[PLANES - 2 :, :], side[0:2, :])
+    near_face[size + 4 :, :] = jnp.zeros((FACE - size - 4, COLS), F32)
+    far_face[size + 4 :, :] = jnp.zeros((FACE - size - 4, COLS), F32)
 
 
 def strided(ref, row):
@@ -85,36 +98,40 @@
     return ref[plane * ROWS : (plane + 1) * ROWS, :]
 
 
-def deep_kernel(vol, near_side, far_side, deep, low_side, high_side, mixed):
+def smooth_kernel(vol, pair_row, next_row, near_face, far_face, smooth, mixed, low_side, high_side):
     odd = (lax.axis_index("depth") & 1) == 1
+    size = 2 * ROWS
+    near, far = near_face[...], far_face[...]
+    below_face, above_face = jnp.where(odd, near, far), jnp.where(odd, far, near)
     lane = lax.broadcasted_iota(jnp.int32, (ROWS, COLS), 1)
     first, last = lane == 0, lane == COLS - 1
-    mixed[0] = smooth_lanes(jnp.where(odd, cells(near_side, 1), cells(far_side, 1)), first, last)
+    mixed[0] = smooth_lanes(below_face[ROWS:size, :], first, last)
     for plane in range(PLANES):
         mixed[plane + 1] = smooth_lanes(cells(vol, plane), first, last)
     for plane in range(2):
-        mixed[PLANES + 1 + plane] = smooth_lanes(
-            jnp.where(odd, cells(far_side, plane), cells(near_side, plane)), first, last
+        mixed[PLANES + 1 + plane] = smooth_lanes(above_face[plane * ROWS : (plane + 1) * ROWS, :], first, last)
+    side_lane = lax.broadcasted_iota(jnp.int32, (PLANES + 3, COLS), 1)
+    sides = []
+    for place, ref, own in zip((size, size + 2), (low_side, high_side), side_rows(pair_row[...], next_row[...])):
+        ref[0:1, :] = below_face[place + 1 : place + 2, :]
+        ref[1 : PLANES + 1, :] = own
+        ref[PLANES + 1 : PLANES + 3, :] = above_face[place : place + 2, :]
+        ref[0 : PLANES + 3, :] = smooth_lanes(ref[0 : PLANES + 3, :], side_lane == 0, side_lane == COLS - 1)
+        sides.append(
+            0.25 * (ref[0 : PLANES + 1, :] + 2.0 * ref[1 : PLANES + 2, :] + ref[2 : PLANES + 3, :])
         )
-    for plane in range(PLANES + 1):
-        deep[plane * ROWS : (plane + 1) * ROWS, :] = 0.25 * (
-            mixed[plane] + 2.0 * mixed[plane + 1] + mixed[plane + 2]
-        )
-    low_side[...] = deep[pl.ds(0, PLANES + 1, stride=ROWS), :]
-    high_side[...] = deep[pl.ds(ROWS - 1, PLANES + 1, stride=ROWS), :]
-
-
-def plane_kernel(vol, deep, low_row, high_row, port, factor, back, rest, mid, smooth):
-    depth_last = lax.axis_index("depth") == lax.axis_size("depth") - 1
-    z_open = jnp.where(depth_last, 0.0, TAU3).astype(F32)
     row_index = lax.broadcasted_iota(jnp.int32, (ROWS, COLS), 0)
     top, bottom = row_index == 0, row_index == ROWS - 1
     for plane in range(PLANES + 1):
-        span = slice(plane * ROWS, (plane + 1) * ROWS)
-        here = deep[span, :]
-        above = jnp.where(top, low_row[plane : plane + 1, :], pltpu.roll(here, 1, 0))
-        below = jnp.where(bottom, high_row[plane : plane + 1, :], pltpu.roll(here, ROWS - 1, 0))
-        smooth[span, :] = 0.25 * (above + 2.0 * here + below)
+        here = 0.25 * (mixed[plane] + 2.0 * mixed[plane + 1] + mixed[plane + 2])
+        above = jnp.where(top, sides[0][plane : plane + 1, :], pltpu.roll(here, 1, 0))
+        below = jnp.where(bottom, sides[1][plane : plane + 1, :], pltpu.roll(here, ROWS - 1, 0))
+        smooth[plane * ROWS : (plane + 1) * ROWS, :] = 0.25 * (above + 2.0 * here + below)
+
+
+def plane_kernel(vol, smooth, port, factor, back, rest, mid):
+    depth_last = lax.axis_index("depth") == lax.axis_size("depth") - 1
+    z_open = jnp.where(depth_last, 0.0, TAU3).astype(F32)
 
     def resist(plane):
         return resistance(cells(smooth, plane + 1) - cells(smooth, plane))
@@ -254,9 +271,8 @@
         out[place] = value
 
 
-def finish_kernel(
-    ends_y, y_factor, y_back, y_rest, own, near, pair, quad, z_factor, z_back, z_rest, z_mid, solved_x,
-    out, acc,
+def finish_plane_kernel(
+    own, near, pair, quad, factor, back, rest, mid, solved_x, out,
 ):
     index = lax.axis_index("depth")
     zero = jnp.zeros((ROWS, COLS), F32)
@@ -280,24 +296,32 @@
     share = c * inverse
     first = (left_source + ns + share * source) / (left_ground + ng + share * ground)
     after = share * first + source * inverse
-    middle = z_mid[0] * first + z_mid[1] * after + z_mid[2]
+    middle = mid[0] * first + mid[1] * after + mid[2]
     half = PLANES // 2
-    y_first = ends_y[:, 0, :]
-    value = ends_y[:, 1, :]
-    acc[pl.ds(0, PLANES, stride=ROWS), :] = y_first
-    acc[pl.ds(ROWS - 1, PLANES, stride=ROWS), :] = value
-    for row in range(ROWS - 2, 0, -1):
-        value = y_factor[row] * value + (y_back[row] * y_first + y_rest[row])
-        acc[pl.ds(row, PLANES, stride=ROWS), :] = value
-    third = 1.0 / 3.0
     for start, near_value, far_value in ((0, first, middle), (half, middle, after)):
         value = far_value
         for plane in range(start + half - 1, start, -1):
             span = slice(plane * ROWS, (plane + 1) * ROWS)
-            value = z_factor[span, :] * value + (z_back[span, :] * near_value + z_rest[span, :])
-            out[span, :] = (solved_x[span, :] + acc[span, :] + value) * third
+            value = factor[span, :] * value + (back[span, :] * near_value + rest[span, :])
+            out[span, :] = solved_x[span, :] + value
         span = slice(start * ROWS, (start + 1) * ROWS)
-        out[span, :] = (solved_x[span, :] + acc[span, :] + near_value) * third
+        out[span, :] = solved_x[span, :] + near_value
+
+
+def finish_row_kernel(ends, factor, back, rest, others, out):
+    third = 1.0 / 3.0
+
+    def put(row, value):
+        place = pl.ds(row, PLANES, stride=ROWS)
+        out[place, :] = (others[place, :] + value) * third
+
+    first = ends[:, 0, :]
+    value = ends[:, 1, :]
+    put(0, first)
+    put(ROWS - 1, value)
+    for row in range(ROWS - 2, 0, -1):
+        value = factor[row] * value + (back[row] * first + rest[row])
+        put(row, value)
 
 
 def call(kernel, outs, scratch=(), flops=1000000, moved=500000, **options):
@@ -339,30 +363,29 @@
     whole = shaped(PLANES * ROWS, COLS)
     tall = shaped((PLANES + 1) * ROWS, COLS)
     port = shaped(5, ROWS, COLS)
-    side = shaped(PLANES + 1, COLS)
-    to_near, to_far = call(
-        edge_kernel,
-        (shaped(2 * ROWS, COLS), shaped(2 * ROWS, COLS)),
-        (pltpu.SemaphoreType.DMA((2,)),),
-        in_specs=[pl.BlockSpec(memory_space=pl.ANY)],
-    )(flat)
-    far_side = lax.ppermute(to_far, "depth", next_perm("depth"))
-    near_side = lax.ppermute(to_near, "depth", swap_perm("depth", 1))
-    deep, row_low, row_high = call(
-        deep_kernel, (tall, side, side), (pltpu.VMEM((PLANES + 3, ROWS, COLS), F32),)
-    )(flat, near_side, far_side)
-    low_row = lax.ppermute(row_high, "lat", line_perm("lat", 1))
-    high_row = lax.ppermute(row_low, "lat", line_perm("lat", -1))
-    z_port, z_factor, z_back, z_rest, z_mid, smooth = call(
-        plane_kernel, (port, whole, whole, whole, shaped(3, ROWS, COLS), tall)
-    )(flat, deep, low_row, high_row)
-    near = lax.ppermute(z_port, "depth", swap_perm("depth", 1))
+    to_pair, to_next = call(side_kernel, (shaped(PLANES, COLS), shaped(PLANES, COLS)))(flat)
+    next_row = lax.ppermute(to_next, "lat", next_perm("lat"))
+    pair_row = lax.ppermute(to_pair, "lat", swap_perm("lat", 1))
+    to_near, to_far = call(face_kernel, (shaped(FACE, COLS), shaped(FACE, COLS)))(flat, pair_row, next_row)
+    far_face = lax.ppermute(to_far, "depth", next_perm("depth"))
+    near_face = lax.ppermute(to_near, "depth", swap_perm("depth", 1))
+    smooth = call(
+        smooth_kernel,
+        tall,
+        (
+            pltpu.VMEM((PLANES + 3, ROWS, COLS), F32),
+            pltpu.VMEM((40, COLS), F32),
+            pltpu.VMEM((40, COLS), F32),
+        ),
+    )(flat, pair_row, next_row, near_face, far_face)
     y_port, y_factor, y_back, y_rest = call(row_kernel, (shaped(PLANES * PORT, COLS), lines, lines, lines))(
         flat, smooth
     )
-    pair_own = call(lambda *refs: join_kernel(1, *refs), port)(z_port, near)
-    flat_later, smooth_later, pair_own = lax.optimization_barrier((flat, smooth, pair_own))
-    pair = lax.ppermute(pair_own, "depth", swap_perm("depth", 2))
+    ports = lax.all_to_all(y_port, "lat", 0, 0, tiled=True)
+    z_port, z_factor, z_back, z_rest, z_mid = call(
+        plane_kernel, (port, whole, whole, whole, shaped(3, ROWS, COLS))
+    )(flat, smooth)
+    near = lax.ppermute(z_port, "depth", swap_perm("depth", 1))
     solved_x = call(
         column_kernel,
         whole,
@@ -373,19 +396,19 @@
             pltpu.VMEM((16, 32, COLS), F32),
             pltpu.VMEM((16, 32, COLS), F32),
         ),
-    )(flat_later, smooth_later)
-    y_port, solved_x = lax.optimization_barrier((y_port, solved_x))
-    ports = lax.all_to_all(y_port, "lat", 0, 0, tiled=True)
-    ports, pair = lax.optimization_barrier((ports, pair))
+    )(flat, smooth)
+    pair_own = call(lambda *refs: join_kernel(1, *refs), port)(z_port, near)
+    pair = lax.ppermute(pair_own, "depth", swap_perm("depth", 2))
     quad_own = call(lambda *refs: join_kernel(2, *refs), port)(pair_own, pair)
-    ports, quad_own = lax.optimization_barrier((ports, quad_own))
+    ports, quad_own, solved_x = lax.optimization_barrier((ports, quad_own, solved_x))
+    ends = call(row_reduced_kernel, shaped(BLOCKS, 2, COLS))(ports)
+    ends, quad_own = lax.optimization_barrier((ends, quad_own))
     quad = lax.ppermute(quad_own, "depth", swap_perm("depth", 4))
-    ends = call(row_reduced_kernel, shaped(BLOCKS, 2, COLS))(ports)
+    others = call(finish_plane_kernel, whole)(
+        z_port, near, pair, quad, z_factor, z_back, z_rest, z_mid, solved_x
+    )
     ends_y = lax.all_to_all(ends, "lat", 0, 0, tiled=True)
-    ends_y, quad = lax.optimization_barrier((ends_y, quad))
-    out = call(finish_kernel, whole, (pltpu.VMEM((PLANES * ROWS, COLS), F32),))(
-        ends_y, y_factor, y_back, y_rest, z_port, near, pair, quad, z_factor, z_back, z_rest, z_mid, solved_x
-    )
+    out = call(finish_row_kernel, whole)(ends_y, y_factor, y_back, y_rest, others)
     return out.reshape(PLANES, ROWS, COLS)
 
 

time: 55.9 us -> 54.2 us (0.970)
  waiting for transfers between devices: 24.1 us -> 19.3 us
  starting transfers between devices: 26.4 us -> 29.5 us
    all_to_all x1, starting transfers between devices: 11.2 us -> 15 us  [shards(): ports = lax.all_to_all(y_port, 'lat', 0, 0, tiled=True)]
    ppermute x4, waiting for transfers between devices: 5.79 us -> 2.62 us  [the longest x1 1.45 us: shards(): far_face = lax.ppermute(to_far, 'depth', next_perm('depth'))]
    ppermute x4, starting transfers between devices: 8.84 us -> 6.93 us  [the longest x1 4.18 us: shards(): far_face = lax.ppermute(to_far, 'depth', next_perm('depth'))]
    all_to_all x1, waiting for transfers between devices: 6.67 us -> 5.27 us  [shards(): ports = lax.all_to_all(y_port, 'lat', 0, 0, tiled=True)]
    ppermute x1, waiting for transfers between devices: 3.99 us -> 3.01 us  [shards(): pair = lax.ppermute(pair_own, 'depth', swap_perm('depth', 2))]
    ppermute x1, waiting for transfers between devices: 0.19 us -> 1.01 us  [shards(): near = lax.ppermute(z_port, 'depth', swap_perm('depth', 1))]
    all_to_all x1, starting transfers between devices: 3.85 us -> 4.53 us  [shards(): ends_y = lax.all_to_all(ends, 'lat', 0, 0, tiled=True)]
    pallas_call x4 -> x6, Pallas kernels: 1.5 us -> 1.52 us  [the longest x1 0.89 us: shards(): call(finish_row_kernel, whole)(ends_y, y_factor, y_back, y_rest, others)]
  transfers between devices with their start and end apart: 9 -> 9, of which waited for: 8 -> 7; matrix products, arithmetic and copies ran while one was open for 0% -> 0% of each run, Pallas kernels for 2% -> 2%
where the time goes in v8:
time: 54.2 us; the launch traced here: 53.9 us
  starting transfers between devices  29.5 us (54%)
  waiting for transfers between devices  19.3 us (36%)
  Pallas kernels  3.99 us (7%)
  local copies, waits for them, and re-layouts  0.95 us (2%)
    all_to_all x1, starting transfers between devices, shards(): ports = lax.all_to_all(y_port, 'lat', 0, 0, tiled=True)  15 us
    all_to_all x1, waiting for transfers between devices, shards(): ports = lax.all_to_all(y_port, 'lat', 0, 0, tiled=True)  5.27 us
    all_to_all x1, starting transfers between devices, shards(): ends_y = lax.all_to_all(ends, 'lat', 0, 0, tiled=True)  4.53 us
    all_to_all x1, waiting for transfers between devices, shards(): ends_y = lax.all_to_all(ends, 'lat', 0, 0, tiled=True)  4.21 us
    ppermute x1, starting transfers between devices, shards(): far_face = lax.ppermute(to_far, 'depth', next_perm('depth'))  4.18 us
    ppermute x1, waiting for transfers between devices, shards(): quad = lax.ppermute(quad_own, 'depth', swap_perm('depth', 4))  3.21 us
    ppermute x1, waiting for transfers between devices, shards(): pair = lax.ppermute(pair_own, 'depth', swap_perm('depth', 2))  3.01 us
    ppermute x1, starting transfers between devices, shards(): quad = lax.ppermute(quad_own, 'depth', swap_perm('depth', 4))  2.38 us
  transfers between devices with their start and end apart: 9, of which 7 were waited for; matrix products, arithmetic and copies ran while one was open for 0% of the time, Pallas kernels for 2%

profile of v8, /device:TPU:8, one launch (start us, length us, event | category | flops | bytes accessed | tf_op | source)
XLA Modules:
  0.0 53.9 jit_solution(1430758449199259845)
XLA Ops:
  0.0 0.0 copy-start
  0.0 0.9 %copy-done = f32[32,16,128]{2,1,0:T(8,128)S(1)} copy-done((f32[32,16,128]{2,1,0:T(8,128)S(1)}, f32[32,16,128]{2,1,0:T(8,128)}, u32[]{:S(2)}) %copy-start) | copy-done | bytes 262168
  1.0 2.0 %collective-permute-start = (f32[32,128]{1,0:T(8,128)S(1)}, f32[32,128]{1,0:T(8,128)S(1)}, u32[]{:S(2)}, u32[]{:S(2)}) collective-permute-start(f32[32,128]{1,0:T(8,128)S(1)} %get-tuple-element.23), channel_id=1, source_target_pairs={{0,1},{1,0},{2,3},{3,2},{4,5},{5,4},{6,7},{7,6},{8,9},{9,8},{10,11... | collective-permute-start | bytes 49160 | tf_op jit(solution)/shard_map/ppermute | solution.py:368
  3.0 0.7 %collective-permute-start.1 = (f32[32,128]{1,0:T(8,128)S(1)}, f32[32,128]{1,0:T(8,128)S(1)}, u32[]{:S(2)}, u32[]{:S(2)}) collective-permute-start(f32[32,128]{1,0:T(8,128)S(1)} %get-tuple-element.24), channel_id=1, source_target_pairs={{1,2},{2,1},{3,4},{4,3},{5,6},{6,5},{7,8},{8,7},{9,10},{10,9},{11,... | collective-permute-start | bytes 49160 | tf_op jit(solution)/shard_map/ppermute | solution.py:367
  3.6 1.2 %collective-permute-done.pair_row = f32[32,128]{1,0:T(8,128)S(1)} collective-permute-done((f32[32,128]{1,0:T(8,128)S(1)}, f32[32,128]{1,0:T(8,128)S(1)}, u32[]{:S(2)}, u32[]{:S(2)}) %collective-permute-start) | collective-permute-done | bytes 16416 | tf_op jit(solution)/shard_map/ppermute | solution.py:368
  4.8 0.0 collective-permute-done.1.next_row
  4.8 0.1 collective-permute-start.2
  4.9 4.2 %collective-permute-start.3 = (f32[40,128]{1,0:T(8,128)S(1)}, f32[40,128]{1,0:T(8,128)S(1)}, u32[]{:S(2)}, u32[]{:S(2)}) collective-permute-start(f32[40,128]{1,0:T(8,128)S(1)} %get-tuple-element.26), channel_id=1, source_target_pairs={{32,64},{64,32},{96,128},{128,96},{160,192},{192,160},{33,65},{65,... | collective-permute-start | bytes 61448 | tf_op jit(solution)/shard_map/ppermute | solution.py:370
  9.1 0.0 collective-permute-done.2.near_face
  9.1 1.4 %collective-permute-done.3.far_face = f32[40,128]{1,0:T(8,128)S(1)} collective-permute-done((f32[40,128]{1,0:T(8,128)S(1)}, f32[40,128]{1,0:T(8,128)S(1)}, u32[]{:S(2)}, u32[]{:S(2)}) %collective-permute-start.3) | collective-permute-done | bytes 20512 | tf_op jit(solution)/shard_map/ppermute | solution.py:370
  10.6 0.3 shard_map.19.smooth
  10.9 1.0 %shard_map.20 = (f32[256,128]{1,0:T(8,128)}, f32[16,32,128]{2,1,0:T(8,128)S(1)}, f32[16,32,128]{2,1,0:T(8,128)S(1)}, f32[16,32,128]{2,1,0:T(8,128)S(1)}) custom-call(f32[512,128]{1,0:T(8,128)S(1)} %bitcast.7, f32[528,128]{1,0:T(8,128)S(1)} %shard_map.19.smooth), custom_call_target="tpu_custom_call" | custom-call | flops 1000000 | bytes 500000 | tf_op jit(solution)/shard_map/pallas_call | solution.py:381
  11.9 0.0 copy-start.1
  11.9 15.0 %all-to-all-start = ((f32[32,8,128]{2,1,0:T(8,128)}), f32[32,8,128]{2,1,0:T(8,128)S(1)}, u32[]{:S(2)}, u32[]{:S(2)}) async-start(f32[32,8,128]{2,1,0:T(8,128)} %bitcast.1), calls=%async_computation | async-start | bytes 262144 | tf_op jit(solution)/shard_map/all_to_all | solution.py:384
  26.9 0.0 copy-done.1
  26.9 0.2 shard_map.21
  27.1 0.3 collective-permute-start.4
  27.4 1.0 %collective-permute-done.4.refs_1_.near = f32[5,16,128]{2,1,0:T(8,128)S(1)} collective-permute-done((f32[5,16,128]{2,1,0:T(8,128)S(1)}, f32[5,16,128]{2,1,0:T(8,128)S(1)}, u32[]{:S(2)}, u32[]{:S(2)}) %collective-permute-start.4) | collective-permute-done | bytes 40992 | tf_op jit(solution)/shard_map/ppermute | solution.py:388
  28.4 0.4 collective-permute-start.5
  28.8 0.7 %shard_map.24.solved_x = f32[512,128]{1,0:T(8,128)S(1)} custom-call(f32[512,128]{1,0:T(8,128)S(1)} %bitcast.9, f32[528,128]{1,0:T(8,128)S(1)} %shard_map.19.smooth), custom_call_target="tpu_custom_call" | custom-call | flops 1000000 | bytes 500000 | tf_op jit(solution)/shard_map/pallas_call | solution.py:389
  29.5 3.0 %collective-permute-done.5.refs_1_.pair = f32[5,16,128]{2,1,0:T(8,128)S(1)} collective-permute-done((f32[5,16,128]{2,1,0:T(8,128)S(1)}, f32[5,16,128]{2,1,0:T(8,128)S(1)}, u32[]{:S(2)}, u32[]{:S(2)}) %collective-permute-start.5) | collective-permute-done | bytes 40992 | tf_op jit(solution)/shard_map/ppermute | solution.py:401
  32.5 5.3 %all-to-all-done = f32[32,8,128]{2,1,0:T(8,128)S(1)} async-done(((f32[32,8,128]{2,1,0:T(8,128)}), f32[32,8,128]{2,1,0:T(8,128)S(1)}, u32[]{:S(2)}, u32[]{:S(2)}) %all-to-all-start) | async-done | bytes 131104 | tf_op jit(solution)/shard_map/all_to_all | solution.py:384
  37.8 0.8 %shard_map.25 = f32[32,2,128]{2,1,0:T(2,128)} custom-call(f32[256,128]{1,0:T(8,128)S(1)} %bitcast.10), custom_call_target="tpu_custom_call" | custom-call | flops 1000000 | bytes 500000 | tf_op jit(solution)/shard_map/pallas_call | solution.py:404
  38.6 4.5 %all-to-all-start.1 = ((f32[32,2,128]{2,1,0:T(2,128)}), f32[32,2,128]{2,1,0:T(2,128)S(1)}, u32[]{:S(2)}, u32[]{:S(2)}) async-start(f32[32,2,128]{2,1,0:T(2,128)} %shard_map.25), calls=%async_computation.1 | async-start | bytes 65536 | tf_op jit(solution)/shard_map/all_to_all | solution.py:410
  43.1 2.4 %collective-permute-start.6 = (f32[5,16,128]{2,1,0:T(8,128)S(1)}, f32[5,16,128]{2,1,0:T(8,128)S(1)}, u32[]{:S(2)}, u32[]{:S(2)}) collective-permute-start(f32[5,16,128]{2,1,0:T(8,128)S(1)} %shard_map.23), channel_id=1, source_target_pairs={{0,128},{32,160},{64,192},{96,224},{128,0},{160,32},{192,64},{224,... | collective-permute-start | bytes 122888 | tf_op jit(solution)/shard_map/ppermute | solution.py:406
  45.5 3.2 %collective-permute-done.6.quad = f32[5,16,128]{2,1,0:T(8,128)S(1)} collective-permute-done((f32[5,16,128]{2,1,0:T(8,128)S(1)}, f32[5,16,128]{2,1,0:T(8,128)S(1)}, u32[]{:S(2)}, u32[]{:S(2)}) %collective-permute-start.6) | collective-permute-done | bytes 40992 | tf_op jit(solution)/shard_map/ppermute | solution.py:406
  48.7 0.1 shard_map.26.others
  48.8 4.2 %all-to-all-done.1.ends = f32[32,2,128]{2,1,0:T(2,128)S(1)} async-done(((f32[32,2,128]{2,1,0:T(2,128)}), f32[32,2,128]{2,1,0:T(2,128)S(1)}, u32[]{:S(2)}, u32[]{:S(2)}) %all-to-all-start.1) | async-done | bytes 32800 | tf_op jit(solution)/shard_map/all_to_all | solution.py:410
  53.0 0.9 %shard_map.27 = f32[512,128]{1,0:T(8,128)} custom-call(f32[32,2,128]{2,1,0:T(2,128)S(1)} %all-to-all-done.1.ends, f32[16,32,128]{2,1,0:T(8,128)S(1)} %get-tuple-element.32.factor, f32[16,32,128]{2,1,0:T(8,128)S(1)} %get-tuple-element.33.back, f32[16,32,128]{2,1,0:T(8,128)S(1)} %get-tuple-element.34.rest, f32[512,128]{1,0:T(8,128)S(1)} %shard_map.26.others), custom_call_target="tpu_custom_call" | custom-call | flops 1000000 | bytes 500000 | tf_op jit(solution)/shard_map/pallas_call | solution.py:411
  (4 shorter events, 0.1 us)
Async XLA Ops:
  0.0 0.9 %copy-start = (f32[32,16,128]{2,1,0:T(8,128)S(1)}, f32[32,16,128]{2,1,0:T(8,128)}, u32[]{:S(2)}) copy-start(f32[32,16,128]{2,1,0:T(8,128)} %param.1) | copy-start | bytes 786436
  1.0 3.8 %collective-permute-start = (f32[32,128]{1,0:T(8,128)S(1)}, f32[32,128]{1,0:T(8,128)S(1)}, u32[]{:S(2)}, u32[]{:S(2)}) collective-permute-start(f32[32,128]{1,0:T(8,128)S(1)} %get-tuple-element.23), channel_id=1, source_target_pairs={{0,1},{1,0},{2,3},{3,2},{4,5},{5,4},{6,7},{7,6},{8,9},{9,8},{10,11... | collective-permute-start | bytes 49160 | tf_op jit(solution)/shard_map/ppermute | solution.py:368
  3.0 1.8 %collective-permute-start.1 = (f32[32,128]{1,0:T(8,128)S(1)}, f32[32,128]{1,0:T(8,128)S(1)}, u32[]{:S(2)}, u32[]{:S(2)}) collective-permute-start(f32[32,128]{1,0:T(8,128)S(1)} %get-tuple-element.24), channel_id=1, source_target_pairs={{1,2},{2,1},{3,4},{4,3},{5,6},{6,5},{7,8},{8,7},{9,10},{10,9},{11,... | collective-permute-start | bytes 49160 | tf_op jit(solution)/shard_map/ppermute | solution.py:367
  4.8 4.3 %collective-permute-start.2 = (f32[40,128]{1,0:T(8,128)S(1)}, f32[40,128]{1,0:T(8,128)S(1)}, u32[]{:S(2)}, u32[]{:S(2)}) collective-permute-start(f32[40,128]{1,0:T(8,128)S(1)} %get-tuple-element.25), channel_id=1, source_target_pairs={{0,32},{32,0},{64,96},{96,64},{128,160},{160,128},{192,224},{224,1... | collective-permute-start | bytes 61448 | tf_op jit(solution)/shard_map/ppermute | solution.py:371
  4.9 5.7 %collective-permute-start.3 = (f32[40,128]{1,0:T(8,128)S(1)}, f32[40,128]{1,0:T(8,128)S(1)}, u32[]{:S(2)}, u32[]{:S(2)}) collective-permute-start(f32[40,128]{1,0:T(8,128)S(1)} %get-tuple-element.26), channel_id=1, source_target_pairs={{32,64},{64,32},{96,128},{128,96},{160,192},{192,160},{33,65},{65,... | collective-permute-start | bytes 61448 | tf_op jit(solution)/shard_map/ppermute | solution.py:370
  11.9 15.0 %copy-start.1 = (f32[32,16,128]{2,1,0:T(8,128)S(1)}, f32[32,16,128]{2,1,0:T(8,128)}, u32[]{:S(2)}) copy-start(f32[32,16,128]{2,1,0:T(8,128)} %param.1) | copy-start | bytes 786436
  11.9 25.9 %all-to-all-start = ((f32[32,8,128]{2,1,0:T(8,128)}), f32[32,8,128]{2,1,0:T(8,128)S(1)}, u32[]{:S(2)}, u32[]{:S(2)}) async-start(f32[32,8,128]{2,1,0:T(8,128)} %bitcast.1), calls=%async_computation | async-start | bytes 262144 | tf_op jit(solution)/shard_map/all_to_all | solution.py:384
  27.1 1.3 %collective-permute-start.4 = (f32[5,16,128]{2,1,0:T(8,128)S(1)}, f32[5,16,128]{2,1,0:T(8,128)S(1)}, u32[]{:S(2)}, u32[]{:S(2)}) collective-permute-start(f32[5,16,128]{2,1,0:T(8,128)S(1)} %get-tuple-element.28.refs_0_.own), channel_id=1, source_target_pairs={{0,32},{32,0},{64,96},{96,64},{128,160},{160,128},{192,224},{224,1... | collective-permute-start | bytes 122888 | tf_op jit(solution)/shard_map/ppermute | solution.py:388
  28.4 4.1 %collective-permute-start.5 = (f32[5,16,128]{2,1,0:T(8,128)S(1)}, f32[5,16,128]{2,1,0:T(8,128)S(1)}, u32[]{:S(2)}, u32[]{:S(2)}) collective-permute-start(f32[5,16,128]{2,1,0:T(8,128)S(1)} %shard_map.22.refs_0_), channel_id=1, source_target_pairs={{0,64},{32,96},{64,0},{96,32},{128,192},{160,224},{192,128},{224,1... | collective-permute-start | bytes 122888 | tf_op jit(solution)/shard_map/ppermute | solution.py:401
  38.6 14.5 %all-to-all-start.1 = ((f32[32,2,128]{2,1,0:T(2,128)}), f32[32,2,128]{2,1,0:T(2,128)S(1)}, u32[]{:S(2)}, u32[]{:S(2)}) async-start(f32[32,2,128]{2,1,0:T(2,128)} %shard_map.25), calls=%async_computation.1 | async-start | bytes 65536 | tf_op jit(solution)/shard_map/all_to_all | solution.py:410
  43.1 5.6 %collective-permute-start.6 = (f32[5,16,128]{2,1,0:T(8,128)S(1)}, f32[5,16,128]{2,1,0:T(8,128)S(1)}, u32[]{:S(2)}, u32[]{:S(2)}) collective-permute-start(f32[5,16,128]{2,1,0:T(8,128)S(1)} %shard_map.23), channel_id=1, source_target_pairs={{0,128},{32,160},{64,192},{96,224},{128,0},{160,32},{192,64},{224,... | collective-permute-start | bytes 122888 | tf_op jit(solution)/shard_map/ppermute | solution.py:406

commit v9 on v6

--- a/solution.py
+++ b/solution.py
@@ -63,19 +63,12 @@
     ), (to_left, to_right, source * inverse)
 
 
-def edge_kernel(vol, near_side, far_side, sems):
+def edge_kernel(parity, vol, out, sem):
     odd = lax.axis_index("depth") & 1
-    high = (PLANES - 2) * ROWS
-    near_start = pl.multiple_of((1 - odd) * high, ROWS)
-    far_start = pl.multiple_of(odd * high, ROWS)
-    copies = (
-        pltpu.make_async_copy(vol.at[pl.ds(near_start, 2 * ROWS), :], near_side, sems.at[0]),
-        pltpu.make_async_copy(vol.at[pl.ds(far_start, 2 * ROWS), :], far_side, sems.at[1]),
-    )
-    for copy in copies:
-        copy.start()
-    for copy in copies:
-        copy.wait()
+    start = pl.multiple_of((odd ^ parity) * ((PLANES - 2) * ROWS), ROWS)
+    copy = pltpu.make_async_copy(vol.at[pl.ds(start, 2 * ROWS), :], out, sem)
+    copy.start()
+    copy.wait()
 
 
 def strided(ref, row):
@@ -375,12 +368,16 @@
     tall = shaped((PLANES + 1) * ROWS, COLS)
     port = shaped(5, ROWS, COLS)
     side = shaped(PLANES + 1, COLS)
-    to_near, to_far = call(
-        edge_kernel,
-        (shaped(2 * ROWS, COLS), shaped(2 * ROWS, COLS)),
-        (pltpu.SemaphoreType.DMA((2,)),),
-        in_specs=[pl.BlockSpec(memory_space=pl.ANY)],
-    )(flat)
+    to_far, to_near = (
+        call(
+            lambda *refs, parity=parity: edge_kernel(parity, *refs),
+            shaped(2 * ROWS, COLS),
+            (pltpu.SemaphoreType.DMA,),
+            in_specs=[pl.BlockSpec(memory_space=pl.ANY)],
+            flops=flops,
+        )(flat)
+        for parity, flops in ((0, 1), (1, LONG))
+    )
     far_side = lax.ppermute(to_far, "depth", next_perm("depth"))
     near_side = lax.ppermute(to_near, "depth", swap_perm("depth", 1))
     deep, to_pair, to_next = call(
@@ -393,7 +390,7 @@
     )
     ports = lax.all_to_all(y_port, "lat", 0, 0, tiled=True)
     z_port, z_factor, z_back, z_rest, z_mid, smooth = call(
-        plane_kernel, (port, whole, whole, whole, shaped(3, ROWS, COLS), tall), moved=500000,flops=LONG
+        plane_kernel, (port, whole, whole, whole, shaped(3, ROWS, COLS), tall), flops=LONG
     )(flat, deep, pair_row, next_row)
     near = lax.ppermute(z_port, "depth", swap_perm("depth", 1))
     solved_x = call(
@@ -410,11 +407,10 @@
     pair_own = call(lambda *refs: join_kernel(1, *refs), port)(z_port, near)
     pair = lax.ppermute(pair_own, "depth", swap_perm("depth", 2))
     quad_own = call(lambda *refs: join_kernel(2, *refs), port)(pair_own, pair)
-    ports, quad_own, solved_x = lax.optimization_barrier((ports, quad_own, solved_x))
+    quad = lax.ppermute(quad_own, "depth", swap_perm("depth", 4))
+    ports, solved_x = lax.optimization_barrier((ports, solved_x))
     ends = call(row_reduced_kernel, shaped(BLOCKS, 4, COLS))(ports)
-    ends, quad_own = lax.optimization_barrier((ends, quad_own))
-    quad = lax.ppermute(quad_own, "depth", swap_perm("depth", 4))
-    others = call(finish_plane_kernel, whole)(
+    others = call(finish_plane_kernel, whole, flops=LONG)(
         z_port, near, pair, quad, z_factor, z_back, z_rest, z_mid, solved_x
     )
     ends_y = lax.all_to_all(ends, "lat", 0, 0, tiled=True)

time: 51.6 us -> 53.3 us (1.033)
  starting transfers between devices: 24.4 us -> 27.5 us
  waiting for transfers between devices: 21.5 us -> 20.2 us
    all_to_all x1, waiting for transfers between devices: 4.33 us -> 9.93 us  [shards(): ends_y = lax.all_to_all(ends, 'lat', 0, 0, tiled=True)]
    ppermute x1, waiting for transfers between devices: 4.56 us -> 0.01 us  [shards(): quad = lax.ppermute(quad_own, 'depth', swap_perm('depth', 4))]
    all_to_all x1, waiting for transfers between devices: 6.7 us -> 3.63 us  [shards(): ports = lax.all_to_all(y_port, 'lat', 0, 0, tiled=True)]
    all_to_all x1, starting transfers between devices: 4.44 us -> 6.16 us  [shards(): ends_y = lax.all_to_all(ends, 'lat', 0, 0, tiled=True)]
    ppermute x1, starting transfers between devices: 1.04 us -> 2.38 us  [shards(): quad = lax.ppermute(quad_own, 'depth', swap_perm('depth', 4))]
    ppermute x1, waiting for transfers between devices: 3.3 us -> 3.99 us  [shards(): pair = lax.ppermute(pair_own, 'depth', swap_perm('depth', 2))]
  transfers between devices with their start and end apart: 9 -> 9, of which waited for: 6 -> 5; matrix products, arithmetic and copies ran while one was open for 0% -> 0% of each run, Pallas kernels for 4% -> 6%
where the time goes in v9:
time: 53.3 us; the launch traced here: 53 us
  starting transfers between devices  27.5 us (52%)
  waiting for transfers between devices  20.2 us (38%)
  Pallas kernels  4.26 us (8%)
  local copies, waits for them, and re-layouts  0.95 us (2%)
    all_to_all x1, starting transfers between devices, shards(): ports = lax.all_to_all(y_port, 'lat', 0, 0, tiled=True)  12.4 us
    all_to_all x1, waiting for transfers between devices, shards(): ends_y = lax.all_to_all(ends, 'lat', 0, 0, tiled=True)  9.93 us
    all_to_all x1, starting transfers between devices, shards(): ends_y = lax.all_to_all(ends, 'lat', 0, 0, tiled=True)  6.16 us
    ppermute x1, starting transfers between devices, shards(): far_side = lax.ppermute(to_far, 'depth', next_perm('depth'))  4.17 us
    ppermute x1, waiting for transfers between devices, shards(): pair = lax.ppermute(pair_own, 'depth', swap_perm('depth', 2))  3.99 us
    all_to_all x1, waiting for transfers between devices, shards(): ports = lax.all_to_all(y_port, 'lat', 0, 0, tiled=True)  3.63 us
    ppermute x1, starting transfers between devices, shards(): quad = lax.ppermute(quad_own, 'depth', swap_perm('depth', 4))  2.38 us
    ppermute x1, starting transfers between devices, shards(): pair_row = lax.ppermute(to_pair, 'lat', swap_perm('lat', 1))  1.47 us
  transfers between devices with their start and end apart: 9, of which 5 were waited for; matrix products, arithmetic and copies ran while one was open for 0% of the time, Pallas kernels for 6%

profile of v9, /device:TPU:8, one launch (start us, length us, event | category | flops | bytes accessed | tf_op | source)
XLA Modules:
  0.0 53.0 jit_solution(2890573135790226831)
XLA Ops:
  0.0 0.0 copy-start
  0.0 0.9 %copy-done = f32[32,16,128]{2,1,0:T(8,128)S(1)} copy-done((f32[32,16,128]{2,1,0:T(8,128)S(1)}, f32[32,16,128]{2,1,0:T(8,128)}, u32[]{:S(2)}) %copy-start) | copy-done | bytes 262168
  1.0 0.1 collective-permute-start
  1.1 4.2 %collective-permute-start.1 = (f32[32,128]{1,0:T(8,128)S(1)}, f32[32,128]{1,0:T(8,128)S(1)}, u32[]{:S(2)}, u32[]{:S(2)}) collective-permute-start(f32[32,128]{1,0:T(8,128)S(1)} %shard_map.18), channel_id=1, source_target_pairs={{32,64},{64,32},{96,128},{128,96},{160,192},{192,160},{33,65},{65,... | collective-permute-start | bytes 49160 | tf_op jit(solution)/shard_map/ppermute | solution.py:381
  5.3 0.0 collective-permute-done.near_side
  5.3 1.4 %collective-permute-done.1.far_side = f32[32,128]{1,0:T(8,128)S(1)} collective-permute-done((f32[32,128]{1,0:T(8,128)S(1)}, f32[32,128]{1,0:T(8,128)S(1)}, u32[]{:S(2)}, u32[]{:S(2)}) %collective-permute-start.1) | collective-permute-done | bytes 16416 | tf_op jit(solution)/shard_map/ppermute | solution.py:381
  6.7 0.2 shard_map.19
  7.0 1.5 %collective-permute-start.2 = (f32[33,128]{1,0:T(8,128)S(1)}, f32[33,128]{1,0:T(8,128)S(1)}, u32[]{:S(2)}, u32[]{:S(2)}) collective-permute-start(f32[33,128]{1,0:T(8,128)S(1)} %get-tuple-element.22), channel_id=1, source_target_pairs={{0,1},{1,0},{2,3},{3,2},{4,5},{5,4},{6,7},{7,6},{8,9},{9,8},{10,11... | collective-permute-start | bytes 50696 | tf_op jit(solution)/shard_map/ppermute | solution.py:387
  8.4 0.7 %collective-permute-start.3 = (f32[33,128]{1,0:T(8,128)S(1)}, f32[33,128]{1,0:T(8,128)S(1)}, u32[]{:S(2)}, u32[]{:S(2)}) collective-permute-start(f32[33,128]{1,0:T(8,128)S(1)} %get-tuple-element.23), channel_id=1, source_target_pairs={{1,2},{2,1},{3,4},{4,3},{5,6},{6,5},{7,8},{8,7},{9,10},{10,9},{11,... | collective-permute-start | bytes 50696 | tf_op jit(solution)/shard_map/ppermute | solution.py:386
  9.1 1.1 %shard_map.20 = (f32[512,128]{1,0:T(8,128)}, f32[16,32,128]{2,1,0:T(8,128)S(1)}, f32[16,32,128]{2,1,0:T(8,128)S(1)}, f32[16,32,128]{2,1,0:T(8,128)S(1)}) custom-call(f32[512,128]{1,0:T(8,128)S(1)} %bitcast.7, f32[528,128]{1,0:T(8,128)S(1)} %get-tuple-element.20.deep), custom_call_target="tpu_custom_call" | custom-call | flops 1000000 | bytes 500000 | tf_op jit(solution)/shard_map/pallas_call | solution.py:388
  10.2 0.0 copy-start.1
  10.2 12.4 %all-to-all-start = ((f32[32,16,128]{2,1,0:T(8,128)}), f32[32,16,128]{2,1,0:T(8,128)S(1)}, u32[]{:S(2)}, u32[]{:S(2)}) async-start(f32[32,16,128]{2,1,0:T(8,128)} %bitcast.1), calls=%async_computation | async-start | bytes 524288 | tf_op jit(solution)/shard_map/all_to_all | solution.py:391
  22.5 0.0 collective-permute-done.2.pair_row
  22.5 0.0 collective-permute-done.3.next_row
  22.6 0.0 copy-done.1
  22.6 0.3 shard_map.21
  22.9 0.1 collective-permute-start.4
  23.0 1.2 %collective-permute-done.4.refs_1_.near = f32[5,16,128]{2,1,0:T(8,128)S(1)} collective-permute-done((f32[5,16,128]{2,1,0:T(8,128)S(1)}, f32[5,16,128]{2,1,0:T(8,128)S(1)}, u32[]{:S(2)}, u32[]{:S(2)}) %collective-permute-start.4) | collective-permute-done | bytes 40992 | tf_op jit(solution)/shard_map/ppermute | solution.py:395
  24.2 0.1 collective-permute-start.5
  24.3 4.0 %collective-permute-done.5.refs_1_.pair = f32[5,16,128]{2,1,0:T(8,128)S(1)} collective-permute-done((f32[5,16,128]{2,1,0:T(8,128)S(1)}, f32[5,16,128]{2,1,0:T(8,128)S(1)}, u32[]{:S(2)}, u32[]{:S(2)}) %collective-permute-start.5) | collective-permute-done | bytes 40992 | tf_op jit(solution)/shard_map/ppermute | solution.py:408
  28.3 2.4 %collective-permute-start.6 = (f32[5,16,128]{2,1,0:T(8,128)S(1)}, f32[5,16,128]{2,1,0:T(8,128)S(1)}, u32[]{:S(2)}, u32[]{:S(2)}) collective-permute-start(f32[5,16,128]{2,1,0:T(8,128)S(1)} %shard_map.25), channel_id=1, source_target_pairs={{0,128},{32,160},{64,192},{96,224},{128,0},{160,32},{192,64},{224,... | collective-permute-start | bytes 122888 | tf_op jit(solution)/shard_map/ppermute | solution.py:410
  30.7 0.7 %shard_map.22.solved_x = f32[512,128]{1,0:T(8,128)S(1)} custom-call(f32[512,128]{1,0:T(8,128)S(1)} %bitcast.9, f32[528,128]{1,0:T(8,128)S(1)} %get-tuple-element.24.smooth), custom_call_target="tpu_custom_call" | custom-call | flops 1000000 | bytes 500000 | tf_op jit(solution)/shard_map/pallas_call | solution.py:396
  31.4 3.6 %all-to-all-done = f32[32,16,128]{2,1,0:T(8,128)S(1)} async-done(((f32[32,16,128]{2,1,0:T(8,128)}), f32[32,16,128]{2,1,0:T(8,128)S(1)}, u32[]{:S(2)}, u32[]{:S(2)}) %all-to-all-start) | async-done | bytes 262176 | tf_op jit(solution)/shard_map/all_to_all | solution.py:391
  35.0 0.8 %shard_map.23 = f32[32,4,128]{2,1,0:T(4,128)} custom-call(f32[512,128]{1,0:T(8,128)S(1)} %bitcast.10), custom_call_target="tpu_custom_call" | custom-call | flops 1000000 | bytes 500000 | tf_op jit(solution)/shard_map/pallas_call | solution.py:412
  35.9 6.2 %all-to-all-start.1 = ((f32[32,4,128]{2,1,0:T(4,128)}), f32[32,4,128]{2,1,0:T(4,128)S(1)}, u32[]{:S(2)}, u32[]{:S(2)}) async-start(f32[32,4,128]{2,1,0:T(4,128)} %shard_map.23), calls=%async_computation.1 | async-start | bytes 131072 | tf_op jit(solution)/shard_map/all_to_all | solution.py:416
  42.1 0.0 collective-permute-done.6.quad
  42.1 0.1 shard_map.26.others
  42.2 9.9 %all-to-all-done.1.ends = f32[32,4,128]{2,1,0:T(4,128)S(1)} async-done(((f32[32,4,128]{2,1,0:T(4,128)}), f32[32,4,128]{2,1,0:T(4,128)S(1)}, u32[]{:S(2)}, u32[]{:S(2)}) %all-to-all-start.1) | async-done | bytes 65568 | tf_op jit(solution)/shard_map/all_to_all | solution.py:416
  52.1 0.9 %shard_map.27 = f32[512,128]{1,0:T(8,128)} custom-call(f32[32,4,128]{2,1,0:T(4,128)S(1)} %all-to-all-done.1.ends, f32[16,32,128]{2,1,0:T(8,128)S(1)} %get-tuple-element.26.factor, f32[16,32,128]{2,1,0:T(8,128)S(1)} %get-tuple-element.27.back, f32[16,32,128]{2,1,0:T(8,128)S(1)} %get-tuple-element.28.rest, f32[512,128]{1,0:T(8,128)S(1)} %shard_map.26.others), custom_call_target="tpu_custom_call" | custom-call | flops 1000000 | bytes 500000 | tf_op jit(solution)/shard_map/pallas_call | solution.py:417
  (4 shorter events, 0.1 us)
Async XLA Ops:
  0.0 0.9 %copy-start = (f32[32,16,128]{2,1,0:T(8,128)S(1)}, f32[32,16,128]{2,1,0:T(8,128)}, u32[]{:S(2)}) copy-start(f32[32,16,128]{2,1,0:T(8,128)} %param.1) | copy-start | bytes 786436
  1.0 4.3 %collective-permute-start = (f32[32,128]{1,0:T(8,128)S(1)}, f32[32,128]{1,0:T(8,128)S(1)}, u32[]{:S(2)}, u32[]{:S(2)}) collective-permute-start(f32[32,128]{1,0:T(8,128)S(1)} %shard_map.17), channel_id=1, source_target_pairs={{0,32},{32,0},{64,96},{96,64},{128,160},{160,128},{192,224},{224,1... | collective-permute-start | bytes 49160 | tf_op jit(solution)/shard_map/ppermute | solution.py:382
  1.1 5.6 %collective-permute-start.1 = (f32[32,128]{1,0:T(8,128)S(1)}, f32[32,128]{1,0:T(8,128)S(1)}, u32[]{:S(2)}, u32[]{:S(2)}) collective-permute-start(f32[32,128]{1,0:T(8,128)S(1)} %shard_map.18), channel_id=1, source_target_pairs={{32,64},{64,32},{96,128},{128,96},{160,192},{192,160},{33,65},{65,... | collective-permute-start | bytes 49160 | tf_op jit(solution)/shard_map/ppermute | solution.py:381
  7.0 15.6 %collective-permute-start.2 = (f32[33,128]{1,0:T(8,128)S(1)}, f32[33,128]{1,0:T(8,128)S(1)}, u32[]{:S(2)}, u32[]{:S(2)}) collective-permute-start(f32[33,128]{1,0:T(8,128)S(1)} %get-tuple-element.22), channel_id=1, source_target_pairs={{0,1},{1,0},{2,3},{3,2},{4,5},{5,4},{6,7},{7,6},{8,9},{9,8},{10,11... | collective-permute-start | bytes 50696 | tf_op jit(solution)/shard_map/ppermute | solution.py:387
  8.4 14.1 %collective-permute-start.3 = (f32[33,128]{1,0:T(8,128)S(1)}, f32[33,128]{1,0:T(8,128)S(1)}, u32[]{:S(2)}, u32[]{:S(2)}) collective-permute-start(f32[33,128]{1,0:T(8,128)S(1)} %get-tuple-element.23), channel_id=1, source_target_pairs={{1,2},{2,1},{3,4},{4,3},{5,6},{6,5},{7,8},{8,7},{9,10},{10,9},{11,... | collective-permute-start | bytes 50696 | tf_op jit(solution)/shard_map/ppermute | solution.py:386
  10.2 12.4 %copy-start.1 = (f32[32,16,128]{2,1,0:T(8,128)S(1)}, f32[32,16,128]{2,1,0:T(8,128)}, u32[]{:S(2)}) copy-start(f32[32,16,128]{2,1,0:T(8,128)} %param.1) | copy-start | bytes 786436
  10.2 24.9 %all-to-all-start = ((f32[32,16,128]{2,1,0:T(8,128)}), f32[32,16,128]{2,1,0:T(8,128)S(1)}, u32[]{:S(2)}, u32[]{:S(2)}) async-start(f32[32,16,128]{2,1,0:T(8,128)} %bitcast.1), calls=%async_computation | async-start | bytes 524288 | tf_op jit(solution)/shard_map/all_to_all | solution.py:391
  22.9 1.3 %collective-permute-start.4 = (f32[5,16,128]{2,1,0:T(8,128)S(1)}, f32[5,16,128]{2,1,0:T(8,128)S(1)}, u32[]{:S(2)}, u32[]{:S(2)}) collective-permute-start(f32[5,16,128]{2,1,0:T(8,128)S(1)} %get-tuple-element.29.refs_0_.own), channel_id=1, source_target_pairs={{0,32},{32,0},{64,96},{96,64},{128,160},{160,128},{192,224},{224,1... | collective-permute-start | bytes 122888 | tf_op jit(solution)/shard_map/ppermute | solution.py:395
  24.2 4.1 %collective-permute-start.5 = (f32[5,16,128]{2,1,0:T(8,128)S(1)}, f32[5,16,128]{2,1,0:T(8,128)S(1)}, u32[]{:S(2)}, u32[]{:S(2)}) collective-permute-start(f32[5,16,128]{2,1,0:T(8,128)S(1)} %shard_map.24.refs_0_), channel_id=1, source_target_pairs={{0,64},{32,96},{64,0},{96,32},{128,192},{160,224},{192,128},{224,1... | collective-permute-start | bytes 122888 | tf_op jit(solution)/shard_map/ppermute | solution.py:408
  28.3 13.7 %collective-permute-start.6 = (f32[5,16,128]{2,1,0:T(8,128)S(1)}, f32[5,16,128]{2,1,0:T(8,128)S(1)}, u32[]{:S(2)}, u32[]{:S(2)}) collective-permute-start(f32[5,16,128]{2,1,0:T(8,128)S(1)} %shard_map.25), channel_id=1, source_target_pairs={{0,128},{32,160},{64,192},{96,224},{128,0},{160,32},{192,64},{224,... | collective-permute-start | bytes 122888 | tf_op jit(solution)/shard_map/ppermute | solution.py:410
  35.9 16.2 %all-to-all-start.1 = ((f32[32,4,128]{2,1,0:T(4,128)}), f32[32,4,128]{2,1,0:T(4,128)S(1)}, u32[]{:S(2)}, u32[]{:S(2)}) async-start(f32[32,4,128]{2,1,0:T(4,128)} %shard_map.23), calls=%async_computation.1 | async-start | bytes 131072 | tf_op jit(solution)/shard_map/all_to_all | solution.py:416

commit v10 on v6

--- a/solution.py
+++ b/solution.py
@@ -12,7 +12,7 @@
 COLS = 128
 BLOCKS = 32
 PORT = 16
-LONG = 100_000_000_000
+CORNER = 8
 F32 = jnp.float32
 
 
@@ -78,6 +78,28 @@
         copy.wait()
 
 
+def side_kernel(vol, pair_row, next_row):
+    odd = (lax.axis_index("lat") & 1) == 1
+    low = vol[pl.ds(0, PLANES, stride=ROWS), :]
+    high = vol[pl.ds(ROWS - 1, PLANES, stride=ROWS), :]
+    pair_row[...] = jnp.where(odd, low, high)
+    next_row[...] = jnp.where(odd, high, low)
+
+
+def side_rows(pair_row, next_row):
+    odd = (lax.axis_index("lat") & 1) == 1
+    return jnp.where(odd, pair_row, next_row), jnp.where(odd, next_row, pair_row)
+
+
+def corner_kernel(pair_row, next_row, near_corner, far_corner):
+    odd = (lax.axis_index("depth") & 1) == 1
+    for place, side in zip((0, 2), side_rows(pair_row[...], next_row[...])):
+        near_corner[place : place + 2, :] = jnp.where(odd, side[0:2, :], side[PLANES - 2 :, :])
+        far_corner[place : place + 2, :] = jnp.where(odd, side[PLANES - 2 :, :], side[0:2, :])
+    near_corner[4:CORNER, :] = jnp.zeros((CORNER - 4, COLS), F32)
+    far_corner[4:CORNER, :] = jnp.zeros((CORNER - 4, COLS), F32)
+
+
 def strided(ref, row):
     return ref[pl.ds(row, 32, stride=16), :]
 
@@ -86,7 +108,7 @@
     return ref[plane * ROWS : (plane + 1) * ROWS, :]
 
 
-def deep_kernel(vol, near_side, far_side, deep, pair_row, next_row, mixed):
+def deep_kernel(vol, near_side, far_side, deep, mixed):
     odd = (lax.axis_index("depth") & 1) == 1
     lane = lax.broadcasted_iota(jnp.int32, (ROWS, COLS), 1)
     first, last = lane == 0, lane == COLS - 1
@@ -101,26 +123,35 @@
         deep[plane * ROWS : (plane + 1) * ROWS, :] = 0.25 * (
             mixed[plane] + 2.0 * mixed[plane + 1] + mixed[plane + 2]
         )
-    odd_row = (lax.axis_index("lat") & 1) == 1
-    low = deep[pl.ds(0, PLANES + 1, stride=ROWS), :]
-    high = deep[pl.ds(ROWS - 1, PLANES + 1, stride=ROWS), :]
-    pair_row[...] = jnp.where(odd_row, low, high)
-    next_row[...] = jnp.where(odd_row, high, low)
-
-
-def plane_kernel(vol, deep, pair_row, next_row, port, factor, back, rest, mid, smooth):
-    odd_row = (lax.axis_index("lat") & 1) == 1
-    low_row = jnp.where(odd_row, pair_row[...], next_row[...])
-    high_row = jnp.where(odd_row, next_row[...], pair_row[...])
+
+
+def plane_kernel(
+    vol, deep, pair_row, next_row, near_corner, far_corner,
+    port, factor, back, rest, mid, smooth,
+    low_side, high_side,
+):
+    odd = (lax.axis_index("depth") & 1) == 1
     depth_last = lax.axis_index("depth") == lax.axis_size("depth") - 1
     z_open = jnp.where(depth_last, 0.0, TAU3).astype(F32)
+    near, far = near_corner[...], far_corner[...]
+    below_corner, above_corner = jnp.where(odd, near, far), jnp.where(odd, far, near)
+    side_lane = lax.broadcasted_iota(jnp.int32, (PLANES + 3, COLS), 1)
+    sides = []
+    for place, ref, own in zip((0, 2), (low_side, high_side), side_rows(pair_row[...], next_row[...])):
+        ref[0:1, :] = below_corner[place + 1 : place + 2, :]
+        ref[1 : PLANES + 1, :] = own
+        ref[PLANES + 1 : PLANES + 3, :] = above_corner[place : place + 2, :]
+        ref[0 : PLANES + 3, :] = smooth_lanes(ref[0 : PLANES + 3, :], side_lane == 0, side_lane == COLS - 1)
+        sides.append(
+            0.25 * (ref[0 : PLANES + 1, :] + 2.0 * ref[1 : PLANES + 2, :] + ref[2 : PLANES + 3, :])
+        )
     row_index = lax.broadcasted_iota(jnp.int32, (ROWS, COLS), 0)
     top, bottom = row_index == 0, row_index == ROWS - 1
     for plane in range(PLANES + 1):
         span = slice(plane * ROWS, (plane + 1) * ROWS)
         here = deep[span, :]
-        above = jnp.where(top, low_row[plane : plane + 1, :], pltpu.roll(here, 1, 0))
-        below = jnp.where(bottom, high_row[plane : plane + 1, :], pltpu.roll(here, ROWS - 1, 0))
+        above = jnp.where(top, sides[0][plane : plane + 1, :], pltpu.roll(here, 1, 0))
+        below = jnp.where(bottom, sides[1][plane : plane + 1, :], pltpu.roll(here, ROWS - 1, 0))
         smooth[span, :] = 0.25 * (above + 2.0 * here + below)
 
     def resist(plane):
@@ -374,27 +405,32 @@
     whole = shaped(PLANES * ROWS, COLS)
     tall = shaped((PLANES + 1) * ROWS, COLS)
     port = shaped(5, ROWS, COLS)
-    side = shaped(PLANES + 1, COLS)
     to_near, to_far = call(
         edge_kernel,
         (shaped(2 * ROWS, COLS), shaped(2 * ROWS, COLS)),
         (pltpu.SemaphoreType.DMA((2,)),),
         in_specs=[pl.BlockSpec(memory_space=pl.ANY)],
     )(flat)
+    to_pair, to_next = call(side_kernel, (shaped(PLANES, COLS), shaped(PLANES, COLS)))(flat)
+    next_row = lax.ppermute(to_next, "lat", next_perm("lat"))
+    pair_row = lax.ppermute(to_pair, "lat", swap_perm("lat", 1))
     far_side = lax.ppermute(to_far, "depth", next_perm("depth"))
     near_side = lax.ppermute(to_near, "depth", swap_perm("depth", 1))
-    deep, to_pair, to_next = call(
-        deep_kernel, (tall, side, side), (pltpu.VMEM((PLANES + 3, ROWS, COLS), F32),)
-    )(flat, near_side, far_side)
-    next_row = lax.ppermute(to_next, "lat", next_perm("lat"))
-    pair_row = lax.ppermute(to_pair, "lat", swap_perm("lat", 1))
+    next_row, pair_row, far_side, near_side = lax.optimization_barrier((next_row, pair_row, far_side, near_side))
+    deep = call(deep_kernel, tall, (pltpu.VMEM((PLANES + 3, ROWS, COLS), F32),))(flat, near_side, far_side)
     y_port, y_factor, y_back, y_rest = call(row_kernel, (shaped(PLANES * PORT, COLS), lines, lines, lines))(
         flat, deep
     )
     ports = lax.all_to_all(y_port, "lat", 0, 0, tiled=True)
+    corner = shaped(CORNER, COLS)
+    to_near, to_far = call(corner_kernel, (corner, corner))(pair_row, next_row)
+    far_corner = lax.ppermute(to_far, "depth", next_perm("depth"))
+    near_corner = lax.ppermute(to_near, "depth", swap_perm("depth", 1))
     z_port, z_factor, z_back, z_rest, z_mid, smooth = call(
-        plane_kernel, (port, whole, whole, whole, shaped(3, ROWS, COLS), tall), moved=500000,flops=LONG
-    )(flat, deep, pair_row, next_row)
+        plane_kernel,
+        (port, whole, whole, whole, shaped(3, ROWS, COLS), tall),
+        (pltpu.VMEM((40, COLS), F32), pltpu.VMEM((40, COLS), F32)),
+    )(flat, deep, pair_row, next_row, near_corner, far_corner)
     near = lax.ppermute(z_port, "depth", swap_perm("depth", 1))
     solved_x = call(
         column_kernel,

time: 51.6 us -> 57.5 us (1.11)
  starting transfers between devices: 24.4 us -> 34.8 us
  waiting for transfers between devices: 21.5 us -> 17 us
    all_to_all x1, waiting for transfers between devices: 6.7 us -> 0.08 us  [shards(): ports = lax.all_to_all(y_port, 'lat', 0, 0, tiled=True)]
    all_to_all x1, starting transfers between devices: 4.44 us -> 9.72 us  [shards(): ends_y = lax.all_to_all(ends, 'lat', 0, 0, tiled=True)]
    ppermute x1, starting transfers between devices: 1.45 us -> 5.17 us  [shards(): pair_row = lax.ppermute(to_pair, 'lat', swap_perm('lat', 1))]
    ppermute x0 -> x2, starting transfers between devices: none -> 2.54 us  [the longest x1 2.45 us: shards(): far_corner = lax.ppermute(to_far, 'depth', next_perm('depth'))]
    ppermute x0 -> x2, waiting for transfers between devices: none -> 2.46 us  [the longest x1 2.46 us: shards(): far_corner = lax.ppermute(to_far, 'depth', next_perm('depth'))]
    ppermute x1, starting transfers between devices: 4.18 us -> 1.92 us  [shards(): far_side = lax.ppermute(to_far, 'depth', next_perm('depth'))]
    ppermute x1, waiting for transfers between devices: 0.01 us -> 1.71 us  [shards(): pair_row = lax.ppermute(to_pair, 'lat', swap_perm('lat', 1))]
    ppermute x1, starting transfers between devices: 0.09 us -> 1.77 us  [shards(): near_side = lax.ppermute(to_near, 'depth', swap_perm('depth', 1))]
  transfers between devices with their start and end apart: 9 -> 11, of which waited for: 6 -> 7; matrix products, arithmetic and copies ran while one was open for 0% -> 0% of each run, Pallas kernels for 4% -> 2%
where the time goes in v10:
time: 57.5 us; the launch traced here: 57.2 us
  starting transfers between devices  34.8 us (61%)
  waiting for transfers between devices  17 us (30%)
  Pallas kernels  4.33 us (8%)
  local copies, waits for them, and re-layouts  0.95 us (2%)
    all_to_all x1, starting transfers between devices, shards(): ports = lax.all_to_all(y_port, 'lat', 0, 0, tiled=True)  10.7 us
    all_to_all x1, starting transfers between devices, shards(): ends_y = lax.all_to_all(ends, 'lat', 0, 0, tiled=True)  9.72 us
    ppermute x1, starting transfers between devices, shards(): pair_row = lax.ppermute(to_pair, 'lat', swap_perm('lat', 1))  5.17 us
    ppermute x1, waiting for transfers between devices, shards(): quad = lax.ppermute(quad_own, 'depth', swap_perm('depth', 4))  4.68 us
    all_to_all x1, waiting for transfers between devices, shards(): ends_y = lax.all_to_all(ends, 'lat', 0, 0, tiled=True)  4.3 us
    ppermute x1, waiting for transfers between devices, shards(): pair = lax.ppermute(pair_own, 'depth', swap_perm('depth', 2))  2.87 us
    ppermute x1, waiting for transfers between devices, shards(): far_corner = lax.ppermute(to_far, 'depth', next_perm('depth'))  2.46 us
    ppermute x1, starting transfers between devices, shards(): far_corner = lax.ppermute(to_far, 'depth', next_perm('depth'))  2.45 us
  transfers between devices with their start and end apart: 11, of which 7 were waited for; matrix products, arithmetic and copies ran while one was open for 0% of the time, Pallas kernels for 2%

profile of v10, /device:TPU:8, one launch (start us, length us, event | category | flops | bytes accessed | tf_op | source)
XLA Modules:
  0.0 57.2 jit_solution(7340532711978333654)
XLA Ops:
  0.0 0.0 copy-start
  0.0 0.9 %copy-done = f32[32,16,128]{2,1,0:T(8,128)S(1)} copy-done((f32[32,16,128]{2,1,0:T(8,128)S(1)}, f32[32,16,128]{2,1,0:T(8,128)}, u32[]{:S(2)}) %copy-start) | copy-done | bytes 262168
  1.0 1.9 %collective-permute-start.2 = (f32[32,128]{1,0:T(8,128)S(1)}, f32[32,128]{1,0:T(8,128)S(1)}, u32[]{:S(2)}, u32[]{:S(2)}) collective-permute-start(f32[32,128]{1,0:T(8,128)S(1)} %get-tuple-element.32), channel_id=1, source_target_pairs={{32,64},{64,32},{96,128},{128,96},{160,192},{192,160},{33,65},{65,... | collective-permute-start | bytes 49160 | tf_op jit(solution)/shard_map/ppermute | solution.py:417
  2.9 1.8 %collective-permute-start.3 = (f32[32,128]{1,0:T(8,128)S(1)}, f32[32,128]{1,0:T(8,128)S(1)}, u32[]{:S(2)}, u32[]{:S(2)}) collective-permute-start(f32[32,128]{1,0:T(8,128)S(1)} %get-tuple-element.33), channel_id=1, source_target_pairs={{0,32},{32,0},{64,96},{96,64},{128,160},{160,128},{192,224},{224,1... | collective-permute-start | bytes 49160 | tf_op jit(solution)/shard_map/ppermute | solution.py:418
  4.7 0.7 %collective-permute-start = (f32[32,128]{1,0:T(8,128)S(1)}, f32[32,128]{1,0:T(8,128)S(1)}, u32[]{:S(2)}, u32[]{:S(2)}) collective-permute-start(f32[32,128]{1,0:T(8,128)S(1)} %get-tuple-element.30), channel_id=1, source_target_pairs={{1,2},{2,1},{3,4},{4,3},{5,6},{6,5},{7,8},{8,7},{9,10},{10,9},{11,... | collective-permute-start | bytes 49160 | tf_op jit(solution)/shard_map/ppermute | solution.py:415
  5.4 5.2 %collective-permute-start.1 = (f32[32,128]{1,0:T(8,128)S(1)}, f32[32,128]{1,0:T(8,128)S(1)}, u32[]{:S(2)}, u32[]{:S(2)}) collective-permute-start(f32[32,128]{1,0:T(8,128)S(1)} %get-tuple-element.31), channel_id=1, source_target_pairs={{0,1},{1,0},{2,3},{3,2},{4,5},{5,4},{6,7},{7,6},{8,9},{9,8},{10,11... | collective-permute-start | bytes 49160 | tf_op jit(solution)/shard_map/ppermute | solution.py:416
  10.5 0.0 collective-permute-done.2.far_side
  10.5 0.0 collective-permute-done.3.near_side
  10.5 0.0 collective-permute-done.next_row
  10.6 1.7 %collective-permute-done.1.pair_row = f32[32,128]{1,0:T(8,128)S(1)} collective-permute-done((f32[32,128]{1,0:T(8,128)S(1)}, f32[32,128]{1,0:T(8,128)S(1)}, u32[]{:S(2)}, u32[]{:S(2)}) %collective-permute-start.1) | collective-permute-done | bytes 16416 | tf_op jit(solution)/shard_map/ppermute | solution.py:416
  12.3 0.2 shard_map.19.deep
  12.5 1.1 %shard_map.20 = (f32[512,128]{1,0:T(8,128)}, f32[16,32,128]{2,1,0:T(8,128)S(1)}, f32[16,32,128]{2,1,0:T(8,128)S(1)}, f32[16,32,128]{2,1,0:T(8,128)S(1)}) custom-call(f32[512,128]{1,0:T(8,128)S(1)} %bitcast.7, f32[528,128]{1,0:T(8,128)S(1)} %shard_map.19.deep), custom_call_target="tpu_custom_call" | custom-call | flops 1000000 | bytes 500000 | tf_op jit(solution)/shard_map/pallas_call | solution.py:421
  13.6 0.0 copy-start.1
  13.6 10.7 %all-to-all-start = ((f32[32,16,128]{2,1,0:T(8,128)}), f32[32,16,128]{2,1,0:T(8,128)S(1)}, u32[]{:S(2)}, u32[]{:S(2)}) async-start(f32[32,16,128]{2,1,0:T(8,128)} %bitcast.1), calls=%async_computation | async-start | bytes 524288 | tf_op jit(solution)/shard_map/all_to_all | solution.py:424
  24.3 0.1 collective-permute-start.4
  24.4 2.4 %collective-permute-start.5 = (f32[8,128]{1,0:T(8,128)S(1)}, f32[8,128]{1,0:T(8,128)S(1)}, u32[]{:S(2)}, u32[]{:S(2)}) collective-permute-start(f32[8,128]{1,0:T(8,128)S(1)} %get-tuple-element.40), channel_id=1, source_target_pairs={{32,64},{64,32},{96,128},{128,96},{160,192},{192,160},{33,65},{65,... | collective-permute-start | bytes 12296 | tf_op jit(solution)/shard_map/ppermute | solution.py:427
  26.9 0.0 collective-permute-done.4.near_corner
  26.9 2.5 %collective-permute-done.5.far_corner = f32[8,128]{1,0:T(8,128)S(1)} collective-permute-done((f32[8,128]{1,0:T(8,128)S(1)}, f32[8,128]{1,0:T(8,128)S(1)}, u32[]{:S(2)}, u32[]{:S(2)}) %collective-permute-start.5) | collective-permute-done | bytes 4128 | tf_op jit(solution)/shard_map/ppermute | solution.py:427
  29.4 0.0 copy-done.1
  29.4 0.4 shard_map.22
  29.8 0.9 %collective-permute-start.6 = (f32[5,16,128]{2,1,0:T(8,128)S(1)}, f32[5,16,128]{2,1,0:T(8,128)S(1)}, u32[]{:S(2)}, u32[]{:S(2)}) collective-permute-start(f32[5,16,128]{2,1,0:T(8,128)S(1)} %get-tuple-element.41.refs_0_.own), channel_id=1, source_target_pairs={{0,32},{32,0},{64,96},{96,64},{128,160},{160,128},{192,224},{224,1... | collective-permute-start | bytes 122888 | tf_op jit(solution)/shard_map/ppermute | solution.py:434
  30.6 0.9 %collective-permute-done.6.refs_1_.near = f32[5,16,128]{2,1,0:T(8,128)S(1)} collective-permute-done((f32[5,16,128]{2,1,0:T(8,128)S(1)}, f32[5,16,128]{2,1,0:T(8,128)S(1)}, u32[]{:S(2)}, u32[]{:S(2)}) %collective-permute-start.6) | collective-permute-done | bytes 40992 | tf_op jit(solution)/shard_map/ppermute | solution.py:434
  31.5 0.5 collective-permute-start.7
  32.1 0.7 %shard_map.25.solved_x = f32[512,128]{1,0:T(8,128)S(1)} custom-call(f32[512,128]{1,0:T(8,128)S(1)} %bitcast.9, f32[528,128]{1,0:T(8,128)S(1)} %get-tuple-element.42.smooth), custom_call_target="tpu_custom_call" | custom-call | flops 1000000 | bytes 500000 | tf_op jit(solution)/shard_map/pallas_call | solution.py:435
  32.7 2.9 %collective-permute-done.7.refs_1_.pair = f32[5,16,128]{2,1,0:T(8,128)S(1)} collective-permute-done((f32[5,16,128]{2,1,0:T(8,128)S(1)}, f32[5,16,128]{2,1,0:T(8,128)S(1)}, u32[]{:S(2)}, u32[]{:S(2)}) %collective-permute-start.7) | collective-permute-done | bytes 40992 | tf_op jit(solution)/shard_map/ppermute | solution.py:447
  35.6 0.1 all-to-all-done
  35.7 0.8 %shard_map.26 = f32[32,4,128]{2,1,0:T(4,128)} custom-call(f32[512,128]{1,0:T(8,128)S(1)} %bitcast.10), custom_call_target="tpu_custom_call" | custom-call | flops 1000000 | bytes 500000 | tf_op jit(solution)/shard_map/pallas_call | solution.py:450
  36.6 9.7 %all-to-all-start.1 = ((f32[32,4,128]{2,1,0:T(4,128)}), f32[32,4,128]{2,1,0:T(4,128)S(1)}, u32[]{:S(2)}, u32[]{:S(2)}) async-start(f32[32,4,128]{2,1,0:T(4,128)} %shard_map.26), calls=%async_computation.1 | async-start | bytes 131072 | tf_op jit(solution)/shard_map/all_to_all | solution.py:456
  46.3 0.9 %collective-permute-start.8 = (f32[5,16,128]{2,1,0:T(8,128)S(1)}, f32[5,16,128]{2,1,0:T(8,128)S(1)}, u32[]{:S(2)}, u32[]{:S(2)}) collective-permute-start(f32[5,16,128]{2,1,0:T(8,128)S(1)} %shard_map.24), channel_id=1, source_target_pairs={{0,128},{32,160},{64,192},{96,224},{128,0},{160,32},{192,64},{224,... | collective-permute-start | bytes 122888 | tf_op jit(solution)/shard_map/ppermute | solution.py:452
  47.2 4.7 %collective-permute-done.8.quad = f32[5,16,128]{2,1,0:T(8,128)S(1)} collective-permute-done((f32[5,16,128]{2,1,0:T(8,128)S(1)}, f32[5,16,128]{2,1,0:T(8,128)S(1)}, u32[]{:S(2)}, u32[]{:S(2)}) %collective-permute-start.8) | collective-permute-done | bytes 40992 | tf_op jit(solution)/shard_map/ppermute | solution.py:452
  51.9 0.1 shard_map.27.others
  52.0 4.3 %all-to-all-done.1.ends = f32[32,4,128]{2,1,0:T(4,128)S(1)} async-done(((f32[32,4,128]{2,1,0:T(4,128)}), f32[32,4,128]{2,1,0:T(4,128)S(1)}, u32[]{:S(2)}, u32[]{:S(2)}) %all-to-all-start.1) | async-done | bytes 65568 | tf_op jit(solution)/shard_map/all_to_all | solution.py:456
  56.3 0.9 %shard_map.28 = f32[512,128]{1,0:T(8,128)} custom-call(f32[32,4,128]{2,1,0:T(4,128)S(1)} %all-to-all-done.1.ends, f32[16,32,128]{2,1,0:T(8,128)S(1)} %get-tuple-element.46.factor, f32[16,32,128]{2,1,0:T(8,128)S(1)} %get-tuple-element.47.back, f32[16,32,128]{2,1,0:T(8,128)S(1)} %get-tuple-element.48.rest, f32[512,128]{1,0:T(8,128)S(1)} %shard_map.27.others), custom_call_target="tpu_custom_call" | custom-call | flops 1000000 | bytes 500000 | tf_op jit(solution)/shard_map/pallas_call | solution.py:457
  (5 shorter events, 0.1 us)
Async XLA Ops:
  0.0 0.9 %copy-start = (f32[32,16,128]{2,1,0:T(8,128)S(1)}, f32[32,16,128]{2,1,0:T(8,128)}, u32[]{:S(2)}) copy-start(f32[32,16,128]{2,1,0:T(8,128)} %param.1) | copy-start | bytes 786436
  1.0 9.6 %collective-permute-start.2 = (f32[32,128]{1,0:T(8,128)S(1)}, f32[32,128]{1,0:T(8,128)S(1)}, u32[]{:S(2)}, u32[]{:S(2)}) collective-permute-start(f32[32,128]{1,0:T(8,128)S(1)} %get-tuple-element.32), channel_id=1, source_target_pairs={{32,64},{64,32},{96,128},{128,96},{160,192},{192,160},{33,65},{65,... | collective-permute-start | bytes 49160 | tf_op jit(solution)/shard_map/ppermute | solution.py:417
  2.9 7.6 %collective-permute-start.3 = (f32[32,128]{1,0:T(8,128)S(1)}, f32[32,128]{1,0:T(8,128)S(1)}, u32[]{:S(2)}, u32[]{:S(2)}) collective-permute-start(f32[32,128]{1,0:T(8,128)S(1)} %get-tuple-element.33), channel_id=1, source_target_pairs={{0,32},{32,0},{64,96},{96,64},{128,160},{160,128},{192,224},{224,1... | collective-permute-start | bytes 49160 | tf_op jit(solution)/shard_map/ppermute | solution.py:418
  4.7 5.8 %collective-permute-start = (f32[32,128]{1,0:T(8,128)S(1)}, f32[32,128]{1,0:T(8,128)S(1)}, u32[]{:S(2)}, u32[]{:S(2)}) collective-permute-start(f32[32,128]{1,0:T(8,128)S(1)} %get-tuple-element.30), channel_id=1, source_target_pairs={{1,2},{2,1},{3,4},{4,3},{5,6},{6,5},{7,8},{8,7},{9,10},{10,9},{11,... | collective-permute-start | bytes 49160 | tf_op jit(solution)/shard_map/ppermute | solution.py:415
  5.4 6.9 %collective-permute-start.1 = (f32[32,128]{1,0:T(8,128)S(1)}, f32[32,128]{1,0:T(8,128)S(1)}, u32[]{:S(2)}, u32[]{:S(2)}) collective-permute-start(f32[32,128]{1,0:T(8,128)S(1)} %get-tuple-element.31), channel_id=1, source_target_pairs={{0,1},{1,0},{2,3},{3,2},{4,5},{5,4},{6,7},{7,6},{8,9},{9,8},{10,11... | collective-permute-start | bytes 49160 | tf_op jit(solution)/shard_map/ppermute | solution.py:416
  13.6 15.8 %copy-start.1 = (f32[32,16,128]{2,1,0:T(8,128)S(1)}, f32[32,16,128]{2,1,0:T(8,128)}, u32[]{:S(2)}) copy-start(f32[32,16,128]{2,1,0:T(8,128)} %param.1) | copy-start | bytes 786436
  13.6 22.1 %all-to-all-start = ((f32[32,16,128]{2,1,0:T(8,128)}), f32[32,16,128]{2,1,0:T(8,128)S(1)}, u32[]{:S(2)}, u32[]{:S(2)}) async-start(f32[32,16,128]{2,1,0:T(8,128)} %bitcast.1), calls=%async_computation | async-start | bytes 524288 | tf_op jit(solution)/shard_map/all_to_all | solution.py:424
  24.3 2.6 %collective-permute-start.4 = (f32[8,128]{1,0:T(8,128)S(1)}, f32[8,128]{1,0:T(8,128)S(1)}, u32[]{:S(2)}, u32[]{:S(2)}) collective-permute-start(f32[8,128]{1,0:T(8,128)S(1)} %get-tuple-element.39), channel_id=1, source_target_pairs={{0,32},{32,0},{64,96},{96,64},{128,160},{160,128},{192,224},{224,1... | collective-permute-start | bytes 12296 | tf_op jit(solution)/shard_map/ppermute | solution.py:428
  24.4 4.9 %collective-permute-start.5 = (f32[8,128]{1,0:T(8,128)S(1)}, f32[8,128]{1,0:T(8,128)S(1)}, u32[]{:S(2)}, u32[]{:S(2)}) collective-permute-start(f32[8,128]{1,0:T(8,128)S(1)} %get-tuple-element.40), channel_id=1, source_target_pairs={{32,64},{64,32},{96,128},{128,96},{160,192},{192,160},{33,65},{65,... | collective-permute-start | bytes 12296 | tf_op jit(solution)/shard_map/ppermute | solution.py:427
  29.8 1.7 %collective-permute-start.6 = (f32[5,16,128]{2,1,0:T(8,128)S(1)}, f32[5,16,128]{2,1,0:T(8,128)S(1)}, u32[]{:S(2)}, u32[]{:S(2)}) collective-permute-start(f32[5,16,128]{2,1,0:T(8,128)S(1)} %get-tuple-element.41.refs_0_.own), channel_id=1, source_target_pairs={{0,32},{32,0},{64,96},{96,64},{128,160},{160,128},{192,224},{224,1... | collective-permute-start | bytes 122888 | tf_op jit(solution)/shard_map/ppermute | solution.py:434
  31.5 4.1 %collective-permute-start.7 = (f32[5,16,128]{2,1,0:T(8,128)S(1)}, f32[5,16,128]{2,1,0:T(8,128)S(1)}, u32[]{:S(2)}, u32[]{:S(2)}) collective-permute-start(f32[5,16,128]{2,1,0:T(8,128)S(1)} %shard_map.23.refs_0_), channel_id=1, source_target_pairs={{0,64},{32,96},{64,0},{96,32},{128,192},{160,224},{192,128},{224,1... | collective-permute-start | bytes 122888 | tf_op jit(solution)/shard_map/ppermute | solution.py:447
  36.6 19.7 %all-to-all-start.1 = ((f32[32,4,128]{2,1,0:T(4,128)}), f32[32,4,128]{2,1,0:T(4,128)S(1)}, u32[]{:S(2)}, u32[]{:S(2)}) async-start(f32[32,4,128]{2,1,0:T(4,128)} %shard_map.26), calls=%async_computation.1 | async-start | bytes 131072 | tf_op jit(solution)/shard_map/all_to_all | solution.py:456
  46.3 5.6 %collective-permute-start.8 = (f32[5,16,128]{2,1,0:T(8,128)S(1)}, f32[5,16,128]{2,1,0:T(8,128)S(1)}, u32[]{:S(2)}, u32[]{:S(2)}) collective-permute-start(f32[5,16,128]{2,1,0:T(8,128)S(1)} %shard_map.24), channel_id=1, source_target_pairs={{0,128},{32,160},{64,192},{96,224},{128,0},{160,32},{192,64},{224,... | collective-permute-start | bytes 122888 | tf_op jit(solution)/shard_map/ppermute | solution.py:452

commit v11 on v4

--- a/solution.py
+++ b/solution.py
@@ -283,16 +283,16 @@
 
 
 def finish_plane_kernel(
-    own, near, pair, across, skew, factor, back, rest, mid, solved_x, out,
+    own, near, across, beside, factor, back, rest, mid, solved_x, out,
 ):
     index = lax.axis_index("depth")
     odd = (index & 2) != 0
-    straight = tuple(across[place] for place in range(5))
-    crossed = tuple(skew[place] for place in range(5))
+    crossed = tuple(across[place] for place in range(5))
+    straight = tuple(beside[place] for place in range(5, 10))
     quad, _ = join(pick(odd, crossed, straight), pick(odd, straight, crossed))
     zero = jnp.zeros((ROWS, COLS), F32)
     left_ground, left_source, right_ground, right_source = zero, zero, zero, zero
-    for bit, ref in ((4, quad), (2, pair), (1, near)):
+    for bit, ref in ((4, quad), (2, beside), (1, near)):
         on_left = (index & bit) != 0
         c, ng, fg, ns, fs = (ref[place] for place in range(5))
         ground, source = ng + left_ground, ns + left_source
@@ -397,7 +397,7 @@
     )
     ports = lax.all_to_all(y_port, "lat", 0, 0, tiled=True)
     z_port, z_factor, z_back, z_rest, z_mid, smooth = call(
-        plane_kernel, (port, whole, whole, whole, shaped(3, ROWS, COLS), tall), moved=500000,flops=LONG
+        plane_kernel, (port, whole, whole, whole, shaped(3, ROWS, COLS), tall), flops=LONG
     )(flat, deep, pair_row, next_row)
     near = lax.ppermute(z_port, "depth", swap_perm("depth", 1))
     solved_x = call(
@@ -412,11 +412,14 @@
         ),
     )(flat, smooth)
     pair_own = call(lambda *refs: join_kernel(1, *refs), port)(z_port, near)
-    ports, pair_own, solved_x = lax.optimization_barrier((ports, pair_own, solved_x))
+    across = lax.ppermute(pair_own, "depth", swap_perm("depth", 6))
+    both = jnp.concatenate([pair_own, across], axis=0)
+    ports, both, solved_x = lax.optimization_barrier((ports, both, solved_x))
     ends = call(row_reduced_kernel, shaped(BLOCKS, 4, COLS))(ports)
-    across, skew, pair = (lax.ppermute(pair_own, "depth", swap_perm("depth", bits)) for bits in (4, 6, 2))
-    others = call(finish_plane_kernel, whole, flops=LONG)(
-        z_port, near, pair, across, skew, z_factor, z_back, z_rest, z_mid, solved_x
+    ends, both = lax.optimization_barrier((ends, both))
+    beside = lax.ppermute(both, "depth", swap_perm("depth", 2))
+    others = call(finish_plane_kernel, whole)(
+        z_port, near, across, beside, z_factor, z_back, z_rest, z_mid, solved_x
     )
     ends_y = lax.all_to_all(ends, "lat", 0, 0, tiled=True)
     out = call(finish_row_kernel, whole)(ends_y, y_factor, y_back, y_rest, others)

time: 55.7 us -> 51.6 us (0.926)
  starting transfers between devices: 27.4 us -> 25.1 us
  waiting for transfers between devices: 22.7 us -> 20.8 us
    ppermute x3 -> x2, waiting for transfers between devices: 0.01 us -> 6.1 us  [the longest x1 4.36 us: shards(): beside = lax.ppermute(both, 'depth', swap_perm('depth', 2))]
    all_to_all x1, waiting for transfers between devices: 9.91 us -> 5.38 us  [shards(): ends_y = lax.all_to_all(ends, 'lat', 0, 0, tiled=True)]
    all_to_all x1, waiting for transfers between devices: 10.8 us -> 6.71 us  [shards(): ports = lax.all_to_all(y_port, 'lat', 0, 0, tiled=True)]
    ppermute x3 -> x2, starting transfers between devices: 4.09 us -> 1.83 us  [the longest x1 1.66 us: shards(): across = lax.ppermute(pair_own, 'depth', swap_perm('depth', 6))]
    ppermute x1, waiting for transfers between devices: 0.52 us -> 1.21 us  [shards(): near = lax.ppermute(z_port, 'depth', swap_perm('depth', 1))]
  transfers between devices with their start and end apart: 10 -> 9, of which waited for: 4 -> 6; matrix products, arithmetic and copies ran while one was open for 0% -> 0% of each run, Pallas kernels for 6% -> 4%
where the time goes in v11:
time: 51.6 us; the launch traced here: 51.3 us
  starting transfers between devices  25.1 us (49%)
  waiting for transfers between devices  20.8 us (40%)
  Pallas kernels  4.25 us (8%)
  local copies, waits for them, and re-layouts  0.95 us (2%)
    all_to_all x1, starting transfers between devices, shards(): ports = lax.all_to_all(y_port, 'lat', 0, 0, tiled=True)  12.4 us
    all_to_all x1, waiting for transfers between devices, shards(): ports = lax.all_to_all(y_port, 'lat', 0, 0, tiled=True)  6.71 us
    all_to_all x1, waiting for transfers between devices, shards(): ends_y = lax.all_to_all(ends, 'lat', 0, 0, tiled=True)  5.38 us
    all_to_all x1, starting transfers between devices, shards(): ends_y = lax.all_to_all(ends, 'lat', 0, 0, tiled=True)  4.44 us
    ppermute x1, waiting for transfers between devices, shards(): beside = lax.ppermute(both, 'depth', swap_perm('depth', 2))  4.36 us
    ppermute x1, starting transfers between devices, shards(): far_side = lax.ppermute(to_far, 'depth', next_perm('depth'))  4.18 us
    ppermute x1, waiting for transfers between devices, shards(): across = lax.ppermute(pair_own, 'depth', swap_perm('depth', 6))  1.74 us
    ppermute x1, starting transfers between devices, shards(): across = lax.ppermute(pair_own, 'depth', swap_perm('depth', 6))  1.66 us
  transfers between devices with their start and end apart: 9, of which 6 were waited for; matrix products, arithmetic and copies ran while one was open for 0% of the time, Pallas kernels for 4%

profile of v11, /device:TPU:8, one launch (start us, length us, event | category | flops | bytes accessed | tf_op | source)
XLA Modules:
  0.0 51.3 jit_solution(2658768500168774842)
XLA Ops:
  0.0 0.0 copy-start
  0.0 0.9 %copy-done = f32[32,16,128]{2,1,0:T(8,128)S(1)} copy-done((f32[32,16,128]{2,1,0:T(8,128)S(1)}, f32[32,16,128]{2,1,0:T(8,128)}, u32[]{:S(2)}) %copy-start) | copy-done | bytes 262168
  1.0 0.1 collective-permute-start
  1.1 4.2 %collective-permute-start.1 = (f32[32,128]{1,0:T(8,128)S(1)}, f32[32,128]{1,0:T(8,128)S(1)}, u32[]{:S(2)}, u32[]{:S(2)}) collective-permute-start(f32[32,128]{1,0:T(8,128)S(1)} %get-tuple-element.26), channel_id=1, source_target_pairs={{32,64},{64,32},{96,128},{128,96},{160,192},{192,160},{33,65},{65,... | collective-permute-start | bytes 49160 | tf_op jit(solution)/shard_map/ppermute | solution.py:388
  5.3 0.0 collective-permute-done.near_side
  5.3 1.4 %collective-permute-done.1.far_side = f32[32,128]{1,0:T(8,128)S(1)} collective-permute-done((f32[32,128]{1,0:T(8,128)S(1)}, f32[32,128]{1,0:T(8,128)S(1)}, u32[]{:S(2)}, u32[]{:S(2)}) %collective-permute-start.1) | collective-permute-done | bytes 16416 | tf_op jit(solution)/shard_map/ppermute | solution.py:388
  6.7 0.2 shard_map.18
  6.9 1.4 %collective-permute-start.2 = (f32[33,128]{1,0:T(8,128)S(1)}, f32[33,128]{1,0:T(8,128)S(1)}, u32[]{:S(2)}, u32[]{:S(2)}) collective-permute-start(f32[33,128]{1,0:T(8,128)S(1)} %get-tuple-element.29), channel_id=1, source_target_pairs={{0,1},{1,0},{2,3},{3,2},{4,5},{5,4},{6,7},{7,6},{8,9},{9,8},{10,11... | collective-permute-start | bytes 50696 | tf_op jit(solution)/shard_map/ppermute | solution.py:394
  8.4 0.7 %collective-permute-start.3 = (f32[33,128]{1,0:T(8,128)S(1)}, f32[33,128]{1,0:T(8,128)S(1)}, u32[]{:S(2)}, u32[]{:S(2)}) collective-permute-start(f32[33,128]{1,0:T(8,128)S(1)} %get-tuple-element.30), channel_id=1, source_target_pairs={{1,2},{2,1},{3,4},{4,3},{5,6},{6,5},{7,8},{8,7},{9,10},{10,9},{11,... | collective-permute-start | bytes 50696 | tf_op jit(solution)/shard_map/ppermute | solution.py:393
  9.1 1.1 %shard_map.19 = (f32[512,128]{1,0:T(8,128)}, f32[16,32,128]{2,1,0:T(8,128)S(1)}, f32[16,32,128]{2,1,0:T(8,128)S(1)}, f32[16,32,128]{2,1,0:T(8,128)S(1)}) custom-call(f32[512,128]{1,0:T(8,128)S(1)} %bitcast.6, f32[528,128]{1,0:T(8,128)S(1)} %get-tuple-element.27.deep), custom_call_target="tpu_custom_call" | custom-call | flops 1000000 | bytes 500000 | tf_op jit(solution)/shard_map/pallas_call | solution.py:395
  10.1 0.0 copy-start.1
  10.1 12.4 %all-to-all-start = ((f32[32,16,128]{2,1,0:T(8,128)}), f32[32,16,128]{2,1,0:T(8,128)S(1)}, u32[]{:S(2)}, u32[]{:S(2)}) async-start(f32[32,16,128]{2,1,0:T(8,128)} %bitcast.1), calls=%async_computation | async-start | bytes 524288 | tf_op jit(solution)/shard_map/all_to_all | solution.py:398
  22.5 0.0 collective-permute-done.2.pair_row
  22.5 0.0 collective-permute-done.3.next_row
  22.5 0.0 copy-done.1
  22.5 0.3 shard_map.20
  22.9 0.1 collective-permute-start.4
  23.0 1.2 %collective-permute-done.4.refs_1_.near = f32[5,16,128]{2,1,0:T(8,128)S(1)} collective-permute-done((f32[5,16,128]{2,1,0:T(8,128)S(1)}, f32[5,16,128]{2,1,0:T(8,128)S(1)}, u32[]{:S(2)}, u32[]{:S(2)}) %collective-permute-start.4) | collective-permute-done | bytes 40992 | tf_op jit(solution)/shard_map/ppermute | solution.py:402
  24.2 1.7 %collective-permute-start.5 = (f32[5,16,128]{2,1,0:T(8,128)S(1)}, f32[5,16,128]{2,1,0:T(8,128)S(1)}, u32[]{:S(2)}, u32[]{:S(2)}) collective-permute-start(f32[5,16,128]{2,1,0:T(8,128)S(1)} %shard_map.21), channel_id=1, source_target_pairs={{0,192},{32,224},{64,128},{96,160},{128,64},{160,96},{192,0},{224,... | collective-permute-start | bytes 122888 | tf_op jit(solution)/shard_map/ppermute | solution.py:415
  25.9 0.7 %shard_map.22.solved_x = f32[512,128]{1,0:T(8,128)S(1)} custom-call(f32[512,128]{1,0:T(8,128)S(1)} %bitcast.8, f32[528,128]{1,0:T(8,128)S(1)} %get-tuple-element.32.smooth), custom_call_target="tpu_custom_call" | custom-call | flops 1000000 | bytes 500000 | tf_op jit(solution)/shard_map/pallas_call | solution.py:403
  26.5 1.7 %collective-permute-done.5.across = f32[5,16,128]{2,1,0:T(8,128)S(1)} collective-permute-done((f32[5,16,128]{2,1,0:T(8,128)S(1)}, f32[5,16,128]{2,1,0:T(8,128)S(1)}, u32[]{:S(2)}, u32[]{:S(2)}) %collective-permute-start.5) | collective-permute-done | bytes 40992 | tf_op jit(solution)/shard_map/ppermute | solution.py:415
  28.3 6.7 %all-to-all-done = f32[32,16,128]{2,1,0:T(8,128)S(1)} async-done(((f32[32,16,128]{2,1,0:T(8,128)}), f32[32,16,128]{2,1,0:T(8,128)S(1)}, u32[]{:S(2)}, u32[]{:S(2)}) %all-to-all-start) | async-done | bytes 262176 | tf_op jit(solution)/shard_map/all_to_all | solution.py:398
  35.0 0.8 %shard_map.23 = f32[32,4,128]{2,1,0:T(4,128)} custom-call(f32[512,128]{1,0:T(8,128)S(1)} %bitcast.9), custom_call_target="tpu_custom_call" | custom-call | flops 1000000 | bytes 500000 | tf_op jit(solution)/shard_map/pallas_call | solution.py:418
  35.9 4.4 %all-to-all-start.1 = ((f32[32,4,128]{2,1,0:T(4,128)}), f32[32,4,128]{2,1,0:T(4,128)S(1)}, u32[]{:S(2)}, u32[]{:S(2)}) async-start(f32[32,4,128]{2,1,0:T(4,128)} %shard_map.23), calls=%async_computation.1 | async-start | bytes 131072 | tf_op jit(solution)/shard_map/all_to_all | solution.py:424
  40.3 0.2 collective-permute-start.6
  40.5 4.4 %collective-permute-done.6.beside = f32[10,16,128]{2,1,0:T(8,128)S(1)} collective-permute-done((f32[10,16,128]{2,1,0:T(8,128)S(1)}, f32[10,16,128]{2,1,0:T(8,128)S(1)}, u32[]{:S(2)}, u32[]{:S(2)}) %collective-permute-start.6) | collective-permute-done | bytes 81952 | tf_op jit(solution)/shard_map/ppermute | solution.py:420
  44.8 0.1 shard_map.24.others
  45.0 5.4 %all-to-all-done.1.ends = f32[32,4,128]{2,1,0:T(4,128)S(1)} async-done(((f32[32,4,128]{2,1,0:T(4,128)}), f32[32,4,128]{2,1,0:T(4,128)S(1)}, u32[]{:S(2)}, u32[]{:S(2)}) %all-to-all-start.1) | async-done | bytes 65568 | tf_op jit(solution)/shard_map/all_to_all | solution.py:424
  50.4 0.9 %shard_map.25 = f32[512,128]{1,0:T(8,128)} custom-call(f32[32,4,128]{2,1,0:T(4,128)S(1)} %all-to-all-done.1.ends, f32[16,32,128]{2,1,0:T(8,128)S(1)} %get-tuple-element.36.factor, f32[16,32,128]{2,1,0:T(8,128)S(1)} %get-tuple-element.37.back, f32[16,32,128]{2,1,0:T(8,128)S(1)} %get-tuple-element.38.rest, f32[512,128]{1,0:T(8,128)S(1)} %shard_map.24.others), custom_call_target="tpu_custom_call" | custom-call | flops 1000000 | bytes 500000 | tf_op jit(solution)/shard_map/pallas_call | solution.py:425
  (3 shorter events, 0.1 us)
Async XLA Ops:
  0.0 0.9 %copy-start = (f32[32,16,128]{2,1,0:T(8,128)S(1)}, f32[32,16,128]{2,1,0:T(8,128)}, u32[]{:S(2)}) copy-start(f32[32,16,128]{2,1,0:T(8,128)} %param.1) | copy-start | bytes 786436
  1.0 4.3 %collective-permute-start = (f32[32,128]{1,0:T(8,128)S(1)}, f32[32,128]{1,0:T(8,128)S(1)}, u32[]{:S(2)}, u32[]{:S(2)}) collective-permute-start(f32[32,128]{1,0:T(8,128)S(1)} %get-tuple-element.25), channel_id=1, source_target_pairs={{0,32},{32,0},{64,96},{96,64},{128,160},{160,128},{192,224},{224,1... | collective-permute-start | bytes 49160 | tf_op jit(solution)/shard_map/ppermute | solution.py:389
  1.1 5.6 %collective-permute-start.1 = (f32[32,128]{1,0:T(8,128)S(1)}, f32[32,128]{1,0:T(8,128)S(1)}, u32[]{:S(2)}, u32[]{:S(2)}) collective-permute-start(f32[32,128]{1,0:T(8,128)S(1)} %get-tuple-element.26), channel_id=1, source_target_pairs={{32,64},{64,32},{96,128},{128,96},{160,192},{192,160},{33,65},{65,... | collective-permute-start | bytes 49160 | tf_op jit(solution)/shard_map/ppermute | solution.py:388
  6.9 15.6 %collective-permute-start.2 = (f32[33,128]{1,0:T(8,128)S(1)}, f32[33,128]{1,0:T(8,128)S(1)}, u32[]{:S(2)}, u32[]{:S(2)}) collective-permute-start(f32[33,128]{1,0:T(8,128)S(1)} %get-tuple-element.29), channel_id=1, source_target_pairs={{0,1},{1,0},{2,3},{3,2},{4,5},{5,4},{6,7},{7,6},{8,9},{9,8},{10,11... | collective-permute-start | bytes 50696 | tf_op jit(solution)/shard_map/ppermute | solution.py:394
  8.4 14.1 %collective-permute-start.3 = (f32[33,128]{1,0:T(8,128)S(1)}, f32[33,128]{1,0:T(8,128)S(1)}, u32[]{:S(2)}, u32[]{:S(2)}) collective-permute-start(f32[33,128]{1,0:T(8,128)S(1)} %get-tuple-element.30), channel_id=1, source_target_pairs={{1,2},{2,1},{3,4},{4,3},{5,6},{6,5},{7,8},{8,7},{9,10},{10,9},{11,... | collective-permute-start | bytes 50696 | tf_op jit(solution)/shard_map/ppermute | solution.py:393
  10.1 12.4 %copy-start.1 = (f32[32,16,128]{2,1,0:T(8,128)S(1)}, f32[32,16,128]{2,1,0:T(8,128)}, u32[]{:S(2)}) copy-start(f32[32,16,128]{2,1,0:T(8,128)} %param.1) | copy-start | bytes 786436
  10.1 24.9 %all-to-all-start = ((f32[32,16,128]{2,1,0:T(8,128)}), f32[32,16,128]{2,1,0:T(8,128)S(1)}, u32[]{:S(2)}, u32[]{:S(2)}) async-start(f32[32,16,128]{2,1,0:T(8,128)} %bitcast.1), calls=%async_computation | async-start | bytes 524288 | tf_op jit(solution)/shard_map/all_to_all | solution.py:398
  22.9 1.3 %collective-permute-start.4 = (f32[5,16,128]{2,1,0:T(8,128)S(1)}, f32[5,16,128]{2,1,0:T(8,128)S(1)}, u32[]{:S(2)}, u32[]{:S(2)}) collective-permute-start(f32[5,16,128]{2,1,0:T(8,128)S(1)} %get-tuple-element.31.refs_0_.own), channel_id=1, source_target_pairs={{0,32},{32,0},{64,96},{96,64},{128,160},{160,128},{192,224},{224,1... | collective-permute-start | bytes 122888 | tf_op jit(solution)/shard_map/ppermute | solution.py:402
  24.2 4.1 %collective-permute-start.5 = (f32[5,16,128]{2,1,0:T(8,128)S(1)}, f32[5,16,128]{2,1,0:T(8,128)S(1)}, u32[]{:S(2)}, u32[]{:S(2)}) collective-permute-start(f32[5,16,128]{2,1,0:T(8,128)S(1)} %shard_map.21), channel_id=1, source_target_pairs={{0,192},{32,224},{64,128},{96,160},{128,64},{160,96},{192,0},{224,... | collective-permute-start | bytes 122888 | tf_op jit(solution)/shard_map/ppermute | solution.py:415
  35.9 14.5 %all-to-all-start.1 = ((f32[32,4,128]{2,1,0:T(4,128)}), f32[32,4,128]{2,1,0:T(4,128)S(1)}, u32[]{:S(2)}, u32[]{:S(2)}) async-start(f32[32,4,128]{2,1,0:T(4,128)} %shard_map.23), calls=%async_computation.1 | async-start | bytes 131072 | tf_op jit(solution)/shard_map/all_to_all | solution.py:424
  40.3 4.5 %collective-permute-start.6 = (f32[10,16,128]{2,1,0:T(8,128)S(1)}, f32[10,16,128]{2,1,0:T(8,128)S(1)}, u32[]{:S(2)}, u32[]{:S(2)}) collective-permute-start(f32[10,16,128]{2,1,0:T(8,128)S(1)} %pad_maximum_fusion), channel_id=1, source_target_pairs={{0,64},{32,96},{64,0},{96,32},{128,192},{160,224},{192,128},{224,1... | collective-permute-start | bytes 245768 | tf_op jit(solution)/shard_map/ppermute | solution.py:420

commit v12 on v3

--- a/solution.py
+++ b/solution.py
@@ -12,6 +12,7 @@
 COLS = 128
 BLOCKS = 32
 PORT = 8
+GATHER = 256
 F32 = jnp.float32
 
 
@@ -85,7 +86,7 @@
     return ref[plane * ROWS : (plane + 1) * ROWS, :]
 
 
-def deep_kernel(vol, near_side, far_side, deep, low_side, high_side, mixed):
+def deep_kernel(vol, near_side, far_side, deep, pair_row, next_row, mixed):
     odd = (lax.axis_index("depth") & 1) == 1
     lane = lax.broadcasted_iota(jnp.int32, (ROWS, COLS), 1)
     first, last = lane == 0, lane == COLS - 1
@@ -100,11 +101,17 @@
         deep[plane * ROWS : (plane + 1) * ROWS, :] = 0.25 * (
             mixed[plane] + 2.0 * mixed[plane + 1] + mixed[plane + 2]
         )
-    low_side[...] = deep[pl.ds(0, PLANES + 1, stride=ROWS), :]
-    high_side[...] = deep[pl.ds(ROWS - 1, PLANES + 1, stride=ROWS), :]
-
-
-def plane_kernel(vol, deep, low_row, high_row, port, factor, back, rest, mid, smooth):
+    odd_row = (lax.axis_index("lat") & 1) == 1
+    low = deep[pl.ds(0, PLANES + 1, stride=ROWS), :]
+    high = deep[pl.ds(ROWS - 1, PLANES + 1, stride=ROWS), :]
+    pair_row[...] = jnp.where(odd_row, low, high)
+    next_row[...] = jnp.where(odd_row, high, low)
+
+
+def plane_kernel(vol, deep, pair_row, next_row, port, factor, back, rest, mid, smooth):
+    odd_row = (lax.axis_index("lat") & 1) == 1
+    low_row = jnp.where(odd_row, pair_row[...], next_row[...])
+    high_row = jnp.where(odd_row, next_row[...], pair_row[...])
     depth_last = lax.axis_index("depth") == lax.axis_size("depth") - 1
     z_open = jnp.where(depth_last, 0.0, TAU3).astype(F32)
     row_index = lax.broadcasted_iota(jnp.int32, (ROWS, COLS), 0)
@@ -140,7 +147,8 @@
             factor[span, :], back[span, :], rest[span, :] = saved
     joined, middle = join(*[(c, ng, fg, ns, fs) for c, fg, fs, ng, ns in states])
     for place, value in enumerate(joined):
-        port[place] = value
+        port[place * ROWS : (place + 1) * ROWS, :] = value
+    port[5 * ROWS :, :] = jnp.zeros((GATHER - 5 * ROWS, COLS), F32)
     for place, value in enumerate(middle):
         mid[place] = value
 
@@ -241,63 +249,65 @@
     out[:, 1, :] = at_high[0] * first + at_high[1] * pltpu.roll(first, BLOCKS - 1, 0) + at_high[2]
 
 
-def pick(flag, there, here):
-    return tuple(jnp.where(flag, a, b) for a, b in zip(there, here))
-
-
-def join_kernel(bit, own, other, out):
-    upper = (lax.axis_index("depth") & bit) != 0
-    mine = tuple(own[place] for place in range(5))
-    theirs = tuple(other[place] for place in range(5))
-    port, _ = join(pick(upper, theirs, mine), pick(upper, mine, theirs))
-    for place, value in enumerate(port):
-        out[place] = value
-
-
-def finish_kernel(
-    ends_y, y_factor, y_back, y_rest, own, near, pair, quad, z_factor, z_back, z_rest, z_mid, solved_x,
-    out, acc,
-):
+def finish_plane_kernel(own, gathered, factor, back, rest, mid, others, out, ports, sem):
+    copy = pltpu.make_async_copy(gathered.at[:, pl.ds(0, 5 * ROWS), :], ports, sem)
+    copy.start()
+    copy.wait()
+
+    def port(block):
+        return [ports[block, place * ROWS : (place + 1) * ROWS, :] for place in range(5)]
+
     index = lax.axis_index("depth")
+    count = lax.axis_size("depth")
     zero = jnp.zeros((ROWS, COLS), F32)
-    left_ground, left_source, right_ground, right_source = zero, zero, zero, zero
-    for bit, ref in ((4, quad), (2, pair), (1, near)):
-        on_left = (index & bit) != 0
-        c, ng, fg, ns, fs = (ref[place] for place in range(5))
+    left_ground, left_source = zero, zero
+    for block in range(count - 1):
+        c, ng, fg, ns, fs = port(block)
         ground, source = ng + left_ground, ns + left_source
         share = c / (c + ground)
-        left_ground = jnp.where(on_left, fg + share * ground, left_ground)
-        left_source = jnp.where(on_left, fs + share * source, left_source)
+        left_ground = jnp.where(block < index, fg + share * ground, left_ground)
+        left_source = jnp.where(block < index, fs + share * source, left_source)
+    c, ng, fg, ns, fs = port(count - 1)
+    right_ground = jnp.where(index < count - 1, ng, zero)
+    right_source = jnp.where(index < count - 1, ns, zero)
+    for block in range(count - 2, 0, -1):
+        c, ng, fg, ns, fs = port(block)
         ground, source = fg + right_ground, fs + right_source
-        total = c + ground
-        share = jnp.where(total > 0.0, c / jnp.where(total > 0.0, total, 1.0), 0.0)
-        right_ground = jnp.where(on_left, right_ground, ng + share * ground)
-        right_source = jnp.where(on_left, right_source, ns + share * source)
-    c, ng, fg, ns, fs = (own[place] for place in range(5))
+        share = c / (c + ground)
+        right_ground = jnp.where(block > index, ng + share * ground, right_ground)
+        right_source = jnp.where(block > index, ns + share * source, right_source)
+    c, ng, fg, ns, fs = [own[place * ROWS : (place + 1) * ROWS, :] for place in range(5)]
     ground, source = fg + right_ground, fs + right_source
     total = c + ground
     inverse = jnp.where(total > 0.0, 1.0 / jnp.where(total > 0.0, total, 1.0), 0.0)
     share = c * inverse
     first = (left_source + ns + share * source) / (left_ground + ng + share * ground)
     after = share * first + source * inverse
-    middle = z_mid[0] * first + z_mid[1] * after + z_mid[2]
+    middle = mid[0] * first + mid[1] * after + mid[2]
     half = PLANES // 2
-    y_first = ends_y[:, 0, :]
-    value = ends_y[:, 1, :]
-    acc[pl.ds(0, PLANES, stride=ROWS), :] = y_first
-    acc[pl.ds(ROWS - 1, PLANES, stride=ROWS), :] = value
-    for row in range(ROWS - 2, 0, -1):
-        value = y_factor[row] * value + (y_back[row] * y_first + y_rest[row])
-        acc[pl.ds(row, PLANES, stride=ROWS), :] = value
     third = 1.0 / 3.0
     for start, near_value, far_value in ((0, first, middle), (half, middle, after)):
         value = far_value
         for plane in range(start + half - 1, start, -1):
             span = slice(plane * ROWS, (plane + 1) * ROWS)
-            value = z_factor[span, :] * value + (z_back[span, :] * near_value + z_rest[span, :])
-            out[span, :] = (solved_x[span, :] + acc[span, :] + value) * third
+            value = factor[span, :] * value + (back[span, :] * near_value + rest[span, :])
+            out[span, :] = (others[span, :] + value) * third
         span = slice(start * ROWS, (start + 1) * ROWS)
-        out[span, :] = (solved_x[span, :] + acc[span, :] + near_value) * third
+        out[span, :] = (others[span, :] + near_value) * third
+
+
+def finish_row_kernel(ends, factor, back, rest, solved_x, out):
+    def put(row, value):
+        place = pl.ds(row, PLANES, stride=ROWS)
+        out[place, :] = solved_x[place, :] + value
+
+    first = ends[:, 0, :]
+    value = ends[:, 1, :]
+    put(0, first)
+    put(ROWS - 1, value)
+    for row in range(ROWS - 2, 0, -1):
+        value = factor[row] * value + (back[row] * first + rest[row])
+        put(row, value)
 
 
 def call(kernel, outs, scratch=(), flops=1000000, moved=500000, **options):
@@ -338,7 +348,6 @@
     lines = shaped(ROWS, PLANES, COLS)
     whole = shaped(PLANES * ROWS, COLS)
     tall = shaped((PLANES + 1) * ROWS, COLS)
-    port = shaped(5, ROWS, COLS)
     side = shaped(PLANES + 1, COLS)
     to_near, to_far = call(
         edge_kernel,
@@ -348,21 +357,22 @@
     )(flat)
     far_side = lax.ppermute(to_far, "depth", next_perm("depth"))
     near_side = lax.ppermute(to_near, "depth", swap_perm("depth", 1))
-    deep, row_low, row_high = call(
+    deep, to_pair, to_next = call(
         deep_kernel, (tall, side, side), (pltpu.VMEM((PLANES + 3, ROWS, COLS), F32),)
     )(flat, near_side, far_side)
-    low_row = lax.ppermute(row_high, "lat", line_perm("lat", 1))
-    high_row = lax.ppermute(row_low, "lat", line_perm("lat", -1))
+    next_row = lax.ppermute(to_next, "lat", next_perm("lat"))
+    pair_row = lax.ppermute(to_pair, "lat", swap_perm("lat", 1))
     z_port, z_factor, z_back, z_rest, z_mid, smooth = call(
-        plane_kernel, (port, whole, whole, whole, shaped(3, ROWS, COLS), tall)
-    )(flat, deep, low_row, high_row)
-    near = lax.ppermute(z_port, "depth", swap_perm("depth", 1))
+        plane_kernel, (shaped(GATHER, COLS), whole, whole, whole, shaped(3, ROWS, COLS), tall)
+    )(flat, deep, pair_row, next_row)
+    gathered = lax.all_gather(z_port, "depth", axis=0, tiled=True)
     y_port, y_factor, y_back, y_rest = call(row_kernel, (shaped(PLANES * PORT, COLS), lines, lines, lines))(
         flat, smooth
     )
-    pair_own = call(lambda *refs: join_kernel(1, *refs), port)(z_port, near)
-    flat_later, smooth_later, pair_own = lax.optimization_barrier((flat, smooth, pair_own))
-    pair = lax.ppermute(pair_own, "depth", swap_perm("depth", 2))
+    ports = lax.all_to_all(y_port, "lat", 0, 0, tiled=True)
+    ends = call(row_reduced_kernel, shaped(BLOCKS, 2, COLS))(ports)
+    ends = lax.all_to_all(ends, "lat", 0, 0, tiled=True)
+    ends, smooth_later = lax.optimization_barrier((ends, smooth))
     solved_x = call(
         column_kernel,
         whole,
@@ -373,19 +383,16 @@
             pltpu.VMEM((16, 32, COLS), F32),
             pltpu.VMEM((16, 32, COLS), F32),
         ),
-    )(flat_later, smooth_later)
-    y_port, solved_x = lax.optimization_barrier((y_port, solved_x))
-    ports = lax.all_to_all(y_port, "lat", 0, 0, tiled=True)
-    ports, pair = lax.optimization_barrier((ports, pair))
-    quad_own = call(lambda *refs: join_kernel(2, *refs), port)(pair_own, pair)
-    ports, quad_own = lax.optimization_barrier((ports, quad_own))
-    quad = lax.ppermute(quad_own, "depth", swap_perm("depth", 4))
-    ends = call(row_reduced_kernel, shaped(BLOCKS, 2, COLS))(ports)
-    ends_y = lax.all_to_all(ends, "lat", 0, 0, tiled=True)
-    ends_y, quad = lax.optimization_barrier((ends_y, quad))
-    out = call(finish_kernel, whole, (pltpu.VMEM((PLANES * ROWS, COLS), F32),))(
-        ends_y, y_factor, y_back, y_rest, z_port, near, pair, quad, z_factor, z_back, z_rest, z_mid, solved_x
-    )
+    )(flat, smooth_later)
+    others = call(finish_row_kernel, whole)(ends, y_factor, y_back, y_rest, solved_x)
+    spec = pl.BlockSpec(memory_space=pltpu.VMEM)
+    blocks = lax.axis_size("depth")
+    out = call(
+        finish_plane_kernel,
+        whole,
+        (pltpu.VMEM((blocks, 5 * ROWS, COLS), F32), pltpu.SemaphoreType.DMA),
+        in_specs=[spec, pl.BlockSpec(memory_space=pl.ANY)] + [spec] * 5,
+    )(z_port, gathered.reshape(blocks, GATHER, COLS), z_factor, z_back, z_rest, z_mid, others)
     return out.reshape(PLANES, ROWS, COLS)
 
 

time: 55.9 us -> 68.3 us (1.22)
  blocking collectives: 0 us -> 38.4 us
  waiting for transfers between devices: 24.1 us -> 3.21 us
  starting transfers between devices: 26.4 us -> 6.38 us
  between operations: 0.13 us -> 13.5 us
  local copies, waits for them, and re-layouts: 0.96 us -> 2.17 us
    all_to_all x0 -> x2, blocking collectives: none -> 38.4 us  [the longest x1 25.1 us: shards(): ports = lax.all_to_all(y_port, 'lat', 0, 0, tiled=True)]
    all_to_all x2 -> x0, starting transfers between devices: 15 us -> none  [the longest x1 11.2 us: shards(): ports = lax.all_to_all(y_port, 'lat', 0, 0, tiled=True)]
    all_to_all x2 -> x0, waiting for transfers between devices: 10.9 us -> none  [the longest x1 6.67 us: shards(): ports = lax.all_to_all(y_port, 'lat', 0, 0, tiled=True)]
    ppermute x5 -> x2, waiting for transfers between devices: 11.8 us -> 1.76 us  [the longest x1 1.76 us: shards(): pair_row = lax.ppermute(to_pair, 'lat', swap_perm('lat', 1))]
    ppermute x5 -> x2, starting transfers between devices: 7.13 us -> 2.1 us  [the longest x1 1.45 us: shards(): pair_row = lax.ppermute(to_pair, 'lat', swap_perm('lat', 1))]
    pallas_call x4 -> x3, Pallas kernels: 1.27 us -> 2.99 us  [the longest x1 1.82 us: shards(): call(finish_plane_kernel, whole, (pltpu.VMEM((blocks, 5 * ROWS, COLS), F3...]
    unnamed x4 -> x6, local copies, waits for them, and re-layouts: 0.96 us -> 2.17 us
    pallas_call x1, Pallas kernels: 1 us -> 0.26 us  [shards(): call(row_kernel, (shaped(PLANES * PORT, COLS), lines, lines, lines))]
  transfers between devices with their start and end apart: 9 -> 5, of which waited for: 8 -> 2; matrix products, arithmetic and copies ran while one was open for 0% -> 0% of each run, Pallas kernels for 2% -> 2%
where the time goes in v12:
time: 68.3 us; the launch traced here: 68 us
  blocking collectives  38.4 us (56%)
  between operations  13.5 us (20%)
  starting transfers between devices  6.38 us (9%)
  Pallas kernels  4.34 us (6%)
  waiting for transfers between devices  3.21 us (5%)
  local copies, waits for them, and re-layouts  2.17 us (3%)
    all_to_all x1, blocking collectives, shards(): ports = lax.all_to_all(y_port, 'lat', 0, 0, tiled=True)  25.1 us
    all_to_all x1, blocking collectives, shards(): ends = lax.all_to_all(ends, 'lat', 0, 0, tiled=True)  13.4 us
    ppermute x1, starting transfers between devices, shards(): far_side = lax.ppermute(to_far, 'depth', next_perm('depth'))  4.18 us
    unnamed x6, local copies, waits for them, and re-layouts  2.17 us
    pallas_call x1, Pallas kernels, shards(): call(finish_plane_kernel, whole, (pltpu.VMEM((blocks, 5 * ROWS, COLS), F3...  1.82 us
    ppermute x1, waiting for transfers between devices, shards(): pair_row = lax.ppermute(to_pair, 'lat', swap_perm('lat', 1))  1.76 us
    ppermute x1, starting transfers between devices, shards(): pair_row = lax.ppermute(to_pair, 'lat', swap_perm('lat', 1))  1.45 us
    ppermute x1, waiting for transfers between devices, shards(): far_side = lax.ppermute(to_far, 'depth', next_perm('depth'))  1.41 us
  transfers between devices with their start and end apart: 5, of which 2 were waited for; matrix products, arithmetic and copies ran while one was open for 0% of the time, Pallas kernels for 2%

profile of v12, /device:TPU:8, one launch (start us, length us, event | category | flops | bytes accessed | tf_op | source)
XLA Modules:
  0.0 68.0 jit_solution(18319029694400119430)
XLA Ops:
  6.5 0.0 all-gather.2.cloned.1.call-start
  6.5 0.0 copy-start
  6.5 0.9 %copy-done = f32[32,16,128]{2,1,0:T(8,128)S(1)} copy-done((f32[32,16,128]{2,1,0:T(8,128)S(1)}, f32[32,16,128]{2,1,0:T(8,128)}, u32[]{:S(2)}) %copy-start) | copy-done | bytes 262168
  7.5 0.1 collective-permute-start
  7.6 4.2 %collective-permute-start.1 = (f32[32,128]{1,0:T(8,128)S(1)}, f32[32,128]{1,0:T(8,128)S(1)}, u32[]{:S(2)}, u32[]{:S(2)}) collective-permute-start(f32[32,128]{1,0:T(8,128)S(1)} %get-tuple-element.23), channel_id=1, source_target_pairs={{32,64},{64,32},{96,128},{128,96},{160,192},{192,160},{33,65},{65,... | collective-permute-start | bytes 49160 | tf_op jit(solution)/shard_map/ppermute | solution.py:358
  11.8 0.0 collective-permute-done.near_side
  11.8 1.4 %collective-permute-done.1.far_side = f32[32,128]{1,0:T(8,128)S(1)} collective-permute-done((f32[32,128]{1,0:T(8,128)S(1)}, f32[32,128]{1,0:T(8,128)S(1)}, u32[]{:S(2)}, u32[]{:S(2)}) %collective-permute-start.1) | collective-permute-done | bytes 16416 | tf_op jit(solution)/shard_map/ppermute | solution.py:358
  13.2 0.2 shard_map.18
  13.5 1.4 %collective-permute-start.2 = (f32[33,128]{1,0:T(8,128)S(1)}, f32[33,128]{1,0:T(8,128)S(1)}, u32[]{:S(2)}, u32[]{:S(2)}) collective-permute-start(f32[33,128]{1,0:T(8,128)S(1)} %get-tuple-element.25), channel_id=1, source_target_pairs={{0,1},{1,0},{2,3},{3,2},{4,5},{5,4},{6,7},{7,6},{8,9},{9,8},{10,11... | collective-permute-start | bytes 50696 | tf_op jit(solution)/shard_map/ppermute | solution.py:364
  14.9 0.7 collective-permute-start.3
  15.6 1.8 %collective-permute-done.2.pair_row = f32[33,128]{1,0:T(8,128)S(1)} collective-permute-done((f32[33,128]{1,0:T(8,128)S(1)}, f32[33,128]{1,0:T(8,128)S(1)}, u32[]{:S(2)}, u32[]{:S(2)}) %collective-permute-start.2) | collective-permute-done | bytes 16928 | tf_op jit(solution)/shard_map/ppermute | solution.py:364
  17.3 0.0 collective-permute-done.3.next_row
  17.4 0.0 copy-start.1
  17.4 1.0 %shard_map.19 = (f32[256,128]{1,0:T(8,128)}, f32[512,128]{1,0:T(8,128)S(1)}, f32[512,128]{1,0:T(8,128)S(1)}, f32[512,128]{1,0:T(8,128)S(1)}, f32[3,16,128]{2,1,0:T(8,128)S(1)}, /*index=5*/f32[528,128]{1,0:T(8,128)S(1)}) custom-call(f32[512,128]{1,0:T(8,128)S(1)} %bitcast.7, f32[528,128]{1,0:T(8,128)S(1)} %get-tuple-element.24.deep, ...), custom_call_target="tpu_custom_call" | custom-call | flops 1000000 | bytes 500000 | tf_op jit(solution)/shard_map/pallas_call | solution.py:365
  18.3 0.0 all-gather.2.cloned.1.call-update
  18.4 0.0 copy-done.1
  18.4 0.3 shard_map.20
  18.6 25.1 %all_to_all.16 = f32[32,8,128]{2,1,0:T(8,128)S(1)} all-to-all(f32[32,8,128]{2,1,0:T(8,128)S(1)} %bitcast.12), channel_id=1, replica_groups=mesh['depth'=8,'lat'=32] {'lat'}, dimensions={0} | all-to-all | bytes 262144 | tf_op jit(solution)/shard_map/all_to_all | solution.py:372
  43.7 0.1 shard_map.21
  43.9 13.4 %all_to_all.17.ends = f32[32,2,128]{2,1,0:T(2,128)S(1)} all-to-all(f32[32,2,128]{2,1,0:T(2,128)S(1)} %shard_map.21), channel_id=1, replica_groups=mesh['depth'=8,'lat'=32] {'lat'}, dimensions={0} | all-to-all | bytes 65536 | tf_op jit(solution)/shard_map/all_to_all | solution.py:374
  57.2 0.7 shard_map.22.solved_x
  57.9 0.2 shard_map.23.others
  58.1 0.0 all-gather.2.cloned.1.call-done
  58.1 0.0 copy-start.2
  58.1 1.2 %copy-done.2 = f32[2048,128]{1,0:T(8,128)S(1)} copy-done((f32[2048,128]{1,0:T(8,128)S(1)}, f32[2048,128]{1,0:T(8,128)}, u32[]{:S(2)}) %copy-start.2) | copy-done | bytes 1048600
  59.4 1.8 %shard_map.24 = f32[512,128]{1,0:T(8,128)} custom-call(f32[256,128]{1,0:T(8,128)} %get-tuple-element.27.own, f32[8,256,128]{2,1,0:T(8,128)S(1)} %bitcast.10, f32[512,128]{1,0:T(8,128)S(1)} %get-tuple-element.28.factor, f32[512,128]{1,0:T(8,128)S(1)} %get-tuple-element.29.back, f32[512,128]{1,0:T(8,128)S(1)} %get-tuple-element.30.rest, ...), custom_call_target="tpu_custom_call" | custom-call | flops 1000000 | bytes 500000 | tf_op jit(solution)/shard_map/pallas_call | solution.py:390
  (1 shorter events, 0.0 us)
Async XLA Ops:
  6.5 51.6 %all-gather.2.cloned.1.call-start = ((), (), s32[]{:S(2)}) async-start(), calls=%async_computation.2 | async-start | bytes 1179648 | tf_op jit(solution)/shard_map/all_gather | solution.py:368
  6.5 0.9 %copy-start = (f32[32,16,128]{2,1,0:T(8,128)S(1)}, f32[32,16,128]{2,1,0:T(8,128)}, u32[]{:S(2)}) copy-start(f32[32,16,128]{2,1,0:T(8,128)} %param.1) | copy-start | bytes 786436
  7.5 4.3 %collective-permute-start = (f32[32,128]{1,0:T(8,128)S(1)}, f32[32,128]{1,0:T(8,128)S(1)}, u32[]{:S(2)}, u32[]{:S(2)}) collective-permute-start(f32[32,128]{1,0:T(8,128)S(1)} %get-tuple-element.22), channel_id=1, source_target_pairs={{0,32},{32,0},{64,96},{96,64},{128,160},{160,128},{192,224},{224,1... | collective-permute-start | bytes 49160 | tf_op jit(solution)/shard_map/ppermute | solution.py:359
  7.6 5.6 %collective-permute-start.1 = (f32[32,128]{1,0:T(8,128)S(1)}, f32[32,128]{1,0:T(8,128)S(1)}, u32[]{:S(2)}, u32[]{:S(2)}) collective-permute-start(f32[32,128]{1,0:T(8,128)S(1)} %get-tuple-element.23), channel_id=1, source_target_pairs={{32,64},{64,32},{96,128},{128,96},{160,192},{192,160},{33,65},{65,... | collective-permute-start | bytes 49160 | tf_op jit(solution)/shard_map/ppermute | solution.py:358
  13.5 3.9 %collective-permute-start.2 = (f32[33,128]{1,0:T(8,128)S(1)}, f32[33,128]{1,0:T(8,128)S(1)}, u32[]{:S(2)}, u32[]{:S(2)}) collective-permute-start(f32[33,128]{1,0:T(8,128)S(1)} %get-tuple-element.25), channel_id=1, source_target_pairs={{0,1},{1,0},{2,3},{3,2},{4,5},{5,4},{6,7},{7,6},{8,9},{9,8},{10,11... | collective-permute-start | bytes 50696 | tf_op jit(solution)/shard_map/ppermute | solution.py:364
  14.9 2.4 %collective-permute-start.3 = (f32[33,128]{1,0:T(8,128)S(1)}, f32[33,128]{1,0:T(8,128)S(1)}, u32[]{:S(2)}, u32[]{:S(2)}) collective-permute-start(f32[33,128]{1,0:T(8,128)S(1)} %get-tuple-element.26), channel_id=1, source_target_pairs={{1,2},{2,1},{3,4},{4,3},{5,6},{6,5},{7,8},{8,7},{9,10},{10,9},{11,... | collective-permute-start | bytes 50696 | tf_op jit(solution)/shard_map/ppermute | solution.py:363
  17.4 1.0 %copy-start.1 = (f32[32,16,128]{2,1,0:T(8,128)S(1)}, f32[32,16,128]{2,1,0:T(8,128)}, u32[]{:S(2)}) copy-start(f32[32,16,128]{2,1,0:T(8,128)} %param.1) | copy-start | bytes 786436
  58.1 1.2 %copy-start.2 = (f32[2048,128]{1,0:T(8,128)S(1)}, f32[2048,128]{1,0:T(8,128)}, u32[]{:S(2)}) copy-start(f32[2048,128]{1,0:T(8,128)} %all-gather.2.cloned.1.call-done) | copy-start | bytes 3145732
Sparse Core Ops, SparseCore 0:
  18.5 30.8 all-gather.1

commit v13 on v6

--- a/solution.py
+++ b/solution.py
@@ -86,26 +86,28 @@
     return ref[plane * ROWS : (plane + 1) * ROWS, :]
 
 
-def deep_kernel(vol, near_side, far_side, deep, pair_row, next_row, mixed):
+def faces(near_side, far_side):
     odd = (lax.axis_index("depth") & 1) == 1
-    lane = lax.broadcasted_iota(jnp.int32, (ROWS, COLS), 1)
-    first, last = lane == 0, lane == COLS - 1
-    mixed[0] = smooth_lanes(jnp.where(odd, cells(near_side, 1), cells(far_side, 1)), first, last)
-    for plane in range(PLANES):
-        mixed[plane + 1] = smooth_lanes(cells(vol, plane), first, last)
-    for plane in range(2):
-        mixed[PLANES + 1 + plane] = smooth_lanes(
-            jnp.where(odd, cells(far_side, plane), cells(near_side, plane)), first, last
+    near, far = near_side[...], far_side[...]
+    return jnp.where(odd, near, far)[ROWS:, :], jnp.where(odd, far, near)
+
+
+def side_kernel(vol, near_side, far_side, pair_row, next_row, low_side, high_side):
+    odd_row = (lax.axis_index("lat") & 1) == 1
+    below, above = faces(near_side, far_side)
+    lane = lax.broadcasted_iota(jnp.int32, (PLANES + 3, COLS), 1)
+    sides = []
+    for row, ref in ((0, low_side), (ROWS - 1, high_side)):
+        ref[0:1, :] = below[row : row + 1, :]
+        ref[1 : PLANES + 1, :] = vol[pl.ds(row, PLANES, stride=ROWS), :]
+        ref[PLANES + 1 : PLANES + 2, :] = above[row : row + 1, :]
+        ref[PLANES + 2 : PLANES + 3, :] = above[ROWS + row : ROWS + row + 1, :]
+        ref[0 : PLANES + 3, :] = smooth_lanes(ref[0 : PLANES + 3, :], lane == 0, lane == COLS - 1)
+        sides.append(
+            0.25 * (ref[0 : PLANES + 1, :] + 2.0 * ref[1 : PLANES + 2, :] + ref[2 : PLANES + 3, :])
         )
-    for plane in range(PLANES + 1):
-        deep[plane * ROWS : (plane + 1) * ROWS, :] = 0.25 * (
-            mixed[plane] + 2.0 * mixed[plane + 1] + mixed[plane + 2]
-        )
-    odd_row = (lax.axis_index("lat") & 1) == 1
-    low = deep[pl.ds(0, PLANES + 1, stride=ROWS), :]
-    high = deep[pl.ds(ROWS - 1, PLANES + 1, stride=ROWS), :]
-    pair_row[...] = jnp.where(odd_row, low, high)
-    next_row[...] = jnp.where(odd_row, high, low)
+    pair_row[...] = jnp.where(odd_row, sides[0], sides[1])
+    next_row[...] = jnp.where(odd_row, sides[1], sides[0])
 
 
 def plane_kernel(vol, deep, pair_row, next_row, port, factor, back, rest, mid, smooth):
@@ -152,7 +154,19 @@
         mid[place] = value
 
 
-def row_kernel(vol, deep, port, factor, back, rest):
+def row_kernel(vol, near_side, far_side, port, factor, back, rest, inner, deep, mixed):
+    below, above = faces(near_side, far_side)
+    lane = lax.broadcasted_iota(jnp.int32, (ROWS, COLS), 1)
+    first, last = lane == 0, lane == COLS - 1
+    mixed[0] = smooth_lanes(below, first, last)
+    for plane in range(PLANES):
+        mixed[plane + 1] = smooth_lanes(cells(vol, plane), first, last)
+    for plane in range(2):
+        mixed[PLANES + 1 + plane] = smooth_lanes(above[plane * ROWS : (plane + 1) * ROWS, :], first, last)
+    for plane in range(PLANES + 1):
+        deep[plane * ROWS : (plane + 1) * ROWS, :] = 0.25 * (
+            mixed[plane] + 2.0 * mixed[plane + 1] + mixed[plane + 2]
+        )
     part = [strided(deep, row) for row in range(ROWS)]
     low_sum = 2.0 * part[0] + part[1]
     high_sum = part[ROWS - 2] + 2.0 * part[ROWS - 1]
@@ -172,6 +186,8 @@
     )
     for place, value in enumerate(values):
         port[pl.ds(place, PLANES, stride=PORT), :] = value
+    for place in range(5):
+        inner[place] = values[place]
     for place in range(len(values), PORT):
         port[pl.ds(place, PLANES, stride=PORT), :] = jnp.zeros((PLANES, COLS), F32)
 
@@ -251,7 +267,7 @@
     across = jnp.where(block_last, 0.0, 1.0 / resistance(across))
     zero = jnp.zeros_like(coupling)
     one = jnp.ones_like(coupling)
-    before, at_low = join(
+    before, _ = join(
         (enter, one, zero, low_cell, zero), (coupling, near_ground, far_ground, near_source, far_source)
     )
     after, at_high = join((leave, zero, one, zero, high_cell), (across, zero, zero, zero, zero))
@@ -262,11 +278,8 @@
     def middle(weights, left, right):
         return weights[0] * left + weights[1] * right + weights[2]
 
-    inner_high = middle(between, first, later)
     out[:, 0, :] = first
-    out[:, 1, :] = middle(at_low, first, inner_high)
-    out[:, 2, :] = inner_high
-    out[:, 3, :] = middle(at_high, inner_high, later)
+    out[:, 1, :] = middle(at_high, middle(between, first, later), later)
 
 
 def pick(flag, there, here):
@@ -283,7 +296,7 @@
 
 
 def finish_plane_kernel(
-    own, near, pair, quad, factor, back, rest, mid, solved_x, out,
+    own, near, pair, quad, factor, back, rest, mid, solved_x, inner, smooth, out, ends,
 ):
     index = lax.axis_index("depth")
     zero = jnp.zeros((ROWS, COLS), F32)
@@ -317,19 +330,34 @@
             out[span, :] = solved_x[span, :] + value
         span = slice(start * ROWS, (start + 1) * ROWS)
         out[span, :] = solved_x[span, :] + near_value
-
-
-def finish_row_kernel(ends, factor, back, rest, others, out):
+    coupling, near_ground, far_ground, near_source, far_source = (inner[place] for place in range(5))
+    enter = 1.0 / resistance(strided(smooth, 1) - strided(smooth, 0))
+    leave = 1.0 / resistance(strided(smooth, ROWS - 1) - strided(smooth, ROWS - 2))
+    inverse = 1.0 / (enter + near_ground + coupling)
+    to_low, to_high, at_low = enter * inverse, coupling * inverse, near_source * inverse
+    total = 1.0 / (leave + far_ground + to_high * (enter + near_ground))
+    values = (
+        to_low, to_high, at_low,
+        coupling * to_low * total, leave * total, (far_source + coupling * at_low) * total,
+    )
+    for place, value in enumerate(values):
+        ends[place] = value
+
+
+def finish_row_kernel(solved, ends, factor, back, rest, others, out):
     third = 1.0 / 3.0
 
     def put(row, value):
         place = pl.ds(row, PLANES, stride=ROWS)
         out[place, :] = (others[place, :] + value) * third
 
-    for place, row in ((0, 0), (1, 1), (2, ROWS - 2), (3, ROWS - 1)):
-        put(row, ends[:, place, :])
-    first = ends[:, 1, :]
-    value = ends[:, 2, :]
+    low, high = solved[:, 0, :], solved[:, 1, :]
+    value = ends[3] * low + (ends[4] * high + ends[5])
+    first = ends[0] * low + (ends[1] * value + ends[2])
+    put(0, low)
+    put(1, first)
+    put(ROWS - 2, value)
+    put(ROWS - 1, high)
     for row in range(ROWS - 3, 1, -1):
         value = factor[row] * value + (back[row] * first + rest[row])
         put(row, value)
@@ -383,17 +411,19 @@
     )(flat)
     far_side = lax.ppermute(to_far, "depth", next_perm("depth"))
     near_side = lax.ppermute(to_near, "depth", swap_perm("depth", 1))
-    deep, to_pair, to_next = call(
-        deep_kernel, (tall, side, side), (pltpu.VMEM((PLANES + 3, ROWS, COLS), F32),)
+    to_pair, to_next = call(
+        side_kernel, (side, side), (pltpu.VMEM((40, COLS), F32), pltpu.VMEM((40, COLS), F32))
     )(flat, near_side, far_side)
     next_row = lax.ppermute(to_next, "lat", next_perm("lat"))
     pair_row = lax.ppermute(to_pair, "lat", swap_perm("lat", 1))
-    y_port, y_factor, y_back, y_rest = call(row_kernel, (shaped(PLANES * PORT, COLS), lines, lines, lines))(
-        flat, deep
-    )
+    y_port, y_factor, y_back, y_rest, y_inner, deep = call(
+        row_kernel,
+        (shaped(PLANES * PORT, COLS), lines, lines, lines, shaped(5, PLANES, COLS), tall),
+        (pltpu.VMEM((PLANES + 3, ROWS, COLS), F32),),
+    )(flat, near_side, far_side)
     ports = lax.all_to_all(y_port, "lat", 0, 0, tiled=True)
     z_port, z_factor, z_back, z_rest, z_mid, smooth = call(
-        plane_kernel, (port, whole, whole, whole, shaped(3, ROWS, COLS), tall), moved=500000,flops=LONG
+        plane_kernel, (port, whole, whole, whole, shaped(3, ROWS, COLS), tall), flops=LONG
     )(flat, deep, pair_row, next_row)
     near = lax.ppermute(z_port, "depth", swap_perm("depth", 1))
     solved_x = call(
@@ -411,14 +441,14 @@
     pair = lax.ppermute(pair_own, "depth", swap_perm("depth", 2))
     quad_own = call(lambda *refs: join_kernel(2, *refs), port)(pair_own, pair)
     ports, quad_own, solved_x = lax.optimization_barrier((ports, quad_own, solved_x))
-    ends = call(row_reduced_kernel, shaped(BLOCKS, 4, COLS))(ports)
+    ends = call(row_reduced_kernel, shaped(BLOCKS, 2, COLS))(ports)
     ends, quad_own = lax.optimization_barrier((ends, quad_own))
-    quad = lax.ppermute(quad_own, "depth", swap_perm("depth", 4))
-    others = call(finish_plane_kernel, whole)(
-        z_port, near, pair, quad, z_factor, z_back, z_rest, z_mid, solved_x
+    quad = lax.ppermute(quad_own, "depth", swap_perm("depth", 6))
+    others, y_ends = call(finish_plane_kernel, (whole, shaped(6, PLANES, COLS)))(
+        z_port, near, pair, quad, z_factor, z_back, z_rest, z_mid, solved_x, y_inner, smooth
     )
     ends_y = lax.all_to_all(ends, "lat", 0, 0, tiled=True)
-    out = call(finish_row_kernel, whole)(ends_y, y_factor, y_back, y_rest, others)
+    out = call(finish_row_kernel, whole)(ends_y, y_ends, y_factor, y_back, y_rest, others)
     return out.reshape(PLANES, ROWS, COLS)
 
 

time: 51.6 us -> 51.5 us (level)
  waiting for transfers between devices: 21.5 us -> 20.8 us
  starting transfers between devices: 24.4 us -> 25 us
    ppermute x1, waiting for transfers between devices: 4.56 us -> 2.43 us  [shards(): quad = lax.ppermute(quad_own, 'depth', swap_perm('depth', 6))]
    all_to_all x1, waiting for transfers between devices: 4.33 us -> 5.72 us  [shards(): ends_y = lax.all_to_all(ends, 'lat', 0, 0, tiled=True)]
    ppermute x1, starting transfers between devices: 1.04 us -> 1.66 us  [shards(): quad = lax.ppermute(quad_own, 'depth', swap_perm('depth', 6))]
  transfers between devices with their start and end apart: 9 -> 9, of which waited for: 6 -> 6; matrix products, arithmetic and copies ran while one was open for 0% -> 0% of each run, Pallas kernels for 4% -> 5%
where the time goes in v13:
time: 51.5 us; the launch traced here: 51.2 us
  starting transfers between devices  25 us (49%)
  waiting for transfers between devices  20.8 us (40%)
  Pallas kernels  4.31 us (8%)
  local copies, waits for them, and re-layouts  0.95 us (2%)
    all_to_all x1, starting transfers between devices, shards(): ports = lax.all_to_all(y_port, 'lat', 0, 0, tiled=True)  12.4 us
    all_to_all x1, waiting for transfers between devices, shards(): ports = lax.all_to_all(y_port, 'lat', 0, 0, tiled=True)  6.7 us
    all_to_all x1, waiting for transfers between devices, shards(): ends_y = lax.all_to_all(ends, 'lat', 0, 0, tiled=True)  5.72 us
    all_to_all x1, starting transfers between devices, shards(): ends_y = lax.all_to_all(ends, 'lat', 0, 0, tiled=True)  4.44 us
    ppermute x1, starting transfers between devices, shards(): far_side = lax.ppermute(to_far, 'depth', next_perm('depth'))  4.18 us
    ppermute x1, waiting for transfers between devices, shards(): pair = lax.ppermute(pair_own, 'depth', swap_perm('depth', 2))  3.3 us
    ppermute x1, waiting for transfers between devices, shards(): quad = lax.ppermute(quad_own, 'depth', swap_perm('depth', 6))  2.43 us
    ppermute x1, starting transfers between devices, shards(): quad = lax.ppermute(quad_own, 'depth', swap_perm('depth', 6))  1.66 us
  transfers between devices with their start and end apart: 9, of which 6 were waited for; matrix products, arithmetic and copies ran while one was open for 0% of the time, Pallas kernels for 5%

profile of v13, /device:TPU:8, one launch (start us, length us, event | category | flops | bytes accessed | tf_op | source)
XLA Modules:
  0.0 51.2 jit_solution(6745017892365857203)
XLA Ops:
  0.0 0.0 copy-start
  0.0 0.9 %copy-done = f32[32,16,128]{2,1,0:T(8,128)S(1)} copy-done((f32[32,16,128]{2,1,0:T(8,128)S(1)}, f32[32,16,128]{2,1,0:T(8,128)}, u32[]{:S(2)}) %copy-start) | copy-done | bytes 262168
  1.0 0.1 collective-permute-start
  1.1 4.2 %collective-permute-start.1 = (f32[32,128]{1,0:T(8,128)S(1)}, f32[32,128]{1,0:T(8,128)S(1)}, u32[]{:S(2)}, u32[]{:S(2)}) collective-permute-start(f32[32,128]{1,0:T(8,128)S(1)} %get-tuple-element.29), channel_id=1, source_target_pairs={{32,64},{64,32},{96,128},{128,96},{160,192},{192,160},{33,65},{65,... | collective-permute-start | bytes 49160 | tf_op jit(solution)/shard_map/ppermute | solution.py:412
  5.3 0.0 collective-permute-done.near_side
  5.3 1.4 %collective-permute-done.1.far_side = f32[32,128]{1,0:T(8,128)S(1)} collective-permute-done((f32[32,128]{1,0:T(8,128)S(1)}, f32[32,128]{1,0:T(8,128)S(1)}, u32[]{:S(2)}, u32[]{:S(2)}) %collective-permute-start.1) | collective-permute-done | bytes 16416 | tf_op jit(solution)/shard_map/ppermute | solution.py:412
  6.7 0.1 shard_map.19
  6.8 1.4 %collective-permute-start.2 = (f32[33,128]{1,0:T(8,128)S(1)}, f32[33,128]{1,0:T(8,128)S(1)}, u32[]{:S(2)}, u32[]{:S(2)}) collective-permute-start(f32[33,128]{1,0:T(8,128)S(1)} %get-tuple-element.32), channel_id=1, source_target_pairs={{0,1},{1,0},{2,3},{3,2},{4,5},{5,4},{6,7},{7,6},{8,9},{9,8},{10,11... | collective-permute-start | bytes 50696 | tf_op jit(solution)/shard_map/ppermute | solution.py:418
  8.3 0.7 %collective-permute-start.3 = (f32[33,128]{1,0:T(8,128)S(1)}, f32[33,128]{1,0:T(8,128)S(1)}, u32[]{:S(2)}, u32[]{:S(2)}) collective-permute-start(f32[33,128]{1,0:T(8,128)S(1)} %get-tuple-element.33), channel_id=1, source_target_pairs={{1,2},{2,1},{3,4},{4,3},{5,6},{6,5},{7,8},{8,7},{9,10},{10,9},{11,... | collective-permute-start | bytes 50696 | tf_op jit(solution)/shard_map/ppermute | solution.py:417
  8.9 1.3 %shard_map.18 = (f32[512,128]{1,0:T(8,128)}, f32[16,32,128]{2,1,0:T(8,128)S(1)}, f32[16,32,128]{2,1,0:T(8,128)S(1)}, f32[16,32,128]{2,1,0:T(8,128)S(1)}, f32[5,3...) custom-call(f32[512,128]{1,0:T(8,128)S(1)} %bitcast.6, f32[32,128]{1,0:T(8,128)S(1)} %collective-permute-done.near_side, ...), custom_call_target="tpu_custom_call" | custom-call | flops 1000000 | bytes 500000 | tf_op jit(solution)/shard_map/pallas_call | solution.py:419
  10.2 0.0 copy-start.1
  10.2 12.4 %all-to-all-start = ((f32[32,16,128]{2,1,0:T(8,128)}), f32[32,16,128]{2,1,0:T(8,128)S(1)}, u32[]{:S(2)}, u32[]{:S(2)}) async-start(f32[32,16,128]{2,1,0:T(8,128)} %bitcast.1), calls=%async_computation | async-start | bytes 524288 | tf_op jit(solution)/shard_map/all_to_all | solution.py:424
  22.6 0.0 collective-permute-done.2.pair_row
  22.6 0.0 collective-permute-done.3.next_row
  22.6 0.0 copy-done.1
  22.6 0.3 shard_map.20
  23.0 0.1 collective-permute-start.4
  23.1 1.2 %collective-permute-done.4.refs_1_.near = f32[5,16,128]{2,1,0:T(8,128)S(1)} collective-permute-done((f32[5,16,128]{2,1,0:T(8,128)S(1)}, f32[5,16,128]{2,1,0:T(8,128)S(1)}, u32[]{:S(2)}, u32[]{:S(2)}) %collective-permute-start.4) | collective-permute-done | bytes 40992 | tf_op jit(solution)/shard_map/ppermute | solution.py:428
  24.3 0.1 collective-permute-start.5
  24.4 0.7 %shard_map.23.solved_x = f32[512,128]{1,0:T(8,128)S(1)} custom-call(f32[512,128]{1,0:T(8,128)S(1)} %bitcast.8, f32[528,128]{1,0:T(8,128)S(1)} %get-tuple-element.35.smooth), custom_call_target="tpu_custom_call" | custom-call | flops 1000000 | bytes 500000 | tf_op jit(solution)/shard_map/pallas_call | solution.py:429
  25.1 3.3 %collective-permute-done.5.refs_1_.pair = f32[5,16,128]{2,1,0:T(8,128)S(1)} collective-permute-done((f32[5,16,128]{2,1,0:T(8,128)S(1)}, f32[5,16,128]{2,1,0:T(8,128)S(1)}, u32[]{:S(2)}, u32[]{:S(2)}) %collective-permute-start.5) | collective-permute-done | bytes 40992 | tf_op jit(solution)/shard_map/ppermute | solution.py:441
  28.4 6.7 %all-to-all-done = f32[32,16,128]{2,1,0:T(8,128)S(1)} async-done(((f32[32,16,128]{2,1,0:T(8,128)}), f32[32,16,128]{2,1,0:T(8,128)S(1)}, u32[]{:S(2)}, u32[]{:S(2)}) %all-to-all-start) | async-done | bytes 262176 | tf_op jit(solution)/shard_map/all_to_all | solution.py:424
  35.1 0.8 %shard_map.24 = f32[32,2,128]{2,1,0:T(2,128)} custom-call(f32[512,128]{1,0:T(8,128)S(1)} %bitcast.9), custom_call_target="tpu_custom_call" | custom-call | flops 1000000 | bytes 500000 | tf_op jit(solution)/shard_map/pallas_call | solution.py:444
  35.9 4.4 %all-to-all-start.1 = ((f32[32,2,128]{2,1,0:T(2,128)}), f32[32,2,128]{2,1,0:T(2,128)S(1)}, u32[]{:S(2)}, u32[]{:S(2)}) async-start(f32[32,2,128]{2,1,0:T(2,128)} %shard_map.24), calls=%async_computation.1 | async-start | bytes 65536 | tf_op jit(solution)/shard_map/all_to_all | solution.py:450
  40.4 1.7 %collective-permute-start.6 = (f32[5,16,128]{2,1,0:T(8,128)S(1)}, f32[5,16,128]{2,1,0:T(8,128)S(1)}, u32[]{:S(2)}, u32[]{:S(2)}) collective-permute-start(f32[5,16,128]{2,1,0:T(8,128)S(1)} %shard_map.22), channel_id=1, source_target_pairs={{0,192},{32,224},{64,128},{96,160},{128,64},{160,96},{192,0},{224,... | collective-permute-start | bytes 122888 | tf_op jit(solution)/shard_map/ppermute | solution.py:446
  42.0 2.4 %collective-permute-done.6.quad = f32[5,16,128]{2,1,0:T(8,128)S(1)} collective-permute-done((f32[5,16,128]{2,1,0:T(8,128)S(1)}, f32[5,16,128]{2,1,0:T(8,128)S(1)}, u32[]{:S(2)}, u32[]{:S(2)}) %collective-permute-start.6) | collective-permute-done | bytes 40992 | tf_op jit(solution)/shard_map/ppermute | solution.py:446
  44.5 0.1 shard_map.25
  44.6 5.7 %all-to-all-done.1.solved = f32[32,2,128]{2,1,0:T(2,128)S(1)} async-done(((f32[32,2,128]{2,1,0:T(2,128)}), f32[32,2,128]{2,1,0:T(2,128)S(1)}, u32[]{:S(2)}, u32[]{:S(2)}) %all-to-all-start.1) | async-done | bytes 32800 | tf_op jit(solution)/shard_map/all_to_all | solution.py:450
  50.3 0.9 %shard_map.26 = f32[512,128]{1,0:T(8,128)} custom-call(f32[32,2,128]{2,1,0:T(2,128)S(1)} %all-to-all-done.1.solved, f32[6,32,128]{2,1,0:T(8,128)S(1)} %get-tuple-element.46.ends, f32[16,32,128]{2,1,0:T(8,128)S(1)} %get-tuple-element.47.factor, f32[16,32,128]{2,1,0:T(8,128)S(1)} %get-tuple-element.48.back, f32[16,32,128]{2,1,0:T(8,128)S(1)} %get-tuple-element.49.rest, ...), custom_call_target="tpu_custom_call" | custom-call | flops 1000000 | bytes 500000 | tf_op jit(solution)/shard_map/pallas_call | solution.py:451
  (3 shorter events, 0.1 us)
Async XLA Ops:
  0.0 0.9 %copy-start = (f32[32,16,128]{2,1,0:T(8,128)S(1)}, f32[32,16,128]{2,1,0:T(8,128)}, u32[]{:S(2)}) copy-start(f32[32,16,128]{2,1,0:T(8,128)} %param.1) | copy-start | bytes 786436
  1.0 4.3 %collective-permute-start = (f32[32,128]{1,0:T(8,128)S(1)}, f32[32,128]{1,0:T(8,128)S(1)}, u32[]{:S(2)}, u32[]{:S(2)}) collective-permute-start(f32[32,128]{1,0:T(8,128)S(1)} %get-tuple-element.28), channel_id=1, source_target_pairs={{0,32},{32,0},{64,96},{96,64},{128,160},{160,128},{192,224},{224,1... | collective-permute-start | bytes 49160 | tf_op jit(solution)/shard_map/ppermute | solution.py:413
  1.1 5.6 %collective-permute-start.1 = (f32[32,128]{1,0:T(8,128)S(1)}, f32[32,128]{1,0:T(8,128)S(1)}, u32[]{:S(2)}, u32[]{:S(2)}) collective-permute-start(f32[32,128]{1,0:T(8,128)S(1)} %get-tuple-element.29), channel_id=1, source_target_pairs={{32,64},{64,32},{96,128},{128,96},{160,192},{192,160},{33,65},{65,... | collective-permute-start | bytes 49160 | tf_op jit(solution)/shard_map/ppermute | solution.py:412
  6.8 15.8 %collective-permute-start.2 = (f32[33,128]{1,0:T(8,128)S(1)}, f32[33,128]{1,0:T(8,128)S(1)}, u32[]{:S(2)}, u32[]{:S(2)}) collective-permute-start(f32[33,128]{1,0:T(8,128)S(1)} %get-tuple-element.32), channel_id=1, source_target_pairs={{0,1},{1,0},{2,3},{3,2},{4,5},{5,4},{6,7},{7,6},{8,9},{9,8},{10,11... | collective-permute-start | bytes 50696 | tf_op jit(solution)/shard_map/ppermute | solution.py:418
  8.3 14.3 %collective-permute-start.3 = (f32[33,128]{1,0:T(8,128)S(1)}, f32[33,128]{1,0:T(8,128)S(1)}, u32[]{:S(2)}, u32[]{:S(2)}) collective-permute-start(f32[33,128]{1,0:T(8,128)S(1)} %get-tuple-element.33), channel_id=1, source_target_pairs={{1,2},{2,1},{3,4},{4,3},{5,6},{6,5},{7,8},{8,7},{9,10},{10,9},{11,... | collective-permute-start | bytes 50696 | tf_op jit(solution)/shard_map/ppermute | solution.py:417
  10.2 12.4 %copy-start.1 = (f32[32,16,128]{2,1,0:T(8,128)S(1)}, f32[32,16,128]{2,1,0:T(8,128)}, u32[]{:S(2)}) copy-start(f32[32,16,128]{2,1,0:T(8,128)} %param.1) | copy-start | bytes 786436
  10.2 24.9 %all-to-all-start = ((f32[32,16,128]{2,1,0:T(8,128)}), f32[32,16,128]{2,1,0:T(8,128)S(1)}, u32[]{:S(2)}, u32[]{:S(2)}) async-start(f32[32,16,128]{2,1,0:T(8,128)} %bitcast.1), calls=%async_computation | async-start | bytes 524288 | tf_op jit(solution)/shard_map/all_to_all | solution.py:424
  23.0 1.3 %collective-permute-start.4 = (f32[5,16,128]{2,1,0:T(8,128)S(1)}, f32[5,16,128]{2,1,0:T(8,128)S(1)}, u32[]{:S(2)}, u32[]{:S(2)}) collective-permute-start(f32[5,16,128]{2,1,0:T(8,128)S(1)} %get-tuple-element.34.refs_0_.own), channel_id=1, source_target_pairs={{0,32},{32,0},{64,96},{96,64},{128,160},{160,128},{192,224},{224,1... | collective-permute-start | bytes 122888 | tf_op jit(solution)/shard_map/ppermute | solution.py:428
  24.3 4.1 %collective-permute-start.5 = (f32[5,16,128]{2,1,0:T(8,128)S(1)}, f32[5,16,128]{2,1,0:T(8,128)S(1)}, u32[]{:S(2)}, u32[]{:S(2)}) collective-permute-start(f32[5,16,128]{2,1,0:T(8,128)S(1)} %shard_map.21.refs_0_), channel_id=1, source_target_pairs={{0,64},{32,96},{64,0},{96,32},{128,192},{160,224},{192,128},{224,1... | collective-permute-start | bytes 122888 | tf_op jit(solution)/shard_map/ppermute | solution.py:441
  35.9 14.4 %all-to-all-start.1 = ((f32[32,2,128]{2,1,0:T(2,128)}), f32[32,2,128]{2,1,0:T(2,128)S(1)}, u32[]{:S(2)}, u32[]{:S(2)}) async-start(f32[32,2,128]{2,1,0:T(2,128)} %shard_map.24), calls=%async_computation.1 | async-start | bytes 65536 | tf_op jit(solution)/shard_map/all_to_all | solution.py:450
  40.4 4.1 %collective-permute-start.6 = (f32[5,16,128]{2,1,0:T(8,128)S(1)}, f32[5,16,128]{2,1,0:T(8,128)S(1)}, u32[]{:S(2)}, u32[]{:S(2)}) collective-permute-start(f32[5,16,128]{2,1,0:T(8,128)S(1)} %shard_map.22), channel_id=1, source_target_pairs={{0,192},{32,224},{64,128},{96,160},{128,64},{160,96},{192,0},{224,... | collective-permute-start | bytes 122888 | tf_op jit(solution)/shard_map/ppermute | solution.py:446

commit v14 on v13

--- a/solution.py
+++ b/solution.py
@@ -440,13 +440,12 @@
     pair_own = call(lambda *refs: join_kernel(1, *refs), port)(z_port, near)
     pair = lax.ppermute(pair_own, "depth", swap_perm("depth", 2))
     quad_own = call(lambda *refs: join_kernel(2, *refs), port)(pair_own, pair)
-    ports, quad_own, solved_x = lax.optimization_barrier((ports, quad_own, solved_x))
-    ends = call(row_reduced_kernel, shaped(BLOCKS, 2, COLS))(ports)
-    ends, quad_own = lax.optimization_barrier((ends, quad_own))
     quad = lax.ppermute(quad_own, "depth", swap_perm("depth", 6))
     others, y_ends = call(finish_plane_kernel, (whole, shaped(6, PLANES, COLS)))(
         z_port, near, pair, quad, z_factor, z_back, z_rest, z_mid, solved_x, y_inner, smooth
     )
+    ports, others, y_ends = lax.optimization_barrier((ports, others, y_ends))
+    ends = call(row_reduced_kernel, shaped(BLOCKS, 2, COLS))(ports)
     ends_y = lax.all_to_all(ends, "lat", 0, 0, tiled=True)
     out = call(finish_row_kernel, whole)(ends_y, y_ends, y_factor, y_back, y_rest, others)
     return out.reshape(PLANES, ROWS, COLS)

time: 51.5 us -> 54.8 us (1.064)
  the two profiles are of different devices: /device:TPU:8 before, /device:TPU:24 now
where the time goes in v14:
time: 54.8 us; the launch traced here: 54.5 us
  blocking collectives  19.5 us (36%)
  starting transfers between devices  18.9 us (34%)
  waiting for transfers between devices  11.3 us (21%)
  Pallas kernels  3.7 us (7%)
  local copies, waits for them, and re-layouts  0.95 us (2%)
    all_to_all x1, blocking collectives, shards(): ends_y = lax.all_to_all(ends, 'lat', 0, 0, tiled=True)  19.5 us
    all_to_all x1, starting transfers between devices, shards(): ports = lax.all_to_all(y_port, 'lat', 0, 0, tiled=True)  12.4 us
    ppermute x1, waiting for transfers between devices, shards(): quad = lax.ppermute(quad_own, 'depth', swap_perm('depth', 6))  4.51 us
    ppermute x1, waiting for transfers between devices, shards(): pair = lax.ppermute(pair_own, 'depth', swap_perm('depth', 2))  3.26 us
    ppermute x1, starting transfers between devices, shards(): far_side = lax.ppermute(to_far, 'depth', next_perm('depth'))  2.74 us
    ppermute x1, waiting for transfers between devices, shards(): far_side = lax.ppermute(to_far, 'depth', next_perm('depth'))  2.3 us
    ppermute x1, starting transfers between devices, shards(): pair_row = lax.ppermute(to_pair, 'lat', swap_perm('lat', 1))  2 us
    pallas_call x1, Pallas kernels, shards(): call(row_kernel, (shaped(PLANES * PORT, COLS), lines, lines, lines, shape...  1.28 us
  transfers between devices with their start and end apart: 8, of which 4 were waited for; matrix products, arithmetic and copies ran while one was open for 0% of the time, Pallas kernels for 5%

profile of v14, /device:TPU:24, one launch (start us, length us, event | category | flops | bytes accessed | tf_op | source)
XLA Modules:
  0.0 54.5 jit_solution(6253184988175765903)
XLA Ops:
  0.0 0.0 copy-start
  0.0 0.9 %copy-done = f32[32,16,128]{2,1,0:T(8,128)S(1)} copy-done((f32[32,16,128]{2,1,0:T(8,128)S(1)}, f32[32,16,128]{2,1,0:T(8,128)}, u32[]{:S(2)}) %copy-start) | copy-done | bytes 262168
  1.0 0.1 collective-permute-start
  1.1 2.7 %collective-permute-start.1 = (f32[32,128]{1,0:T(8,128)S(1)}, f32[32,128]{1,0:T(8,128)S(1)}, u32[]{:S(2)}, u32[]{:S(2)}) collective-permute-start(f32[32,128]{1,0:T(8,128)S(1)} %get-tuple-element.27), channel_id=1, source_target_pairs={{32,64},{64,32},{96,128},{128,96},{160,192},{192,160},{33,65},{65,... | collective-permute-start | bytes 49160 | tf_op jit(solution)/shard_map/ppermute | solution.py:412
  3.8 0.0 collective-permute-done.near_side
  3.9 2.3 %collective-permute-done.1.far_side = f32[32,128]{1,0:T(8,128)S(1)} collective-permute-done((f32[32,128]{1,0:T(8,128)S(1)}, f32[32,128]{1,0:T(8,128)S(1)}, u32[]{:S(2)}, u32[]{:S(2)}) %collective-permute-start.1) | collective-permute-done | bytes 16416 | tf_op jit(solution)/shard_map/ppermute | solution.py:412
  6.2 0.1 shard_map.19
  6.3 2.0 %collective-permute-start.2 = (f32[33,128]{1,0:T(8,128)S(1)}, f32[33,128]{1,0:T(8,128)S(1)}, u32[]{:S(2)}, u32[]{:S(2)}) collective-permute-start(f32[33,128]{1,0:T(8,128)S(1)} %get-tuple-element.30), channel_id=1, source_target_pairs={{0,1},{1,0},{2,3},{3,2},{4,5},{5,4},{6,7},{7,6},{8,9},{9,8},{10,11... | collective-permute-start | bytes 50696 | tf_op jit(solution)/shard_map/ppermute | solution.py:418
  8.3 0.7 %collective-permute-start.3 = (f32[33,128]{1,0:T(8,128)S(1)}, f32[33,128]{1,0:T(8,128)S(1)}, u32[]{:S(2)}, u32[]{:S(2)}) collective-permute-start(f32[33,128]{1,0:T(8,128)S(1)} %get-tuple-element.31), channel_id=1, source_target_pairs={{1,2},{2,1},{3,4},{4,3},{5,6},{6,5},{7,8},{8,7},{9,10},{10,9},{11,... | collective-permute-start | bytes 50696 | tf_op jit(solution)/shard_map/ppermute | solution.py:417
  8.9 1.3 %shard_map.18 = (f32[512,128]{1,0:T(8,128)}, f32[16,32,128]{2,1,0:T(8,128)S(1)}, f32[16,32,128]{2,1,0:T(8,128)S(1)}, f32[16,32,128]{2,1,0:T(8,128)S(1)}, f32[5,3...) custom-call(f32[512,128]{1,0:T(8,128)S(1)} %bitcast.6, f32[32,128]{1,0:T(8,128)S(1)} %collective-permute-done.near_side, ...), custom_call_target="tpu_custom_call" | custom-call | flops 1000000 | bytes 500000 | tf_op jit(solution)/shard_map/pallas_call | solution.py:419
  10.2 0.0 copy-start.1
  10.2 12.4 %all-to-all-start = ((f32[32,16,128]{2,1,0:T(8,128)}), f32[32,16,128]{2,1,0:T(8,128)S(1)}, u32[]{:S(2)}, u32[]{:S(2)}) async-start(f32[32,16,128]{2,1,0:T(8,128)} %bitcast.1), calls=%async_computation | async-start | bytes 524288 | tf_op jit(solution)/shard_map/all_to_all | solution.py:424
  22.6 0.0 collective-permute-done.2.pair_row
  22.6 0.0 collective-permute-done.3.next_row
  22.6 0.0 copy-done.1
  22.6 0.3 shard_map.20
  23.0 0.1 collective-permute-start.4
  23.1 1.2 %collective-permute-done.4.refs_1_.near = f32[5,16,128]{2,1,0:T(8,128)S(1)} collective-permute-done((f32[5,16,128]{2,1,0:T(8,128)S(1)}, f32[5,16,128]{2,1,0:T(8,128)S(1)}, u32[]{:S(2)}, u32[]{:S(2)}) %collective-permute-start.4) | collective-permute-done | bytes 40992 | tf_op jit(solution)/shard_map/ppermute | solution.py:428
  24.3 0.8 %collective-permute-start.5 = (f32[5,16,128]{2,1,0:T(8,128)S(1)}, f32[5,16,128]{2,1,0:T(8,128)S(1)}, u32[]{:S(2)}, u32[]{:S(2)}) collective-permute-start(f32[5,16,128]{2,1,0:T(8,128)S(1)} %shard_map.21.refs_0_), channel_id=1, source_target_pairs={{0,64},{32,96},{64,0},{96,32},{128,192},{160,224},{192,128},{224,1... | collective-permute-start | bytes 122888 | tf_op jit(solution)/shard_map/ppermute | solution.py:441
  25.1 3.3 %collective-permute-done.5.refs_1_.pair = f32[5,16,128]{2,1,0:T(8,128)S(1)} collective-permute-done((f32[5,16,128]{2,1,0:T(8,128)S(1)}, f32[5,16,128]{2,1,0:T(8,128)S(1)}, u32[]{:S(2)}, u32[]{:S(2)}) %collective-permute-start.5) | collective-permute-done | bytes 40992 | tf_op jit(solution)/shard_map/ppermute | solution.py:441
  28.4 0.1 collective-permute-start.6
  28.5 0.7 %shard_map.23.solved_x = f32[512,128]{1,0:T(8,128)S(1)} custom-call(f32[512,128]{1,0:T(8,128)S(1)} %bitcast.8, f32[528,128]{1,0:T(8,128)S(1)} %get-tuple-element.37.smooth), custom_call_target="tpu_custom_call" | custom-call | flops 1000000 | bytes 500000 | tf_op jit(solution)/shard_map/pallas_call | solution.py:429
  29.2 4.5 %collective-permute-done.6.quad = f32[5,16,128]{2,1,0:T(8,128)S(1)} collective-permute-done((f32[5,16,128]{2,1,0:T(8,128)S(1)}, f32[5,16,128]{2,1,0:T(8,128)S(1)}, u32[]{:S(2)}, u32[]{:S(2)}) %collective-permute-start.6) | collective-permute-done | bytes 40992 | tf_op jit(solution)/shard_map/ppermute | solution.py:443
  33.7 0.2 shard_map.24
  33.9 0.0 all-to-all-done
  33.9 0.2 shard_map.25
  34.1 19.5 %all_to_all.17.solved = f32[32,2,128]{2,1,0:T(2,128)S(1)} all-to-all(f32[32,2,128]{2,1,0:T(2,128)S(1)} %shard_map.25), channel_id=1, replica_groups=mesh['depth'=8,'lat'=32] {'lat'}, dimensions={0} | all-to-all | bytes 65536 | tf_op jit(solution)/shard_map/all_to_all | solution.py:449
  53.6 0.9 %shard_map.26 = f32[512,128]{1,0:T(8,128)} custom-call(f32[32,2,128]{2,1,0:T(2,128)S(1)} %all_to_all.17.solved, f32[6,32,128]{2,1,0:T(8,128)S(1)} %get-tuple-element.42.ends, f32[16,32,128]{2,1,0:T(8,128)S(1)} %get-tuple-element.43.factor, f32[16,32,128]{2,1,0:T(8,128)S(1)} %get-tuple-element.44.back, f32[16,32,128]{2,1,0:T(8,128)S(1)} %get-tuple-element.45.rest, ...), custom_call_target="tpu_custom_call" | custom-call | flops 1000000 | bytes 500000 | tf_op jit(solution)/shard_map/pallas_call | solution.py:450
  (3 shorter events, 0.1 us)
Async XLA Ops:
  0.0 0.9 %copy-start = (f32[32,16,128]{2,1,0:T(8,128)S(1)}, f32[32,16,128]{2,1,0:T(8,128)}, u32[]{:S(2)}) copy-start(f32[32,16,128]{2,1,0:T(8,128)} %param.1) | copy-start | bytes 786436
  1.0 2.9 %collective-permute-start = (f32[32,128]{1,0:T(8,128)S(1)}, f32[32,128]{1,0:T(8,128)S(1)}, u32[]{:S(2)}, u32[]{:S(2)}) collective-permute-start(f32[32,128]{1,0:T(8,128)S(1)} %get-tuple-element.26), channel_id=1, source_target_pairs={{0,32},{32,0},{64,96},{96,64},{128,160},{160,128},{192,224},{224,1... | collective-permute-start | bytes 49160 | tf_op jit(solution)/shard_map/ppermute | solution.py:413
  1.1 5.1 %collective-permute-start.1 = (f32[32,128]{1,0:T(8,128)S(1)}, f32[32,128]{1,0:T(8,128)S(1)}, u32[]{:S(2)}, u32[]{:S(2)}) collective-permute-start(f32[32,128]{1,0:T(8,128)S(1)} %get-tuple-element.27), channel_id=1, source_target_pairs={{32,64},{64,32},{96,128},{128,96},{160,192},{192,160},{33,65},{65,... | collective-permute-start | bytes 49160 | tf_op jit(solution)/shard_map/ppermute | solution.py:412
  6.3 16.3 %collective-permute-start.2 = (f32[33,128]{1,0:T(8,128)S(1)}, f32[33,128]{1,0:T(8,128)S(1)}, u32[]{:S(2)}, u32[]{:S(2)}) collective-permute-start(f32[33,128]{1,0:T(8,128)S(1)} %get-tuple-element.30), channel_id=1, source_target_pairs={{0,1},{1,0},{2,3},{3,2},{4,5},{5,4},{6,7},{7,6},{8,9},{9,8},{10,11... | collective-permute-start | bytes 50696 | tf_op jit(solution)/shard_map/ppermute | solution.py:418
  8.3 14.3 %collective-permute-start.3 = (f32[33,128]{1,0:T(8,128)S(1)}, f32[33,128]{1,0:T(8,128)S(1)}, u32[]{:S(2)}, u32[]{:S(2)}) collective-permute-start(f32[33,128]{1,0:T(8,128)S(1)} %get-tuple-element.31), channel_id=1, source_target_pairs={{1,2},{2,1},{3,4},{4,3},{5,6},{6,5},{7,8},{8,7},{9,10},{10,9},{11,... | collective-permute-start | bytes 50696 | tf_op jit(solution)/shard_map/ppermute | solution.py:417
  10.2 12.4 %copy-start.1 = (f32[32,16,128]{2,1,0:T(8,128)S(1)}, f32[32,16,128]{2,1,0:T(8,128)}, u32[]{:S(2)}) copy-start(f32[32,16,128]{2,1,0:T(8,128)} %param.1) | copy-start | bytes 786436
  10.2 23.6 %all-to-all-start = ((f32[32,16,128]{2,1,0:T(8,128)}), f32[32,16,128]{2,1,0:T(8,128)S(1)}, u32[]{:S(2)}, u32[]{:S(2)}) async-start(f32[32,16,128]{2,1,0:T(8,128)} %bitcast.1), calls=%async_computation | async-start | bytes 524288 | tf_op jit(solution)/shard_map/all_to_all | solution.py:424
  23.0 1.3 %collective-permute-start.4 = (f32[5,16,128]{2,1,0:T(8,128)S(1)}, f32[5,16,128]{2,1,0:T(8,128)S(1)}, u32[]{:S(2)}, u32[]{:S(2)}) collective-permute-start(f32[5,16,128]{2,1,0:T(8,128)S(1)} %get-tuple-element.32.refs_0_.own), channel_id=1, source_target_pairs={{0,32},{32,0},{64,96},{96,64},{128,160},{160,128},{192,224},{224,1... | collective-permute-start | bytes 122888 | tf_op jit(solution)/shard_map/ppermute | solution.py:428
  24.3 4.1 %collective-permute-start.5 = (f32[5,16,128]{2,1,0:T(8,128)S(1)}, f32[5,16,128]{2,1,0:T(8,128)S(1)}, u32[]{:S(2)}, u32[]{:S(2)}) collective-permute-start(f32[5,16,128]{2,1,0:T(8,128)S(1)} %shard_map.21.refs_0_), channel_id=1, source_target_pairs={{0,64},{32,96},{64,0},{96,32},{128,192},{160,224},{192,128},{224,1... | collective-permute-start | bytes 122888 | tf_op jit(solution)/shard_map/ppermute | solution.py:441
  28.4 5.3 %collective-permute-start.6 = (f32[5,16,128]{2,1,0:T(8,128)S(1)}, f32[5,16,128]{2,1,0:T(8,128)S(1)}, u32[]{:S(2)}, u32[]{:S(2)}) collective-permute-start(f32[5,16,128]{2,1,0:T(8,128)S(1)} %shard_map.22), channel_id=1, source_target_pairs={{0,192},{32,224},{64,128},{96,160},{128,64},{160,96},{192,0},{224,... | collective-permute-start | bytes 122888 | tf_op jit(solution)/shard_map/ppermute | solution.py:443

commit v15 on v14

--- a/solution.py
+++ b/solution.py
@@ -12,7 +12,6 @@
 COLS = 128
 BLOCKS = 32
 PORT = 16
-LONG = 100_000_000_000
 F32 = jnp.float32
 
 
@@ -423,7 +422,7 @@
     )(flat, near_side, far_side)
     ports = lax.all_to_all(y_port, "lat", 0, 0, tiled=True)
     z_port, z_factor, z_back, z_rest, z_mid, smooth = call(
-        plane_kernel, (port, whole, whole, whole, shaped(3, ROWS, COLS), tall), flops=LONG
+        plane_kernel, (port, whole, whole, whole, shaped(3, ROWS, COLS), tall)
     )(flat, deep, pair_row, next_row)
     near = lax.ppermute(z_port, "depth", swap_perm("depth", 1))
     solved_x = call(
@@ -438,14 +437,15 @@
         ),
     )(flat, smooth)
     pair_own = call(lambda *refs: join_kernel(1, *refs), port)(z_port, near)
+    ports, pair_own, solved_x = lax.optimization_barrier((ports, pair_own, solved_x))
+    ends = call(row_reduced_kernel, shaped(BLOCKS, 2, COLS))(ports)
+    ends, pair_own = lax.optimization_barrier((ends, pair_own))
     pair = lax.ppermute(pair_own, "depth", swap_perm("depth", 2))
     quad_own = call(lambda *refs: join_kernel(2, *refs), port)(pair_own, pair)
     quad = lax.ppermute(quad_own, "depth", swap_perm("depth", 6))
     others, y_ends = call(finish_plane_kernel, (whole, shaped(6, PLANES, COLS)))(
         z_port, near, pair, quad, z_factor, z_back, z_rest, z_mid, solved_x, y_inner, smooth
     )
-    ports, others, y_ends = lax.optimization_barrier((ports, others, y_ends))
-    ends = call(row_reduced_kernel, shaped(BLOCKS, 2, COLS))(ports)
     ends_y = lax.all_to_all(ends, "lat", 0, 0, tiled=True)
     out = call(finish_row_kernel, whole)(ends_y, y_ends, y_factor, y_back, y_rest, others)
     return out.reshape(PLANES, ROWS, COLS)

time: 54.8 us -> 51.2 us (0.934)
  the two profiles are of different devices: /device:TPU:24 before, /device:TPU:16 now
where the time goes in v15:
time: 51.2 us; the launch traced here: 50.9 us
  starting transfers between devices  24.4 us (48%)
  waiting for transfers between devices  21.1 us (41%)
  Pallas kernels  4.33 us (8%)
  local copies, waits for them, and re-layouts  0.95 us (2%)
    all_to_all x1, starting transfers between devices, shards(): ports = lax.all_to_all(y_port, 'lat', 0, 0, tiled=True)  11.4 us
    all_to_all x1, starting transfers between devices, shards(): ends_y = lax.all_to_all(ends, 'lat', 0, 0, tiled=True)  7.65 us
    ppermute x1, waiting for transfers between devices, shards(): pair_row = lax.ppermute(to_pair, 'lat', swap_perm('lat', 1))  6.04 us
    all_to_all x1, waiting for transfers between devices, shards(): ends_y = lax.all_to_all(ends, 'lat', 0, 0, tiled=True)  5.58 us
    ppermute x1, waiting for transfers between devices, shards(): quad = lax.ppermute(quad_own, 'depth', swap_perm('depth', 6))  3.99 us
    ppermute x1, waiting for transfers between devices, shards(): far_side = lax.ppermute(to_far, 'depth', next_perm('depth'))  2.59 us
    ppermute x1, starting transfers between devices, shards(): far_side = lax.ppermute(to_far, 'depth', next_perm('depth'))  2.45 us
    all_to_all x1, waiting for transfers between devices, shards(): ports = lax.all_to_all(y_port, 'lat', 0, 0, tiled=True)  2.38 us
  transfers between devices with their start and end apart: 9, of which 6 were waited for; matrix products, arithmetic and copies ran while one was open for 0% of the time, Pallas kernels for 3%

profile of v15, /device:TPU:16, one launch (start us, length us, event | category | flops | bytes accessed | tf_op | source)
XLA Modules:
  0.0 50.9 jit_solution(3033123651839497731)
XLA Ops:
  0.0 0.0 copy-start
  0.0 0.9 %copy-done = f32[32,16,128]{2,1,0:T(8,128)S(1)} copy-done((f32[32,16,128]{2,1,0:T(8,128)S(1)}, f32[32,16,128]{2,1,0:T(8,128)}, u32[]{:S(2)}) %copy-start) | copy-done | bytes 262168
  1.0 0.1 collective-permute-start
  1.1 2.4 %collective-permute-start.1 = (f32[32,128]{1,0:T(8,128)S(1)}, f32[32,128]{1,0:T(8,128)S(1)}, u32[]{:S(2)}, u32[]{:S(2)}) collective-permute-start(f32[32,128]{1,0:T(8,128)S(1)} %get-tuple-element.29), channel_id=1, source_target_pairs={{32,64},{64,32},{96,128},{128,96},{160,192},{192,160},{33,65},{65,... | collective-permute-start | bytes 49160 | tf_op jit(solution)/shard_map/ppermute | solution.py:411
  3.5 0.0 collective-permute-done.near_side
  3.6 2.6 %collective-permute-done.1.far_side = f32[32,128]{1,0:T(8,128)S(1)} collective-permute-done((f32[32,128]{1,0:T(8,128)S(1)}, f32[32,128]{1,0:T(8,128)S(1)}, u32[]{:S(2)}, u32[]{:S(2)}) %collective-permute-start.1) | collective-permute-done | bytes 16416 | tf_op jit(solution)/shard_map/ppermute | solution.py:411
  6.2 1.3 %shard_map.18 = (f32[512,128]{1,0:T(8,128)}, f32[16,32,128]{2,1,0:T(8,128)S(1)}, f32[16,32,128]{2,1,0:T(8,128)S(1)}, f32[16,32,128]{2,1,0:T(8,128)S(1)}, f32[5,3...) custom-call(f32[512,128]{1,0:T(8,128)S(1)} %bitcast.5, f32[32,128]{1,0:T(8,128)S(1)} %collective-permute-done.near_side, ...), custom_call_target="tpu_custom_call" | custom-call | flops 1000000 | bytes 500000 | tf_op jit(solution)/shard_map/pallas_call | solution.py:418
  7.4 0.0 copy-start.1
  7.4 11.4 %all-to-all-start = ((f32[32,16,128]{2,1,0:T(8,128)}), f32[32,16,128]{2,1,0:T(8,128)S(1)}, u32[]{:S(2)}, u32[]{:S(2)}) async-start(f32[32,16,128]{2,1,0:T(8,128)} %bitcast.1), calls=%async_computation | async-start | bytes 524288 | tf_op jit(solution)/shard_map/all_to_all | solution.py:423
  18.9 0.0 copy-done.1
  18.9 0.1 shard_map.19
  19.0 1.9 %collective-permute-start.2 = (f32[33,128]{1,0:T(8,128)S(1)}, f32[33,128]{1,0:T(8,128)S(1)}, u32[]{:S(2)}, u32[]{:S(2)}) collective-permute-start(f32[33,128]{1,0:T(8,128)S(1)} %get-tuple-element.32), channel_id=1, source_target_pairs={{0,1},{1,0},{2,3},{3,2},{4,5},{5,4},{6,7},{7,6},{8,9},{9,8},{10,11... | collective-permute-start | bytes 50696 | tf_op jit(solution)/shard_map/ppermute | solution.py:417
  20.9 0.7 %collective-permute-start.3 = (f32[33,128]{1,0:T(8,128)S(1)}, f32[33,128]{1,0:T(8,128)S(1)}, u32[]{:S(2)}, u32[]{:S(2)}) collective-permute-start(f32[33,128]{1,0:T(8,128)S(1)} %get-tuple-element.33), channel_id=1, source_target_pairs={{1,2},{2,1},{3,4},{4,3},{5,6},{6,5},{7,8},{8,7},{9,10},{10,9},{11,... | collective-permute-start | bytes 50696 | tf_op jit(solution)/shard_map/ppermute | solution.py:416
  21.6 6.0 %collective-permute-done.2.pair_row = f32[33,128]{1,0:T(8,128)S(1)} collective-permute-done((f32[33,128]{1,0:T(8,128)S(1)}, f32[33,128]{1,0:T(8,128)S(1)}, u32[]{:S(2)}, u32[]{:S(2)}) %collective-permute-start.2) | collective-permute-done | bytes 16928 | tf_op jit(solution)/shard_map/ppermute | solution.py:417
  27.6 0.0 collective-permute-done.3.next_row
  27.6 0.3 shard_map.20
  27.9 0.1 collective-permute-start.4
  28.0 0.7 %shard_map.22.solved_x = f32[512,128]{1,0:T(8,128)S(1)} custom-call(f32[512,128]{1,0:T(8,128)S(1)} %bitcast.8, f32[528,128]{1,0:T(8,128)S(1)} %get-tuple-element.35.smooth), custom_call_target="tpu_custom_call" | custom-call | flops 1000000 | bytes 500000 | tf_op jit(solution)/shard_map/pallas_call | solution.py:428
  28.7 0.5 %collective-permute-done.4.refs_1_.near = f32[5,16,128]{2,1,0:T(8,128)S(1)} collective-permute-done((f32[5,16,128]{2,1,0:T(8,128)S(1)}, f32[5,16,128]{2,1,0:T(8,128)S(1)}, u32[]{:S(2)}, u32[]{:S(2)}) %collective-permute-start.4) | collective-permute-done | bytes 40992 | tf_op jit(solution)/shard_map/ppermute | solution.py:427
  29.3 2.4 %all-to-all-done = f32[32,16,128]{2,1,0:T(8,128)S(1)} async-done(((f32[32,16,128]{2,1,0:T(8,128)}), f32[32,16,128]{2,1,0:T(8,128)S(1)}, u32[]{:S(2)}, u32[]{:S(2)}) %all-to-all-start) | async-done | bytes 262176 | tf_op jit(solution)/shard_map/all_to_all | solution.py:423
  31.6 0.8 %shard_map.23 = f32[32,2,128]{2,1,0:T(2,128)} custom-call(f32[512,128]{1,0:T(8,128)S(1)} %bitcast.9), custom_call_target="tpu_custom_call" | custom-call | flops 1000000 | bytes 500000 | tf_op jit(solution)/shard_map/pallas_call | solution.py:441
  32.5 0.0 collective-permute-start.5
  32.5 7.6 %all-to-all-start.1 = ((f32[32,2,128]{2,1,0:T(2,128)}), f32[32,2,128]{2,1,0:T(2,128)S(1)}, u32[]{:S(2)}, u32[]{:S(2)}) async-start(f32[32,2,128]{2,1,0:T(2,128)} %shard_map.23), calls=%async_computation.1 | async-start | bytes 65536 | tf_op jit(solution)/shard_map/all_to_all | solution.py:449
  40.1 0.0 collective-permute-done.5.refs_1_.pair
  40.2 0.1 collective-permute-start.6
  40.3 4.0 %collective-permute-done.6.quad = f32[5,16,128]{2,1,0:T(8,128)S(1)} collective-permute-done((f32[5,16,128]{2,1,0:T(8,128)S(1)}, f32[5,16,128]{2,1,0:T(8,128)S(1)}, u32[]{:S(2)}, u32[]{:S(2)}) %collective-permute-start.6) | collective-permute-done | bytes 40992 | tf_op jit(solution)/shard_map/ppermute | solution.py:445
  44.2 0.2 shard_map.25
  44.4 5.6 %all-to-all-done.1.solved = f32[32,2,128]{2,1,0:T(2,128)S(1)} async-done(((f32[32,2,128]{2,1,0:T(2,128)}), f32[32,2,128]{2,1,0:T(2,128)S(1)}, u32[]{:S(2)}, u32[]{:S(2)}) %all-to-all-start.1) | async-done | bytes 32800 | tf_op jit(solution)/shard_map/all_to_all | solution.py:449
  50.0 0.9 %shard_map.26 = f32[512,128]{1,0:T(8,128)} custom-call(f32[32,2,128]{2,1,0:T(2,128)S(1)} %all-to-all-done.1.solved, f32[6,32,128]{2,1,0:T(8,128)S(1)} %get-tuple-element.46.ends, f32[16,32,128]{2,1,0:T(8,128)S(1)} %get-tuple-element.47.factor, f32[16,32,128]{2,1,0:T(8,128)S(1)} %get-tuple-element.48.back, f32[16,32,128]{2,1,0:T(8,128)S(1)} %get-tuple-element.49.rest, ...), custom_call_target="tpu_custom_call" | custom-call | flops 1000000 | bytes 500000 | tf_op jit(solution)/shard_map/pallas_call | solution.py:450
  (3 shorter events, 0.1 us)
Async XLA Ops:
  0.0 0.9 %copy-start = (f32[32,16,128]{2,1,0:T(8,128)S(1)}, f32[32,16,128]{2,1,0:T(8,128)}, u32[]{:S(2)}) copy-start(f32[32,16,128]{2,1,0:T(8,128)} %param.1) | copy-start | bytes 786436
  1.0 2.6 %collective-permute-start = (f32[32,128]{1,0:T(8,128)S(1)}, f32[32,128]{1,0:T(8,128)S(1)}, u32[]{:S(2)}, u32[]{:S(2)}) collective-permute-start(f32[32,128]{1,0:T(8,128)S(1)} %get-tuple-element.28), channel_id=1, source_target_pairs={{0,32},{32,0},{64,96},{96,64},{128,160},{160,128},{192,224},{224,1... | collective-permute-start | bytes 49160 | tf_op jit(solution)/shard_map/ppermute | solution.py:412
  1.1 5.1 %collective-permute-start.1 = (f32[32,128]{1,0:T(8,128)S(1)}, f32[32,128]{1,0:T(8,128)S(1)}, u32[]{:S(2)}, u32[]{:S(2)}) collective-permute-start(f32[32,128]{1,0:T(8,128)S(1)} %get-tuple-element.29), channel_id=1, source_target_pairs={{32,64},{64,32},{96,128},{128,96},{160,192},{192,160},{33,65},{65,... | collective-permute-start | bytes 49160 | tf_op jit(solution)/shard_map/ppermute | solution.py:411
  7.4 11.5 %copy-start.1 = (f32[32,16,128]{2,1,0:T(8,128)S(1)}, f32[32,16,128]{2,1,0:T(8,128)}, u32[]{:S(2)}) copy-start(f32[32,16,128]{2,1,0:T(8,128)} %param.1) | copy-start | bytes 786436
  7.4 24.2 %all-to-all-start = ((f32[32,16,128]{2,1,0:T(8,128)}), f32[32,16,128]{2,1,0:T(8,128)S(1)}, u32[]{:S(2)}, u32[]{:S(2)}) async-start(f32[32,16,128]{2,1,0:T(8,128)} %bitcast.1), calls=%async_computation | async-start | bytes 524288 | tf_op jit(solution)/shard_map/all_to_all | solution.py:423
  19.0 8.6 %collective-permute-start.2 = (f32[33,128]{1,0:T(8,128)S(1)}, f32[33,128]{1,0:T(8,128)S(1)}, u32[]{:S(2)}, u32[]{:S(2)}) collective-permute-start(f32[33,128]{1,0:T(8,128)S(1)} %get-tuple-element.32), channel_id=1, source_target_pairs={{0,1},{1,0},{2,3},{3,2},{4,5},{5,4},{6,7},{7,6},{8,9},{9,8},{10,11... | collective-permute-start | bytes 50696 | tf_op jit(solution)/shard_map/ppermute | solution.py:417
  20.9 6.7 %collective-permute-start.3 = (f32[33,128]{1,0:T(8,128)S(1)}, f32[33,128]{1,0:T(8,128)S(1)}, u32[]{:S(2)}, u32[]{:S(2)}) collective-permute-start(f32[33,128]{1,0:T(8,128)S(1)} %get-tuple-element.33), channel_id=1, source_target_pairs={{1,2},{2,1},{3,4},{4,3},{5,6},{6,5},{7,8},{8,7},{9,10},{10,9},{11,... | collective-permute-start | bytes 50696 | tf_op jit(solution)/shard_map/ppermute | solution.py:416
  27.9 1.3 %collective-permute-start.4 = (f32[5,16,128]{2,1,0:T(8,128)S(1)}, f32[5,16,128]{2,1,0:T(8,128)S(1)}, u32[]{:S(2)}, u32[]{:S(2)}) collective-permute-start(f32[5,16,128]{2,1,0:T(8,128)S(1)} %get-tuple-element.34.refs_0_.own), channel_id=1, source_target_pairs={{0,32},{32,0},{64,96},{96,64},{128,160},{160,128},{192,224},{224,1... | collective-permute-start | bytes 122888 | tf_op jit(solution)/shard_map/ppermute | solution.py:427
  32.5 7.7 %collective-permute-start.5 = (f32[5,16,128]{2,1,0:T(8,128)S(1)}, f32[5,16,128]{2,1,0:T(8,128)S(1)}, u32[]{:S(2)}, u32[]{:S(2)}) collective-permute-start(f32[5,16,128]{2,1,0:T(8,128)S(1)} %shard_map.21.refs_0_), channel_id=1, source_target_pairs={{0,64},{32,96},{64,0},{96,32},{128,192},{160,224},{192,128},{224,1... | collective-permute-start | bytes 122888 | tf_op jit(solution)/shard_map/ppermute | solution.py:443
  32.5 17.5 %all-to-all-start.1 = ((f32[32,2,128]{2,1,0:T(2,128)}), f32[32,2,128]{2,1,0:T(2,128)S(1)}, u32[]{:S(2)}, u32[]{:S(2)}) async-start(f32[32,2,128]{2,1,0:T(2,128)} %shard_map.23), calls=%async_computation.1 | async-start | bytes 65536 | tf_op jit(solution)/shard_map/all_to_all | solution.py:449
  40.2 4.1 %collective-permute-start.6 = (f32[5,16,128]{2,1,0:T(8,128)S(1)}, f32[5,16,128]{2,1,0:T(8,128)S(1)}, u32[]{:S(2)}, u32[]{:S(2)}) collective-permute-start(f32[5,16,128]{2,1,0:T(8,128)S(1)} %shard_map.24), channel_id=1, source_target_pairs={{0,192},{32,224},{64,128},{96,160},{128,64},{160,96},{192,0},{224,... | collective-permute-start | bytes 122888 | tf_op jit(solution)/shard_map/ppermute | solution.py:445

commit v16 on v15

--- a/solution.py
+++ b/solution.py
@@ -153,7 +153,7 @@
         mid[place] = value
 
 
-def row_kernel(vol, near_side, far_side, port, factor, back, rest, inner, deep, mixed):
+def row_kernel(vol, near_side, far_side, port, factor, back, rest, deep, mixed):
     below, above = faces(near_side, far_side)
     lane = lax.broadcasted_iota(jnp.int32, (ROWS, COLS), 1)
     first, last = lane == 0, lane == COLS - 1
@@ -185,8 +185,6 @@
     )
     for place, value in enumerate(values):
         port[pl.ds(place, PLANES, stride=PORT), :] = value
-    for place in range(5):
-        inner[place] = values[place]
     for place in range(len(values), PORT):
         port[pl.ds(place, PLANES, stride=PORT), :] = jnp.zeros((PLANES, COLS), F32)
 
@@ -266,7 +264,7 @@
     across = jnp.where(block_last, 0.0, 1.0 / resistance(across))
     zero = jnp.zeros_like(coupling)
     one = jnp.ones_like(coupling)
-    before, _ = join(
+    before, at_low = join(
         (enter, one, zero, low_cell, zero), (coupling, near_ground, far_ground, near_source, far_source)
     )
     after, at_high = join((leave, zero, one, zero, high_cell), (across, zero, zero, zero, zero))
@@ -278,7 +276,10 @@
         return weights[0] * left + weights[1] * right + weights[2]
 
     out[:, 0, :] = first
-    out[:, 1, :] = middle(at_high, middle(between, first, later), later)
+    inner_high = middle(between, first, later)
+    out[:, 1, :] = middle(at_low, first, inner_high)
+    out[:, 2, :] = inner_high
+    out[:, 3, :] = middle(at_high, inner_high, later)
 
 
 def pick(flag, there, here):
@@ -295,7 +296,7 @@
 
 
 def finish_plane_kernel(
-    own, near, pair, quad, factor, back, rest, mid, solved_x, inner, smooth, out, ends,
+    own, near, pair, quad, factor, back, rest, mid, solved_x, out,
 ):
     index = lax.axis_index("depth")
     zero = jnp.zeros((ROWS, COLS), F32)
@@ -329,34 +330,19 @@
             out[span, :] = solved_x[span, :] + value
         span = slice(start * ROWS, (start + 1) * ROWS)
         out[span, :] = solved_x[span, :] + near_value
-    coupling, near_ground, far_ground, near_source, far_source = (inner[place] for place in range(5))
-    enter = 1.0 / resistance(strided(smooth, 1) - strided(smooth, 0))
-    leave = 1.0 / resistance(strided(smooth, ROWS - 1) - strided(smooth, ROWS - 2))
-    inverse = 1.0 / (enter + near_ground + coupling)
-    to_low, to_high, at_low = enter * inverse, coupling * inverse, near_source * inverse
-    total = 1.0 / (leave + far_ground + to_high * (enter + near_ground))
-    values = (
-        to_low, to_high, at_low,
-        coupling * to_low * total, leave * total, (far_source + coupling * at_low) * total,
-    )
-    for place, value in enumerate(values):
-        ends[place] = value
-
-
-def finish_row_kernel(solved, ends, factor, back, rest, others, out):
+
+
+def finish_row_kernel(solved, factor, back, rest, others, out):
     third = 1.0 / 3.0
 
     def put(row, value):
         place = pl.ds(row, PLANES, stride=ROWS)
         out[place, :] = (others[place, :] + value) * third
 
-    low, high = solved[:, 0, :], solved[:, 1, :]
-    value = ends[3] * low + (ends[4] * high + ends[5])
-    first = ends[0] * low + (ends[1] * value + ends[2])
-    put(0, low)
-    put(1, first)
-    put(ROWS - 2, value)
-    put(ROWS - 1, high)
+    for place, row in ((0, 0), (1, 1), (2, ROWS - 2), (3, ROWS - 1)):
+        put(row, solved[:, place, :])
+    first = solved[:, 1, :]
+    value = solved[:, 2, :]
     for row in range(ROWS - 3, 1, -1):
         value = factor[row] * value + (back[row] * first + rest[row])
         put(row, value)
@@ -415,9 +401,9 @@
     )(flat, near_side, far_side)
     next_row = lax.ppermute(to_next, "lat", next_perm("lat"))
     pair_row = lax.ppermute(to_pair, "lat", swap_perm("lat", 1))
-    y_port, y_factor, y_back, y_rest, y_inner, deep = call(
+    y_port, y_factor, y_back, y_rest, deep = call(
         row_kernel,
-        (shaped(PLANES * PORT, COLS), lines, lines, lines, shaped(5, PLANES, COLS), tall),
+        (shaped(PLANES * PORT, COLS), lines, lines, lines, tall),
         (pltpu.VMEM((PLANES + 3, ROWS, COLS), F32),),
     )(flat, near_side, far_side)
     ports = lax.all_to_all(y_port, "lat", 0, 0, tiled=True)
@@ -438,16 +424,16 @@
     )(flat, smooth)
     pair_own = call(lambda *refs: join_kernel(1, *refs), port)(z_port, near)
     ports, pair_own, solved_x = lax.optimization_barrier((ports, pair_own, solved_x))
-    ends = call(row_reduced_kernel, shaped(BLOCKS, 2, COLS))(ports)
+    ends = call(row_reduced_kernel, shaped(BLOCKS, 4, COLS))(ports)
     ends, pair_own = lax.optimization_barrier((ends, pair_own))
     pair = lax.ppermute(pair_own, "depth", swap_perm("depth", 2))
     quad_own = call(lambda *refs: join_kernel(2, *refs), port)(pair_own, pair)
     quad = lax.ppermute(quad_own, "depth", swap_perm("depth", 6))
-    others, y_ends = call(finish_plane_kernel, (whole, shaped(6, PLANES, COLS)))(
-        z_port, near, pair, quad, z_factor, z_back, z_rest, z_mid, solved_x, y_inner, smooth
+    others = call(finish_plane_kernel, whole)(
+        z_port, near, pair, quad, z_factor, z_back, z_rest, z_mid, solved_x
     )
     ends_y = lax.all_to_all(ends, "lat", 0, 0, tiled=True)
-    out = call(finish_row_kernel, whole)(ends_y, y_ends, y_factor, y_back, y_rest, others)
+    out = call(finish_row_kernel, whole)(ends_y, y_factor, y_back, y_rest, others)
     return out.reshape(PLANES, ROWS, COLS)
 
 

time: 51.2 us -> 50.1 us (0.979)
  the two profiles are of different devices: /device:TPU:16 before, /device:TPU:8 now
where the time goes in v16:
time: 50.1 us; the launch traced here: 49.8 us
  starting transfers between devices  25.9 us (52%)
  waiting for transfers between devices  18.5 us (37%)
  Pallas kernels  4.33 us (9%)
  local copies, waits for them, and re-layouts  0.95 us (2%)
    all_to_all x1, starting transfers between devices, shards(): ports = lax.all_to_all(y_port, 'lat', 0, 0, tiled=True)  10.9 us
    all_to_all x1, starting transfers between devices, shards(): ends_y = lax.all_to_all(ends, 'lat', 0, 0, tiled=True)  6.37 us
    ppermute x1, waiting for transfers between devices, shards(): pair_row = lax.ppermute(to_pair, 'lat', swap_perm('lat', 1))  6.04 us
    ppermute x1, starting transfers between devices, shards(): far_side = lax.ppermute(to_far, 'depth', next_perm('depth'))  4.18 us
    ppermute x1, waiting for transfers between devices, shards(): pair = lax.ppermute(pair_own, 'depth', swap_perm('depth', 2))  3.99 us
    ppermute x1, waiting for transfers between devices, shards(): quad = lax.ppermute(quad_own, 'depth', swap_perm('depth', 6))  2.43 us
    all_to_all x1, waiting for transfers between devices, shards(): ports = lax.all_to_all(y_port, 'lat', 0, 0, tiled=True)  2.38 us
    ppermute x1, starting transfers between devices, shards(): pair_row = lax.ppermute(to_pair, 'lat', swap_perm('lat', 1))  1.88 us
  transfers between devices with their start and end apart: 9, of which 7 were waited for; matrix products, arithmetic and copies ran while one was open for 0% of the time, Pallas kernels for 3%

profile of v16, /device:TPU:8, one launch (start us, length us, event | category | flops | bytes accessed | tf_op | source)
XLA Modules:
  0.0 49.8 jit_solution(6188419451016070786)
XLA Ops:
  0.0 0.0 copy-start
  0.0 0.9 %copy-done = f32[32,16,128]{2,1,0:T(8,128)S(1)} copy-done((f32[32,16,128]{2,1,0:T(8,128)S(1)}, f32[32,16,128]{2,1,0:T(8,128)}, u32[]{:S(2)}) %copy-start) | copy-done | bytes 262168
  1.0 0.1 collective-permute-start
  1.1 4.2 %collective-permute-start.1 = (f32[32,128]{1,0:T(8,128)S(1)}, f32[32,128]{1,0:T(8,128)S(1)}, u32[]{:S(2)}, u32[]{:S(2)}) collective-permute-start(f32[32,128]{1,0:T(8,128)S(1)} %get-tuple-element.26), channel_id=1, source_target_pairs={{32,64},{64,32},{96,128},{128,96},{160,192},{192,160},{33,65},{65,... | collective-permute-start | bytes 49160 | tf_op jit(solution)/shard_map/ppermute | solution.py:397
  5.3 0.0 collective-permute-done.near_side
  5.3 1.4 %collective-permute-done.1.far_side = f32[32,128]{1,0:T(8,128)S(1)} collective-permute-done((f32[32,128]{1,0:T(8,128)S(1)}, f32[32,128]{1,0:T(8,128)S(1)}, u32[]{:S(2)}, u32[]{:S(2)}) %collective-permute-start.1) | collective-permute-done | bytes 16416 | tf_op jit(solution)/shard_map/ppermute | solution.py:397
  6.7 1.3 %shard_map.18 = (f32[512,128]{1,0:T(8,128)}, f32[16,32,128]{2,1,0:T(8,128)S(1)}, f32[16,32,128]{2,1,0:T(8,128)S(1)}, f32[16,32,128]{2,1,0:T(8,128)S(1)}, f32[528,128]{1,0:T(8,128)S(1)}) custom-call(f32[512,128]{1,0:T(8,128)S(1)} %bitcast.5, f32[32,128]{1,0:T(8,128)S(1)} %collective-permute-done.near_side, f32[32,128]{1,0:T(8,128)S(1)} %collective-permute-done.1.far_side), custom_call_target="tpu_custom_call" | custom-call | flops 1000000 | bytes 500000 | tf_op jit(solution)/shard_map/pallas_call | solution.py:404
  8.0 0.0 copy-start.1
  8.0 10.9 %all-to-all-start = ((f32[32,16,128]{2,1,0:T(8,128)}), f32[32,16,128]{2,1,0:T(8,128)S(1)}, u32[]{:S(2)}, u32[]{:S(2)}) async-start(f32[32,16,128]{2,1,0:T(8,128)} %bitcast.1), calls=%async_computation | async-start | bytes 524288 | tf_op jit(solution)/shard_map/all_to_all | solution.py:409
  18.9 0.0 copy-done.1
  18.9 0.1 shard_map.19
  19.0 1.9 %collective-permute-start.2 = (f32[33,128]{1,0:T(8,128)S(1)}, f32[33,128]{1,0:T(8,128)S(1)}, u32[]{:S(2)}, u32[]{:S(2)}) collective-permute-start(f32[33,128]{1,0:T(8,128)S(1)} %get-tuple-element.29), channel_id=1, source_target_pairs={{0,1},{1,0},{2,3},{3,2},{4,5},{5,4},{6,7},{7,6},{8,9},{9,8},{10,11... | collective-permute-start | bytes 50696 | tf_op jit(solution)/shard_map/ppermute | solution.py:403
  20.9 0.7 %collective-permute-start.3 = (f32[33,128]{1,0:T(8,128)S(1)}, f32[33,128]{1,0:T(8,128)S(1)}, u32[]{:S(2)}, u32[]{:S(2)}) collective-permute-start(f32[33,128]{1,0:T(8,128)S(1)} %get-tuple-element.30), channel_id=1, source_target_pairs={{1,2},{2,1},{3,4},{4,3},{5,6},{6,5},{7,8},{8,7},{9,10},{10,9},{11,... | collective-permute-start | bytes 50696 | tf_op jit(solution)/shard_map/ppermute | solution.py:402
  21.6 6.0 %collective-permute-done.2.pair_row = f32[33,128]{1,0:T(8,128)S(1)} collective-permute-done((f32[33,128]{1,0:T(8,128)S(1)}, f32[33,128]{1,0:T(8,128)S(1)}, u32[]{:S(2)}, u32[]{:S(2)}) %collective-permute-start.2) | collective-permute-done | bytes 16928 | tf_op jit(solution)/shard_map/ppermute | solution.py:403
  27.6 0.0 collective-permute-done.3.next_row
  27.6 0.3 shard_map.20
  27.9 0.1 collective-permute-start.4
  28.0 0.7 %shard_map.22.solved_x = f32[512,128]{1,0:T(8,128)S(1)} custom-call(f32[512,128]{1,0:T(8,128)S(1)} %bitcast.8, f32[528,128]{1,0:T(8,128)S(1)} %get-tuple-element.32.smooth), custom_call_target="tpu_custom_call" | custom-call | flops 1000000 | bytes 500000 | tf_op jit(solution)/shard_map/pallas_call | solution.py:414
  28.7 0.5 %collective-permute-done.4.refs_1_.near = f32[5,16,128]{2,1,0:T(8,128)S(1)} collective-permute-done((f32[5,16,128]{2,1,0:T(8,128)S(1)}, f32[5,16,128]{2,1,0:T(8,128)S(1)}, u32[]{:S(2)}, u32[]{:S(2)}) %collective-permute-start.4) | collective-permute-done | bytes 40992 | tf_op jit(solution)/shard_map/ppermute | solution.py:413
  29.3 2.4 %all-to-all-done = f32[32,16,128]{2,1,0:T(8,128)S(1)} async-done(((f32[32,16,128]{2,1,0:T(8,128)}), f32[32,16,128]{2,1,0:T(8,128)S(1)}, u32[]{:S(2)}, u32[]{:S(2)}) %all-to-all-start) | async-done | bytes 262176 | tf_op jit(solution)/shard_map/all_to_all | solution.py:409
  31.6 0.8 %shard_map.23 = f32[32,4,128]{2,1,0:T(4,128)} custom-call(f32[512,128]{1,0:T(8,128)S(1)} %bitcast.9), custom_call_target="tpu_custom_call" | custom-call | flops 1000000 | bytes 500000 | tf_op jit(solution)/shard_map/pallas_call | solution.py:427
  32.5 6.4 %all-to-all-start.1 = ((f32[32,4,128]{2,1,0:T(4,128)}), f32[32,4,128]{2,1,0:T(4,128)S(1)}, u32[]{:S(2)}, u32[]{:S(2)}) async-start(f32[32,4,128]{2,1,0:T(4,128)} %shard_map.23), calls=%async_computation.1 | async-start | bytes 131072 | tf_op jit(solution)/shard_map/all_to_all | solution.py:435
  38.9 0.1 collective-permute-start.5
  39.0 4.0 %collective-permute-done.5.refs_1_.pair = f32[5,16,128]{2,1,0:T(8,128)S(1)} collective-permute-done((f32[5,16,128]{2,1,0:T(8,128)S(1)}, f32[5,16,128]{2,1,0:T(8,128)S(1)}, u32[]{:S(2)}, u32[]{:S(2)}) %collective-permute-start.5) | collective-permute-done | bytes 40992 | tf_op jit(solution)/shard_map/ppermute | solution.py:429
  43.0 1.7 %collective-permute-start.6 = (f32[5,16,128]{2,1,0:T(8,128)S(1)}, f32[5,16,128]{2,1,0:T(8,128)S(1)}, u32[]{:S(2)}, u32[]{:S(2)}) collective-permute-start(f32[5,16,128]{2,1,0:T(8,128)S(1)} %shard_map.24), channel_id=1, source_target_pairs={{0,192},{32,224},{64,128},{96,160},{128,64},{160,96},{192,0},{224,... | collective-permute-start | bytes 122888 | tf_op jit(solution)/shard_map/ppermute | solution.py:431
  44.6 2.4 %collective-permute-done.6.quad = f32[5,16,128]{2,1,0:T(8,128)S(1)} collective-permute-done((f32[5,16,128]{2,1,0:T(8,128)S(1)}, f32[5,16,128]{2,1,0:T(8,128)S(1)}, u32[]{:S(2)}, u32[]{:S(2)}) %collective-permute-start.6) | collective-permute-done | bytes 40992 | tf_op jit(solution)/shard_map/ppermute | solution.py:431
  47.1 0.1 shard_map.25.others
  47.2 1.7 %all-to-all-done.1.solved = f32[32,4,128]{2,1,0:T(4,128)S(1)} async-done(((f32[32,4,128]{2,1,0:T(4,128)}), f32[32,4,128]{2,1,0:T(4,128)S(1)}, u32[]{:S(2)}, u32[]{:S(2)}) %all-to-all-start.1) | async-done | bytes 65568 | tf_op jit(solution)/shard_map/all_to_all | solution.py:435
  48.9 0.9 %shard_map.26 = f32[512,128]{1,0:T(8,128)} custom-call(f32[32,4,128]{2,1,0:T(4,128)S(1)} %all-to-all-done.1.solved, f32[16,32,128]{2,1,0:T(8,128)S(1)} %get-tuple-element.36.factor, f32[16,32,128]{2,1,0:T(8,128)S(1)} %get-tuple-element.37.back, f32[16,32,128]{2,1,0:T(8,128)S(1)} %get-tuple-element.38.rest, f32[512,128]{1,0:T(8,128)S(1)} %shard_map.25.others), custom_call_target="tpu_custom_call" | custom-call | flops 1000000 | bytes 500000 | tf_op jit(solution)/shard_map/pallas_call | solution.py:436
  (3 shorter events, 0.1 us)
Async XLA Ops:
  0.0 0.9 %copy-start = (f32[32,16,128]{2,1,0:T(8,128)S(1)}, f32[32,16,128]{2,1,0:T(8,128)}, u32[]{:S(2)}) copy-start(f32[32,16,128]{2,1,0:T(8,128)} %param.1) | copy-start | bytes 786436
  1.0 4.3 %collective-permute-start = (f32[32,128]{1,0:T(8,128)S(1)}, f32[32,128]{1,0:T(8,128)S(1)}, u32[]{:S(2)}, u32[]{:S(2)}) collective-permute-start(f32[32,128]{1,0:T(8,128)S(1)} %get-tuple-element.25), channel_id=1, source_target_pairs={{0,32},{32,0},{64,96},{96,64},{128,160},{160,128},{192,224},{224,1... | collective-permute-start | bytes 49160 | tf_op jit(solution)/shard_map/ppermute | solution.py:398
  1.1 5.6 %collective-permute-start.1 = (f32[32,128]{1,0:T(8,128)S(1)}, f32[32,128]{1,0:T(8,128)S(1)}, u32[]{:S(2)}, u32[]{:S(2)}) collective-permute-start(f32[32,128]{1,0:T(8,128)S(1)} %get-tuple-element.26), channel_id=1, source_target_pairs={{32,64},{64,32},{96,128},{128,96},{160,192},{192,160},{33,65},{65,... | collective-permute-start | bytes 49160 | tf_op jit(solution)/shard_map/ppermute | solution.py:397
  8.0 10.9 %copy-start.1 = (f32[32,16,128]{2,1,0:T(8,128)S(1)}, f32[32,16,128]{2,1,0:T(8,128)}, u32[]{:S(2)}) copy-start(f32[32,16,128]{2,1,0:T(8,128)} %param.1) | copy-start | bytes 786436
  8.0 23.7 %all-to-all-start = ((f32[32,16,128]{2,1,0:T(8,128)}), f32[32,16,128]{2,1,0:T(8,128)S(1)}, u32[]{:S(2)}, u32[]{:S(2)}) async-start(f32[32,16,128]{2,1,0:T(8,128)} %bitcast.1), calls=%async_computation | async-start | bytes 524288 | tf_op jit(solution)/shard_map/all_to_all | solution.py:409
  19.0 8.6 %collective-permute-start.2 = (f32[33,128]{1,0:T(8,128)S(1)}, f32[33,128]{1,0:T(8,128)S(1)}, u32[]{:S(2)}, u32[]{:S(2)}) collective-permute-start(f32[33,128]{1,0:T(8,128)S(1)} %get-tuple-element.29), channel_id=1, source_target_pairs={{0,1},{1,0},{2,3},{3,2},{4,5},{5,4},{6,7},{7,6},{8,9},{9,8},{10,11... | collective-permute-start | bytes 50696 | tf_op jit(solution)/shard_map/ppermute | solution.py:403
  20.9 6.7 %collective-permute-start.3 = (f32[33,128]{1,0:T(8,128)S(1)}, f32[33,128]{1,0:T(8,128)S(1)}, u32[]{:S(2)}, u32[]{:S(2)}) collective-permute-start(f32[33,128]{1,0:T(8,128)S(1)} %get-tuple-element.30), channel_id=1, source_target_pairs={{1,2},{2,1},{3,4},{4,3},{5,6},{6,5},{7,8},{8,7},{9,10},{10,9},{11,... | collective-permute-start | bytes 50696 | tf_op jit(solution)/shard_map/ppermute | solution.py:402
  27.9 1.3 %collective-permute-start.4 = (f32[5,16,128]{2,1,0:T(8,128)S(1)}, f32[5,16,128]{2,1,0:T(8,128)S(1)}, u32[]{:S(2)}, u32[]{:S(2)}) collective-permute-start(f32[5,16,128]{2,1,0:T(8,128)S(1)} %get-tuple-element.31.refs_0_.own), channel_id=1, source_target_pairs={{0,32},{32,0},{64,96},{96,64},{128,160},{160,128},{192,224},{224,1... | collective-permute-start | bytes 122888 | tf_op jit(solution)/shard_map/ppermute | solution.py:413
  32.5 16.4 %all-to-all-start.1 = ((f32[32,4,128]{2,1,0:T(4,128)}), f32[32,4,128]{2,1,0:T(4,128)S(1)}, u32[]{:S(2)}, u32[]{:S(2)}) async-start(f32[32,4,128]{2,1,0:T(4,128)} %shard_map.23), calls=%async_computation.1 | async-start | bytes 131072 | tf_op jit(solution)/shard_map/all_to_all | solution.py:435
  38.9 4.1 %collective-permute-start.5 = (f32[5,16,128]{2,1,0:T(8,128)S(1)}, f32[5,16,128]{2,1,0:T(8,128)S(1)}, u32[]{:S(2)}, u32[]{:S(2)}) collective-permute-start(f32[5,16,128]{2,1,0:T(8,128)S(1)} %shard_map.21.refs_0_), channel_id=1, source_target_pairs={{0,64},{32,96},{64,0},{96,32},{128,192},{160,224},{192,128},{224,1... | collective-permute-start | bytes 122888 | tf_op jit(solution)/shard_map/ppermute | solution.py:429
  43.0 4.1 %collective-permute-start.6 = (f32[5,16,128]{2,1,0:T(8,128)S(1)}, f32[5,16,128]{2,1,0:T(8,128)S(1)}, u32[]{:S(2)}, u32[]{:S(2)}) collective-permute-start(f32[5,16,128]{2,1,0:T(8,128)S(1)} %shard_map.24), channel_id=1, source_target_pairs={{0,192},{32,224},{64,128},{96,160},{128,64},{160,96},{192,0},{224,... | collective-permute-start | bytes 122888 | tf_op jit(solution)/shard_map/ppermute | solution.py:431

commit v17 on v16

--- a/solution.py
+++ b/solution.py
@@ -428,7 +428,7 @@
     ends, pair_own = lax.optimization_barrier((ends, pair_own))
     pair = lax.ppermute(pair_own, "depth", swap_perm("depth", 2))
     quad_own = call(lambda *refs: join_kernel(2, *refs), port)(pair_own, pair)
-    quad = lax.ppermute(quad_own, "depth", swap_perm("depth", 6))
+    quad = lax.ppermute(quad_own, "depth", swap_perm("depth", 4))
     others = call(finish_plane_kernel, whole)(
         z_port, near, pair, quad, z_factor, z_back, z_rest, z_mid, solved_x
     )

time: 50.1 us -> 50.2 us (level)
  waiting for transfers between devices: 18.5 us -> 17.7 us
  starting transfers between devices: 25.9 us -> 26.6 us
    all_to_all x1, waiting for transfers between devices: 1.69 us -> 0.19 us  [shards(): ends_y = lax.all_to_all(ends, 'lat', 0, 0, tiled=True)]
    ppermute x1, waiting for transfers between devices: 2.43 us -> 3.21 us  [shards(): quad = lax.ppermute(quad_own, 'depth', swap_perm('depth', 4))]
    ppermute x1, starting transfers between devices: 1.66 us -> 2.38 us  [shards(): quad = lax.ppermute(quad_own, 'depth', swap_perm('depth', 4))]
where the time goes in v17:
time: 50.2 us; the launch traced here: 49.8 us
  starting transfers between devices  26.6 us (53%)
  waiting for transfers between devices  17.7 us (35%)
  Pallas kernels  4.33 us (9%)
  local copies, waits for them, and re-layouts  0.95 us (2%)
    all_to_all x1, starting transfers between devices, shards(): ports = lax.all_to_all(y_port, 'lat', 0, 0, tiled=True)  10.9 us
    all_to_all x1, starting transfers between devices, shards(): ends_y = lax.all_to_all(ends, 'lat', 0, 0, tiled=True)  6.37 us
    ppermute x1, waiting for transfers between devices, shards(): pair_row = lax.ppermute(to_pair, 'lat', swap_perm('lat', 1))  6.04 us
    ppermute x1, starting transfers between devices, shards(): far_side = lax.ppermute(to_far, 'depth', next_perm('depth'))  4.18 us
    ppermute x1, waiting for transfers between devices, shards(): pair = lax.ppermute(pair_own, 'depth', swap_perm('depth', 2))  3.99 us
    ppermute x1, waiting for transfers between devices, shards(): quad = lax.ppermute(quad_own, 'depth', swap_perm('depth', 4))  3.21 us
    ppermute x1, starting transfers between devices, shards(): quad = lax.ppermute(quad_own, 'depth', swap_perm('depth', 4))  2.38 us
    all_to_all x1, waiting for transfers between devices, shards(): ports = lax.all_to_all(y_port, 'lat', 0, 0, tiled=True)  2.38 us
  transfers between devices with their start and end apart: 9, of which 7 were waited for; matrix products, arithmetic and copies ran while one was open for 0% of the time, Pallas kernels for 3%

profile of v17, /device:TPU:8, one launch (start us, length us, event | category | flops | bytes accessed | tf_op | source)
XLA Modules:
  0.0 49.8 jit_solution(4248262156435731722)
XLA Ops:
  0.0 0.0 copy-start
  0.0 0.9 %copy-done = f32[32,16,128]{2,1,0:T(8,128)S(1)} copy-done((f32[32,16,128]{2,1,0:T(8,128)S(1)}, f32[32,16,128]{2,1,0:T(8,128)}, u32[]{:S(2)}) %copy-start) | copy-done | bytes 262168
  1.0 0.1 collective-permute-start
  1.1 4.2 %collective-permute-start.1 = (f32[32,128]{1,0:T(8,128)S(1)}, f32[32,128]{1,0:T(8,128)S(1)}, u32[]{:S(2)}, u32[]{:S(2)}) collective-permute-start(f32[32,128]{1,0:T(8,128)S(1)} %get-tuple-element.26), channel_id=1, source_target_pairs={{32,64},{64,32},{96,128},{128,96},{160,192},{192,160},{33,65},{65,... | collective-permute-start | bytes 49160 | tf_op jit(solution)/shard_map/ppermute | solution.py:397
  5.3 0.0 collective-permute-done.near_side
  5.3 1.4 %collective-permute-done.1.far_side = f32[32,128]{1,0:T(8,128)S(1)} collective-permute-done((f32[32,128]{1,0:T(8,128)S(1)}, f32[32,128]{1,0:T(8,128)S(1)}, u32[]{:S(2)}, u32[]{:S(2)}) %collective-permute-start.1) | collective-permute-done | bytes 16416 | tf_op jit(solution)/shard_map/ppermute | solution.py:397
  6.7 1.3 %shard_map.18 = (f32[512,128]{1,0:T(8,128)}, f32[16,32,128]{2,1,0:T(8,128)S(1)}, f32[16,32,128]{2,1,0:T(8,128)S(1)}, f32[16,32,128]{2,1,0:T(8,128)S(1)}, f32[528,128]{1,0:T(8,128)S(1)}) custom-call(f32[512,128]{1,0:T(8,128)S(1)} %bitcast.5, f32[32,128]{1,0:T(8,128)S(1)} %collective-permute-done.near_side, f32[32,128]{1,0:T(8,128)S(1)} %collective-permute-done.1.far_side), custom_call_target="tpu_custom_call" | custom-call | flops 1000000 | bytes 500000 | tf_op jit(solution)/shard_map/pallas_call | solution.py:404
  8.0 0.0 copy-start.1
  8.0 10.9 %all-to-all-start = ((f32[32,16,128]{2,1,0:T(8,128)}), f32[32,16,128]{2,1,0:T(8,128)S(1)}, u32[]{:S(2)}, u32[]{:S(2)}) async-start(f32[32,16,128]{2,1,0:T(8,128)} %bitcast.1), calls=%async_computation | async-start | bytes 524288 | tf_op jit(solution)/shard_map/all_to_all | solution.py:409
  18.9 0.0 copy-done.1
  18.9 0.1 shard_map.19
  19.0 1.9 %collective-permute-start.2 = (f32[33,128]{1,0:T(8,128)S(1)}, f32[33,128]{1,0:T(8,128)S(1)}, u32[]{:S(2)}, u32[]{:S(2)}) collective-permute-start(f32[33,128]{1,0:T(8,128)S(1)} %get-tuple-element.29), channel_id=1, source_target_pairs={{0,1},{1,0},{2,3},{3,2},{4,5},{5,4},{6,7},{7,6},{8,9},{9,8},{10,11... | collective-permute-start | bytes 50696 | tf_op jit(solution)/shard_map/ppermute | solution.py:403
  20.9 0.7 %collective-permute-start.3 = (f32[33,128]{1,0:T(8,128)S(1)}, f32[33,128]{1,0:T(8,128)S(1)}, u32[]{:S(2)}, u32[]{:S(2)}) collective-permute-start(f32[33,128]{1,0:T(8,128)S(1)} %get-tuple-element.30), channel_id=1, source_target_pairs={{1,2},{2,1},{3,4},{4,3},{5,6},{6,5},{7,8},{8,7},{9,10},{10,9},{11,... | collective-permute-start | bytes 50696 | tf_op jit(solution)/shard_map/ppermute | solution.py:402
  21.6 6.0 %collective-permute-done.2.pair_row = f32[33,128]{1,0:T(8,128)S(1)} collective-permute-done((f32[33,128]{1,0:T(8,128)S(1)}, f32[33,128]{1,0:T(8,128)S(1)}, u32[]{:S(2)}, u32[]{:S(2)}) %collective-permute-start.2) | collective-permute-done | bytes 16928 | tf_op jit(solution)/shard_map/ppermute | solution.py:403
  27.6 0.0 collective-permute-done.3.next_row
  27.6 0.3 shard_map.20
  27.9 0.1 collective-permute-start.4
  28.0 0.7 %shard_map.22.solved_x = f32[512,128]{1,0:T(8,128)S(1)} custom-call(f32[512,128]{1,0:T(8,128)S(1)} %bitcast.8, f32[528,128]{1,0:T(8,128)S(1)} %get-tuple-element.32.smooth), custom_call_target="tpu_custom_call" | custom-call | flops 1000000 | bytes 500000 | tf_op jit(solution)/shard_map/pallas_call | solution.py:414
  28.7 0.5 %collective-permute-done.4.refs_1_.near = f32[5,16,128]{2,1,0:T(8,128)S(1)} collective-permute-done((f32[5,16,128]{2,1,0:T(8,128)S(1)}, f32[5,16,128]{2,1,0:T(8,128)S(1)}, u32[]{:S(2)}, u32[]{:S(2)}) %collective-permute-start.4) | collective-permute-done | bytes 40992 | tf_op jit(solution)/shard_map/ppermute | solution.py:413
  29.3 2.4 %all-to-all-done = f32[32,16,128]{2,1,0:T(8,128)S(1)} async-done(((f32[32,16,128]{2,1,0:T(8,128)}), f32[32,16,128]{2,1,0:T(8,128)S(1)}, u32[]{:S(2)}, u32[]{:S(2)}) %all-to-all-start) | async-done | bytes 262176 | tf_op jit(solution)/shard_map/all_to_all | solution.py:409
  31.6 0.8 %shard_map.23 = f32[32,4,128]{2,1,0:T(4,128)} custom-call(f32[512,128]{1,0:T(8,128)S(1)} %bitcast.9), custom_call_target="tpu_custom_call" | custom-call | flops 1000000 | bytes 500000 | tf_op jit(solution)/shard_map/pallas_call | solution.py:427
  32.5 6.4 %all-to-all-start.1 = ((f32[32,4,128]{2,1,0:T(4,128)}), f32[32,4,128]{2,1,0:T(4,128)S(1)}, u32[]{:S(2)}, u32[]{:S(2)}) async-start(f32[32,4,128]{2,1,0:T(4,128)} %shard_map.23), calls=%async_computation.1 | async-start | bytes 131072 | tf_op jit(solution)/shard_map/all_to_all | solution.py:435
  38.9 0.1 collective-permute-start.5
  39.0 4.0 %collective-permute-done.5.refs_1_.pair = f32[5,16,128]{2,1,0:T(8,128)S(1)} collective-permute-done((f32[5,16,128]{2,1,0:T(8,128)S(1)}, f32[5,16,128]{2,1,0:T(8,128)S(1)}, u32[]{:S(2)}, u32[]{:S(2)}) %collective-permute-start.5) | collective-permute-done | bytes 40992 | tf_op jit(solution)/shard_map/ppermute | solution.py:429
  43.0 2.4 %collective-permute-start.6 = (f32[5,16,128]{2,1,0:T(8,128)S(1)}, f32[5,16,128]{2,1,0:T(8,128)S(1)}, u32[]{:S(2)}, u32[]{:S(2)}) collective-permute-start(f32[5,16,128]{2,1,0:T(8,128)S(1)} %shard_map.24), channel_id=1, source_target_pairs={{0,128},{32,160},{64,192},{96,224},{128,0},{160,32},{192,64},{224,... | collective-permute-start | bytes 122888 | tf_op jit(solution)/shard_map/ppermute | solution.py:431
  45.4 3.2 %collective-permute-done.6.quad = f32[5,16,128]{2,1,0:T(8,128)S(1)} collective-permute-done((f32[5,16,128]{2,1,0:T(8,128)S(1)}, f32[5,16,128]{2,1,0:T(8,128)S(1)}, u32[]{:S(2)}, u32[]{:S(2)}) %collective-permute-start.6) | collective-permute-done | bytes 40992 | tf_op jit(solution)/shard_map/ppermute | solution.py:431
  48.6 0.1 shard_map.25.others
  48.7 0.2 all-to-all-done.1.solved
  48.9 0.9 %shard_map.26 = f32[512,128]{1,0:T(8,128)} custom-call(f32[32,4,128]{2,1,0:T(4,128)S(1)} %all-to-all-done.1.solved, f32[16,32,128]{2,1,0:T(8,128)S(1)} %get-tuple-element.36.factor, f32[16,32,128]{2,1,0:T(8,128)S(1)} %get-tuple-element.37.back, f32[16,32,128]{2,1,0:T(8,128)S(1)} %get-tuple-element.38.rest, f32[512,128]{1,0:T(8,128)S(1)} %shard_map.25.others), custom_call_target="tpu_custom_call" | custom-call | flops 1000000 | bytes 500000 | tf_op jit(solution)/shard_map/pallas_call | solution.py:436
  (3 shorter events, 0.1 us)
Async XLA Ops:
  0.0 0.9 %copy-start = (f32[32,16,128]{2,1,0:T(8,128)S(1)}, f32[32,16,128]{2,1,0:T(8,128)}, u32[]{:S(2)}) copy-start(f32[32,16,128]{2,1,0:T(8,128)} %param.1) | copy-start | bytes 786436
  1.0 4.3 %collective-permute-start = (f32[32,128]{1,0:T(8,128)S(1)}, f32[32,128]{1,0:T(8,128)S(1)}, u32[]{:S(2)}, u32[]{:S(2)}) collective-permute-start(f32[32,128]{1,0:T(8,128)S(1)} %get-tuple-element.25), channel_id=1, source_target_pairs={{0,32},{32,0},{64,96},{96,64},{128,160},{160,128},{192,224},{224,1... | collective-permute-start | bytes 49160 | tf_op jit(solution)/shard_map/ppermute | solution.py:398
  1.1 5.6 %collective-permute-start.1 = (f32[32,128]{1,0:T(8,128)S(1)}, f32[32,128]{1,0:T(8,128)S(1)}, u32[]{:S(2)}, u32[]{:S(2)}) collective-permute-start(f32[32,128]{1,0:T(8,128)S(1)} %get-tuple-element.26), channel_id=1, source_target_pairs={{32,64},{64,32},{96,128},{128,96},{160,192},{192,160},{33,65},{65,... | collective-permute-start | bytes 49160 | tf_op jit(solution)/shard_map/ppermute | solution.py:397
  8.0 10.9 %copy-start.1 = (f32[32,16,128]{2,1,0:T(8,128)S(1)}, f32[32,16,128]{2,1,0:T(8,128)}, u32[]{:S(2)}) copy-start(f32[32,16,128]{2,1,0:T(8,128)} %param.1) | copy-start | bytes 786436
  8.0 23.7 %all-to-all-start = ((f32[32,16,128]{2,1,0:T(8,128)}), f32[32,16,128]{2,1,0:T(8,128)S(1)}, u32[]{:S(2)}, u32[]{:S(2)}) async-start(f32[32,16,128]{2,1,0:T(8,128)} %bitcast.1), calls=%async_computation | async-start | bytes 524288 | tf_op jit(solution)/shard_map/all_to_all | solution.py:409
  19.0 8.6 %collective-permute-start.2 = (f32[33,128]{1,0:T(8,128)S(1)}, f32[33,128]{1,0:T(8,128)S(1)}, u32[]{:S(2)}, u32[]{:S(2)}) collective-permute-start(f32[33,128]{1,0:T(8,128)S(1)} %get-tuple-element.29), channel_id=1, source_target_pairs={{0,1},{1,0},{2,3},{3,2},{4,5},{5,4},{6,7},{7,6},{8,9},{9,8},{10,11... | collective-permute-start | bytes 50696 | tf_op jit(solution)/shard_map/ppermute | solution.py:403
  20.9 6.7 %collective-permute-start.3 = (f32[33,128]{1,0:T(8,128)S(1)}, f32[33,128]{1,0:T(8,128)S(1)}, u32[]{:S(2)}, u32[]{:S(2)}) collective-permute-start(f32[33,128]{1,0:T(8,128)S(1)} %get-tuple-element.30), channel_id=1, source_target_pairs={{1,2},{2,1},{3,4},{4,3},{5,6},{6,5},{7,8},{8,7},{9,10},{10,9},{11,... | collective-permute-start | bytes 50696 | tf_op jit(solution)/shard_map/ppermute | solution.py:402
  27.9 1.3 %collective-permute-start.4 = (f32[5,16,128]{2,1,0:T(8,128)S(1)}, f32[5,16,128]{2,1,0:T(8,128)S(1)}, u32[]{:S(2)}, u32[]{:S(2)}) collective-permute-start(f32[5,16,128]{2,1,0:T(8,128)S(1)} %get-tuple-element.31.refs_0_.own), channel_id=1, source_target_pairs={{0,32},{32,0},{64,96},{96,64},{128,160},{160,128},{192,224},{224,1... | collective-permute-start | bytes 122888 | tf_op jit(solution)/shard_map/ppermute | solution.py:413
  32.5 16.4 %all-to-all-start.1 = ((f32[32,4,128]{2,1,0:T(4,128)}), f32[32,4,128]{2,1,0:T(4,128)S(1)}, u32[]{:S(2)}, u32[]{:S(2)}) async-start(f32[32,4,128]{2,1,0:T(4,128)} %shard_map.23), calls=%async_computation.1 | async-start | bytes 131072 | tf_op jit(solution)/shard_map/all_to_all | solution.py:435
  38.9 4.1 %collective-permute-start.5 = (f32[5,16,128]{2,1,0:T(8,128)S(1)}, f32[5,16,128]{2,1,0:T(8,128)S(1)}, u32[]{:S(2)}, u32[]{:S(2)}) collective-permute-start(f32[5,16,128]{2,1,0:T(8,128)S(1)} %shard_map.21.refs_0_), channel_id=1, source_target_pairs={{0,64},{32,96},{64,0},{96,32},{128,192},{160,224},{192,128},{224,1... | collective-permute-start | bytes 122888 | tf_op jit(solution)/shard_map/ppermute | solution.py:429
  43.0 5.6 %collective-permute-start.6 = (f32[5,16,128]{2,1,0:T(8,128)S(1)}, f32[5,16,128]{2,1,0:T(8,128)S(1)}, u32[]{:S(2)}, u32[]{:S(2)}) collective-permute-start(f32[5,16,128]{2,1,0:T(8,128)S(1)} %shard_map.24), channel_id=1, source_target_pairs={{0,128},{32,160},{64,192},{96,224},{128,0},{160,32},{192,64},{224,... | collective-permute-start | bytes 122888 | tf_op jit(solution)/shard_map/ppermute | solution.py:431

commit v18 on v16

--- a/solution.py
+++ b/solution.py
@@ -60,21 +60,6 @@
         ls + to_left * source,
         rt + to_right * source,
     ), (to_left, to_right, source * inverse)
-
-
-def edge_kernel(vol, near_side, far_side, sems):
-    odd = lax.axis_index("depth") & 1
-    high = (PLANES - 2) * ROWS
-    near_start = pl.multiple_of((1 - odd) * high, ROWS)
-    far_start = pl.multiple_of(odd * high, ROWS)
-    copies = (
-        pltpu.make_async_copy(vol.at[pl.ds(near_start, 2 * ROWS), :], near_side, sems.at[0]),
-        pltpu.make_async_copy(vol.at[pl.ds(far_start, 2 * ROWS), :], far_side, sems.at[1]),
-    )
-    for copy in copies:
-        copy.start()
-    for copy in copies:
-        copy.wait()
 
 
 def strided(ref, row):
@@ -388,12 +373,10 @@
     tall = shaped((PLANES + 1) * ROWS, COLS)
     port = shaped(5, ROWS, COLS)
     side = shaped(PLANES + 1, COLS)
-    to_near, to_far = call(
-        edge_kernel,
-        (shaped(2 * ROWS, COLS), shaped(2 * ROWS, COLS)),
-        (pltpu.SemaphoreType.DMA((2,)),),
-        in_specs=[pl.BlockSpec(memory_space=pl.ANY)],
-    )(flat)
+    odd = (lax.axis_index("depth") & 1) == 1
+    low_planes, high_planes = flat[: 2 * ROWS], flat[(PLANES - 2) * ROWS :]
+    to_near = jnp.where(odd, low_planes, high_planes)
+    to_far = jnp.where(odd, high_planes, low_planes)
     far_side = lax.ppermute(to_far, "depth", next_perm("depth"))
     near_side = lax.ppermute(to_near, "depth", swap_perm("depth", 1))
     to_pair, to_next = call(

time: 50.1 us -> 50.8 us (1.014)
  other arithmetic: 0 us -> 0.74 us
    select_n x0 -> x1, other arithmetic: none -> 0.74 us  [shards(): to_far = jnp.where(odd, high_planes, low_planes)]
where the time goes in v18:
time: 50.8 us; the launch traced here: 50.4 us
  starting transfers between devices  26.1 us (51%)
  waiting for transfers between devices  18.2 us (36%)
  Pallas kernels  4.3 us (8%)
  local copies, waits for them, and re-layouts  0.95 us (2%)
  other arithmetic  0.74 us (1%)
    all_to_all x1, starting transfers between devices, shards(): ports = lax.all_to_all(y_port, 'lat', 0, 0, tiled=True)  10.9 us
    all_to_all x1, starting transfers between devices, shards(): ends_y = lax.all_to_all(ends, 'lat', 0, 0, tiled=True)  6.64 us
    ppermute x1, waiting for transfers between devices, shards(): pair_row = lax.ppermute(to_pair, 'lat', swap_perm('lat', 1))  6.06 us
    ppermute x1, starting transfers between devices, shards(): far_side = lax.ppermute(to_far, 'depth', next_perm('depth'))  4.19 us
    ppermute x1, waiting for transfers between devices, shards(): pair = lax.ppermute(pair_own, 'depth', swap_perm('depth', 2))  3.99 us
    ppermute x1, waiting for transfers between devices, shards(): quad = lax.ppermute(quad_own, 'depth', swap_perm('depth', 6))  2.43 us
    all_to_all x1, waiting for transfers between devices, shards(): ports = lax.all_to_all(y_port, 'lat', 0, 0, tiled=True)  2.09 us
    ppermute x1, starting transfers between devices, shards(): pair_row = lax.ppermute(to_pair, 'lat', swap_perm('lat', 1))  1.88 us
  transfers between devices with their start and end apart: 9, of which 7 were waited for; matrix products, arithmetic and copies ran while one was open for 0% of the time, Pallas kernels for 3%

profile of v18, /device:TPU:8, one launch (start us, length us, event | category | flops | bytes accessed | tf_op | source)
XLA Modules:
  0.0 50.4 jit_solution(1415448044714720214)
XLA Ops:
  0.0 0.7 %slice_select_fusion = (f32[2,16,128]{2,1,0:T(8,128)S(1)}, f32[2,16,128]{2,1,0:T(8,128)S(1)}) fusion(f32[32,16,128]{2,1,0:T(8,128)} %param.1, pred[]{:T(512)S(6)} %eq.3), kind=kLoop, calls=%fused_computation | loop fusion | flops 8192 | bytes 65537 | tf_op jit(solution)/shard_map/jit(_where)/select_n | solution.py:379
  0.7 0.0 collective-permute-start
  0.7 4.2 %collective-permute-start.1 = (f32[32,128]{1,0:T(8,128)S(1)}, f32[32,128]{1,0:T(8,128)S(1)}, u32[]{:S(2)}, u32[]{:S(2)}) collective-permute-start(f32[32,128]{1,0:T(8,128)S(1)} %bitcast.11), channel_id=1, source_target_pairs={{32,64},{64,32},{96,128},{128,96},{160,192},{192,160},{33,65},{65,... | collective-permute-start | bytes 49160 | tf_op jit(solution)/shard_map/ppermute | solution.py:380
  4.9 0.0 collective-permute-done.near_side
  5.0 1.4 %collective-permute-done.1.far_side = f32[32,128]{1,0:T(8,128)S(1)} collective-permute-done((f32[32,128]{1,0:T(8,128)S(1)}, f32[32,128]{1,0:T(8,128)S(1)}, u32[]{:S(2)}, u32[]{:S(2)}) %collective-permute-start.1) | collective-permute-done | bytes 16416 | tf_op jit(solution)/shard_map/ppermute | solution.py:380
  6.4 0.0 copy-start
  6.4 0.9 %copy-done = f32[32,16,128]{2,1,0:T(8,128)S(1)} copy-done((f32[32,16,128]{2,1,0:T(8,128)S(1)}, f32[32,16,128]{2,1,0:T(8,128)}, u32[]{:S(2)}) %copy-start) | copy-done | bytes 262168
  7.3 1.3 %shard_map.17 = (f32[512,128]{1,0:T(8,128)}, f32[16,32,128]{2,1,0:T(8,128)S(1)}, f32[16,32,128]{2,1,0:T(8,128)S(1)}, f32[16,32,128]{2,1,0:T(8,128)S(1)}, f32[528,128]{1,0:T(8,128)S(1)}) custom-call(f32[512,128]{1,0:T(8,128)S(1)} %bitcast.6, f32[32,128]{1,0:T(8,128)S(1)} %collective-permute-done.near_side, f32[32,128]{1,0:T(8,128)S(1)} %collective-permute-done.1.far_side), custom_call_target="tpu_custom_call" | custom-call | flops 1000000 | bytes 500000 | tf_op jit(solution)/shard_map/pallas_call | solution.py:387
  8.6 0.0 copy-start.1
  8.6 10.9 %all-to-all-start = ((f32[32,16,128]{2,1,0:T(8,128)}), f32[32,16,128]{2,1,0:T(8,128)S(1)}, u32[]{:S(2)}, u32[]{:S(2)}) async-start(f32[32,16,128]{2,1,0:T(8,128)} %bitcast.3), calls=%async_computation | async-start | bytes 524288 | tf_op jit(solution)/shard_map/all_to_all | solution.py:392
  19.5 0.0 copy-done.1
  19.5 0.1 shard_map.18
  19.6 1.9 %collective-permute-start.2 = (f32[33,128]{1,0:T(8,128)S(1)}, f32[33,128]{1,0:T(8,128)S(1)}, u32[]{:S(2)}, u32[]{:S(2)}) collective-permute-start(f32[33,128]{1,0:T(8,128)S(1)} %get-tuple-element.25), channel_id=1, source_target_pairs={{0,1},{1,0},{2,3},{3,2},{4,5},{5,4},{6,7},{7,6},{8,9},{9,8},{10,11... | collective-permute-start | bytes 50696 | tf_op jit(solution)/shard_map/ppermute | solution.py:386
  21.5 0.7 %collective-permute-start.3 = (f32[33,128]{1,0:T(8,128)S(1)}, f32[33,128]{1,0:T(8,128)S(1)}, u32[]{:S(2)}, u32[]{:S(2)}) collective-permute-start(f32[33,128]{1,0:T(8,128)S(1)} %get-tuple-element.26), channel_id=1, source_target_pairs={{1,2},{2,1},{3,4},{4,3},{5,6},{6,5},{7,8},{8,7},{9,10},{10,9},{11,... | collective-permute-start | bytes 50696 | tf_op jit(solution)/shard_map/ppermute | solution.py:385
  22.1 6.1 %collective-permute-done.2.pair_row = f32[33,128]{1,0:T(8,128)S(1)} collective-permute-done((f32[33,128]{1,0:T(8,128)S(1)}, f32[33,128]{1,0:T(8,128)S(1)}, u32[]{:S(2)}, u32[]{:S(2)}) %collective-permute-start.2) | collective-permute-done | bytes 16928 | tf_op jit(solution)/shard_map/ppermute | solution.py:386
  28.2 0.0 collective-permute-done.3.next_row
  28.2 0.3 shard_map.19
  28.5 0.1 collective-permute-start.4
  28.6 0.7 %shard_map.21.solved_x = f32[512,128]{1,0:T(8,128)S(1)} custom-call(f32[512,128]{1,0:T(8,128)S(1)} %bitcast.9, f32[528,128]{1,0:T(8,128)S(1)} %get-tuple-element.28.smooth), custom_call_target="tpu_custom_call" | custom-call | flops 1000000 | bytes 500000 | tf_op jit(solution)/shard_map/pallas_call | solution.py:397
  29.3 0.5 %collective-permute-done.4.refs_1_.near = f32[5,16,128]{2,1,0:T(8,128)S(1)} collective-permute-done((f32[5,16,128]{2,1,0:T(8,128)S(1)}, f32[5,16,128]{2,1,0:T(8,128)S(1)}, u32[]{:S(2)}, u32[]{:S(2)}) %collective-permute-start.4) | collective-permute-done | bytes 40992 | tf_op jit(solution)/shard_map/ppermute | solution.py:396
  29.9 2.1 %all-to-all-done = f32[32,16,128]{2,1,0:T(8,128)S(1)} async-done(((f32[32,16,128]{2,1,0:T(8,128)}), f32[32,16,128]{2,1,0:T(8,128)S(1)}, u32[]{:S(2)}, u32[]{:S(2)}) %all-to-all-start) | async-done | bytes 262176 | tf_op jit(solution)/shard_map/all_to_all | solution.py:392
  32.0 0.8 %shard_map.22 = f32[32,4,128]{2,1,0:T(4,128)} custom-call(f32[512,128]{1,0:T(8,128)S(1)} %bitcast.10), custom_call_target="tpu_custom_call" | custom-call | flops 1000000 | bytes 500000 | tf_op jit(solution)/shard_map/pallas_call | solution.py:410
  32.8 6.6 %all-to-all-start.1 = ((f32[32,4,128]{2,1,0:T(4,128)}), f32[32,4,128]{2,1,0:T(4,128)S(1)}, u32[]{:S(2)}, u32[]{:S(2)}) async-start(f32[32,4,128]{2,1,0:T(4,128)} %shard_map.22), calls=%async_computation.1 | async-start | bytes 131072 | tf_op jit(solution)/shard_map/all_to_all | solution.py:418
  39.5 0.1 collective-permute-start.5
  39.6 4.0 %collective-permute-done.5.refs_1_.pair = f32[5,16,128]{2,1,0:T(8,128)S(1)} collective-permute-done((f32[5,16,128]{2,1,0:T(8,128)S(1)}, f32[5,16,128]{2,1,0:T(8,128)S(1)}, u32[]{:S(2)}, u32[]{:S(2)}) %collective-permute-start.5) | collective-permute-done | bytes 40992 | tf_op jit(solution)/shard_map/ppermute | solution.py:412
  43.6 1.7 %collective-permute-start.6 = (f32[5,16,128]{2,1,0:T(8,128)S(1)}, f32[5,16,128]{2,1,0:T(8,128)S(1)}, u32[]{:S(2)}, u32[]{:S(2)}) collective-permute-start(f32[5,16,128]{2,1,0:T(8,128)S(1)} %shard_map.23), channel_id=1, source_target_pairs={{0,192},{32,224},{64,128},{96,160},{128,64},{160,96},{192,0},{224,... | collective-permute-start | bytes 122888 | tf_op jit(solution)/shard_map/ppermute | solution.py:414
  45.2 2.4 %collective-permute-done.6.quad = f32[5,16,128]{2,1,0:T(8,128)S(1)} collective-permute-done((f32[5,16,128]{2,1,0:T(8,128)S(1)}, f32[5,16,128]{2,1,0:T(8,128)S(1)}, u32[]{:S(2)}, u32[]{:S(2)}) %collective-permute-start.6) | collective-permute-done | bytes 40992 | tf_op jit(solution)/shard_map/ppermute | solution.py:414
  47.7 0.1 shard_map.24.others
  47.8 1.7 %all-to-all-done.1.solved = f32[32,4,128]{2,1,0:T(4,128)S(1)} async-done(((f32[32,4,128]{2,1,0:T(4,128)}), f32[32,4,128]{2,1,0:T(4,128)S(1)}, u32[]{:S(2)}, u32[]{:S(2)}) %all-to-all-start.1) | async-done | bytes 65568 | tf_op jit(solution)/shard_map/all_to_all | solution.py:418
  49.5 0.9 %shard_map.25 = f32[512,128]{1,0:T(8,128)} custom-call(f32[32,4,128]{2,1,0:T(4,128)S(1)} %all-to-all-done.1.solved, f32[16,32,128]{2,1,0:T(8,128)S(1)} %get-tuple-element.32.factor, f32[16,32,128]{2,1,0:T(8,128)S(1)} %get-tuple-element.33.back, f32[16,32,128]{2,1,0:T(8,128)S(1)} %get-tuple-element.34.rest, f32[512,128]{1,0:T(8,128)S(1)} %shard_map.24.others), custom_call_target="tpu_custom_call" | custom-call | flops 1000000 | bytes 500000 | tf_op jit(solution)/shard_map/pallas_call | solution.py:419
  (2 shorter events, 0.0 us)
Async XLA Ops:
  0.7 4.2 %collective-permute-start = (f32[32,128]{1,0:T(8,128)S(1)}, f32[32,128]{1,0:T(8,128)S(1)}, u32[]{:S(2)}, u32[]{:S(2)}) collective-permute-start(f32[32,128]{1,0:T(8,128)S(1)} %bitcast.12), channel_id=1, source_target_pairs={{0,32},{32,0},{64,96},{96,64},{128,160},{160,128},{192,224},{224,1... | collective-permute-start | bytes 49160 | tf_op jit(solution)/shard_map/ppermute | solution.py:381
  0.7 5.6 %collective-permute-start.1 = (f32[32,128]{1,0:T(8,128)S(1)}, f32[32,128]{1,0:T(8,128)S(1)}, u32[]{:S(2)}, u32[]{:S(2)}) collective-permute-start(f32[32,128]{1,0:T(8,128)S(1)} %bitcast.11), channel_id=1, source_target_pairs={{32,64},{64,32},{96,128},{128,96},{160,192},{192,160},{33,65},{65,... | collective-permute-start | bytes 49160 | tf_op jit(solution)/shard_map/ppermute | solution.py:380
  6.4 0.9 %copy-start = (f32[32,16,128]{2,1,0:T(8,128)S(1)}, f32[32,16,128]{2,1,0:T(8,128)}, u32[]{:S(2)}) copy-start(f32[32,16,128]{2,1,0:T(8,128)} %param.1) | copy-start | bytes 786436
  8.6 10.9 %copy-start.1 = (f32[32,16,128]{2,1,0:T(8,128)S(1)}, f32[32,16,128]{2,1,0:T(8,128)}, u32[]{:S(2)}) copy-start(f32[32,16,128]{2,1,0:T(8,128)} %param.1) | copy-start | bytes 786436
  8.6 23.4 %all-to-all-start = ((f32[32,16,128]{2,1,0:T(8,128)}), f32[32,16,128]{2,1,0:T(8,128)S(1)}, u32[]{:S(2)}, u32[]{:S(2)}) async-start(f32[32,16,128]{2,1,0:T(8,128)} %bitcast.3), calls=%async_computation | async-start | bytes 524288 | tf_op jit(solution)/shard_map/all_to_all | solution.py:392
  19.6 8.6 %collective-permute-start.2 = (f32[33,128]{1,0:T(8,128)S(1)}, f32[33,128]{1,0:T(8,128)S(1)}, u32[]{:S(2)}, u32[]{:S(2)}) collective-permute-start(f32[33,128]{1,0:T(8,128)S(1)} %get-tuple-element.25), channel_id=1, source_target_pairs={{0,1},{1,0},{2,3},{3,2},{4,5},{5,4},{6,7},{7,6},{8,9},{9,8},{10,11... | collective-permute-start | bytes 50696 | tf_op jit(solution)/shard_map/ppermute | solution.py:386
  21.5 6.7 %collective-permute-start.3 = (f32[33,128]{1,0:T(8,128)S(1)}, f32[33,128]{1,0:T(8,128)S(1)}, u32[]{:S(2)}, u32[]{:S(2)}) collective-permute-start(f32[33,128]{1,0:T(8,128)S(1)} %get-tuple-element.26), channel_id=1, source_target_pairs={{1,2},{2,1},{3,4},{4,3},{5,6},{6,5},{7,8},{8,7},{9,10},{10,9},{11,... | collective-permute-start | bytes 50696 | tf_op jit(solution)/shard_map/ppermute | solution.py:385
  28.5 1.3 %collective-permute-start.4 = (f32[5,16,128]{2,1,0:T(8,128)S(1)}, f32[5,16,128]{2,1,0:T(8,128)S(1)}, u32[]{:S(2)}, u32[]{:S(2)}) collective-permute-start(f32[5,16,128]{2,1,0:T(8,128)S(1)} %get-tuple-element.27.refs_0_.own), channel_id=1, source_target_pairs={{0,32},{32,0},{64,96},{96,64},{128,160},{160,128},{192,224},{224,1... | collective-permute-start | bytes 122888 | tf_op jit(solution)/shard_map/ppermute | solution.py:396
  32.8 16.7 %all-to-all-start.1 = ((f32[32,4,128]{2,1,0:T(4,128)}), f32[32,4,128]{2,1,0:T(4,128)S(1)}, u32[]{:S(2)}, u32[]{:S(2)}) async-start(f32[32,4,128]{2,1,0:T(4,128)} %shard_map.22), calls=%async_computation.1 | async-start | bytes 131072 | tf_op jit(solution)/shard_map/all_to_all | solution.py:418
  39.5 4.1 %collective-permute-start.5 = (f32[5,16,128]{2,1,0:T(8,128)S(1)}, f32[5,16,128]{2,1,0:T(8,128)S(1)}, u32[]{:S(2)}, u32[]{:S(2)}) collective-permute-start(f32[5,16,128]{2,1,0:T(8,128)S(1)} %shard_map.20.refs_0_), channel_id=1, source_target_pairs={{0,64},{32,96},{64,0},{96,32},{128,192},{160,224},{192,128},{224,1... | collective-permute-start | bytes 122888 | tf_op jit(solution)/shard_map/ppermute | solution.py:412
  43.6 4.1 %collective-permute-start.6 = (f32[5,16,128]{2,1,0:T(8,128)S(1)}, f32[5,16,128]{2,1,0:T(8,128)S(1)}, u32[]{:S(2)}, u32[]{:S(2)}) collective-permute-start(f32[5,16,128]{2,1,0:T(8,128)S(1)} %shard_map.23), channel_id=1, source_target_pairs={{0,192},{32,224},{64,128},{96,160},{128,64},{160,96},{192,0},{224,... | collective-permute-start | bytes 122888 | tf_op jit(solution)/shard_map/ppermute | solution.py:414
